TPU v7x, 32 devices: a whole 2x2x4 slice. The times are simulated.
32 devices in a mesh: group: 4 (over y, x), shard: 8 (over z, core).
Axes of the slice: x: 2, y: 2, z: 4, core: 2. Of those that a mesh axis runs over, the one named last changes fastest.
Arguments:
- entity: float32 [16384, 400], P(('group', 'shard')), may hold values from -6 to 6
- entity_state: float32 [16384], P(('group', 'shard')), may hold values from 0.1 to 10
- relation: float32 [1345, 400], replicated, may hold values from -6 to 6
- relation_state: float32 [1345], replicated, may hold values from 10 to 1000
- src_send: int32 [32, 8, 128], P(('group', 'shard')), may hold values from 0 to 511
- dst_send: int32 [32, 8, 128], P(('group', 'shard')), may hold values from 0 to 511
- edge_source: int32 [32768], P(('group', 'shard')), may hold values from 0 to 1023
- edge_relation: int32 [32768], P(('group', 'shard')), may hold values from 0 to 1344
- edge_target: int32 [32768], P(('group', 'shard')), may hold values from 0 to 1023
- neg_slots: int32 [64, 1000], P(('group', 'shard')), may hold values from 0 to 1023
- edge_count: int32 [32], P(('group', 'shard')), may hold values from 1 to 1024, 10922 in all
Outputs:
- entity_new: float32 [16384, 400], P(('group', 'shard'))
- relation_new: float32 [1345, 400], replicated
- edge_loss: float32 [32768], P(('group', 'shard'))
Inputs may be any that keep to these rules, and one draw needn't show every extreme that they name: The live edges of a device are its first edge_count slots; some device has all 1024 live.
All inputs are finite; a program needn't handle non-finite values.
Results may differ from a plain program's by a relative error of at most 0.0003.
Values sent between devices are 32-bit elements; how exact they have to be, the bound alone decides.
No kernel may reach another device: no remote copies, remote signals or barrier semaphores. Data moves between devices by JAX's collectives and lax.ppermute only.
A program may use at most 128 MiB of HBM per device.

v0:
```python
import functools

import jax
import jax.numpy as jnp
from jax import lax
from jax.experimental import pallas as pl
from jax.experimental.pallas import tpu as pltpu
from jax.sharding import PartitionSpec as P


SPAN = 512
LANES = 128
CHUNK = 256


learn_rate = 0.5

F32, BF16, I32 = jnp.float32, jnp.bfloat16, jnp.int32
VMEM = pl.BlockSpec(memory_space=pltpu.VMEM)
SMEM = pl.BlockSpec(memory_space=pltpu.SMEM)
VMEM_LIMIT = 60 << 20


def kernel_call(kernel, outs, flops, moved, **kw):
    semantics = ("arbitrary",) if "grid" in kw else None
    return pl.pallas_call(
        kernel,
        out_shape=outs,
        compiler_params=pltpu.CompilerParams(
            vmem_limit_bytes=VMEM_LIMIT, dimension_semantics=semantics
        ),
        cost_estimate=pl.CostEstimate(flops=flops, bytes_accessed=moved, transcendentals=0),
        **kw,
    )


def shape(dims, dtype=F32):
    return jax.ShapeDtypeStruct(dims, dtype)


def held(dims):
    return pl.BlockSpec(dims, lambda i: (0,) * len(dims))


def split2(x):
    hi = x.astype(BF16)
    return hi, (x - hi.astype(F32)).astype(BF16)


def split3(x):
    hi = x.astype(BF16)
    rest = x - hi.astype(F32)
    mid = rest.astype(BF16)
    return hi, mid, (rest - mid.astype(F32)).astype(BF16)


def dot(a, b):
    return jnp.dot(a, b, preferred_element_type=F32)


def dot_nt(a, b):
    return lax.dot_general(a, b, (((1,), (1,)), ((), ())), preferred_element_type=F32)


def one_hot(mask):
    return jnp.where(mask, 1.0, 0.0).astype(BF16)


def rows_hot(length, slots):
    return one_hot(lax.broadcasted_iota(I32, (length, slots.shape[1]), 0) == slots)


def columns_hot(slots, length):
    return one_hot(lax.broadcasted_iota(I32, (slots.shape[0], length), 1) == slots)


def complex_product(a, b):
    half = a.shape[0] // 2
    ar, ai, br, bi = a[:half], a[half:], b[:half], b[half:]
    return jnp.concatenate([ar * br - ai * bi, ar * bi + ai * br], axis=0)


def conj_product(a, b):
    half = a.shape[0] // 2
    ar, ai, br, bi = a[:half], a[half:], b[:half], b[half:]
    return jnp.concatenate([ar * br + ai * bi, ai * br - ar * bi], axis=0)


def hops(peers):
    chips = peers // 2
    ahead = [(k, b) for k in range(1, chips) for b in (0, 1)]
    return ahead + [(0, 1), (0, 0)]


def partner(me, hop, peers, sign):
    chips = peers // 2
    return (me // 2 + sign * hop[0]) % chips * 2 + (me % 2 + hop[1]) % 2


def places_of(me, owner, peers):
    chips = peers // 2
    k = (me // 2 - owner // 2) % chips
    b = (me + owner) % 2
    return (k - 1) % chips * 2 + jnp.where(k == 0, 1 - b, b)


def pick_kernel(order_ref, rows_ref, slots_ref, *outs):
    hi, mid, lo = split3(rows_ref[...])
    block = slots_ref.shape[1]
    together = max(1, CHUNK // block)
    for first in range(0, len(outs), together):
        group = outs[first:first + together]
        slots = [slots_ref[pl.ds(order_ref[first + i], 1), :] for i in range(len(group))]
        hot = rows_hot(rows_ref.shape[1], jnp.concatenate(slots, axis=1))
        picked = dot(hi, hot) + dot(mid, hot) + dot(lo, hot)
        for i, out in enumerate(group):
            out[...] = picked[:, i * block:(i + 1) * block]


def pick_blocks(order, rows, slots):
    features, length = rows.shape
    block = slots.shape[1]
    count = order.shape[0]
    return kernel_call(
        pick_kernel, [shape((features, block))] * count,
        6 * features * length * count * block, 8 * features * count * block,
        in_specs=[SMEM, VMEM, VMEM], out_specs=[VMEM] * count,
    )(order, rows, slots)


def relation_kernel(rel_ref, edge_rel_ref, out_ref, pieces):
    count = rel_ref.shape[1]
    padded = pieces.shape[2]

    @pl.when(pl.program_id(0) == 0)
    def _():
        features = rel_ref.shape[0]
        tail = padded - count // LANES * LANES
        for piece, value in enumerate(split3(rel_ref[...])):
            pieces[piece, :, padded - tail:] = jnp.zeros((features, tail), BF16)
            pieces[piece, :, :count] = value

    hot = rows_hot(padded, edge_rel_ref[...])
    out_ref[...] = dot(pieces[0], hot) + dot(pieces[1], hot) + dot(pieces[2], hot)


def relation_rows(relation, edge_relation):
    features, count = relation.shape
    edges = edge_relation.shape[1]
    padded = pl.cdiv(count, LANES) * LANES
    return kernel_call(
        relation_kernel, shape((features, edges)),
        6 * features * padded * edges, 8 * features * edges,
        grid=(edges // CHUNK,),
        in_specs=[held((features, count)), pl.BlockSpec((1, CHUNK), lambda i: (0, i))],
        out_specs=pl.BlockSpec((features, CHUNK), lambda i: (0, i)),
        scratch_shapes=[pltpu.VMEM((3, features, padded), BF16)],
    )(relation, edge_relation)


def count_kernel(slots_ref, out_ref):
    table_rows = out_ref.shape[2]
    hits = lax.broadcasted_iota(I32, (slots_ref.shape[1], table_rows), 1) == slots_ref[0]
    out_ref[0] = jnp.sum(jnp.where(hits, 1.0, 0.0), axis=0, keepdims=True)


def slot_counts(neg_slots, table_rows):
    spans, negatives = neg_slots.shape
    return kernel_call(
        count_kernel, shape((spans, 1, table_rows)),
        2 * spans * negatives * table_rows, 512 * spans * negatives,
        grid=(spans,),
        in_specs=[pl.BlockSpec((1, negatives, 1), lambda i: (i, 0, 0))],
        out_specs=pl.BlockSpec((1, 1, table_rows), lambda i: (i, 0, 0)),
    )(neg_slots[:, :, None])


def hot_kernel(order_ref, slots_ref, out_ref):
    peers, block, _ = slots_ref.shape
    for j in range(peers):
        out_ref[j * block:(j + 1) * block, :] = columns_hot(slots_ref[order_ref[j]], out_ref.shape[1])


def home_hots(order, slots, rows):
    peers, block = slots.shape
    return kernel_call(
        hot_kernel, shape((peers * block, rows), BF16),
        2 * peers * block * rows, 2 * peers * block * rows,
        in_specs=[SMEM, VMEM], out_specs=VMEM,
    )(order, slots[:, :, None])


def query_kernel(*refs):
    edge_source_ref, rels_ref, *blocks = refs[:-4]
    heads_ref, columns_ref, rows_ref, pieces = refs[-4:]
    block = blocks[0].shape[1]

    @pl.when(pl.program_id(0) == 0)
    def _():
        for p, ref in enumerate(blocks):
            for piece, value in enumerate(split3(ref[...])):
                pieces[piece, :, p * block:(p + 1) * block] = value

    hot = rows_hot(pieces.shape[2], edge_source_ref[...])
    heads = dot(pieces[0], hot) + dot(pieces[1], hot) + dot(pieces[2], hot)
    heads_ref[...] = heads
    queries = complex_product(heads, rels_ref[...])
    hi, lo = split2(queries)
    columns_ref[0], columns_ref[1] = hi, lo
    hi, lo = split2(queries.T)
    rows_ref[...] = jnp.concatenate([hi, hi, lo], axis=1)


def query_rows(blocks, edge_source, rels):
    peers = len(blocks)
    features, block = blocks[0].shape
    edges = edge_source.shape[1]
    return kernel_call(
        query_kernel,
        [shape((features, edges)), shape((2, features, edges), BF16), shape((edges, 3 * features), BF16)],
        6 * features * peers * block * edges, 20 * features * edges,
        grid=(edges // CHUNK,),
        in_specs=[
            pl.BlockSpec((1, CHUNK), lambda i: (0, i)),
            pl.BlockSpec((features, CHUNK), lambda i: (0, i)),
        ] + [held((features, block))] * peers,
        out_specs=[
            pl.BlockSpec((features, CHUNK), lambda i: (0, i)),
            pl.BlockSpec((2, features, CHUNK), lambda i: (0, 0, i)),
            pl.BlockSpec((CHUNK, 3 * features), lambda i: (i, 0)),
        ],
        scratch_shapes=[pltpu.VMEM((3, features, peers * block), BF16)],
    )(edge_source, rels, *blocks)


def score_kernel(peers, *refs):
    live_ref, rows_ref, columns_ref, counts_ref, edge_target_ref = refs[:5]
    blocks = refs[5:5 + peers]
    loss_ref, grad_ref, table_ref = refs[5 + peers:8 + peers]
    block_grads = refs[8 + peers:8 + 2 * peers]
    total, = refs[8 + 2 * peers:]
    features, block = blocks[0].shape
    step = pl.program_id(0)

    @pl.when(step == 0)
    def _():
        total[...] = jnp.zeros_like(total)
        for p, ref in enumerate(blocks):
            hi, lo = split2(ref[...])
            at = pl.ds(p * block, block)
            table_ref[:features, at] = hi
            table_ref[features:2 * features, at] = lo
            table_ref[2 * features:, at] = hi

    score = dot(rows_ref[...], table_ref[...])
    counts = counts_ref[0]
    own = lax.broadcasted_iota(I32, score.shape, 1) == edge_target_ref[...]
    pos = jnp.sum(jnp.where(own, score, 0.0), axis=1, keepdims=True)
    peak = jnp.max(jnp.where(counts > 0.0, score, -jnp.inf), axis=1, keepdims=True)
    peak = jnp.maximum(pos, peak)
    weight = counts * jnp.exp(jnp.minimum(score - peak, 0.0))
    pos_weight = jnp.exp(pos - peak)
    sum_all = pos_weight + jnp.sum(weight, axis=1, keepdims=True)
    edge = step * score.shape[0] + lax.broadcasted_iota(I32, pos.shape, 0)
    live = jnp.where(edge < live_ref[0], 1.0, 0.0)
    loss_ref[...] = (peak - pos + jnp.log(sum_all)) * live
    scale = live / sum_all
    pos_grad = pos_weight * scale - live
    grad = weight * scale + jnp.where(own, pos_grad, 0.0)
    hi, lo = split2(grad)
    grad_ref[0], grad_ref[1] = hi, lo
    total[...] += dot(columns_ref[0], hi) + dot(columns_ref[0], lo) + dot(columns_ref[1], hi)

    @pl.when(step == pl.num_programs(0) - 1)
    def _():
        for p, ref in enumerate(block_grads):
            ref[...] = total[:, p * block:(p + 1) * block]


def score_spans(live, blocks, rows, columns, counts, edge_target):
    peers = len(blocks)
    features, block = blocks[0].shape
    edges = edge_target.shape[0]
    table_rows = peers * block
    chunk = CHUNK
    per_span = SPAN // chunk
    return kernel_call(
        functools.partial(score_kernel, peers),
        [
            shape((edges, 1)),
            shape((2, edges, table_rows), BF16),
            shape((3 * features, table_rows), BF16),
        ] + [shape((features, block))] * peers,
        12 * features * table_rows * edges, 30 * features * edges,
        grid=(edges // chunk,),
        in_specs=[
            SMEM,
            pl.BlockSpec((chunk, 3 * features), lambda i: (i, 0)),
            pl.BlockSpec((2, features, chunk), lambda i: (0, 0, i)),
            pl.BlockSpec((1, 1, table_rows), lambda i: (i // per_span, 0, 0)),
            pl.BlockSpec((chunk, 1), lambda i: (i, 0)),
        ] + [held((features, block))] * peers,
        out_specs=[
            pl.BlockSpec((chunk, 1), lambda i: (i, 0)),
            pl.BlockSpec((2, chunk, table_rows), lambda i: (0, i, 0)),
            held((3 * features, table_rows)),
        ] + [held((features, block))] * peers,
        scratch_shapes=[pltpu.VMEM((features, table_rows), F32)],
    )(live, rows, columns, counts, edge_target, *blocks)


def relation_grad_kernel(
    me_ref, table_ref, grad_ref, heads_ref, rels_ref, edge_rel_ref, source_ref, *refs
):
    outs, total = refs[:-1], refs[-1]
    groups = len(outs) // 2
    half, width = outs[0].shape
    step = pl.program_id(0)

    @pl.when(step == 0)
    def _():
        total[...] = jnp.zeros_like(total)

    features = heads_ref.shape[0]
    hi, lo = table_ref[:features], table_ref[features:2 * features]
    query_grad = dot_nt(hi, grad_ref[0]) + dot_nt(hi, grad_ref[1]) + dot_nt(lo, grad_ref[0])
    source_ref[0], source_ref[1] = split2(conj_product(query_grad, rels_ref[...]))
    hi, lo = split2(conj_product(query_grad, heads_ref[...]))
    hot = columns_hot(edge_rel_ref[...], total.shape[1])
    total[...] += dot(hi, hot) + dot(lo, hot)

    @pl.when(step == pl.num_programs(0) - 1)
    def _():
        group, core = me_ref[0], me_ref[1]
        for j in range(groups):
            at = pl.ds(pl.multiple_of((group ^ j) * width, LANES), width)
            outs[j][...] = total[pl.ds(pl.multiple_of(core * half, 8), half), at]
            outs[groups + j][...] = total[pl.ds(pl.multiple_of((1 - core) * half, 8), half), at]


def relation_grads(me, table, grad, heads, rels, edge_relation, groups, width):
    features, edges = heads.shape
    table_rows = table.shape[1]
    chunk = CHUNK
    return kernel_call(
        relation_grad_kernel,
        [shape((2, features, edges), BF16)] + [shape((features // 2, width))] * (2 * groups),
        10 * features * table_rows * edges, 30 * features * edges,
        grid=(edges // chunk,),
        in_specs=[
            SMEM,
            held((3 * features, table_rows)),
            pl.BlockSpec((2, chunk, table_rows), lambda i: (0, i, 0)),
            pl.BlockSpec((features, chunk), lambda i: (0, i)),
            pl.BlockSpec((features, chunk), lambda i: (0, i)),
            pl.BlockSpec((chunk, 1), lambda i: (i, 0)),
        ],
        out_specs=[pl.BlockSpec((2, features, chunk), lambda i: (0, 0, i))]
        + [held((features // 2, width))] * (2 * groups),
        scratch_shapes=[pltpu.VMEM((features, groups * width), F32)],
    )(me, table, grad, heads, rels, edge_relation)


def source_grad_kernel(rows_ref, edge_source_ref, *refs):
    outs, total = refs[:-1], refs[-1]
    block = outs[0].shape[1]
    step = pl.program_id(0)

    @pl.when(step == 0)
    def _():
        total[...] = jnp.zeros_like(total)

    hot = columns_hot(edge_source_ref[...], total.shape[1])
    total[...] += dot(rows_ref[0], hot) + dot(rows_ref[1], hot)

    @pl.when(step == pl.num_programs(0) - 1)
    def _():
        for p, ref in enumerate(outs):
            ref[...] = total[:, p * block:(p + 1) * block]


def source_grads(rows, edge_source, peers, block):
    _, features, edges = rows.shape
    return kernel_call(
        source_grad_kernel, [shape((features, block))] * peers,
        4 * features * peers * block * edges, 12 * features * edges,
        grid=(edges // CHUNK,),
        in_specs=[
            pl.BlockSpec((2, features, CHUNK), lambda i: (0, 0, i)),
            pl.BlockSpec((CHUNK, 1), lambda i: (i, 0)),
        ],
        out_specs=[held((features, block))] * peers,
        scratch_shapes=[pltpu.VMEM((features, peers * block), F32)],
    )(rows, edge_source)


def put_back(blocks, hot_ref):
    hi, lo = split2(jnp.concatenate([ref[...] for ref in blocks], axis=1))
    return dot(hi, hot_ref[...]) + dot(lo, hot_ref[...])


def target_home_kernel(hot_ref, *refs):
    refs[-1][...] = put_back(refs[:-1], hot_ref)


def target_home(hots, blocks):
    features = blocks[0].shape[0]
    rows = hots.shape[1]
    return kernel_call(
        target_home_kernel, shape((features, rows)),
        4 * features * rows * hots.shape[0], 8 * features * hots.shape[0],
        in_specs=[VMEM] * (1 + len(blocks)), out_specs=VMEM,
    )(hots, *blocks)


def adagrad(params, state, gradient):
    new_state = state + jnp.mean(gradient * gradient, axis=0, keepdims=True)
    return params - learn_rate * gradient / jnp.sqrt(new_state)


def entity_kernel(other_ref, entity_ref, state_ref, hot_ref, *refs):
    gradient = other_ref[...] + put_back(refs[:-1], hot_ref)
    refs[-1][...] = adagrad(entity_ref[...], state_ref[...], gradient)


def entity_update(hots, blocks, other, entity, state):
    features, rows = entity.shape
    return kernel_call(
        entity_kernel, shape((features, rows)),
        4 * features * rows * hots.shape[0], 8 * features * hots.shape[0],
        in_specs=[VMEM] * (4 + len(blocks)), out_specs=VMEM,
    )(other, entity, state, hots, *blocks)


def cut_kernel(me_ref, *refs):
    chips = me_ref.shape[0]
    terms, outs, whole = refs[:-1 - chips], refs[-1 - chips:-1], refs[-1]
    rows, width = outs[0].shape
    have = terms[0].shape[0]
    total = terms[0][...]
    for term in terms[1:]:
        total = total + term[...]
    whole[:have, :] = total
    if have < chips * rows:
        whole[have:, :] = jnp.zeros((chips * rows - have, width), F32)
    for k, out in enumerate(outs):
        out[...] = whole[pl.ds(pl.multiple_of(me_ref[k] * rows, 8), rows), :]


def cut_pieces(order, terms):
    chips = order.shape[0]
    half, width = terms[0].shape
    rows = pl.cdiv(half, 8 * chips) * 8
    return kernel_call(
        cut_kernel, [shape((rows, width))] * chips,
        len(terms) * half * width, 4 * (len(terms) + 1) * half * width,
        in_specs=[SMEM] + [VMEM] * len(terms), out_specs=[VMEM] * chips,
        scratch_shapes=[pltpu.VMEM((chips * rows, width), F32)],
    )(order, *terms)


def sum_kernel(*refs):
    total = refs[0][...]
    for ref in refs[1:-1]:
        total = total + ref[...]
    refs[-1][...] = total


def sum_pieces(pieces):
    rows, width = pieces[0].shape
    return kernel_call(
        sum_kernel, shape((rows, width)),
        len(pieces) * rows * width, 4 * (len(pieces) + 1) * rows * width,
        in_specs=[VMEM] * len(pieces), out_specs=VMEM,
    )(*pieces)


def join_kernel(me_ref, *refs):
    pieces, out_ref, whole = refs[:-2], refs[-2], refs[-1]
    rows = pieces[0].shape[0]
    for k, piece in enumerate(pieces):
        whole[pl.ds(pl.multiple_of(me_ref[k] * rows, 8), rows), :] = piece[...]
    out_ref[...] = whole[:out_ref.shape[0], :]


def join_pieces(order, pieces, half):
    rows, width = pieces[0].shape
    return kernel_call(
        join_kernel, shape((half, width)),
        half * width, 8 * half * width,
        in_specs=[SMEM] + [VMEM] * len(pieces), out_specs=VMEM,
        scratch_shapes=[pltpu.VMEM((len(pieces) * rows, width), F32)],
    )(order, *pieces)


def relation_update_kernel(me_ref, relation_ref, state_ref, *refs):
    parts, out_ref, total = refs[:-2], refs[-2], refs[-1]
    groups = len(parts) // 2
    half, width = parts[0].shape
    group, core = me_ref[0], me_ref[1]
    for j in range(groups):
        at = pl.ds(pl.multiple_of((group ^ j) * width, LANES), width)
        total[pl.ds(pl.multiple_of(core * half, 8), half), at] = parts[j][...]
        total[pl.ds(pl.multiple_of((1 - core) * half, 8), half), at] = parts[groups + j][...]
    gradient = total[:, :out_ref.shape[1]]
    out_ref[...] = adagrad(relation_ref[...], state_ref[...], gradient)


def relation_update(me, relation, state, parts):
    features, count = relation.shape
    _, width = parts[0].shape
    groups = len(parts) // 2
    return kernel_call(
        relation_update_kernel, shape((features, count)),
        8 * features * count, 12 * features * count,
        in_specs=[SMEM] + [VMEM] * (2 + len(parts)), out_specs=VMEM,
        scratch_shapes=[pltpu.VMEM((features, groups * width), F32)],
    )(me, relation, state, *parts)


def sent_on(value, hop, peers):
    return lax.ppermute(value, "shard", [(i, partner(i, hop, peers, 1)) for i in range(peers)])


def sent_across(value, hop, peers, groups, by):
    pairs = [
        (g * peers + i, (g + by) % groups * peers + partner(i, hop, peers, 1))
        for g in range(groups)
        for i in range(peers)
    ]
    return lax.ppermute(value, ("group", "shard"), pairs)


def sent_group(value, bit, groups):
    return lax.ppermute(value, "group", [(g, g ^ bit) for g in range(groups)])


def relation_sum(kept, sent, peers, groups, chip):
    chips = peers // 2
    half = kept[0].shape[0]
    other_core = (0, 1)
    sent = [sent_on(b, other_core, peers) for b in sent]
    mine = [a + b for a, b in zip(kept, sent)]
    terms = [mine[0]] + [sent_group(mine[j], j, groups) for j in range(1, groups)]
    ahead = (chip + jnp.arange(chips, dtype=I32)) % chips
    behind = (chip - jnp.arange(chips, dtype=I32)) % chips
    pieces = cut_pieces(ahead, terms)
    pieces = [pieces[0]] + [sent_on(pieces[k], (k, 0), peers) for k in range(1, chips)]
    piece = sum_pieces(pieces)
    pieces = [piece] + [sent_on(piece, (k, 0), peers) for k in range(1, chips)]
    block = join_pieces(behind, pieces, half)
    blocks = [block] + [sent_group(block, j, groups) for j in range(1, groups)]
    return blocks + [sent_on(b, other_core, peers) for b in blocks]


def on_device(
    entity, entity_state, relation, relation_state, src_send, dst_send,
    edge_source, edge_relation, edge_target, neg_slots, edge_count,
):
    rows, _ = entity.shape
    relations = relation.shape[0]
    peers, block = src_send.shape[1:]
    groups = lax.axis_size("group")
    group = lax.axis_index("group").astype(I32)
    me = lax.axis_index("shard").astype(I32)
    width = pl.cdiv(relations, groups * LANES) * LANES
    entity_t, relation_t = entity.T, relation.T
    ways = hops(peers)
    order = jnp.stack([partner(me, hop, peers, 1) for hop in ways])
    here = jnp.stack([group, me % 2])

    def placed(slots):
        return places_of(me, slots // block, peers) * block + slots % block

    edge_source, edge_target = placed(edge_source), placed(edge_target)
    first = peers // 2
    sources = pick_blocks(order[:first], entity_t, src_send[0])
    sources += pick_blocks(order[first:], entity_t, src_send[0])
    sources = [
        sent_on(value, hop, peers) if hop != (0, 0) else value
        for value, hop in zip(sources, ways)
    ]
    targets = pick_blocks(order, entity_t, dst_send[0])
    targets = [sent_across(value, hop, peers, groups, -1) for value, hop in zip(targets, ways)]
    rels = relation_rows(relation_t, edge_relation.reshape(1, -1))
    counts = slot_counts(placed(neg_slots), peers * block)
    source_hots = home_hots(order, src_send[0], rows)
    target_hots = home_hots(order, dst_send[0], rows)
    heads, query_columns, query_lines = query_rows(sources, edge_source.reshape(1, -1), rels)
    loss, grad, table, *table_grads = score_spans(
        edge_count, targets, query_lines, query_columns, counts, edge_target.reshape(-1, 1)
    )
    back = [(-hop[0], hop[1]) for hop in ways]
    home = [sent_across(value, hop, peers, groups, 1) for value, hop in zip(table_grads, back)]
    source_lines, *halves = relation_grads(
        here, table, grad, heads, rels, edge_relation.reshape(-1, 1), groups, width
    )
    source_parts = source_grads(source_lines, edge_source.reshape(-1, 1), peers, block)
    returned = []
    for value, hop, way in zip(source_parts, back, ways):
        returned.append(sent_on(value, hop, peers) if way != (0, 0) else value)
    parts = relation_sum(halves[:groups], halves[groups:], peers, groups, me // 2)
    relation_new = relation_update(here, relation_t, relation_state.reshape(1, -1), parts)
    target_part = target_home(target_hots, home)
    entity_new = entity_update(
        source_hots, returned, target_part, entity_t, entity_state.reshape(1, -1)
    )
    return entity_new.T, relation_new.T, loss.reshape(-1)


def solution(mesh):
    both = ("group", "shard")
    return jax.shard_map(
        on_device,
        mesh=mesh,
        in_specs=(
            P(both, None), P(both), P(), P(), P(both, None, None), P(both, None, None),
            P(both), P(both), P(both), P(both, None), P(both),
        ),
        out_specs=(P(both, None), P(), P(both)),
        check_vma=False,
    )
```

profile of v0, /device:TPU:0, one launch (start us, length us, event | category | flops | bytes accessed | tf_op | source)
XLA Modules:
  0.0 280.9 jit_solution(17075772998172354689)
XLA Ops:
  1.3 2.9 %shard_map.133 = (f32[400,128]{1,0:T(8,128)}, f32[400,128]{1,0:T(8,128)}, f32[400,128]{1,0:T(8,128)}, f32[400,128]{1,0:T(8,128)}) custom-call(s32[4]{0:T(128)} %pad_add_fusion.1.order_ref, f32[400,512]{1,0:T(8,128)} %bitcast.29, s32[8,128]{1,0:T(8,128)} %bitcast.41), custom_call_target="tpu_custom_call" | custom-call | flops 629145600 | bytes 1638400 | tf_op jit(solution)/shard_map/pallas_call | solution.py:124
  4.2 5.1 %collective-permute-start.4 = (f32[400,128]{1,0:T(8,128)}, f32[400,128]{1,0:T(8,128)S(1)}, u32[]{:S(2)}, u32[]{:S(2)}) collective-permute-start(f32[400,128]{1,0:T(8,128)} %get-tuple-element.58), channel_id=1, source_target_pairs={{0,6},{1,7},{2,0},{3,1},{4,2},{5,3},{6,4},{7,5},{8,14},{9,15},{10,... | collective-permute-start | bytes 614408 | tf_op jit(solution)/shard_map/ppermute | solution.py:522
  10.4 2.9 %shard_map.132 = (f32[400,128]{1,0:T(8,128)}, f32[400,128]{1,0:T(8,128)}, f32[400,128]{1,0:T(8,128)}, f32[400,128]{1,0:T(8,128)}) custom-call(s32[4]{0:T(128)} %pad_add_fusion.order_ref, f32[400,512]{1,0:T(8,128)} %bitcast.30, s32[8,128]{1,0:T(8,128)} %bitcast.42), custom_call_target="tpu_custom_call" | custom-call | flops 629145600 | bytes 1638400 | tf_op jit(solution)/shard_map/pallas_call | solution.py:124
  13.3 1.6 collective-permute-start
  16.9 2.6 shard_map.135.refs_3_
  22.3 7.5 %shard_map.131.refs_1_.rels_ref = f32[400,1024]{1,0:T(8,128)} custom-call(f32[400,1345]{1,0:T(8,128)} %bitcast.26, s32[1,1024]{1,0:T(1,128)} %bitcast.37), custom_call_target="tpu_custom_call" | custom-call | flops 3460300800 | bytes 3276800 | tf_op jit(solution)/shard_map/pallas_call | solution.py:151
  30.4 3.6 %shard_map.136 = (f32[400,128]{1,0:T(8,128)}, f32[400,128]{1,0:T(8,128)}, f32[400,128]{1,0:T(8,128)}, f32[400,128]{1,0:T(8,128)}, f32[400,128]{1,0:T(8,128)}, /*...) custom-call(s32[8]{0:T(128)} %stack.48.order_ref, f32[400,512]{1,0:T(8,128)} %bitcast.31, s32[8,128]{1,0:T(8,128)} %bitcast.39), custom_call_target="tpu_custom_call" | custom-call | flops 1258291200 | bytes 3276800 | tf_op jit(solution)/shard_map/pallas_call | solution.py:124
  34.1 2.2 collective-permute-start.2
  36.8 4.1 %collective-permute-start.10 = (f32[400,128]{1,0:T(8,128)}, f32[400,128]{1,0:T(8,128)S(1)}, u32[]{:S(2)}, u32[]{:S(2)}) collective-permute-start(f32[400,128]{1,0:T(8,128)} %get-tuple-element.67), channel_id=1, source_target_pairs={{0,29},{1,28},{2,31},{3,30},{4,25},{5,24},{6,27},{7,26},{8,5},{9,4... | collective-permute-start | bytes 614408 | tf_op jit(solution)/shard_map/ppermute | solution.py:531
  40.9 1.5 collective-permute-start.11
  44.0 12.3 %collective-permute-done.2.refs_4_ = f32[400,128]{1,0:T(8,128)S(1)} collective-permute-done((f32[400,128]{1,0:T(8,128)S(1)}, f32[400,128]{1,0:T(8,128)S(1)}, u32[]{:S(2)}, u32[]{:S(2)}) %collective-permute-start.2) | collective-permute-done | bytes 204832 | tf_op jit(solution)/shard_map/ppermute | solution.py:522
  56.9 2.3 collective-permute-done.3.refs_5_
  59.3 2.3 collective-permute-start.14
  61.6 3.1 %collective-permute-done.10.refs_8_ = f32[400,128]{1,0:T(8,128)S(1)} collective-permute-done((f32[400,128]{1,0:T(8,128)}, f32[400,128]{1,0:T(8,128)S(1)}, u32[]{:S(2)}, u32[]{:S(2)}) %collective-permute-start.10) | collective-permute-done | bytes 204832 | tf_op jit(solution)/shard_map/ppermute | solution.py:531
  64.7 11.0 %collective-permute-start.7 = (f32[400,128]{1,0:T(8,128)}, f32[400,128]{1,0:T(8,128)S(1)}, u32[]{:S(2)}, u32[]{:S(2)}) collective-permute-start(f32[400,128]{1,0:T(8,128)} %get-tuple-element.64), channel_id=1, source_target_pairs={{0,26},{1,27},{2,28},{3,29},{4,30},{5,31},{6,24},{7,25},{8,2},{9,3... | collective-permute-start | bytes 614408 | tf_op jit(solution)/shard_map/ppermute | solution.py:531
  75.8 4.5 %collective-permute-start.9 = (f32[400,128]{1,0:T(8,128)}, f32[400,128]{1,0:T(8,128)S(1)}, u32[]{:S(2)}, u32[]{:S(2)}) collective-permute-start(f32[400,128]{1,0:T(8,128)} %get-tuple-element.66), channel_id=1, source_target_pairs={{0,28},{1,29},{2,30},{3,31},{4,24},{5,25},{6,26},{7,27},{8,4},{9,5... | collective-permute-start | bytes 614408 | tf_op jit(solution)/shard_map/ppermute | solution.py:531
  80.3 8.3 %shard_map.134 = (f32[400,1024]{1,0:T(8,128)}, bf16[2,400,1024]{2,1,0:T(8,128)(2,1)}, bf16[1024,1200]{1,0:T(8,128)(2,1)}) custom-call(s32[1,1024]{1,0:T(1,128)} %bitcast.34, f32[400,1024]{1,0:T(8,128)} %shard_map.131.refs_1_.rels_ref, f32[400,128]{1,0:T(8,128)} %copy-done.43, f32[400,128]{1,0:T(8,128)} %copy-done.44, f32[400,128]{1,0:T(8,128)} %copy-done.50, ...), custom_call_target="tpu_custom_call" | custom-call | flops 2516582400 | bytes 8192000 | tf_op jit(solution)/shard_map/pallas_call | solution.py:218
  88.7 8.5 %collective-permute-done.9.refs_7_ = f32[400,128]{1,0:T(8,128)S(1)} collective-permute-done((f32[400,128]{1,0:T(8,128)}, f32[400,128]{1,0:T(8,128)S(1)}, u32[]{:S(2)}, u32[]{:S(2)}) %collective-permute-start.9) | collective-permute-done | bytes 204832 | tf_op jit(solution)/shard_map/ppermute | solution.py:531
  97.8 14.3 %shard_map.137 = (f32[1024,1]{1,0:T(8,128)}, bf16[2,1024,1024]{2,1,0:T(8,128)(2,1)}, bf16[1200,1024]{1,0:T(8,128)(2,1)}, f32[400,128]{1,0:T(8,128)}, f32[400,128...) custom-call(s32[1]{0:T(128)S(6)} %copy.20.refs_0_, ...), custom_call_target="tpu_custom_call" | custom-call | flops 5033164800 | bytes 12288000 | tf_op jit(solution)/shard_map/pallas_call | solution.py:287
  112.2 16.2 %shard_map.140 = (bf16[2,400,1024]{2,1,0:T(8,128)(2,1)}, f32[200,384]{1,0:T(8,128)}, f32[200,384]{1,0:T(8,128)}, f32[200,384]{1,0:T(8,128)}, f32[200,384]{1,0:T(...) custom-call(s32[2]{0:T(128)} %pad_add_fusion.2.me_ref, ...), custom_call_target="tpu_custom_call" | custom-call | flops 4194304000 | bytes 12288000 | tf_op jit(solution)/shard_map/pallas_call | solution.py:345
  131.5 1.5 collective-permute-start.36
  134.0 1.6 collective-permute-start.34
  136.2 5.8 %shard_map.141 = (f32[400,128]{1,0:T(8,128)}, f32[400,128]{1,0:T(8,128)}, f32[400,128]{1,0:T(8,128)}, f32[400,128]{1,0:T(8,128)}, f32[400,128]{1,0:T(8,128)}, /*...) custom-call(bf16[2,400,1024]{2,1,0:T(8,128)(2,1)} %get-tuple-element.83.rows_ref, ...), custom_call_target="tpu_custom_call" | custom-call | flops 1677721600 | bytes 4915200 | tf_op jit(solution)/shard_map/pallas_call | solution.py:384
  144.3 4.0 %collective-permute-done.34.refs_2_ = f32[200,384]{1,0:T(8,128)S(1)} collective-permute-done((f32[200,384]{1,0:T(8,128)S(1)}, f32[200,384]{1,0:T(8,128)S(1)}, u32[]{:S(2)}, u32[]{:S(2)}) %collective-permute-start.34) | collective-permute-done | bytes 307232 | tf_op jit(solution)/shard_map/ppermute | solution.py:535
  149.7 2.1 shard_map.143
  151.9 1.7 collective-permute-start.38
  153.6 2.1 collective-permute-start.39
  155.7 2.0 collective-permute-start.25
  157.7 1.6 collective-permute-done.37.refs_1_
  159.3 3.5 %collective-permute-done.38.refs_2_ = f32[56,384]{1,0:T(8,128)S(1)} collective-permute-done((f32[56,384]{1,0:T(8,128)}, f32[56,384]{1,0:T(8,128)S(1)}, u32[]{:S(2)}, u32[]{:S(2)}) %collective-permute-start.38) | collective-permute-done | bytes 86048 | tf_op jit(solution)/shard_map/ppermute | solution.py:522
  162.8 6.7 %collective-permute-start.28 = (f32[400,128]{1,0:T(8,128)}, f32[400,128]{1,0:T(8,128)S(1)}, u32[]{:S(2)}, u32[]{:S(2)}) collective-permute-start(f32[400,128]{1,0:T(8,128)} %get-tuple-element.89), channel_id=1, source_target_pairs={{0,3},{1,2},{2,5},{3,4},{4,7},{5,6},{6,1},{7,0},{8,11},{9,10},{10,... | collective-permute-start | bytes 614408 | tf_op jit(solution)/shard_map/ppermute | solution.py:522
  169.5 4.5 %collective-permute-start.15 = (f32[400,128]{1,0:T(8,128)S(1)}, f32[400,128]{1,0:T(8,128)S(1)}, u32[]{:S(2)}, u32[]{:S(2)}) collective-permute-start(f32[400,128]{1,0:T(8,128)S(1)} %copy-done.39), channel_id=1, source_target_pairs={{0,14},{1,15},{2,8},{3,9},{4,10},{5,11},{6,12},{7,13},{8,22},{9,23... | collective-permute-start | bytes 614408 | tf_op jit(solution)/shard_map/ppermute | solution.py:531
  174.0 1.7 shard_map.144.refs_0_
  175.7 10.1 %collective-permute-done.25.refs_2_ = f32[400,128]{1,0:T(8,128)S(1)} collective-permute-done((f32[400,128]{1,0:T(8,128)}, f32[400,128]{1,0:T(8,128)S(1)}, u32[]{:S(2)}, u32[]{:S(2)}) %collective-permute-start.25) | collective-permute-done | bytes 204832 | tf_op jit(solution)/shard_map/ppermute | solution.py:522
  185.8 2.7 collective-permute-done.26.refs_3_
  188.5 3.3 %collective-permute-start.17 = (f32[400,128]{1,0:T(8,128)}, f32[400,128]{1,0:T(8,128)}, u32[]{:S(2)}, u32[]{:S(2)}) collective-permute-start(f32[400,128]{1,0:T(8,128)} %get-tuple-element.74), channel_id=1, source_target_pairs={{0,12},{1,13},{2,14},{3,15},{4,8},{5,9},{6,10},{7,11},{8,20},{9,21... | collective-permute-start | bytes 614408 | tf_op jit(solution)/shard_map/ppermute | solution.py:531
  191.8 13.8 %collective-permute-start.18 = (f32[400,128]{1,0:T(8,128)}, f32[400,128]{1,0:T(8,128)}, u32[]{:S(2)}, u32[]{:S(2)}) collective-permute-start(f32[400,128]{1,0:T(8,128)} %get-tuple-element.75), channel_id=1, source_target_pairs={{0,13},{1,12},{2,15},{3,14},{4,9},{5,8},{6,11},{7,10},{8,21},{9,20... | collective-permute-start | bytes 614408 | tf_op jit(solution)/shard_map/ppermute | solution.py:531
  206.0 16.0 %collective-permute-done.41.refs_2_ = f32[56,384]{1,0:T(8,128)S(1)} collective-permute-done((f32[56,384]{1,0:T(8,128)}, f32[56,384]{1,0:T(8,128)S(1)}, u32[]{:S(2)}, u32[]{:S(2)}) %collective-permute-start.41) | collective-permute-done | bytes 86048 | tf_op jit(solution)/shard_map/ppermute | solution.py:522
  223.9 1.8 shard_map.145.refs_0_
  227.7 1.5 collective-permute-start.45
  229.2 4.6 %collective-permute-done.19.refs_4_ = f32[400,128]{1,0:T(8,128)S(1)} collective-permute-done((f32[400,128]{1,0:T(8,128)}, f32[400,128]{1,0:T(8,128)S(1)}, u32[]{:S(2)}, u32[]{:S(2)}) %collective-permute-start.19) | collective-permute-done | bytes 204832 | tf_op jit(solution)/shard_map/ppermute | solution.py:531
  234.6 18.9 %collective-permute-done.21.refs_6_ = f32[400,128]{1,0:T(8,128)S(1)} collective-permute-done((f32[400,128]{1,0:T(8,128)S(1)}, f32[400,128]{1,0:T(8,128)S(1)}, u32[]{:S(2)}, u32[]{:S(2)}) %collective-permute-start.21) | collective-permute-done | bytes 204832 | tf_op jit(solution)/shard_map/ppermute | solution.py:531
  254.8 3.0 %collective-permute-done.22.refs_7_ = f32[400,128]{1,0:T(8,128)S(1)} collective-permute-done((f32[400,128]{1,0:T(8,128)}, f32[400,128]{1,0:T(8,128)S(1)}, u32[]{:S(2)}, u32[]{:S(2)}) %collective-permute-start.22) | collective-permute-done | bytes 204832 | tf_op jit(solution)/shard_map/ppermute | solution.py:531
  261.2 2.3 shard_map.130.hot_ref
  263.5 2.3 shard_map.139.hot_ref
  266.6 3.7 %shard_map.138.other_ref = f32[400,512]{1,0:T(8,128)} custom-call(bf16[1024,512]{1,0:T(8,128)(2,1)} %shard_map.130.hot_ref, f32[400,128]{1,0:T(8,128)} %copy-done.19, f32[400,128]{1,0:T(8,128)} %collective-permute-done.16.refs_1_, f32[400,128]{1,0:T(8,128)} %collective-permute-done.17.refs_2_, f32[400,128]{1,0:T(8,128)} %collective-permute-done.18.refs_3_, ...), custom_call_target="tpu_custom_call" | custom-call | flops 838860800 | bytes 3276800 | tf_op jit(solution)/shard_map/pallas_call | solution.py:409
  270.4 4.3 %shard_map.142 = f32[400,512]{1,0:T(8,128)} custom-call(f32[400,512]{1,0:T(8,128)} %shard_map.138.other_ref, f32[400,512]{1,0:T(8,128)} %bitcast.32, f32[1,512]{1,0:T(1,128)} %bitcast.44, bf16[1024,512]{1,0:T(8,128)(2,1)} %shard_map.139.hot_ref, f32[400,128]{1,0:T(8,128)} %copy-done.13, f32[400,128]{1,0:T(8,128)} %copy-done.14, f32[400,128]{1,0:T(8,128)} %copy-done.15, ...), custom_call_target="tpu_custom_call" | custom-call | flops 838860800 | bytes 3276800 | tf_op jit(solution)/shard_map/pallas_call | solution.py:428
  276.3 4.6 %shard_map.146 = f32[400,1345]{1,0:T(8,128)} custom-call(s32[2]{0:T(128)} %pad_add_fusion.2.me_ref, f32[400,1345]{1,0:T(8,128)} %bitcast.27, f32[1,1345]{1,0:T(1,128)} %reshape.36.state_ref, f32[200,384]{1,0:T(8,128)} %shard_map.145.refs_0_, f32[200,384]{1,0:T(8,128)} %copy-done.6, f32[200,384]{1,0:T(8,128)} %copy-done.7, f32[200,384]{1,0:T(8,128)} %copy-done.8, ...), custom_call_target="tpu_custom_call" | custom-call | flops 4304000 | bytes 6456000 | tf_op jit(solution)/shard_map/pallas_call | solution.py:513
  (204 shorter events, 30.9 us)
Async XLA Ops:
  4.2 29.8 %collective-permute-start.4 = (f32[400,128]{1,0:T(8,128)}, f32[400,128]{1,0:T(8,128)S(1)}, u32[]{:S(2)}, u32[]{:S(2)}) collective-permute-start(f32[400,128]{1,0:T(8,128)} %get-tuple-element.58), channel_id=1, source_target_pairs={{0,6},{1,7},{2,0},{3,1},{4,2},{5,3},{6,4},{7,5},{8,14},{9,15},{10,... | collective-permute-start | bytes 614408 | tf_op jit(solution)/shard_map/ppermute | solution.py:522
  9.3 27.0 %collective-permute-start.5 = (f32[400,128]{1,0:T(8,128)}, f32[400,128]{1,0:T(8,128)S(1)}, u32[]{:S(2)}, u32[]{:S(2)}) collective-permute-start(f32[400,128]{1,0:T(8,128)} %get-tuple-element.59), channel_id=1, source_target_pairs={{0,7},{1,6},{2,1},{3,0},{4,3},{5,2},{6,5},{7,4},{8,15},{9,14},{10,... | collective-permute-start | bytes 614408 | tf_op jit(solution)/shard_map/ppermute | solution.py:522
  9.3 27.5 %collective-permute-start.6 = (f32[400,128]{1,0:T(8,128)}, f32[400,128]{1,0:T(8,128)S(1)}, u32[]{:S(2)}, u32[]{:S(2)}) collective-permute-start(f32[400,128]{1,0:T(8,128)} %get-tuple-element.60), channel_id=1, source_target_pairs={{0,1},{1,0},{2,3},{3,2},{4,5},{5,4},{6,7},{7,6},{8,9},{9,8},{10,11... | collective-permute-start | bytes 614408 | tf_op jit(solution)/shard_map/ppermute | solution.py:522
  13.3 27.6 %collective-permute-start = (f32[400,128]{1,0:T(8,128)}, f32[400,128]{1,0:T(8,128)S(1)}, u32[]{:S(2)}, u32[]{:S(2)}) collective-permute-start(f32[400,128]{1,0:T(8,128)} %get-tuple-element.54), channel_id=1, source_target_pairs={{0,2},{1,3},{2,4},{3,5},{4,6},{5,7},{6,0},{7,1},{8,10},{9,11},{10,... | collective-permute-start | bytes 614408 | tf_op jit(solution)/shard_map/ppermute | solution.py:522
  14.9 27.5 %collective-permute-start.1 = (f32[400,128]{1,0:T(8,128)}, f32[400,128]{1,0:T(8,128)S(1)}, u32[]{:S(2)}, u32[]{:S(2)}) collective-permute-start(f32[400,128]{1,0:T(8,128)} %get-tuple-element.55), channel_id=1, source_target_pairs={{0,3},{1,2},{2,5},{3,4},{4,7},{5,6},{6,1},{7,0},{8,11},{9,10},{10,... | collective-permute-start | bytes 614408 | tf_op jit(solution)/shard_map/ppermute | solution.py:522
  34.1 22.2 %collective-permute-start.2 = (f32[400,128]{1,0:T(8,128)S(1)}, f32[400,128]{1,0:T(8,128)S(1)}, u32[]{:S(2)}, u32[]{:S(2)}) collective-permute-start(f32[400,128]{1,0:T(8,128)S(1)} %copy-done.49), channel_id=1, source_target_pairs={{0,4},{1,5},{2,6},{3,7},{4,0},{5,1},{6,2},{7,3},{8,12},{9,13},{10,... | collective-permute-start | bytes 614408 | tf_op jit(solution)/shard_map/ppermute | solution.py:522
  36.3 23.0 %collective-permute-start.3 = (f32[400,128]{1,0:T(8,128)S(1)}, f32[400,128]{1,0:T(8,128)S(1)}, u32[]{:S(2)}, u32[]{:S(2)}) collective-permute-start(f32[400,128]{1,0:T(8,128)S(1)} %copy-done.47), channel_id=1, source_target_pairs={{0,5},{1,4},{2,7},{3,6},{4,1},{5,0},{6,3},{7,2},{8,13},{9,12},{10,... | collective-permute-start | bytes 614408 | tf_op jit(solution)/shard_map/ppermute | solution.py:522
  36.8 27.9 %collective-permute-start.10 = (f32[400,128]{1,0:T(8,128)}, f32[400,128]{1,0:T(8,128)S(1)}, u32[]{:S(2)}, u32[]{:S(2)}) collective-permute-start(f32[400,128]{1,0:T(8,128)} %get-tuple-element.67), channel_id=1, source_target_pairs={{0,29},{1,28},{2,31},{3,30},{4,25},{5,24},{6,27},{7,26},{8,5},{9,4... | collective-permute-start | bytes 614408 | tf_op jit(solution)/shard_map/ppermute | solution.py:531
  40.9 34.9 %collective-permute-start.11 = (f32[400,128]{1,0:T(8,128)}, f32[400,128]{1,0:T(8,128)S(1)}, u32[]{:S(2)}, u32[]{:S(2)}) collective-permute-start(f32[400,128]{1,0:T(8,128)} %get-tuple-element.68), channel_id=1, source_target_pairs={{0,30},{1,31},{2,24},{3,25},{4,26},{5,27},{6,28},{7,29},{8,6},{9,7... | collective-permute-start | bytes 614408 | tf_op jit(solution)/shard_map/ppermute | solution.py:531
  42.4 33.4 %collective-permute-start.12 = (f32[400,128]{1,0:T(8,128)}, f32[400,128]{1,0:T(8,128)S(1)}, u32[]{:S(2)}, u32[]{:S(2)}) collective-permute-start(f32[400,128]{1,0:T(8,128)} %get-tuple-element.69), channel_id=1, source_target_pairs={{0,31},{1,30},{2,25},{3,24},{4,27},{5,26},{6,29},{7,28},{8,7},{9,6... | collective-permute-start | bytes 614408 | tf_op jit(solution)/shard_map/ppermute | solution.py:531
  56.2 32.3 %collective-permute-start.13 = (f32[400,128]{1,0:T(8,128)}, f32[400,128]{1,0:T(8,128)S(1)}, u32[]{:S(2)}, u32[]{:S(2)}) collective-permute-start(f32[400,128]{1,0:T(8,128)} %get-tuple-element.70), channel_id=1, source_target_pairs={{0,25},{1,24},{2,27},{3,26},{4,29},{5,28},{6,31},{7,30},{8,1},{9,0... | collective-permute-start | bytes 614408 | tf_op jit(solution)/shard_map/ppermute | solution.py:531
  59.3 29.3 %collective-permute-start.14 = (f32[400,128]{1,0:T(8,128)}, f32[400,128]{1,0:T(8,128)S(1)}, u32[]{:S(2)}, u32[]{:S(2)}) collective-permute-start(f32[400,128]{1,0:T(8,128)} %get-tuple-element.71), channel_id=1, source_target_pairs={{0,24},{1,25},{2,26},{3,27},{4,28},{5,29},{6,30},{7,31},{8,0},{9,1... | collective-permute-start | bytes 614408 | tf_op jit(solution)/shard_map/ppermute | solution.py:531
  64.7 23.9 %collective-permute-start.7 = (f32[400,128]{1,0:T(8,128)}, f32[400,128]{1,0:T(8,128)S(1)}, u32[]{:S(2)}, u32[]{:S(2)}) collective-permute-start(f32[400,128]{1,0:T(8,128)} %get-tuple-element.64), channel_id=1, source_target_pairs={{0,26},{1,27},{2,28},{3,29},{4,30},{5,31},{6,24},{7,25},{8,2},{9,3... | collective-permute-start | bytes 614408 | tf_op jit(solution)/shard_map/ppermute | solution.py:531
  75.7 12.9 %collective-permute-start.8 = (f32[400,128]{1,0:T(8,128)}, f32[400,128]{1,0:T(8,128)S(1)}, u32[]{:S(2)}, u32[]{:S(2)}) collective-permute-start(f32[400,128]{1,0:T(8,128)} %get-tuple-element.65), channel_id=1, source_target_pairs={{0,27},{1,26},{2,29},{3,28},{4,31},{5,30},{6,25},{7,24},{8,3},{9,2... | collective-permute-start | bytes 614408 | tf_op jit(solution)/shard_map/ppermute | solution.py:531
  75.8 21.4 %collective-permute-start.9 = (f32[400,128]{1,0:T(8,128)}, f32[400,128]{1,0:T(8,128)S(1)}, u32[]{:S(2)}, u32[]{:S(2)}) collective-permute-start(f32[400,128]{1,0:T(8,128)} %get-tuple-element.66), channel_id=1, source_target_pairs={{0,28},{1,29},{2,30},{3,31},{4,24},{5,25},{6,26},{7,27},{8,4},{9,5... | collective-permute-start | bytes 614408 | tf_op jit(solution)/shard_map/ppermute | solution.py:531
  129.0 6.6 %collective-permute-start.31 = (f32[200,384]{1,0:T(8,128)}, f32[200,384]{1,0:T(8,128)S(1)}, u32[]{:S(2)}, u32[]{:S(2)}) collective-permute-start(f32[200,384]{1,0:T(8,128)} %get-tuple-element.95), channel_id=1, source_target_pairs={{0,1},{1,0},{2,3},{3,2},{4,5},{5,4},{6,7},{7,6},{8,9},{9,8},{10,11... | collective-permute-start | bytes 921608 | tf_op jit(solution)/shard_map/ppermute | solution.py:522
  129.0 14.0 %collective-permute-start.30 = (f32[200,384]{1,0:T(8,128)}, f32[200,384]{1,0:T(8,128)S(1)}, u32[]{:S(2)}, u32[]{:S(2)}) collective-permute-start(f32[200,384]{1,0:T(8,128)} %get-tuple-element.93), channel_id=1, source_target_pairs={{0,1},{1,0},{2,3},{3,2},{4,5},{5,4},{6,7},{7,6},{8,9},{9,8},{10,11... | collective-permute-start | bytes 921608 | tf_op jit(solution)/shard_map/ppermute | solution.py:522
  131.5 12.8 %collective-permute-start.36 = (f32[200,384]{1,0:T(8,128)S(1)}, f32[200,384]{1,0:T(8,128)S(1)}, u32[]{:S(2)}, u32[]{:S(2)}) collective-permute-start(f32[200,384]{1,0:T(8,128)S(1)} %add.252), channel_id=1, source_target_pairs={{0,24},{8,16},{16,8},{24,0},{1,25},{9,17},{17,9},{25,1},{2,26},{10... | collective-permute-start | bytes 921608 | tf_op jit(solution)/shard_map/ppermute | solution.py:535
  134.0 14.3 %collective-permute-start.34 = (f32[200,384]{1,0:T(8,128)S(1)}, f32[200,384]{1,0:T(8,128)S(1)}, u32[]{:S(2)}, u32[]{:S(2)}) collective-permute-start(f32[200,384]{1,0:T(8,128)S(1)} %add.251), channel_id=1, source_target_pairs={{0,16},{8,24},{16,0},{24,8},{1,17},{9,25},{17,1},{25,9},{2,18},{10... | collective-permute-start | bytes 921608 | tf_op jit(solution)/shard_map/ppermute | solution.py:535
  135.6 12.7 %collective-permute-start.32 = (f32[200,384]{1,0:T(8,128)S(1)}, f32[200,384]{1,0:T(8,128)S(1)}, u32[]{:S(2)}, u32[]{:S(2)}) collective-permute-start(f32[200,384]{1,0:T(8,128)S(1)} %add.250), channel_id=1, source_target_pairs={{0,8},{8,0},{16,24},{24,16},{1,9},{9,1},{17,25},{25,17},{2,10},{10... | collective-permute-start | bytes 921608 | tf_op jit(solution)/shard_map/ppermute | solution.py:535
  142.0 13.6 %collective-permute-start.23 = (f32[400,128]{1,0:T(8,128)}, f32[400,128]{1,0:T(8,128)S(1)}, u32[]{:S(2)}, u32[]{:S(2)}) collective-permute-start(f32[400,128]{1,0:T(8,128)} %get-tuple-element.84), channel_id=1, source_target_pairs={{0,6},{1,7},{2,0},{3,1},{4,2},{5,3},{6,4},{7,5},{8,14},{9,15},{10,... | collective-permute-start | bytes 614408 | tf_op jit(solution)/shard_map/ppermute | solution.py:522
  143.0 14.7 %collective-permute-start.24 = (f32[400,128]{1,0:T(8,128)}, f32[400,128]{1,0:T(8,128)S(1)}, u32[]{:S(2)}, u32[]{:S(2)}) collective-permute-start(f32[400,128]{1,0:T(8,128)} %get-tuple-element.85), channel_id=1, source_target_pairs={{0,7},{1,6},{2,1},{3,0},{4,3},{5,2},{6,5},{7,4},{8,15},{9,14},{10,... | collective-permute-start | bytes 614408 | tf_op jit(solution)/shard_map/ppermute | solution.py:522
  151.9 7.5 %collective-permute-start.37 = (f32[56,384]{1,0:T(8,128)}, f32[56,384]{1,0:T(8,128)S(1)}, u32[]{:S(2)}, u32[]{:S(2)}) collective-permute-start(f32[56,384]{1,0:T(8,128)} %get-tuple-element.101), channel_id=1, source_target_pairs={{0,2},{1,3},{2,4},{3,5},{4,6},{5,7},{6,0},{7,1},{8,10},{9,11},{10,... | collective-permute-start | bytes 258056 | tf_op jit(solution)/shard_map/ppermute | solution.py:522
  151.9 11.0 %collective-permute-start.38 = (f32[56,384]{1,0:T(8,128)}, f32[56,384]{1,0:T(8,128)S(1)}, u32[]{:S(2)}, u32[]{:S(2)}) collective-permute-start(f32[56,384]{1,0:T(8,128)} %get-tuple-element.102), channel_id=1, source_target_pairs={{0,4},{1,5},{2,6},{3,7},{4,0},{5,1},{6,2},{7,3},{8,12},{9,13},{10,... | collective-permute-start | bytes 258056 | tf_op jit(solution)/shard_map/ppermute | solution.py:522
  153.6 15.9 %collective-permute-start.39 = (f32[56,384]{1,0:T(8,128)}, f32[56,384]{1,0:T(8,128)S(1)}, u32[]{:S(2)}, u32[]{:S(2)}) collective-permute-start(f32[56,384]{1,0:T(8,128)} %get-tuple-element.103), channel_id=1, source_target_pairs={{0,6},{1,7},{2,0},{3,1},{4,2},{5,3},{6,4},{7,5},{8,14},{9,15},{10,... | collective-permute-start | bytes 258056 | tf_op jit(solution)/shard_map/ppermute | solution.py:522
  155.7 30.1 %collective-permute-start.25 = (f32[400,128]{1,0:T(8,128)}, f32[400,128]{1,0:T(8,128)S(1)}, u32[]{:S(2)}, u32[]{:S(2)}) collective-permute-start(f32[400,128]{1,0:T(8,128)} %get-tuple-element.86), channel_id=1, source_target_pairs={{0,4},{1,5},{2,6},{3,7},{4,0},{5,1},{6,2},{7,3},{8,12},{9,13},{10,... | collective-permute-start | bytes 614408 | tf_op jit(solution)/shard_map/ppermute | solution.py:522
  157.7 30.7 %collective-permute-start.26 = (f32[400,128]{1,0:T(8,128)}, f32[400,128]{1,0:T(8,128)S(1)}, u32[]{:S(2)}, u32[]{:S(2)}) collective-permute-start(f32[400,128]{1,0:T(8,128)} %get-tuple-element.87), channel_id=1, source_target_pairs={{0,5},{1,4},{2,7},{3,6},{4,1},{5,0},{6,3},{7,2},{8,13},{9,12},{10,... | collective-permute-start | bytes 614408 | tf_op jit(solution)/shard_map/ppermute | solution.py:522
  159.3 29.1 %collective-permute-start.27 = (f32[400,128]{1,0:T(8,128)}, f32[400,128]{1,0:T(8,128)S(1)}, u32[]{:S(2)}, u32[]{:S(2)}) collective-permute-start(f32[400,128]{1,0:T(8,128)} %get-tuple-element.88), channel_id=1, source_target_pairs={{0,2},{1,3},{2,4},{3,5},{4,6},{5,7},{6,0},{7,1},{8,10},{9,11},{10,... | collective-permute-start | bytes 614408 | tf_op jit(solution)/shard_map/ppermute | solution.py:522
  162.8 28.9 %collective-permute-start.28 = (f32[400,128]{1,0:T(8,128)}, f32[400,128]{1,0:T(8,128)S(1)}, u32[]{:S(2)}, u32[]{:S(2)}) collective-permute-start(f32[400,128]{1,0:T(8,128)} %get-tuple-element.89), channel_id=1, source_target_pairs={{0,3},{1,2},{2,5},{3,4},{4,7},{5,6},{6,1},{7,0},{8,11},{9,10},{10,... | collective-permute-start | bytes 614408 | tf_op jit(solution)/shard_map/ppermute | solution.py:522
  169.5 36.0 %collective-permute-start.15 = (f32[400,128]{1,0:T(8,128)S(1)}, f32[400,128]{1,0:T(8,128)S(1)}, u32[]{:S(2)}, u32[]{:S(2)}) collective-permute-start(f32[400,128]{1,0:T(8,128)S(1)} %copy-done.39), channel_id=1, source_target_pairs={{0,14},{1,15},{2,8},{3,9},{4,10},{5,11},{6,12},{7,13},{8,22},{9,23... | collective-permute-start | bytes 614408 | tf_op jit(solution)/shard_map/ppermute | solution.py:531
  185.8 19.8 %collective-permute-start.40 = (f32[56,384]{1,0:T(8,128)}, f32[56,384]{1,0:T(8,128)S(1)}, u32[]{:S(2)}, u32[]{:S(2)}) collective-permute-start(f32[56,384]{1,0:T(8,128)} %shard_map.144.refs_0_), channel_id=1, source_target_pairs={{0,2},{1,3},{2,4},{3,5},{4,6},{5,7},{6,0},{7,1},{8,10},{9,11},{10,... | collective-permute-start | bytes 258056 | tf_op jit(solution)/shard_map/ppermute | solution.py:522
  188.4 37.3 %collective-permute-start.16 = (f32[400,128]{1,0:T(8,128)}, f32[400,128]{1,0:T(8,128)}, u32[]{:S(2)}, u32[]{:S(2)}) collective-permute-start(f32[400,128]{1,0:T(8,128)} %get-tuple-element.73), channel_id=1, source_target_pairs={{0,15},{1,14},{2,9},{3,8},{4,11},{5,10},{6,13},{7,12},{8,23},{9,22... | collective-permute-start | bytes 614408 | tf_op jit(solution)/shard_map/ppermute | solution.py:531
  188.5 38.3 %collective-permute-start.17 = (f32[400,128]{1,0:T(8,128)}, f32[400,128]{1,0:T(8,128)}, u32[]{:S(2)}, u32[]{:S(2)}) collective-permute-start(f32[400,128]{1,0:T(8,128)} %get-tuple-element.74), channel_id=1, source_target_pairs={{0,12},{1,13},{2,14},{3,15},{4,8},{5,9},{6,10},{7,11},{8,20},{9,21... | collective-permute-start | bytes 614408 | tf_op jit(solution)/shard_map/ppermute | solution.py:531
  191.8 35.9 %collective-permute-start.18 = (f32[400,128]{1,0:T(8,128)}, f32[400,128]{1,0:T(8,128)}, u32[]{:S(2)}, u32[]{:S(2)}) collective-permute-start(f32[400,128]{1,0:T(8,128)} %get-tuple-element.75), channel_id=1, source_target_pairs={{0,13},{1,12},{2,15},{3,14},{4,9},{5,8},{6,11},{7,10},{8,21},{9,20... | collective-permute-start | bytes 614408 | tf_op jit(solution)/shard_map/ppermute | solution.py:531
  205.5 16.5 %collective-permute-start.41 = (f32[56,384]{1,0:T(8,128)}, f32[56,384]{1,0:T(8,128)S(1)}, u32[]{:S(2)}, u32[]{:S(2)}) collective-permute-start(f32[56,384]{1,0:T(8,128)} %shard_map.144.refs_0_), channel_id=1, source_target_pairs={{0,4},{1,5},{2,6},{3,7},{4,0},{5,1},{6,2},{7,3},{8,12},{9,13},{10,... | collective-permute-start | bytes 258056 | tf_op jit(solution)/shard_map/ppermute | solution.py:522
  205.5 16.9 %collective-permute-start.42 = (f32[56,384]{1,0:T(8,128)}, f32[56,384]{1,0:T(8,128)S(1)}, u32[]{:S(2)}, u32[]{:S(2)}) collective-permute-start(f32[56,384]{1,0:T(8,128)} %shard_map.144.refs_0_), channel_id=1, source_target_pairs={{0,6},{1,7},{2,0},{3,1},{4,2},{5,3},{6,4},{7,5},{8,14},{9,15},{10,... | collective-permute-start | bytes 258056 | tf_op jit(solution)/shard_map/ppermute | solution.py:522
  222.0 11.8 %collective-permute-start.19 = (f32[400,128]{1,0:T(8,128)}, f32[400,128]{1,0:T(8,128)S(1)}, u32[]{:S(2)}, u32[]{:S(2)}) collective-permute-start(f32[400,128]{1,0:T(8,128)} %get-tuple-element.76), channel_id=1, source_target_pairs={{0,10},{1,11},{2,12},{3,13},{4,14},{5,15},{6,8},{7,9},{8,18},{9,19... | collective-permute-start | bytes 614408 | tf_op jit(solution)/shard_map/ppermute | solution.py:531
  222.4 11.4 %collective-permute-start.20 = (f32[400,128]{1,0:T(8,128)}, f32[400,128]{1,0:T(8,128)S(1)}, u32[]{:S(2)}, u32[]{:S(2)}) collective-permute-start(f32[400,128]{1,0:T(8,128)} %get-tuple-element.77), channel_id=1, source_target_pairs={{0,11},{1,10},{2,13},{3,12},{4,15},{5,14},{6,9},{7,8},{8,19},{9,18... | collective-permute-start | bytes 614408 | tf_op jit(solution)/shard_map/ppermute | solution.py:531
  225.7 28.4 %collective-permute-start.43 = (f32[200,384]{1,0:T(8,128)}, f32[200,384]{1,0:T(8,128)S(1)}, u32[]{:S(2)}, u32[]{:S(2)}) collective-permute-start(f32[200,384]{1,0:T(8,128)} %shard_map.145.refs_0_), channel_id=1, source_target_pairs={{0,8},{8,0},{16,24},{24,16},{1,9},{9,1},{17,25},{25,17},{2,10},{10... | collective-permute-start | bytes 921608 | tf_op jit(solution)/shard_map/ppermute | solution.py:535
  226.7 27.4 %collective-permute-start.44 = (f32[200,384]{1,0:T(8,128)}, f32[200,384]{1,0:T(8,128)S(1)}, u32[]{:S(2)}, u32[]{:S(2)}) collective-permute-start(f32[200,384]{1,0:T(8,128)} %shard_map.145.refs_0_), channel_id=1, source_target_pairs={{0,16},{8,24},{16,0},{24,8},{1,17},{9,25},{17,1},{25,9},{2,18},{10... | collective-permute-start | bytes 921608 | tf_op jit(solution)/shard_map/ppermute | solution.py:535
  227.7 27.0 %collective-permute-start.45 = (f32[200,384]{1,0:T(8,128)}, f32[200,384]{1,0:T(8,128)S(1)}, u32[]{:S(2)}, u32[]{:S(2)}) collective-permute-start(f32[200,384]{1,0:T(8,128)} %shard_map.145.refs_0_), channel_id=1, source_target_pairs={{0,24},{8,16},{16,8},{24,0},{1,25},{9,17},{17,9},{25,1},{2,26},{10... | collective-permute-start | bytes 921608 | tf_op jit(solution)/shard_map/ppermute | solution.py:535
  233.8 19.7 %collective-permute-start.21 = (f32[400,128]{1,0:T(8,128)S(1)}, f32[400,128]{1,0:T(8,128)S(1)}, u32[]{:S(2)}, u32[]{:S(2)}) collective-permute-start(f32[400,128]{1,0:T(8,128)S(1)} %copy-done.38), channel_id=1, source_target_pairs={{0,9},{1,8},{2,11},{3,10},{4,13},{5,12},{6,15},{7,14},{8,17},{9,16... | collective-permute-start | bytes 614408 | tf_op jit(solution)/shard_map/ppermute | solution.py:531
  233.8 24.0 %collective-permute-start.22 = (f32[400,128]{1,0:T(8,128)}, f32[400,128]{1,0:T(8,128)S(1)}, u32[]{:S(2)}, u32[]{:S(2)}) collective-permute-start(f32[400,128]{1,0:T(8,128)} %get-tuple-element.79), channel_id=1, source_target_pairs={{0,8},{1,9},{2,10},{3,11},{4,12},{5,13},{6,14},{7,15},{8,16},{9,17... | collective-permute-start | bytes 614408 | tf_op jit(solution)/shard_map/ppermute | solution.py:531
  253.5 21.2 %collective-permute-start.46 = (f32[200,384]{1,0:T(8,128)}, f32[200,384]{1,0:T(8,128)S(1)}, u32[]{:S(2)}, u32[]{:S(2)}) collective-permute-start(f32[200,384]{1,0:T(8,128)} %shard_map.145.refs_0_), channel_id=1, source_target_pairs={{0,1},{1,0},{2,3},{3,2},{4,5},{5,4},{6,7},{7,6},{8,9},{9,8},{10,11... | collective-permute-start | bytes 921608 | tf_op jit(solution)/shard_map/ppermute | solution.py:522
  254.1 20.5 %collective-permute-start.47 = (f32[200,384]{1,0:T(8,128)S(1)}, f32[200,384]{1,0:T(8,128)S(1)}, u32[]{:S(2)}, u32[]{:S(2)}) collective-permute-start(f32[200,384]{1,0:T(8,128)S(1)} %collective-permute-done.43.refs_1_), channel_id=1, source_target_pairs={{0,1},{1,0},{2,3},{3,2},{4,5},{5,4},{6,7},{7,6},{8,9},{9,8},{10,11... | collective-permute-start | bytes 921608 | tf_op jit(solution)/shard_map/ppermute | solution.py:522
  254.2 20.5 %collective-permute-start.48 = (f32[200,384]{1,0:T(8,128)S(1)}, f32[200,384]{1,0:T(8,128)S(1)}, u32[]{:S(2)}, u32[]{:S(2)}) collective-permute-start(f32[200,384]{1,0:T(8,128)S(1)} %collective-permute-done.44.refs_2_), channel_id=1, source_target_pairs={{0,1},{1,0},{2,3},{3,2},{4,5},{5,4},{6,7},{7,6},{8,9},{9,8},{10,11... | collective-permute-start | bytes 921608 | tf_op jit(solution)/shard_map/ppermute | solution.py:522
  254.7 20.0 %collective-permute-start.49 = (f32[200,384]{1,0:T(8,128)S(1)}, f32[200,384]{1,0:T(8,128)S(1)}, u32[]{:S(2)}, u32[]{:S(2)}) collective-permute-start(f32[200,384]{1,0:T(8,128)S(1)} %collective-permute-done.45.refs_3_), channel_id=1, source_target_pairs={{0,1},{1,0},{2,3},{3,2},{4,5},{5,4},{6,7},{7,6},{8,9},{9,8},{10,11... | collective-permute-start | bytes 921608 | tf_op jit(solution)/shard_map/ppermute | solution.py:522
  258.5 11.8 %collective-permute-start.29 = (f32[400,128]{1,0:T(8,128)}, f32[400,128]{1,0:T(8,128)}, u32[]{:S(2)}, u32[]{:S(2)}) collective-permute-start(f32[400,128]{1,0:T(8,128)} %get-tuple-element.90), channel_id=1, source_target_pairs={{0,1},{1,0},{2,3},{3,2},{4,5},{5,4},{6,7},{7,6},{8,9},{9,8},{10,11... | collective-permute-start | bytes 614408 | tf_op jit(solution)/shard_map/ppermute | solution.py:522
  (59 other events, 1582.4 us)
where the time goes:
time: 282 us; the launch traced here: 281 us
  waiting for transfers between devices  90.6 us (32%)
  Pallas kernels  86.8 us (31%)
  starting transfers between devices  81.5 us (29%)
  local copies, waits for them, and re-layouts  13.1 us (5%)
  other arithmetic  7.16 us (3%)
    ppermute x16, starting transfers between devices, sent_across(): return lax.ppermute(value, ('group', 'shard'), pairs)  48.6 us
    ppermute x28, waiting for transfers between devices, sent_on(): lax.ppermute(value, 'shard', [(i, partner(i, hop, peers, 1)) for i in ran...  48.5 us
    ppermute x16, waiting for transfers between devices, sent_across(): return lax.ppermute(value, ('group', 'shard'), pairs)  38.1 us
    ppermute x28, starting transfers between devices, sent_on(): lax.ppermute(value, 'shard', [(i, partner(i, hop, peers, 1)) for i in ran...  25.7 us
    pallas_call x1, Pallas kernels, relation_grads(): kernel_call(relation_grad_kernel, [shape((2, features, edges), BF16)] + [...  16.2 us
    pallas_call x1, Pallas kernels, score_spans(): kernel_call(functools.partial(score_kernel, peers), [shape((edges, 1)), s...  14.3 us
    pallas_call x3, Pallas kernels, pick_blocks(): kernel_call(pick_kernel, [shape((features, block))] * count, 6 * features...  9.38 us
    pallas_call x1, Pallas kernels, query_rows(): kernel_call(query_kernel, [shape((features, edges)), shape((2, features,...  8.25 us
  transfers between devices with their start and end apart: 50, of which 13 were waited for; matrix products, arithmetic and copies ran while one was open for 5% of the time, Pallas kernels for 17%

commit v1 on v0

--- a/solution.py
+++ b/solution.py
@@ -1,4 +1,5 @@
 import functools
+import math
 
 import jax
 import jax.numpy as jnp
@@ -11,6 +12,7 @@
 SPAN = 512
 LANES = 128
 CHUNK = 256
+WIDE = 512
 
 
 learn_rate = 0.5
@@ -233,28 +235,8 @@
     )(edge_source, rels, *blocks)
 
 
-def score_kernel(peers, *refs):
-    live_ref, rows_ref, columns_ref, counts_ref, edge_target_ref = refs[:5]
-    blocks = refs[5:5 + peers]
-    loss_ref, grad_ref, table_ref = refs[5 + peers:8 + peers]
-    block_grads = refs[8 + peers:8 + 2 * peers]
-    total, = refs[8 + 2 * peers:]
-    features, block = blocks[0].shape
-    step = pl.program_id(0)
-
-    @pl.when(step == 0)
-    def _():
-        total[...] = jnp.zeros_like(total)
-        for p, ref in enumerate(blocks):
-            hi, lo = split2(ref[...])
-            at = pl.ds(p * block, block)
-            table_ref[:features, at] = hi
-            table_ref[features:2 * features, at] = lo
-            table_ref[2 * features:, at] = hi
-
-    score = dot(rows_ref[...], table_ref[...])
-    counts = counts_ref[0]
-    own = lax.broadcasted_iota(I32, score.shape, 1) == edge_target_ref[...]
+def softmax_step(step, live, score, counts, edge_target, loss_ref, grad_ref):
+    own = lax.broadcasted_iota(I32, score.shape, 1) == edge_target
     pos = jnp.sum(jnp.where(own, score, 0.0), axis=1, keepdims=True)
     peak = jnp.max(jnp.where(counts > 0.0, score, -jnp.inf), axis=1, keepdims=True)
     peak = jnp.maximum(pos, peak)
@@ -262,102 +244,192 @@
     pos_weight = jnp.exp(pos - peak)
     sum_all = pos_weight + jnp.sum(weight, axis=1, keepdims=True)
     edge = step * score.shape[0] + lax.broadcasted_iota(I32, pos.shape, 0)
-    live = jnp.where(edge < live_ref[0], 1.0, 0.0)
-    loss_ref[...] = (peak - pos + jnp.log(sum_all)) * live
-    scale = live / sum_all
-    pos_grad = pos_weight * scale - live
+    is_live = jnp.where(edge < live, 1.0, 0.0)
+    loss_ref[...] = (peak - pos + jnp.log(sum_all)) * is_live
+    scale = is_live / sum_all
+    pos_grad = pos_weight * scale - is_live
     grad = weight * scale + jnp.where(own, pos_grad, 0.0)
-    hi, lo = split2(grad)
-    grad_ref[0], grad_ref[1] = hi, lo
-    total[...] += dot(columns_ref[0], hi) + dot(columns_ref[0], lo) + dot(columns_ref[1], hi)
-
-    @pl.when(step == pl.num_programs(0) - 1)
-    def _():
-        for p, ref in enumerate(block_grads):
-            ref[...] = total[:, p * block:(p + 1) * block]
-
-
-def score_spans(live, blocks, rows, columns, counts, edge_target):
+    grad_ref[0], grad_ref[1] = split2(grad)
+
+
+def score_kernel(peers, *refs):
+    live_ref, rows_ref, counts_ref, edge_target_ref = refs[:4]
+    blocks = refs[4:4 + peers]
+    loss_ref, grad_ref, table_ref, scores = refs[4 + peers:]
+    features, block = blocks[0].shape
+    step = pl.program_id(0)
+    last = pl.num_programs(0) - 1
+
+    @pl.when(step == 0)
+    def _():
+        for p, ref in enumerate(blocks):
+            hi, lo = split2(ref[...])
+            at = pl.ds(p * block, block)
+            table_ref[:features, at] = hi
+            table_ref[features:2 * features, at] = lo
+            table_ref[2 * features:, at] = hi
+
+    def multiply():
+        scores[step % 2] = dot(rows_ref[...], table_ref[...])
+
+    def finish():
+        softmax_step(
+            step - 1, live_ref[0], scores[(step + 1) % 2], counts_ref[0], edge_target_ref[...],
+            loss_ref, grad_ref,
+        )
+
+    @pl.when(step == 0)
+    def _():
+        multiply()
+
+    @pl.when((step > 0) & (step < last))
+    def _():
+        multiply()
+        finish()
+
+    @pl.when(step == last)
+    def _():
+        finish()
+
+
+def score_spans(live, blocks, rows, counts, edge_target):
     peers = len(blocks)
     features, block = blocks[0].shape
     edges = edge_target.shape[0]
     table_rows = peers * block
     chunk = CHUNK
     per_span = SPAN // chunk
+    steps = edges // chunk
+
+    def now(i):
+        return jnp.minimum(i, steps - 1)
+
+    def before(i):
+        return jnp.maximum(i - 1, 0)
+
     return kernel_call(
         functools.partial(score_kernel, peers),
         [
             shape((edges, 1)),
             shape((2, edges, table_rows), BF16),
             shape((3 * features, table_rows), BF16),
-        ] + [shape((features, block))] * peers,
-        12 * features * table_rows * edges, 30 * features * edges,
-        grid=(edges // chunk,),
+        ],
+        6 * features * table_rows * edges, 30 * features * edges,
+        grid=(steps + 1,),
         in_specs=[
             SMEM,
-            pl.BlockSpec((chunk, 3 * features), lambda i: (i, 0)),
-            pl.BlockSpec((2, features, chunk), lambda i: (0, 0, i)),
-            pl.BlockSpec((1, 1, table_rows), lambda i: (i // per_span, 0, 0)),
-            pl.BlockSpec((chunk, 1), lambda i: (i, 0)),
+            pl.BlockSpec((chunk, 3 * features), lambda i: (now(i), 0)),
+            pl.BlockSpec((1, 1, table_rows), lambda i: (before(i) // per_span, 0, 0)),
+            pl.BlockSpec((chunk, 1), lambda i: (before(i), 0)),
         ] + [held((features, block))] * peers,
         out_specs=[
-            pl.BlockSpec((chunk, 1), lambda i: (i, 0)),
-            pl.BlockSpec((2, chunk, table_rows), lambda i: (0, i, 0)),
+            pl.BlockSpec((chunk, 1), lambda i: (before(i), 0)),
+            pl.BlockSpec((2, chunk, table_rows), lambda i: (0, before(i), 0)),
             held((3 * features, table_rows)),
-        ] + [held((features, block))] * peers,
-        scratch_shapes=[pltpu.VMEM((features, table_rows), F32)],
-    )(live, rows, columns, counts, edge_target, *blocks)
+        ],
+        scratch_shapes=[pltpu.VMEM((2, chunk, table_rows), F32)],
+    )(live, rows, counts, edge_target, *blocks)
+
+
+def table_grad_kernel(columns_ref, grad_ref, *outs):
+    step = pl.program_id(0)
+    block = outs[0].shape[1]
+    result = (
+        dot(columns_ref[0], grad_ref[0])
+        + dot(columns_ref[0], grad_ref[1])
+        + dot(columns_ref[1], grad_ref[0])
+    )
+    for pair in range(len(outs) // 2):
+        @pl.when(step == pair)
+        def _():
+            outs[2 * pair][...] = result[:, :block]
+            outs[2 * pair + 1][...] = result[:, block:]
+
+
+def table_grads(columns, grad, block, first, count):
+    _, features, edges = columns.shape
+    return kernel_call(
+        table_grad_kernel, [shape((features, block))] * count,
+        6 * features * count * block * edges, 4 * edges * (features + count * block),
+        grid=(count // 2,),
+        in_specs=[
+            held((2, features, edges)),
+            pl.BlockSpec((2, edges, 2 * block), lambda i: (0, 0, first // 2 + i)),
+        ],
+        out_specs=[held((features, block))] * count,
+    )(columns, grad)
 
 
 def relation_grad_kernel(
-    me_ref, table_ref, grad_ref, heads_ref, rels_ref, edge_rel_ref, source_ref, *refs
+    steps, me_ref, table_ref, grad_ref, heads_ref, rels_ref, edge_rel_ref, source_ref, *refs
 ):
-    outs, total = refs[:-1], refs[-1]
+    outs, lines, total = refs[:-2], refs[-2], refs[-1]
     groups = len(outs) // 2
     half, width = outs[0].shape
     step = pl.program_id(0)
-
-    @pl.when(step == 0)
-    def _():
-        total[...] = jnp.zeros_like(total)
-
-    features = heads_ref.shape[0]
-    hi, lo = table_ref[:features], table_ref[features:2 * features]
-    query_grad = dot_nt(hi, grad_ref[0]) + dot_nt(hi, grad_ref[1]) + dot_nt(lo, grad_ref[0])
-    source_ref[0], source_ref[1] = split2(conj_product(query_grad, rels_ref[...]))
-    hi, lo = split2(conj_product(query_grad, heads_ref[...]))
-    hot = columns_hot(edge_rel_ref[...], total.shape[1])
-    total[...] += dot(hi, hot) + dot(lo, hot)
+    features, chunk = heads_ref.shape
+    tile = total.shape[2]
+
+    @pl.when(step < steps)
+    def _():
+        hi, lo = table_ref[:features], table_ref[features:2 * features]
+        query_grad = dot_nt(hi, grad_ref[0]) + dot_nt(hi, grad_ref[1]) + dot_nt(lo, grad_ref[0])
+        source_ref[0], source_ref[1] = split2(conj_product(query_grad, rels_ref[...]))
+        lines[step] = jnp.concatenate(split2(conj_product(query_grad, heads_ref[...])), axis=1)
+
+    @pl.when(step >= steps)
+    def _():
+        part = None
+        for i in range(steps):
+            slots = edge_rel_ref[i * chunk:(i + 1) * chunk, :] - (step - steps) * tile
+            hot = columns_hot(slots, tile)
+            term = dot(lines[i, :, :chunk], hot) + dot(lines[i, :, chunk:], hot)
+            part = term if part is None else part + term
+        total[step - steps] = part
 
     @pl.when(step == pl.num_programs(0) - 1)
     def _():
         group, core = me_ref[0], me_ref[1]
         for j in range(groups):
-            at = pl.ds(pl.multiple_of((group ^ j) * width, LANES), width)
-            outs[j][...] = total[pl.ds(pl.multiple_of(core * half, 8), half), at]
-            outs[groups + j][...] = total[pl.ds(pl.multiple_of((1 - core) * half, 8), half), at]
+            for at in range(0, width, LANES):
+                start = (group ^ j) * width + at
+                rows = total.at[start // tile, :, pl.ds(pl.multiple_of(start % tile, LANES), LANES)]
+                outs[j][:, at:at + LANES] = rows[pl.ds(pl.multiple_of(core * half, 8), half), :]
+                outs[groups + j][:, at:at + LANES] = rows[
+                    pl.ds(pl.multiple_of((1 - core) * half, 8), half), :
+                ]
 
 
 def relation_grads(me, table, grad, heads, rels, edge_relation, groups, width):
     features, edges = heads.shape
     table_rows = table.shape[1]
     chunk = CHUNK
-    return kernel_call(
-        relation_grad_kernel,
+    steps = edges // chunk
+    tile = math.gcd(groups * width, WIDE)
+    tiles = groups * width // tile
+
+    def now(i):
+        return jnp.minimum(i, steps - 1)
+
+    return kernel_call(
+        functools.partial(relation_grad_kernel, steps),
         [shape((2, features, edges), BF16)] + [shape((features // 2, width))] * (2 * groups),
         10 * features * table_rows * edges, 30 * features * edges,
-        grid=(edges // chunk,),
+        grid=(steps + tiles,),
         in_specs=[
             SMEM,
             held((3 * features, table_rows)),
-            pl.BlockSpec((2, chunk, table_rows), lambda i: (0, i, 0)),
-            pl.BlockSpec((features, chunk), lambda i: (0, i)),
-            pl.BlockSpec((features, chunk), lambda i: (0, i)),
-            pl.BlockSpec((chunk, 1), lambda i: (i, 0)),
+            pl.BlockSpec((2, chunk, table_rows), lambda i: (0, now(i), 0)),
+            pl.BlockSpec((features, chunk), lambda i: (0, now(i))),
+            pl.BlockSpec((features, chunk), lambda i: (0, now(i))),
+            held((edges, 1)),
         ],
-        out_specs=[pl.BlockSpec((2, features, chunk), lambda i: (0, 0, i))]
+        out_specs=[pl.BlockSpec((2, features, chunk), lambda i: (0, 0, now(i)))]
         + [held((features // 2, width))] * (2 * groups),
-        scratch_shapes=[pltpu.VMEM((features, groups * width), F32)],
+        scratch_shapes=[
+            pltpu.VMEM((steps, features, 2 * chunk), BF16),
+            pltpu.VMEM((tiles, features, tile), F32),
+        ],
     )(me, table, grad, heads, rels, edge_relation)
 
 
@@ -587,11 +659,20 @@
     source_hots = home_hots(order, src_send[0], rows)
     target_hots = home_hots(order, dst_send[0], rows)
     heads, query_columns, query_lines = query_rows(sources, edge_source.reshape(1, -1), rels)
-    loss, grad, table, *table_grads = score_spans(
-        edge_count, targets, query_lines, query_columns, counts, edge_target.reshape(-1, 1)
+    loss, grad, table = score_spans(
+        edge_count, targets, query_lines, counts, edge_target.reshape(-1, 1)
     )
+    table_parts = table_grads(query_columns, grad, block, 0, 2)
+    table_parts += table_grads(query_columns, grad, block, 2, peers - 2)
     back = [(-hop[0], hop[1]) for hop in ways]
-    home = [sent_across(value, hop, peers, groups, 1) for value, hop in zip(table_grads, back)]
+    home = [
+        sent_across(value, hop, peers, groups, 1)
+        for value, hop in zip(table_parts[:2], back[:2])
+    ]
+    home += [
+        sent_across(value, hop, peers, groups, 1)
+        for value, hop in zip(table_parts[2:], back[2:])
+    ]
     source_lines, *halves = relation_grads(
         here, table, grad, heads, rels, edge_relation.reshape(-1, 1), groups, width
     )

time: 282 us -> 277 us (0.982)
  starting transfers between devices: 81.5 us -> 64.6 us
  waiting for transfers between devices: 90.6 us -> 100 us
    ppermute x16, starting transfers between devices: 48.6 us -> 35.3 us  [sent_across(): return lax.ppermute(value, ('group', 'shard'), pairs)]
    ppermute x6, waiting for transfers between devices: 4.03 us -> 11.5 us  [sent_group(): return lax.ppermute(value, 'group', [(g, g ^ bit) for g in range(groups)])]
    pallas_call x1 -> x3, Pallas kernels: 16.2 us -> 21.8 us  [the longest x1 12.8 us: relation_grads(): kernel_call(functools.partial(relation_grad_kernel, steps), [shape((2, fe...]
    ppermute x28, starting transfers between devices: 25.7 us -> 22 us  [sent_on(): lax.ppermute(value, 'shard', [(i, partner(i, hop, peers, 1)) for i in ran...]
    pallas_call x1, Pallas kernels: 14.3 us -> 10.6 us  [score_spans(): kernel_call(functools.partial(score_kernel, peers), [shape((edges, 1)), s...]
  transfers between devices with their start and end apart: 50 -> 50, of which waited for: 13 -> 15; matrix products, arithmetic and copies ran while one was open for 5% -> 6% of each run, Pallas kernels for 17% -> 21%
where the time goes in v1:
time: 277 us; the launch traced here: 276 us
  waiting for transfers between devices  100 us (36%)
  Pallas kernels  88.8 us (32%)
  starting transfers between devices  64.6 us (23%)
  local copies, waits for them, and re-layouts  12.3 us (4%)
  other arithmetic  8.27 us (3%)
    ppermute x28, waiting for transfers between devices, sent_on(): lax.ppermute(value, 'shard', [(i, partner(i, hop, peers, 1)) for i in ran...  48.3 us
    ppermute x16, waiting for transfers between devices, sent_across(): return lax.ppermute(value, ('group', 'shard'), pairs)  40.6 us
    ppermute x16, starting transfers between devices, sent_across(): return lax.ppermute(value, ('group', 'shard'), pairs)  35.3 us
    ppermute x28, starting transfers between devices, sent_on(): lax.ppermute(value, 'shard', [(i, partner(i, hop, peers, 1)) for i in ran...  22 us
    pallas_call x1, Pallas kernels, relation_grads(): kernel_call(functools.partial(relation_grad_kernel, steps), [shape((2, fe...  12.8 us
    ppermute x6, waiting for transfers between devices, sent_group(): return lax.ppermute(value, 'group', [(g, g ^ bit) for g in range(groups)])  11.5 us
    pallas_call x1, Pallas kernels, score_spans(): kernel_call(functools.partial(score_kernel, peers), [shape((edges, 1)), s...  10.6 us
    pallas_call x3, Pallas kernels, pick_blocks(): kernel_call(pick_kernel, [shape((features, block))] * count, 6 * features...  9.46 us
  transfers between devices with their start and end apart: 50, of which 15 were waited for; matrix products, arithmetic and copies ran while one was open for 6% of the time, Pallas kernels for 21%

profile of v1, /device:TPU:0, one launch (start us, length us, event | category | flops | bytes accessed | tf_op | source)
XLA Modules:
  0.0 276.2 jit_solution(17245891333853293100)
XLA Ops:
  1.3 2.9 %shard_map.133 = (f32[400,128]{1,0:T(8,128)}, f32[400,128]{1,0:T(8,128)}, f32[400,128]{1,0:T(8,128)}, f32[400,128]{1,0:T(8,128)}) custom-call(s32[4]{0:T(128)} %pad_add_fusion.1.order_ref, f32[400,512]{1,0:T(8,128)} %bitcast.29, s32[8,128]{1,0:T(8,128)} %bitcast.41), custom_call_target="tpu_custom_call" | custom-call | flops 629145600 | bytes 1638400 | tf_op jit(solution)/shard_map/pallas_call | solution.py:126
  4.2 5.1 %collective-permute-start.4 = (f32[400,128]{1,0:T(8,128)}, f32[400,128]{1,0:T(8,128)S(1)}, u32[]{:S(2)}, u32[]{:S(2)}) collective-permute-start(f32[400,128]{1,0:T(8,128)} %get-tuple-element.58), channel_id=1, source_target_pairs={{0,6},{1,7},{2,0},{3,1},{4,2},{5,3},{6,4},{7,5},{8,14},{9,15},{10,... | collective-permute-start | bytes 614408 | tf_op jit(solution)/shard_map/ppermute | solution.py:594
  10.5 2.9 %shard_map.132 = (f32[400,128]{1,0:T(8,128)}, f32[400,128]{1,0:T(8,128)}, f32[400,128]{1,0:T(8,128)}, f32[400,128]{1,0:T(8,128)}) custom-call(s32[4]{0:T(128)} %pad_add_fusion.order_ref, f32[400,512]{1,0:T(8,128)} %bitcast.30, s32[8,128]{1,0:T(8,128)} %bitcast.42), custom_call_target="tpu_custom_call" | custom-call | flops 629145600 | bytes 1638400 | tf_op jit(solution)/shard_map/pallas_call | solution.py:126
  13.4 1.6 collective-permute-start
  17.1 2.6 shard_map.135.refs_2_
  22.5 7.5 %shard_map.131.refs_1_.rels_ref = f32[400,1024]{1,0:T(8,128)} custom-call(f32[400,1345]{1,0:T(8,128)} %bitcast.26, s32[1,1024]{1,0:T(1,128)} %bitcast.37), custom_call_target="tpu_custom_call" | custom-call | flops 3460300800 | bytes 3276800 | tf_op jit(solution)/shard_map/pallas_call | solution.py:153
  30.7 3.6 %shard_map.136 = (f32[400,128]{1,0:T(8,128)}, f32[400,128]{1,0:T(8,128)}, f32[400,128]{1,0:T(8,128)}, f32[400,128]{1,0:T(8,128)}, f32[400,128]{1,0:T(8,128)}, /*...) custom-call(s32[8]{0:T(128)} %stack.48.order_ref, f32[400,512]{1,0:T(8,128)} %bitcast.31, s32[8,128]{1,0:T(8,128)} %bitcast.39), custom_call_target="tpu_custom_call" | custom-call | flops 1258291200 | bytes 3276800 | tf_op jit(solution)/shard_map/pallas_call | solution.py:126
  34.3 2.2 collective-permute-start.2
  37.0 4.1 %collective-permute-start.10 = (f32[400,128]{1,0:T(8,128)}, f32[400,128]{1,0:T(8,128)S(1)}, u32[]{:S(2)}, u32[]{:S(2)}) collective-permute-start(f32[400,128]{1,0:T(8,128)} %get-tuple-element.67), channel_id=1, source_target_pairs={{0,29},{1,28},{2,31},{3,30},{4,25},{5,24},{6,27},{7,26},{8,5},{9,4... | collective-permute-start | bytes 614408 | tf_op jit(solution)/shard_map/ppermute | solution.py:603
  44.2 12.3 %collective-permute-done.2.refs_4_ = f32[400,128]{1,0:T(8,128)S(1)} collective-permute-done((f32[400,128]{1,0:T(8,128)S(1)}, f32[400,128]{1,0:T(8,128)S(1)}, u32[]{:S(2)}, u32[]{:S(2)}) %collective-permute-start.2) | collective-permute-done | bytes 204832 | tf_op jit(solution)/shard_map/ppermute | solution.py:594
  57.2 2.3 collective-permute-done.3.refs_5_
  59.5 2.3 collective-permute-start.14
  61.9 3.1 %collective-permute-done.10.refs_7_ = f32[400,128]{1,0:T(8,128)S(1)} collective-permute-done((f32[400,128]{1,0:T(8,128)}, f32[400,128]{1,0:T(8,128)S(1)}, u32[]{:S(2)}, u32[]{:S(2)}) %collective-permute-start.10) | collective-permute-done | bytes 204832 | tf_op jit(solution)/shard_map/ppermute | solution.py:603
  65.0 11.0 %collective-permute-start.7 = (f32[400,128]{1,0:T(8,128)}, f32[400,128]{1,0:T(8,128)S(1)}, u32[]{:S(2)}, u32[]{:S(2)}) collective-permute-start(f32[400,128]{1,0:T(8,128)} %get-tuple-element.64), channel_id=1, source_target_pairs={{0,26},{1,27},{2,28},{3,29},{4,30},{5,31},{6,24},{7,25},{8,2},{9,3... | collective-permute-start | bytes 614408 | tf_op jit(solution)/shard_map/ppermute | solution.py:603
  76.0 4.5 %collective-permute-start.9 = (f32[400,128]{1,0:T(8,128)}, f32[400,128]{1,0:T(8,128)S(1)}, u32[]{:S(2)}, u32[]{:S(2)}) collective-permute-start(f32[400,128]{1,0:T(8,128)} %get-tuple-element.66), channel_id=1, source_target_pairs={{0,28},{1,29},{2,30},{3,31},{4,24},{5,25},{6,26},{7,27},{8,4},{9,5... | collective-permute-start | bytes 614408 | tf_op jit(solution)/shard_map/ppermute | solution.py:603
  80.6 8.2 %shard_map.134 = (f32[400,1024]{1,0:T(8,128)}, bf16[2,400,1024]{2,1,0:T(8,128)(2,1)}, bf16[1024,1200]{1,0:T(8,128)(2,1)}) custom-call(s32[1,1024]{1,0:T(1,128)} %bitcast.34, f32[400,1024]{1,0:T(8,128)} %shard_map.131.refs_1_.rels_ref, f32[400,128]{1,0:T(8,128)} %copy-done.44, f32[400,128]{1,0:T(8,128)} %copy-done.45, f32[400,128]{1,0:T(8,128)} %copy-done.50, ...), custom_call_target="tpu_custom_call" | custom-call | flops 2516582400 | bytes 8192000 | tf_op jit(solution)/shard_map/pallas_call | solution.py:220
  88.9 8.5 %collective-permute-done.9.refs_6_ = f32[400,128]{1,0:T(8,128)S(1)} collective-permute-done((f32[400,128]{1,0:T(8,128)}, f32[400,128]{1,0:T(8,128)S(1)}, u32[]{:S(2)}, u32[]{:S(2)}) %collective-permute-start.9) | collective-permute-done | bytes 204832 | tf_op jit(solution)/shard_map/ppermute | solution.py:603
  98.1 10.6 %shard_map.137 = (f32[1024,1]{1,0:T(8,128)}, bf16[2,1024,1024]{2,1,0:T(8,128)(2,1)}, bf16[1200,1024]{1,0:T(8,128)(2,1)}) custom-call(s32[1]{0:T(128)S(6)} %copy.20.refs_0_, bf16[1024,1200]{1,0:T(8,128)(2,1)} %get-tuple-element.63.refs_1_, f32[2,1,1024]{2,1,0:T(1,128)} %shard_map.135.refs_2_, s32[1024,1]{1,0:T(8,128)} %copy.16.refs_3_, ...), custom_call_target="tpu_custom_call" | custom-call | flops 2516582400 | bytes 12288000 | tf_op jit(solution)/shard_map/pallas_call | solution.py:310
  108.7 12.8 %shard_map.142 = (bf16[2,400,1024]{2,1,0:T(8,128)(2,1)}, f32[200,384]{1,0:T(8,128)}, f32[200,384]{1,0:T(8,128)}, f32[200,384]{1,0:T(8,128)}, f32[200,384]{1,0:T(...) custom-call(s32[2]{0:T(128)} %pad_add_fusion.2.me_ref, ...), custom_call_target="tpu_custom_call" | custom-call | flops 4194304000 | bytes 12288000 | tf_op jit(solution)/shard_map/pallas_call | solution.py:414
  124.5 1.5 collective-permute-start.36
  127.0 1.6 collective-permute-start.34
  131.2 5.8 %shard_map.143 = (f32[400,128]{1,0:T(8,128)}, f32[400,128]{1,0:T(8,128)}, f32[400,128]{1,0:T(8,128)}, f32[400,128]{1,0:T(8,128)}, f32[400,128]{1,0:T(8,128)}, /*...) custom-call(bf16[2,400,1024]{2,1,0:T(8,128)(2,1)} %get-tuple-element.83.rows_ref, ...), custom_call_target="tpu_custom_call" | custom-call | flops 1677721600 | bytes 4915200 | tf_op jit(solution)/shard_map/pallas_call | solution.py:456
  139.1 2.2 collective-permute-done.34.refs_2_
  142.8 2.1 shard_map.145
  144.9 1.7 collective-permute-start.38
  148.2 2.7 collective-permute-start.27
  152.4 20.3 %collective-permute-done.38.refs_2_ = f32[56,384]{1,0:T(8,128)S(1)} collective-permute-done((f32[56,384]{1,0:T(8,128)}, f32[56,384]{1,0:T(8,128)S(1)}, u32[]{:S(2)}, u32[]{:S(2)}) %collective-permute-start.38) | collective-permute-done | bytes 86048 | tf_op jit(solution)/shard_map/ppermute | solution.py:594
  172.7 5.7 %shard_map.139 = (f32[400,128]{1,0:T(8,128)}, f32[400,128]{1,0:T(8,128)}, f32[400,128]{1,0:T(8,128)}, f32[400,128]{1,0:T(8,128)}, f32[400,128]{1,0:T(8,128)}, /*index=5*/f32[400,128]{1,0:T(8,128)}) custom-call(bf16[2,400,1024]{2,1,0:T(8,128)(2,1)} %get-tuple-element.62.columns_ref, bf16[2,1024,1024]{2,1,0:T(8,128)(2,1)} %get-tuple-element.72.grad_ref), custom_call_target="tpu_custom_call" | custom-call | flops 1887436800 | bytes 4784128 | tf_op jit(solution)/shard_map/pallas_call | solution.py:351
  178.5 3.8 %collective-permute-done.39.refs_3_ = f32[56,384]{1,0:T(8,128)S(1)} collective-permute-done((f32[56,384]{1,0:T(8,128)}, f32[56,384]{1,0:T(8,128)S(1)}, u32[]{:S(2)}, u32[]{:S(2)}) %collective-permute-start.39) | collective-permute-done | bytes 86048 | tf_op jit(solution)/shard_map/ppermute | solution.py:594
  183.1 1.7 shard_map.146.refs_0_
  185.2 2.7 collective-permute-start.18
  187.9 2.0 collective-permute-start.19
  190.8 22.0 %collective-permute-done.17.refs_2_ = f32[400,128]{1,0:T(8,128)S(1)} collective-permute-done((f32[400,128]{1,0:T(8,128)}, f32[400,128]{1,0:T(8,128)S(1)}, u32[]{:S(2)}, u32[]{:S(2)}) %collective-permute-start.17) | collective-permute-done | bytes 204832 | tf_op jit(solution)/shard_map/ppermute | solution.py:603
  212.9 6.4 %collective-permute-done.41.refs_2_ = f32[56,384]{1,0:T(8,128)S(1)} collective-permute-done((f32[56,384]{1,0:T(8,128)}, f32[56,384]{1,0:T(8,128)S(1)}, u32[]{:S(2)}, u32[]{:S(2)}) %collective-permute-start.41) | collective-permute-done | bytes 86048 | tf_op jit(solution)/shard_map/ppermute | solution.py:594
  220.2 1.5 collective-permute-start.22
  222.2 1.8 shard_map.147.refs_0_
  224.1 1.9 collective-permute-start.43
  227.7 3.3 %shard_map.138 = (f32[400,128]{1,0:T(8,128)}, f32[400,128]{1,0:T(8,128)}) custom-call(bf16[2,400,1024]{2,1,0:T(8,128)(2,1)} %get-tuple-element.62.columns_ref, bf16[2,1024,1024]{2,1,0:T(8,128)(2,1)} %get-tuple-element.72.grad_ref), custom_call_target="tpu_custom_call" | custom-call | flops 629145600 | bytes 2686976 | tf_op jit(solution)/shard_map/pallas_call | solution.py:351
  231.0 2.4 collective-permute-start.15
  234.0 7.0 %collective-permute-done.15.refs_0_ = f32[400,128]{1,0:T(8,128)S(1)} collective-permute-done((f32[400,128]{1,0:T(8,128)}, f32[400,128]{1,0:T(8,128)S(1)}, u32[]{:S(2)}, u32[]{:S(2)}) %collective-permute-start.15) | collective-permute-done | bytes 204832 | tf_op jit(solution)/shard_map/ppermute | solution.py:603
  241.1 4.0 %collective-permute-done.43.refs_1_ = f32[200,384]{1,0:T(8,128)S(1)} collective-permute-done((f32[200,384]{1,0:T(8,128)}, f32[200,384]{1,0:T(8,128)S(1)}, u32[]{:S(2)}, u32[]{:S(2)}) %collective-permute-start.43) | collective-permute-done | bytes 307232 | tf_op jit(solution)/shard_map/ppermute | solution.py:607
  245.1 3.0 %collective-permute-start.47 = (f32[200,384]{1,0:T(8,128)S(1)}, f32[200,384]{1,0:T(8,128)S(1)}, u32[]{:S(2)}, u32[]{:S(2)}) collective-permute-start(f32[200,384]{1,0:T(8,128)S(1)} %collective-permute-done.43.refs_1_), channel_id=1, source_target_pairs={{0,1},{1,0},{2,3},{3,2},{4,5},{5,4},{6,7},{7,6},{8,9},{9,8},{10,11... | collective-permute-start | bytes 921608 | tf_op jit(solution)/shard_map/ppermute | solution.py:594
  248.1 5.3 %collective-permute-done.45.refs_3_ = f32[200,384]{1,0:T(8,128)S(1)} collective-permute-done((f32[200,384]{1,0:T(8,128)}, f32[200,384]{1,0:T(8,128)S(1)}, u32[]{:S(2)}, u32[]{:S(2)}) %collective-permute-start.45) | collective-permute-done | bytes 307232 | tf_op jit(solution)/shard_map/ppermute | solution.py:607
  256.6 2.3 shard_map.130.hot_ref
  258.9 2.3 shard_map.141.hot_ref
  262.0 3.7 %shard_map.140.other_ref = f32[400,512]{1,0:T(8,128)} custom-call(bf16[1024,512]{1,0:T(8,128)(2,1)} %shard_map.130.hot_ref, f32[400,128]{1,0:T(8,128)} %copy-done.25, f32[400,128]{1,0:T(8,128)} %copy-done.26, f32[400,128]{1,0:T(8,128)} %copy-done.19, f32[400,128]{1,0:T(8,128)} %copy-done.20, f32[400,128]{1,0:T(8,128)} %copy-done.21, f32[400,128]{1,0:T(8,128)} %copy-done.22, ...), custom_call_target="tpu_custom_call" | custom-call | flops 838860800 | bytes 3276800 | tf_op jit(solution)/shard_map/pallas_call | solution.py:481
  265.7 4.3 %shard_map.144 = f32[400,512]{1,0:T(8,128)} custom-call(f32[400,512]{1,0:T(8,128)} %shard_map.140.other_ref, f32[400,512]{1,0:T(8,128)} %bitcast.32, f32[1,512]{1,0:T(1,128)} %bitcast.44, bf16[1024,512]{1,0:T(8,128)(2,1)} %shard_map.141.hot_ref, f32[400,128]{1,0:T(8,128)} %copy-done.13, f32[400,128]{1,0:T(8,128)} %copy-done.14, f32[400,128]{1,0:T(8,128)} %copy-done.15, ...), custom_call_target="tpu_custom_call" | custom-call | flops 838860800 | bytes 3276800 | tf_op jit(solution)/shard_map/pallas_call | solution.py:500
  271.6 4.6 %shard_map.148 = f32[400,1345]{1,0:T(8,128)} custom-call(s32[2]{0:T(128)} %pad_add_fusion.2.me_ref, f32[400,1345]{1,0:T(8,128)} %bitcast.27, f32[1,1345]{1,0:T(1,128)} %reshape.36.state_ref, f32[200,384]{1,0:T(8,128)} %shard_map.147.refs_0_, f32[200,384]{1,0:T(8,128)} %copy-done.6, f32[200,384]{1,0:T(8,128)} %copy-done.7, f32[200,384]{1,0:T(8,128)} %copy-done.8, ...), custom_call_target="tpu_custom_call" | custom-call | flops 4304000 | bytes 6456000 | tf_op jit(solution)/shard_map/pallas_call | solution.py:585
  (208 shorter events, 36.7 us)
Async XLA Ops:
  4.2 30.1 %collective-permute-start.4 = (f32[400,128]{1,0:T(8,128)}, f32[400,128]{1,0:T(8,128)S(1)}, u32[]{:S(2)}, u32[]{:S(2)}) collective-permute-start(f32[400,128]{1,0:T(8,128)} %get-tuple-element.58), channel_id=1, source_target_pairs={{0,6},{1,7},{2,0},{3,1},{4,2},{5,3},{6,4},{7,5},{8,14},{9,15},{10,... | collective-permute-start | bytes 614408 | tf_op jit(solution)/shard_map/ppermute | solution.py:594
  9.3 27.3 %collective-permute-start.5 = (f32[400,128]{1,0:T(8,128)}, f32[400,128]{1,0:T(8,128)S(1)}, u32[]{:S(2)}, u32[]{:S(2)}) collective-permute-start(f32[400,128]{1,0:T(8,128)} %get-tuple-element.59), channel_id=1, source_target_pairs={{0,7},{1,6},{2,1},{3,0},{4,3},{5,2},{6,5},{7,4},{8,15},{9,14},{10,... | collective-permute-start | bytes 614408 | tf_op jit(solution)/shard_map/ppermute | solution.py:594
  9.3 27.8 %collective-permute-start.6 = (f32[400,128]{1,0:T(8,128)}, f32[400,128]{1,0:T(8,128)S(1)}, u32[]{:S(2)}, u32[]{:S(2)}) collective-permute-start(f32[400,128]{1,0:T(8,128)} %get-tuple-element.60), channel_id=1, source_target_pairs={{0,1},{1,0},{2,3},{3,2},{4,5},{5,4},{6,7},{7,6},{8,9},{9,8},{10,11... | collective-permute-start | bytes 614408 | tf_op jit(solution)/shard_map/ppermute | solution.py:594
  13.4 27.7 %collective-permute-start = (f32[400,128]{1,0:T(8,128)}, f32[400,128]{1,0:T(8,128)S(1)}, u32[]{:S(2)}, u32[]{:S(2)}) collective-permute-start(f32[400,128]{1,0:T(8,128)} %get-tuple-element.54), channel_id=1, source_target_pairs={{0,2},{1,3},{2,4},{3,5},{4,6},{5,7},{6,0},{7,1},{8,10},{9,11},{10,... | collective-permute-start | bytes 614408 | tf_op jit(solution)/shard_map/ppermute | solution.py:594
  15.0 27.7 %collective-permute-start.1 = (f32[400,128]{1,0:T(8,128)}, f32[400,128]{1,0:T(8,128)S(1)}, u32[]{:S(2)}, u32[]{:S(2)}) collective-permute-start(f32[400,128]{1,0:T(8,128)} %get-tuple-element.55), channel_id=1, source_target_pairs={{0,3},{1,2},{2,5},{3,4},{4,7},{5,6},{6,1},{7,0},{8,11},{9,10},{10,... | collective-permute-start | bytes 614408 | tf_op jit(solution)/shard_map/ppermute | solution.py:594
  34.3 22.2 %collective-permute-start.2 = (f32[400,128]{1,0:T(8,128)S(1)}, f32[400,128]{1,0:T(8,128)S(1)}, u32[]{:S(2)}, u32[]{:S(2)}) collective-permute-start(f32[400,128]{1,0:T(8,128)S(1)} %copy-done.48), channel_id=1, source_target_pairs={{0,4},{1,5},{2,6},{3,7},{4,0},{5,1},{6,2},{7,3},{8,12},{9,13},{10,... | collective-permute-start | bytes 614408 | tf_op jit(solution)/shard_map/ppermute | solution.py:594
  36.5 23.0 %collective-permute-start.3 = (f32[400,128]{1,0:T(8,128)S(1)}, f32[400,128]{1,0:T(8,128)S(1)}, u32[]{:S(2)}, u32[]{:S(2)}) collective-permute-start(f32[400,128]{1,0:T(8,128)S(1)} %copy-done.46), channel_id=1, source_target_pairs={{0,5},{1,4},{2,7},{3,6},{4,1},{5,0},{6,3},{7,2},{8,13},{9,12},{10,... | collective-permute-start | bytes 614408 | tf_op jit(solution)/shard_map/ppermute | solution.py:594
  37.0 27.9 %collective-permute-start.10 = (f32[400,128]{1,0:T(8,128)}, f32[400,128]{1,0:T(8,128)S(1)}, u32[]{:S(2)}, u32[]{:S(2)}) collective-permute-start(f32[400,128]{1,0:T(8,128)} %get-tuple-element.67), channel_id=1, source_target_pairs={{0,29},{1,28},{2,31},{3,30},{4,25},{5,24},{6,27},{7,26},{8,5},{9,4... | collective-permute-start | bytes 614408 | tf_op jit(solution)/shard_map/ppermute | solution.py:603
  41.1 34.9 %collective-permute-start.11 = (f32[400,128]{1,0:T(8,128)}, f32[400,128]{1,0:T(8,128)S(1)}, u32[]{:S(2)}, u32[]{:S(2)}) collective-permute-start(f32[400,128]{1,0:T(8,128)} %get-tuple-element.68), channel_id=1, source_target_pairs={{0,30},{1,31},{2,24},{3,25},{4,26},{5,27},{6,28},{7,29},{8,6},{9,7... | collective-permute-start | bytes 614408 | tf_op jit(solution)/shard_map/ppermute | solution.py:603
  42.6 33.4 %collective-permute-start.12 = (f32[400,128]{1,0:T(8,128)}, f32[400,128]{1,0:T(8,128)S(1)}, u32[]{:S(2)}, u32[]{:S(2)}) collective-permute-start(f32[400,128]{1,0:T(8,128)} %get-tuple-element.69), channel_id=1, source_target_pairs={{0,31},{1,30},{2,25},{3,24},{4,27},{5,26},{6,29},{7,28},{8,7},{9,6... | collective-permute-start | bytes 614408 | tf_op jit(solution)/shard_map/ppermute | solution.py:603
  56.5 32.3 %collective-permute-start.13 = (f32[400,128]{1,0:T(8,128)}, f32[400,128]{1,0:T(8,128)S(1)}, u32[]{:S(2)}, u32[]{:S(2)}) collective-permute-start(f32[400,128]{1,0:T(8,128)} %get-tuple-element.70), channel_id=1, source_target_pairs={{0,25},{1,24},{2,27},{3,26},{4,29},{5,28},{6,31},{7,30},{8,1},{9,0... | collective-permute-start | bytes 614408 | tf_op jit(solution)/shard_map/ppermute | solution.py:603
  59.5 29.3 %collective-permute-start.14 = (f32[400,128]{1,0:T(8,128)}, f32[400,128]{1,0:T(8,128)S(1)}, u32[]{:S(2)}, u32[]{:S(2)}) collective-permute-start(f32[400,128]{1,0:T(8,128)} %get-tuple-element.71), channel_id=1, source_target_pairs={{0,24},{1,25},{2,26},{3,27},{4,28},{5,29},{6,30},{7,31},{8,0},{9,1... | collective-permute-start | bytes 614408 | tf_op jit(solution)/shard_map/ppermute | solution.py:603
  65.0 23.9 %collective-permute-start.7 = (f32[400,128]{1,0:T(8,128)}, f32[400,128]{1,0:T(8,128)S(1)}, u32[]{:S(2)}, u32[]{:S(2)}) collective-permute-start(f32[400,128]{1,0:T(8,128)} %get-tuple-element.64), channel_id=1, source_target_pairs={{0,26},{1,27},{2,28},{3,29},{4,30},{5,31},{6,24},{7,25},{8,2},{9,3... | collective-permute-start | bytes 614408 | tf_op jit(solution)/shard_map/ppermute | solution.py:603
  76.0 12.9 %collective-permute-start.8 = (f32[400,128]{1,0:T(8,128)}, f32[400,128]{1,0:T(8,128)S(1)}, u32[]{:S(2)}, u32[]{:S(2)}) collective-permute-start(f32[400,128]{1,0:T(8,128)} %get-tuple-element.65), channel_id=1, source_target_pairs={{0,27},{1,26},{2,29},{3,28},{4,31},{5,30},{6,25},{7,24},{8,3},{9,2... | collective-permute-start | bytes 614408 | tf_op jit(solution)/shard_map/ppermute | solution.py:603
  76.0 21.4 %collective-permute-start.9 = (f32[400,128]{1,0:T(8,128)}, f32[400,128]{1,0:T(8,128)S(1)}, u32[]{:S(2)}, u32[]{:S(2)}) collective-permute-start(f32[400,128]{1,0:T(8,128)} %get-tuple-element.66), channel_id=1, source_target_pairs={{0,28},{1,29},{2,30},{3,31},{4,24},{5,25},{6,26},{7,27},{8,4},{9,5... | collective-permute-start | bytes 614408 | tf_op jit(solution)/shard_map/ppermute | solution.py:603
  122.1 6.4 %collective-permute-start.31 = (f32[200,384]{1,0:T(8,128)}, f32[200,384]{1,0:T(8,128)S(1)}, u32[]{:S(2)}, u32[]{:S(2)}) collective-permute-start(f32[200,384]{1,0:T(8,128)} %get-tuple-element.95), channel_id=1, source_target_pairs={{0,1},{1,0},{2,3},{3,2},{4,5},{5,4},{6,7},{7,6},{8,9},{9,8},{10,11... | collective-permute-start | bytes 921608 | tf_op jit(solution)/shard_map/ppermute | solution.py:594
  122.2 15.6 %collective-permute-start.30 = (f32[200,384]{1,0:T(8,128)}, f32[200,384]{1,0:T(8,128)S(1)}, u32[]{:S(2)}, u32[]{:S(2)}) collective-permute-start(f32[200,384]{1,0:T(8,128)} %get-tuple-element.93), channel_id=1, source_target_pairs={{0,1},{1,0},{2,3},{3,2},{4,5},{5,4},{6,7},{7,6},{8,9},{9,8},{10,11... | collective-permute-start | bytes 921608 | tf_op jit(solution)/shard_map/ppermute | solution.py:594
  124.5 14.7 %collective-permute-start.36 = (f32[200,384]{1,0:T(8,128)S(1)}, f32[200,384]{1,0:T(8,128)S(1)}, u32[]{:S(2)}, u32[]{:S(2)}) collective-permute-start(f32[200,384]{1,0:T(8,128)S(1)} %add.252), channel_id=1, source_target_pairs={{0,24},{8,16},{16,8},{24,0},{1,25},{9,17},{17,9},{25,1},{2,26},{10... | collective-permute-start | bytes 921608 | tf_op jit(solution)/shard_map/ppermute | solution.py:607
  127.0 14.4 %collective-permute-start.34 = (f32[200,384]{1,0:T(8,128)S(1)}, f32[200,384]{1,0:T(8,128)S(1)}, u32[]{:S(2)}, u32[]{:S(2)}) collective-permute-start(f32[200,384]{1,0:T(8,128)S(1)} %add.251), channel_id=1, source_target_pairs={{0,16},{8,24},{16,0},{24,8},{1,17},{9,25},{17,1},{25,9},{2,18},{10... | collective-permute-start | bytes 921608 | tf_op jit(solution)/shard_map/ppermute | solution.py:607
  129.6 11.8 %collective-permute-start.32 = (f32[200,384]{1,0:T(8,128)S(1)}, f32[200,384]{1,0:T(8,128)S(1)}, u32[]{:S(2)}, u32[]{:S(2)}) collective-permute-start(f32[200,384]{1,0:T(8,128)S(1)} %add.250), channel_id=1, source_target_pairs={{0,8},{8,0},{16,24},{24,16},{1,9},{9,1},{17,25},{25,17},{2,10},{10... | collective-permute-start | bytes 921608 | tf_op jit(solution)/shard_map/ppermute | solution.py:607
  137.0 10.8 %collective-permute-start.23 = (f32[400,128]{1,0:T(8,128)}, f32[400,128]{1,0:T(8,128)S(1)}, u32[]{:S(2)}, u32[]{:S(2)}) collective-permute-start(f32[400,128]{1,0:T(8,128)} %get-tuple-element.84), channel_id=1, source_target_pairs={{0,6},{1,7},{2,0},{3,1},{4,2},{5,3},{6,4},{7,5},{8,14},{9,15},{10,... | collective-permute-start | bytes 614408 | tf_op jit(solution)/shard_map/ppermute | solution.py:594
  137.8 10.4 %collective-permute-start.24 = (f32[400,128]{1,0:T(8,128)}, f32[400,128]{1,0:T(8,128)S(1)}, u32[]{:S(2)}, u32[]{:S(2)}) collective-permute-start(f32[400,128]{1,0:T(8,128)} %get-tuple-element.85), channel_id=1, source_target_pairs={{0,7},{1,6},{2,1},{3,0},{4,3},{5,2},{6,5},{7,4},{8,15},{9,14},{10,... | collective-permute-start | bytes 614408 | tf_op jit(solution)/shard_map/ppermute | solution.py:594
  144.9 7.5 %collective-permute-start.37 = (f32[56,384]{1,0:T(8,128)}, f32[56,384]{1,0:T(8,128)S(1)}, u32[]{:S(2)}, u32[]{:S(2)}) collective-permute-start(f32[56,384]{1,0:T(8,128)} %get-tuple-element.101), channel_id=1, source_target_pairs={{0,2},{1,3},{2,4},{3,5},{4,6},{5,7},{6,0},{7,1},{8,10},{9,11},{10,... | collective-permute-start | bytes 258056 | tf_op jit(solution)/shard_map/ppermute | solution.py:594
  144.9 27.8 %collective-permute-start.38 = (f32[56,384]{1,0:T(8,128)}, f32[56,384]{1,0:T(8,128)S(1)}, u32[]{:S(2)}, u32[]{:S(2)}) collective-permute-start(f32[56,384]{1,0:T(8,128)} %get-tuple-element.102), channel_id=1, source_target_pairs={{0,4},{1,5},{2,6},{3,7},{4,0},{5,1},{6,2},{7,3},{8,12},{9,13},{10,... | collective-permute-start | bytes 258056 | tf_op jit(solution)/shard_map/ppermute | solution.py:594
  146.5 38.2 %collective-permute-start.25 = (f32[400,128]{1,0:T(8,128)}, f32[400,128]{1,0:T(8,128)S(1)}, u32[]{:S(2)}, u32[]{:S(2)}) collective-permute-start(f32[400,128]{1,0:T(8,128)} %get-tuple-element.86), channel_id=1, source_target_pairs={{0,4},{1,5},{2,6},{3,7},{4,0},{5,1},{6,2},{7,3},{8,12},{9,13},{10,... | collective-permute-start | bytes 614408 | tf_op jit(solution)/shard_map/ppermute | solution.py:594
  147.8 37.4 %collective-permute-start.26 = (f32[400,128]{1,0:T(8,128)}, f32[400,128]{1,0:T(8,128)S(1)}, u32[]{:S(2)}, u32[]{:S(2)}) collective-permute-start(f32[400,128]{1,0:T(8,128)} %get-tuple-element.87), channel_id=1, source_target_pairs={{0,5},{1,4},{2,7},{3,6},{4,1},{5,0},{6,3},{7,2},{8,13},{9,12},{10,... | collective-permute-start | bytes 614408 | tf_op jit(solution)/shard_map/ppermute | solution.py:594
  148.2 39.7 %collective-permute-start.27 = (f32[400,128]{1,0:T(8,128)}, f32[400,128]{1,0:T(8,128)S(1)}, u32[]{:S(2)}, u32[]{:S(2)}) collective-permute-start(f32[400,128]{1,0:T(8,128)} %get-tuple-element.88), channel_id=1, source_target_pairs={{0,2},{1,3},{2,4},{3,5},{4,6},{5,7},{6,0},{7,1},{8,10},{9,11},{10,... | collective-permute-start | bytes 614408 | tf_op jit(solution)/shard_map/ppermute | solution.py:594
  152.4 37.5 %collective-permute-start.28 = (f32[400,128]{1,0:T(8,128)}, f32[400,128]{1,0:T(8,128)S(1)}, u32[]{:S(2)}, u32[]{:S(2)}) collective-permute-start(f32[400,128]{1,0:T(8,128)} %get-tuple-element.89), channel_id=1, source_target_pairs={{0,3},{1,2},{2,5},{3,4},{4,7},{5,6},{6,1},{7,0},{8,11},{9,10},{10,... | collective-permute-start | bytes 614408 | tf_op jit(solution)/shard_map/ppermute | solution.py:594
  172.7 9.6 %collective-permute-start.39 = (f32[56,384]{1,0:T(8,128)}, f32[56,384]{1,0:T(8,128)S(1)}, u32[]{:S(2)}, u32[]{:S(2)}) collective-permute-start(f32[56,384]{1,0:T(8,128)} %get-tuple-element.103), channel_id=1, source_target_pairs={{0,6},{1,7},{2,0},{3,1},{4,2},{5,3},{6,4},{7,5},{8,14},{9,15},{10,... | collective-permute-start | bytes 258056 | tf_op jit(solution)/shard_map/ppermute | solution.py:594
  182.3 30.5 %collective-permute-start.17 = (f32[400,128]{1,0:T(8,128)}, f32[400,128]{1,0:T(8,128)S(1)}, u32[]{:S(2)}, u32[]{:S(2)}) collective-permute-start(f32[400,128]{1,0:T(8,128)} %get-tuple-element.75), channel_id=1, source_target_pairs={{0,12},{1,13},{2,14},{3,15},{4,8},{5,9},{6,10},{7,11},{8,20},{9,21... | collective-permute-start | bytes 614408 | tf_op jit(solution)/shard_map/ppermute | solution.py:603
  184.8 28.0 %collective-permute-start.40 = (f32[56,384]{1,0:T(8,128)}, f32[56,384]{1,0:T(8,128)S(1)}, u32[]{:S(2)}, u32[]{:S(2)}) collective-permute-start(f32[56,384]{1,0:T(8,128)} %shard_map.146.refs_0_), channel_id=1, source_target_pairs={{0,2},{1,3},{2,4},{3,5},{4,6},{5,7},{6,0},{7,1},{8,10},{9,11},{10,... | collective-permute-start | bytes 258056 | tf_op jit(solution)/shard_map/ppermute | solution.py:594
  185.2 38.9 %collective-permute-start.18 = (f32[400,128]{1,0:T(8,128)}, f32[400,128]{1,0:T(8,128)S(1)}, u32[]{:S(2)}, u32[]{:S(2)}) collective-permute-start(f32[400,128]{1,0:T(8,128)} %get-tuple-element.76), channel_id=1, source_target_pairs={{0,13},{1,12},{2,15},{3,14},{4,9},{5,8},{6,11},{7,10},{8,21},{9,20... | collective-permute-start | bytes 614408 | tf_op jit(solution)/shard_map/ppermute | solution.py:603
  187.9 38.1 %collective-permute-start.19 = (f32[400,128]{1,0:T(8,128)}, f32[400,128]{1,0:T(8,128)S(1)}, u32[]{:S(2)}, u32[]{:S(2)}) collective-permute-start(f32[400,128]{1,0:T(8,128)} %get-tuple-element.77), channel_id=1, source_target_pairs={{0,10},{1,11},{2,12},{3,13},{4,14},{5,15},{6,8},{7,9},{8,18},{9,19... | collective-permute-start | bytes 614408 | tf_op jit(solution)/shard_map/ppermute | solution.py:603
  189.9 36.3 %collective-permute-start.20 = (f32[400,128]{1,0:T(8,128)}, f32[400,128]{1,0:T(8,128)S(1)}, u32[]{:S(2)}, u32[]{:S(2)}) collective-permute-start(f32[400,128]{1,0:T(8,128)} %get-tuple-element.78), channel_id=1, source_target_pairs={{0,11},{1,10},{2,13},{3,12},{4,15},{5,14},{6,9},{7,8},{8,19},{9,18... | collective-permute-start | bytes 614408 | tf_op jit(solution)/shard_map/ppermute | solution.py:603
  212.8 6.5 %collective-permute-start.41 = (f32[56,384]{1,0:T(8,128)}, f32[56,384]{1,0:T(8,128)S(1)}, u32[]{:S(2)}, u32[]{:S(2)}) collective-permute-start(f32[56,384]{1,0:T(8,128)} %shard_map.146.refs_0_), channel_id=1, source_target_pairs={{0,4},{1,5},{2,6},{3,7},{4,0},{5,1},{6,2},{7,3},{8,12},{9,13},{10,... | collective-permute-start | bytes 258056 | tf_op jit(solution)/shard_map/ppermute | solution.py:594
  212.8 7.4 %collective-permute-start.42 = (f32[56,384]{1,0:T(8,128)}, f32[56,384]{1,0:T(8,128)S(1)}, u32[]{:S(2)}, u32[]{:S(2)}) collective-permute-start(f32[56,384]{1,0:T(8,128)} %shard_map.146.refs_0_), channel_id=1, source_target_pairs={{0,6},{1,7},{2,0},{3,1},{4,2},{5,3},{6,4},{7,5},{8,14},{9,15},{10,... | collective-permute-start | bytes 258056 | tf_op jit(solution)/shard_map/ppermute | solution.py:594
  219.3 11.7 %collective-permute-start.21 = (f32[400,128]{1,0:T(8,128)}, f32[400,128]{1,0:T(8,128)S(1)}, u32[]{:S(2)}, u32[]{:S(2)}) collective-permute-start(f32[400,128]{1,0:T(8,128)} %get-tuple-element.79), channel_id=1, source_target_pairs={{0,9},{1,8},{2,11},{3,10},{4,13},{5,12},{6,15},{7,14},{8,17},{9,16... | collective-permute-start | bytes 614408 | tf_op jit(solution)/shard_map/ppermute | solution.py:603
  220.2 13.2 %collective-permute-start.22 = (f32[400,128]{1,0:T(8,128)}, f32[400,128]{1,0:T(8,128)S(1)}, u32[]{:S(2)}, u32[]{:S(2)}) collective-permute-start(f32[400,128]{1,0:T(8,128)} %get-tuple-element.80), channel_id=1, source_target_pairs={{0,8},{1,9},{2,10},{3,11},{4,12},{5,13},{6,14},{7,15},{8,16},{9,17... | collective-permute-start | bytes 614408 | tf_op jit(solution)/shard_map/ppermute | solution.py:603
  224.1 21.0 %collective-permute-start.43 = (f32[200,384]{1,0:T(8,128)}, f32[200,384]{1,0:T(8,128)S(1)}, u32[]{:S(2)}, u32[]{:S(2)}) collective-permute-start(f32[200,384]{1,0:T(8,128)} %shard_map.147.refs_0_), channel_id=1, source_target_pairs={{0,8},{8,0},{16,24},{24,16},{1,9},{9,1},{17,25},{25,17},{2,10},{10... | collective-permute-start | bytes 921608 | tf_op jit(solution)/shard_map/ppermute | solution.py:607
  226.0 22.1 %collective-permute-start.44 = (f32[200,384]{1,0:T(8,128)}, f32[200,384]{1,0:T(8,128)S(1)}, u32[]{:S(2)}, u32[]{:S(2)}) collective-permute-start(f32[200,384]{1,0:T(8,128)} %shard_map.147.refs_0_), channel_id=1, source_target_pairs={{0,16},{8,24},{16,0},{24,8},{1,17},{9,25},{17,1},{25,9},{2,18},{10... | collective-permute-start | bytes 921608 | tf_op jit(solution)/shard_map/ppermute | solution.py:607
  226.2 27.2 %collective-permute-start.45 = (f32[200,384]{1,0:T(8,128)}, f32[200,384]{1,0:T(8,128)S(1)}, u32[]{:S(2)}, u32[]{:S(2)}) collective-permute-start(f32[200,384]{1,0:T(8,128)} %shard_map.147.refs_0_), channel_id=1, source_target_pairs={{0,24},{8,16},{16,8},{24,0},{1,25},{9,17},{17,9},{25,1},{2,26},{10... | collective-permute-start | bytes 921608 | tf_op jit(solution)/shard_map/ppermute | solution.py:607
  231.0 10.1 %collective-permute-start.15 = (f32[400,128]{1,0:T(8,128)}, f32[400,128]{1,0:T(8,128)S(1)}, u32[]{:S(2)}, u32[]{:S(2)}) collective-permute-start(f32[400,128]{1,0:T(8,128)} %get-tuple-element.73), channel_id=1, source_target_pairs={{0,14},{1,15},{2,8},{3,9},{4,10},{5,11},{6,12},{7,13},{8,22},{9,23... | collective-permute-start | bytes 614408 | tf_op jit(solution)/shard_map/ppermute | solution.py:603
  233.4 20.3 %collective-permute-start.16 = (f32[400,128]{1,0:T(8,128)}, f32[400,128]{1,0:T(8,128)S(1)}, u32[]{:S(2)}, u32[]{:S(2)}) collective-permute-start(f32[400,128]{1,0:T(8,128)} %get-tuple-element.74), channel_id=1, source_target_pairs={{0,15},{1,14},{2,9},{3,8},{4,11},{5,10},{6,13},{7,12},{8,23},{9,22... | collective-permute-start | bytes 614408 | tf_op jit(solution)/shard_map/ppermute | solution.py:603
  241.1 28.9 %collective-permute-start.46 = (f32[200,384]{1,0:T(8,128)S(1)}, f32[200,384]{1,0:T(8,128)S(1)}, u32[]{:S(2)}, u32[]{:S(2)}) collective-permute-start(f32[200,384]{1,0:T(8,128)S(1)} %copy-done), channel_id=1, source_target_pairs={{0,1},{1,0},{2,3},{3,2},{4,5},{5,4},{6,7},{7,6},{8,9},{9,8},{10,11... | collective-permute-start | bytes 921608 | tf_op jit(solution)/shard_map/ppermute | solution.py:594
  245.1 24.9 %collective-permute-start.47 = (f32[200,384]{1,0:T(8,128)S(1)}, f32[200,384]{1,0:T(8,128)S(1)}, u32[]{:S(2)}, u32[]{:S(2)}) collective-permute-start(f32[200,384]{1,0:T(8,128)S(1)} %collective-permute-done.43.refs_1_), channel_id=1, source_target_pairs={{0,1},{1,0},{2,3},{3,2},{4,5},{5,4},{6,7},{7,6},{8,9},{9,8},{10,11... | collective-permute-start | bytes 921608 | tf_op jit(solution)/shard_map/ppermute | solution.py:594
  248.1 22.0 %collective-permute-start.48 = (f32[200,384]{1,0:T(8,128)S(1)}, f32[200,384]{1,0:T(8,128)S(1)}, u32[]{:S(2)}, u32[]{:S(2)}) collective-permute-start(f32[200,384]{1,0:T(8,128)S(1)} %collective-permute-done.44.refs_2_), channel_id=1, source_target_pairs={{0,1},{1,0},{2,3},{3,2},{4,5},{5,4},{6,7},{7,6},{8,9},{9,8},{10,11... | collective-permute-start | bytes 921608 | tf_op jit(solution)/shard_map/ppermute | solution.py:594
  253.4 16.6 %collective-permute-start.49 = (f32[200,384]{1,0:T(8,128)S(1)}, f32[200,384]{1,0:T(8,128)S(1)}, u32[]{:S(2)}, u32[]{:S(2)}) collective-permute-start(f32[200,384]{1,0:T(8,128)S(1)} %collective-permute-done.45.refs_3_), channel_id=1, source_target_pairs={{0,1},{1,0},{2,3},{3,2},{4,5},{5,4},{6,7},{7,6},{8,9},{9,8},{10,11... | collective-permute-start | bytes 921608 | tf_op jit(solution)/shard_map/ppermute | solution.py:594
  253.6 12.1 %collective-permute-start.29 = (f32[400,128]{1,0:T(8,128)}, f32[400,128]{1,0:T(8,128)}, u32[]{:S(2)}, u32[]{:S(2)}) collective-permute-start(f32[400,128]{1,0:T(8,128)} %get-tuple-element.90), channel_id=1, source_target_pairs={{0,1},{1,0},{2,3},{3,2},{4,5},{5,4},{6,7},{7,6},{8,9},{9,8},{10,11... | collective-permute-start | bytes 614408 | tf_op jit(solution)/shard_map/ppermute | solution.py:594
  (60 other events, 937.8 us)

commit v2 on v1

--- a/solution.py
+++ b/solution.py
@@ -163,7 +163,8 @@
 def count_kernel(slots_ref, out_ref):
     table_rows = out_ref.shape[2]
     hits = lax.broadcasted_iota(I32, (slots_ref.shape[1], table_rows), 1) == slots_ref[0]
-    out_ref[0] = jnp.sum(jnp.where(hits, 1.0, 0.0), axis=0, keepdims=True)
+    counts = jnp.sum(jnp.where(hits, 1.0, 0.0), axis=0, keepdims=True)
+    out_ref[0] = jnp.where(counts > 0.0, jnp.log(jnp.maximum(counts, 1.0)), -jnp.inf)
 
 
 def slot_counts(neg_slots, table_rows):
@@ -235,12 +236,12 @@
     )(edge_source, rels, *blocks)
 
 
-def softmax_step(step, live, score, counts, edge_target, loss_ref, grad_ref):
+def softmax_step(step, live, score, log_counts, edge_target, loss_ref, grad_ref):
     own = lax.broadcasted_iota(I32, score.shape, 1) == edge_target
     pos = jnp.sum(jnp.where(own, score, 0.0), axis=1, keepdims=True)
-    peak = jnp.max(jnp.where(counts > 0.0, score, -jnp.inf), axis=1, keepdims=True)
-    peak = jnp.maximum(pos, peak)
-    weight = counts * jnp.exp(jnp.minimum(score - peak, 0.0))
+    score = score + log_counts
+    peak = jnp.maximum(pos, jnp.max(score, axis=1, keepdims=True))
+    weight = jnp.exp(score - peak)
     pos_weight = jnp.exp(pos - peak)
     sum_all = pos_weight + jnp.sum(weight, axis=1, keepdims=True)
     edge = step * score.shape[0] + lax.broadcasted_iota(I32, pos.shape, 0)
@@ -662,16 +663,16 @@
     loss, grad, table = score_spans(
         edge_count, targets, query_lines, counts, edge_target.reshape(-1, 1)
     )
-    table_parts = table_grads(query_columns, grad, block, 0, 2)
-    table_parts += table_grads(query_columns, grad, block, 2, peers - 2)
+    table_parts = table_grads(query_columns, grad, block, 0, first)
+    table_parts += table_grads(query_columns, grad, block, first, peers - first)
     back = [(-hop[0], hop[1]) for hop in ways]
     home = [
         sent_across(value, hop, peers, groups, 1)
-        for value, hop in zip(table_parts[:2], back[:2])
+        for value, hop in zip(table_parts[:first], back[:first])
     ]
     home += [
         sent_across(value, hop, peers, groups, 1)
-        for value, hop in zip(table_parts[2:], back[2:])
+        for value, hop in zip(table_parts[first:], back[first:])
     ]
     source_lines, *halves = relation_grads(
         here, table, grad, heads, rels, edge_relation.reshape(-1, 1), groups, width

time: 277 us -> 257 us (0.928)
  waiting for transfers between devices: 100 us -> 72.3 us
  starting transfers between devices: 64.6 us -> 74.4 us
    ppermute x28, waiting for transfers between devices: 48.3 us -> 32.2 us  [sent_on(): lax.ppermute(value, 'shard', [(i, partner(i, hop, peers, 1)) for i in ran...]
    ppermute x28, starting transfers between devices: 22 us -> 32.9 us  [sent_on(): lax.ppermute(value, 'shard', [(i, partner(i, hop, peers, 1)) for i in ran...]
    ppermute x16, waiting for transfers between devices: 40.6 us -> 31.2 us  [sent_across(): return lax.ppermute(value, ('group', 'shard'), pairs)]
  transfers between devices with their start and end apart: 50 -> 50, of which waited for: 15 -> 12; matrix products, arithmetic and copies ran while one was open for 6% -> 6% of each run, Pallas kernels for 21% -> 22%
where the time goes in v2:
time: 257 us; the launch traced here: 256 us
  Pallas kernels  88.2 us (34%)
  starting transfers between devices  74.4 us (29%)
  waiting for transfers between devices  72.3 us (28%)
  local copies, waits for them, and re-layouts  11.8 us (5%)
  other arithmetic  7.32 us (3%)
    ppermute x16, starting transfers between devices, sent_across(): return lax.ppermute(value, ('group', 'shard'), pairs)  34.3 us
    ppermute x28, starting transfers between devices, sent_on(): lax.ppermute(value, 'shard', [(i, partner(i, hop, peers, 1)) for i in ran...  32.9 us
    ppermute x28, waiting for transfers between devices, sent_on(): lax.ppermute(value, 'shard', [(i, partner(i, hop, peers, 1)) for i in ran...  32.2 us
    ppermute x16, waiting for transfers between devices, sent_across(): return lax.ppermute(value, ('group', 'shard'), pairs)  31.2 us
    pallas_call x1, Pallas kernels, relation_grads(): kernel_call(functools.partial(relation_grad_kernel, steps), [shape((2, fe...  12.8 us
    pallas_call x1, Pallas kernels, score_spans(): kernel_call(functools.partial(score_kernel, peers), [shape((edges, 1)), s...  10.4 us
    pallas_call x3, Pallas kernels, pick_blocks(): kernel_call(pick_kernel, [shape((features, block))] * count, 6 * features...  9.46 us
    ppermute x6, waiting for transfers between devices, sent_group(): return lax.ppermute(value, 'group', [(g, g ^ bit) for g in range(groups)])  8.83 us
  transfers between devices with their start and end apart: 50, of which 12 were waited for; matrix products, arithmetic and copies ran while one was open for 6% of the time, Pallas kernels for 22%

profile of v2, /device:TPU:0, one launch (start us, length us, event | category | flops | bytes accessed | tf_op | source)
XLA Modules:
  0.0 255.9 jit_solution(6526699590284879123)
XLA Ops:
  1.3 2.9 %shard_map.133 = (f32[400,128]{1,0:T(8,128)}, f32[400,128]{1,0:T(8,128)}, f32[400,128]{1,0:T(8,128)}, f32[400,128]{1,0:T(8,128)}) custom-call(s32[4]{0:T(128)} %pad_add_fusion.1.order_ref, f32[400,512]{1,0:T(8,128)} %bitcast.29, s32[8,128]{1,0:T(8,128)} %bitcast.41), custom_call_target="tpu_custom_call" | custom-call | flops 629145600 | bytes 1638400 | tf_op jit(solution)/shard_map/pallas_call | solution.py:126
  4.2 5.1 %collective-permute-start.4 = (f32[400,128]{1,0:T(8,128)}, f32[400,128]{1,0:T(8,128)S(1)}, u32[]{:S(2)}, u32[]{:S(2)}) collective-permute-start(f32[400,128]{1,0:T(8,128)} %get-tuple-element.58), channel_id=1, source_target_pairs={{0,6},{1,7},{2,0},{3,1},{4,2},{5,3},{6,4},{7,5},{8,14},{9,15},{10,... | collective-permute-start | bytes 614408 | tf_op jit(solution)/shard_map/ppermute | solution.py:595
  10.5 2.9 %shard_map.132 = (f32[400,128]{1,0:T(8,128)}, f32[400,128]{1,0:T(8,128)}, f32[400,128]{1,0:T(8,128)}, f32[400,128]{1,0:T(8,128)}) custom-call(s32[4]{0:T(128)} %pad_add_fusion.order_ref, f32[400,512]{1,0:T(8,128)} %bitcast.30, s32[8,128]{1,0:T(8,128)} %bitcast.42), custom_call_target="tpu_custom_call" | custom-call | flops 629145600 | bytes 1638400 | tf_op jit(solution)/shard_map/pallas_call | solution.py:126
  13.4 1.6 collective-permute-start
  17.1 2.6 %shard_map.135.refs_2_ = f32[2,1,1024]{2,1,0:T(1,128)} custom-call(s32[2,1000,1]{2,1,0:T(8,128)} %copy.15.slots_ref), custom_call_target="tpu_custom_call" | custom-call | flops 4096000 | bytes 1024000 | tf_op jit(solution)/shard_map/pallas_call | solution.py:172
  22.5 7.5 %shard_map.131.refs_1_.rels_ref = f32[400,1024]{1,0:T(8,128)} custom-call(f32[400,1345]{1,0:T(8,128)} %bitcast.26, s32[1,1024]{1,0:T(1,128)} %bitcast.37), custom_call_target="tpu_custom_call" | custom-call | flops 3460300800 | bytes 3276800 | tf_op jit(solution)/shard_map/pallas_call | solution.py:153
  30.7 3.6 %shard_map.136 = (f32[400,128]{1,0:T(8,128)}, f32[400,128]{1,0:T(8,128)}, f32[400,128]{1,0:T(8,128)}, f32[400,128]{1,0:T(8,128)}, f32[400,128]{1,0:T(8,128)}, /*...) custom-call(s32[8]{0:T(128)} %stack.48.order_ref, f32[400,512]{1,0:T(8,128)} %bitcast.31, s32[8,128]{1,0:T(8,128)} %bitcast.39), custom_call_target="tpu_custom_call" | custom-call | flops 1258291200 | bytes 3276800 | tf_op jit(solution)/shard_map/pallas_call | solution.py:126
  34.4 2.2 collective-permute-start.2
  37.1 4.1 %collective-permute-start.10 = (f32[400,128]{1,0:T(8,128)}, f32[400,128]{1,0:T(8,128)S(1)}, u32[]{:S(2)}, u32[]{:S(2)}) collective-permute-start(f32[400,128]{1,0:T(8,128)} %get-tuple-element.67), channel_id=1, source_target_pairs={{0,29},{1,28},{2,31},{3,30},{4,25},{5,24},{6,27},{7,26},{8,5},{9,4... | collective-permute-start | bytes 614408 | tf_op jit(solution)/shard_map/ppermute | solution.py:604
  41.2 1.5 collective-permute-start.11
  44.3 12.3 %collective-permute-done.2.refs_4_ = f32[400,128]{1,0:T(8,128)S(1)} collective-permute-done((f32[400,128]{1,0:T(8,128)S(1)}, f32[400,128]{1,0:T(8,128)S(1)}, u32[]{:S(2)}, u32[]{:S(2)}) %collective-permute-start.2) | collective-permute-done | bytes 204832 | tf_op jit(solution)/shard_map/ppermute | solution.py:595
  57.2 2.3 collective-permute-done.3.refs_5_
  59.6 2.3 collective-permute-start.14
  61.9 3.1 %collective-permute-done.10.refs_7_ = f32[400,128]{1,0:T(8,128)S(1)} collective-permute-done((f32[400,128]{1,0:T(8,128)}, f32[400,128]{1,0:T(8,128)S(1)}, u32[]{:S(2)}, u32[]{:S(2)}) %collective-permute-start.10) | collective-permute-done | bytes 204832 | tf_op jit(solution)/shard_map/ppermute | solution.py:604
  65.0 11.0 %collective-permute-start.7 = (f32[400,128]{1,0:T(8,128)}, f32[400,128]{1,0:T(8,128)S(1)}, u32[]{:S(2)}, u32[]{:S(2)}) collective-permute-start(f32[400,128]{1,0:T(8,128)} %get-tuple-element.64), channel_id=1, source_target_pairs={{0,26},{1,27},{2,28},{3,29},{4,30},{5,31},{6,24},{7,25},{8,2},{9,3... | collective-permute-start | bytes 614408 | tf_op jit(solution)/shard_map/ppermute | solution.py:604
  76.1 4.5 %collective-permute-start.9 = (f32[400,128]{1,0:T(8,128)}, f32[400,128]{1,0:T(8,128)S(1)}, u32[]{:S(2)}, u32[]{:S(2)}) collective-permute-start(f32[400,128]{1,0:T(8,128)} %get-tuple-element.66), channel_id=1, source_target_pairs={{0,28},{1,29},{2,30},{3,31},{4,24},{5,25},{6,26},{7,27},{8,4},{9,5... | collective-permute-start | bytes 614408 | tf_op jit(solution)/shard_map/ppermute | solution.py:604
  80.6 8.2 %shard_map.134 = (f32[400,1024]{1,0:T(8,128)}, bf16[2,400,1024]{2,1,0:T(8,128)(2,1)}, bf16[1024,1200]{1,0:T(8,128)(2,1)}) custom-call(s32[1,1024]{1,0:T(1,128)} %bitcast.34, f32[400,1024]{1,0:T(8,128)} %shard_map.131.refs_1_.rels_ref, f32[400,128]{1,0:T(8,128)} %copy-done.41, f32[400,128]{1,0:T(8,128)} %copy-done.42, f32[400,128]{1,0:T(8,128)} %copy-done.50, ...), custom_call_target="tpu_custom_call" | custom-call | flops 2516582400 | bytes 8192000 | tf_op jit(solution)/shard_map/pallas_call | solution.py:221
  88.9 8.5 %collective-permute-done.9.refs_6_ = f32[400,128]{1,0:T(8,128)S(1)} collective-permute-done((f32[400,128]{1,0:T(8,128)}, f32[400,128]{1,0:T(8,128)S(1)}, u32[]{:S(2)}, u32[]{:S(2)}) %collective-permute-start.9) | collective-permute-done | bytes 204832 | tf_op jit(solution)/shard_map/ppermute | solution.py:604
  98.1 10.4 %shard_map.137 = (f32[1024,1]{1,0:T(8,128)}, bf16[2,1024,1024]{2,1,0:T(8,128)(2,1)}, bf16[1200,1024]{1,0:T(8,128)(2,1)}) custom-call(s32[1]{0:T(128)S(6)} %copy.20.refs_0_, bf16[1024,1200]{1,0:T(8,128)(2,1)} %get-tuple-element.63.refs_1_, f32[2,1,1024]{2,1,0:T(1,128)} %shard_map.135.refs_2_, s32[1024,1]{1,0:T(8,128)} %copy.16.refs_3_, ...), custom_call_target="tpu_custom_call" | custom-call | flops 2516582400 | bytes 12288000 | tf_op jit(solution)/shard_map/pallas_call | solution.py:311
  108.5 12.8 %shard_map.142 = (bf16[2,400,1024]{2,1,0:T(8,128)(2,1)}, f32[200,384]{1,0:T(8,128)}, f32[200,384]{1,0:T(8,128)}, f32[200,384]{1,0:T(8,128)}, f32[200,384]{1,0:T(...) custom-call(s32[2]{0:T(128)} %pad_add_fusion.2.me_ref, ...), custom_call_target="tpu_custom_call" | custom-call | flops 4194304000 | bytes 12288000 | tf_op jit(solution)/shard_map/pallas_call | solution.py:415
  127.0 1.6 collective-permute-start.34
  129.2 5.8 %shard_map.143 = (f32[400,128]{1,0:T(8,128)}, f32[400,128]{1,0:T(8,128)}, f32[400,128]{1,0:T(8,128)}, f32[400,128]{1,0:T(8,128)}, f32[400,128]{1,0:T(8,128)}, /*...) custom-call(bf16[2,400,1024]{2,1,0:T(8,128)(2,1)} %get-tuple-element.83.rows_ref, ...), custom_call_target="tpu_custom_call" | custom-call | flops 1677721600 | bytes 4915200 | tf_op jit(solution)/shard_map/pallas_call | solution.py:457
  138.4 2.9 %collective-permute-done.34.refs_2_ = f32[200,384]{1,0:T(8,128)S(1)} collective-permute-done((f32[200,384]{1,0:T(8,128)S(1)}, f32[200,384]{1,0:T(8,128)S(1)}, u32[]{:S(2)}, u32[]{:S(2)}) %collective-permute-start.34) | collective-permute-done | bytes 307232 | tf_op jit(solution)/shard_map/ppermute | solution.py:608
  142.8 2.1 shard_map.145
  144.8 1.7 collective-permute-start.38
  146.5 2.2 collective-permute-start.39
  148.7 4.4 %shard_map.139 = (f32[400,128]{1,0:T(8,128)}, f32[400,128]{1,0:T(8,128)}, f32[400,128]{1,0:T(8,128)}, f32[400,128]{1,0:T(8,128)}) custom-call(bf16[2,400,1024]{2,1,0:T(8,128)(2,1)} %get-tuple-element.62.columns_ref, bf16[2,1024,1024]{2,1,0:T(8,128)(2,1)} %get-tuple-element.72.grad_ref), custom_call_target="tpu_custom_call" | custom-call | flops 1258291200 | bytes 3735552 | tf_op jit(solution)/shard_map/pallas_call | solution.py:352
  154.0 10.8 %collective-permute-start.27 = (f32[400,128]{1,0:T(8,128)S(1)}, f32[400,128]{1,0:T(8,128)S(1)}, u32[]{:S(2)}, u32[]{:S(2)}) collective-permute-start(f32[400,128]{1,0:T(8,128)S(1)} %copy-done.44), channel_id=1, source_target_pairs={{0,2},{1,3},{2,4},{3,5},{4,6},{5,7},{6,0},{7,1},{8,10},{9,11},{10,... | collective-permute-start | bytes 614408 | tf_op jit(solution)/shard_map/ppermute | solution.py:595
  164.7 4.1 %collective-permute-done.38.refs_2_ = f32[56,384]{1,0:T(8,128)S(1)} collective-permute-done((f32[56,384]{1,0:T(8,128)}, f32[56,384]{1,0:T(8,128)S(1)}, u32[]{:S(2)}, u32[]{:S(2)}) %collective-permute-start.38) | collective-permute-done | bytes 86048 | tf_op jit(solution)/shard_map/ppermute | solution.py:595
  168.9 3.1 %collective-permute-start.19 = (f32[400,128]{1,0:T(8,128)}, f32[400,128]{1,0:T(8,128)S(1)}, u32[]{:S(2)}, u32[]{:S(2)}) collective-permute-start(f32[400,128]{1,0:T(8,128)} %get-tuple-element.77), channel_id=1, source_target_pairs={{0,10},{1,11},{2,12},{3,13},{4,14},{5,15},{6,8},{7,9},{8,18},{9,19... | collective-permute-start | bytes 614408 | tf_op jit(solution)/shard_map/ppermute | solution.py:604
  172.0 1.7 shard_map.146.refs_0_
  173.7 10.3 %collective-permute-done.26.refs_3_ = f32[400,128]{1,0:T(8,128)S(1)} collective-permute-done((f32[400,128]{1,0:T(8,128)S(1)}, f32[400,128]{1,0:T(8,128)S(1)}, u32[]{:S(2)}, u32[]{:S(2)}) %collective-permute-start.26) | collective-permute-done | bytes 204832 | tf_op jit(solution)/shard_map/ppermute | solution.py:595
  184.1 1.7 collective-permute-start.21
  185.8 1.5 collective-permute-start.22
  188.0 2.7 %collective-permute-start.42 = (f32[56,384]{1,0:T(8,128)}, f32[56,384]{1,0:T(8,128)S(1)}, u32[]{:S(2)}, u32[]{:S(2)}) collective-permute-start(f32[56,384]{1,0:T(8,128)} %shard_map.146.refs_0_), channel_id=1, source_target_pairs={{0,6},{1,7},{2,0},{3,1},{4,2},{5,3},{6,4},{7,5},{8,14},{9,15},{10,... | collective-permute-start | bytes 258056 | tf_op jit(solution)/shard_map/ppermute | solution.py:595
  190.7 4.3 %shard_map.138 = (f32[400,128]{1,0:T(8,128)}, f32[400,128]{1,0:T(8,128)}, f32[400,128]{1,0:T(8,128)}, f32[400,128]{1,0:T(8,128)}) custom-call(bf16[2,400,1024]{2,1,0:T(8,128)(2,1)} %get-tuple-element.62.columns_ref, bf16[2,1024,1024]{2,1,0:T(8,128)(2,1)} %get-tuple-element.72.grad_ref), custom_call_target="tpu_custom_call" | custom-call | flops 1258291200 | bytes 3735552 | tf_op jit(solution)/shard_map/pallas_call | solution.py:352
  195.0 3.1 %collective-permute-done.41.refs_2_ = f32[56,384]{1,0:T(8,128)S(1)} collective-permute-done((f32[56,384]{1,0:T(8,128)}, f32[56,384]{1,0:T(8,128)S(1)}, u32[]{:S(2)}, u32[]{:S(2)}) %collective-permute-start.41) | collective-permute-done | bytes 86048 | tf_op jit(solution)/shard_map/ppermute | solution.py:595
  198.1 2.2 collective-permute-start.15
  201.0 1.8 shard_map.147.refs_0_
  206.3 1.7 collective-permute-done.15.refs_0_
  208.5 1.9 collective-permute-done.16.refs_1_
  210.5 16.0 %collective-permute-done.17.refs_2_ = f32[400,128]{1,0:T(8,128)S(1)} collective-permute-done((f32[400,128]{1,0:T(8,128)}, f32[400,128]{1,0:T(8,128)S(1)}, u32[]{:S(2)}, u32[]{:S(2)}) %collective-permute-start.17) | collective-permute-done | bytes 204832 | tf_op jit(solution)/shard_map/ppermute | solution.py:604
  227.1 5.9 %collective-permute-done.45.refs_3_ = f32[200,384]{1,0:T(8,128)S(1)} collective-permute-done((f32[200,384]{1,0:T(8,128)}, f32[200,384]{1,0:T(8,128)S(1)}, u32[]{:S(2)}, u32[]{:S(2)}) %collective-permute-start.45) | collective-permute-done | bytes 307232 | tf_op jit(solution)/shard_map/ppermute | solution.py:608
  236.2 2.3 shard_map.130.hot_ref
  238.5 2.3 shard_map.141.hot_ref
  241.6 3.7 %shard_map.140.other_ref = f32[400,512]{1,0:T(8,128)} custom-call(bf16[1024,512]{1,0:T(8,128)(2,1)} %shard_map.130.hot_ref, f32[400,128]{1,0:T(8,128)} %copy-done.20, f32[400,128]{1,0:T(8,128)} %copy-done.21, f32[400,128]{1,0:T(8,128)} %copy-done.22, f32[400,128]{1,0:T(8,128)} %copy-done.23, f32[400,128]{1,0:T(8,128)} %copy-done.19, ...), custom_call_target="tpu_custom_call" | custom-call | flops 838860800 | bytes 3276800 | tf_op jit(solution)/shard_map/pallas_call | solution.py:482
  245.3 4.3 %shard_map.144 = f32[400,512]{1,0:T(8,128)} custom-call(f32[400,512]{1,0:T(8,128)} %shard_map.140.other_ref, f32[400,512]{1,0:T(8,128)} %bitcast.32, f32[1,512]{1,0:T(1,128)} %bitcast.44, bf16[1024,512]{1,0:T(8,128)(2,1)} %shard_map.141.hot_ref, f32[400,128]{1,0:T(8,128)} %copy-done.13, f32[400,128]{1,0:T(8,128)} %copy-done.14, f32[400,128]{1,0:T(8,128)} %copy-done.15, ...), custom_call_target="tpu_custom_call" | custom-call | flops 838860800 | bytes 3276800 | tf_op jit(solution)/shard_map/pallas_call | solution.py:501
  251.3 4.6 %shard_map.148 = f32[400,1345]{1,0:T(8,128)} custom-call(s32[2]{0:T(128)} %pad_add_fusion.2.me_ref, f32[400,1345]{1,0:T(8,128)} %bitcast.27, f32[1,1345]{1,0:T(1,128)} %reshape.36.state_ref, f32[200,384]{1,0:T(8,128)} %shard_map.147.refs_0_, f32[200,384]{1,0:T(8,128)} %copy-done.6, f32[200,384]{1,0:T(8,128)} %copy-done.7, f32[200,384]{1,0:T(8,128)} %copy-done.8, ...), custom_call_target="tpu_custom_call" | custom-call | flops 4304000 | bytes 6456000 | tf_op jit(solution)/shard_map/pallas_call | solution.py:586
  (208 shorter events, 33.7 us)
Async XLA Ops:
  4.2 30.2 %collective-permute-start.4 = (f32[400,128]{1,0:T(8,128)}, f32[400,128]{1,0:T(8,128)S(1)}, u32[]{:S(2)}, u32[]{:S(2)}) collective-permute-start(f32[400,128]{1,0:T(8,128)} %get-tuple-element.58), channel_id=1, source_target_pairs={{0,6},{1,7},{2,0},{3,1},{4,2},{5,3},{6,4},{7,5},{8,14},{9,15},{10,... | collective-permute-start | bytes 614408 | tf_op jit(solution)/shard_map/ppermute | solution.py:595
  9.3 27.3 %collective-permute-start.5 = (f32[400,128]{1,0:T(8,128)}, f32[400,128]{1,0:T(8,128)S(1)}, u32[]{:S(2)}, u32[]{:S(2)}) collective-permute-start(f32[400,128]{1,0:T(8,128)} %get-tuple-element.59), channel_id=1, source_target_pairs={{0,7},{1,6},{2,1},{3,0},{4,3},{5,2},{6,5},{7,4},{8,15},{9,14},{10,... | collective-permute-start | bytes 614408 | tf_op jit(solution)/shard_map/ppermute | solution.py:595
  9.3 27.8 %collective-permute-start.6 = (f32[400,128]{1,0:T(8,128)}, f32[400,128]{1,0:T(8,128)S(1)}, u32[]{:S(2)}, u32[]{:S(2)}) collective-permute-start(f32[400,128]{1,0:T(8,128)} %get-tuple-element.60), channel_id=1, source_target_pairs={{0,1},{1,0},{2,3},{3,2},{4,5},{5,4},{6,7},{7,6},{8,9},{9,8},{10,11... | collective-permute-start | bytes 614408 | tf_op jit(solution)/shard_map/ppermute | solution.py:595
  13.4 27.8 %collective-permute-start = (f32[400,128]{1,0:T(8,128)}, f32[400,128]{1,0:T(8,128)S(1)}, u32[]{:S(2)}, u32[]{:S(2)}) collective-permute-start(f32[400,128]{1,0:T(8,128)} %get-tuple-element.54), channel_id=1, source_target_pairs={{0,2},{1,3},{2,4},{3,5},{4,6},{5,7},{6,0},{7,1},{8,10},{9,11},{10,... | collective-permute-start | bytes 614408 | tf_op jit(solution)/shard_map/ppermute | solution.py:595
  15.0 27.7 %collective-permute-start.1 = (f32[400,128]{1,0:T(8,128)}, f32[400,128]{1,0:T(8,128)S(1)}, u32[]{:S(2)}, u32[]{:S(2)}) collective-permute-start(f32[400,128]{1,0:T(8,128)} %get-tuple-element.55), channel_id=1, source_target_pairs={{0,3},{1,2},{2,5},{3,4},{4,7},{5,6},{6,1},{7,0},{8,11},{9,10},{10,... | collective-permute-start | bytes 614408 | tf_op jit(solution)/shard_map/ppermute | solution.py:595
  34.4 22.2 %collective-permute-start.2 = (f32[400,128]{1,0:T(8,128)S(1)}, f32[400,128]{1,0:T(8,128)S(1)}, u32[]{:S(2)}, u32[]{:S(2)}) collective-permute-start(f32[400,128]{1,0:T(8,128)S(1)} %copy-done.48), channel_id=1, source_target_pairs={{0,4},{1,5},{2,6},{3,7},{4,0},{5,1},{6,2},{7,3},{8,12},{9,13},{10,... | collective-permute-start | bytes 614408 | tf_op jit(solution)/shard_map/ppermute | solution.py:595
  36.6 23.0 %collective-permute-start.3 = (f32[400,128]{1,0:T(8,128)S(1)}, f32[400,128]{1,0:T(8,128)S(1)}, u32[]{:S(2)}, u32[]{:S(2)}) collective-permute-start(f32[400,128]{1,0:T(8,128)S(1)} %copy-done.46), channel_id=1, source_target_pairs={{0,5},{1,4},{2,7},{3,6},{4,1},{5,0},{6,3},{7,2},{8,13},{9,12},{10,... | collective-permute-start | bytes 614408 | tf_op jit(solution)/shard_map/ppermute | solution.py:595
  37.1 27.9 %collective-permute-start.10 = (f32[400,128]{1,0:T(8,128)}, f32[400,128]{1,0:T(8,128)S(1)}, u32[]{:S(2)}, u32[]{:S(2)}) collective-permute-start(f32[400,128]{1,0:T(8,128)} %get-tuple-element.67), channel_id=1, source_target_pairs={{0,29},{1,28},{2,31},{3,30},{4,25},{5,24},{6,27},{7,26},{8,5},{9,4... | collective-permute-start | bytes 614408 | tf_op jit(solution)/shard_map/ppermute | solution.py:604
  41.2 34.9 %collective-permute-start.11 = (f32[400,128]{1,0:T(8,128)}, f32[400,128]{1,0:T(8,128)S(1)}, u32[]{:S(2)}, u32[]{:S(2)}) collective-permute-start(f32[400,128]{1,0:T(8,128)} %get-tuple-element.68), channel_id=1, source_target_pairs={{0,30},{1,31},{2,24},{3,25},{4,26},{5,27},{6,28},{7,29},{8,6},{9,7... | collective-permute-start | bytes 614408 | tf_op jit(solution)/shard_map/ppermute | solution.py:604
  42.7 33.4 %collective-permute-start.12 = (f32[400,128]{1,0:T(8,128)}, f32[400,128]{1,0:T(8,128)S(1)}, u32[]{:S(2)}, u32[]{:S(2)}) collective-permute-start(f32[400,128]{1,0:T(8,128)} %get-tuple-element.69), channel_id=1, source_target_pairs={{0,31},{1,30},{2,25},{3,24},{4,27},{5,26},{6,29},{7,28},{8,7},{9,6... | collective-permute-start | bytes 614408 | tf_op jit(solution)/shard_map/ppermute | solution.py:604
  56.5 32.3 %collective-permute-start.13 = (f32[400,128]{1,0:T(8,128)}, f32[400,128]{1,0:T(8,128)S(1)}, u32[]{:S(2)}, u32[]{:S(2)}) collective-permute-start(f32[400,128]{1,0:T(8,128)} %get-tuple-element.70), channel_id=1, source_target_pairs={{0,25},{1,24},{2,27},{3,26},{4,29},{5,28},{6,31},{7,30},{8,1},{9,0... | collective-permute-start | bytes 614408 | tf_op jit(solution)/shard_map/ppermute | solution.py:604
  59.6 29.3 %collective-permute-start.14 = (f32[400,128]{1,0:T(8,128)}, f32[400,128]{1,0:T(8,128)S(1)}, u32[]{:S(2)}, u32[]{:S(2)}) collective-permute-start(f32[400,128]{1,0:T(8,128)} %get-tuple-element.71), channel_id=1, source_target_pairs={{0,24},{1,25},{2,26},{3,27},{4,28},{5,29},{6,30},{7,31},{8,0},{9,1... | collective-permute-start | bytes 614408 | tf_op jit(solution)/shard_map/ppermute | solution.py:604
  65.0 23.9 %collective-permute-start.7 = (f32[400,128]{1,0:T(8,128)}, f32[400,128]{1,0:T(8,128)S(1)}, u32[]{:S(2)}, u32[]{:S(2)}) collective-permute-start(f32[400,128]{1,0:T(8,128)} %get-tuple-element.64), channel_id=1, source_target_pairs={{0,26},{1,27},{2,28},{3,29},{4,30},{5,31},{6,24},{7,25},{8,2},{9,3... | collective-permute-start | bytes 614408 | tf_op jit(solution)/shard_map/ppermute | solution.py:604
  76.0 12.9 %collective-permute-start.8 = (f32[400,128]{1,0:T(8,128)}, f32[400,128]{1,0:T(8,128)S(1)}, u32[]{:S(2)}, u32[]{:S(2)}) collective-permute-start(f32[400,128]{1,0:T(8,128)} %get-tuple-element.65), channel_id=1, source_target_pairs={{0,27},{1,26},{2,29},{3,28},{4,31},{5,30},{6,25},{7,24},{8,3},{9,2... | collective-permute-start | bytes 614408 | tf_op jit(solution)/shard_map/ppermute | solution.py:604
  76.1 21.4 %collective-permute-start.9 = (f32[400,128]{1,0:T(8,128)}, f32[400,128]{1,0:T(8,128)S(1)}, u32[]{:S(2)}, u32[]{:S(2)}) collective-permute-start(f32[400,128]{1,0:T(8,128)} %get-tuple-element.66), channel_id=1, source_target_pairs={{0,28},{1,29},{2,30},{3,31},{4,24},{5,25},{6,26},{7,27},{8,4},{9,5... | collective-permute-start | bytes 614408 | tf_op jit(solution)/shard_map/ppermute | solution.py:604
  121.9 6.7 %collective-permute-start.31 = (f32[200,384]{1,0:T(8,128)}, f32[200,384]{1,0:T(8,128)S(1)}, u32[]{:S(2)}, u32[]{:S(2)}) collective-permute-start(f32[200,384]{1,0:T(8,128)} %get-tuple-element.95), channel_id=1, source_target_pairs={{0,1},{1,0},{2,3},{3,2},{4,5},{5,4},{6,7},{7,6},{8,9},{9,8},{10,11... | collective-permute-start | bytes 921608 | tf_op jit(solution)/shard_map/ppermute | solution.py:595
  122.0 13.8 %collective-permute-start.30 = (f32[200,384]{1,0:T(8,128)}, f32[200,384]{1,0:T(8,128)S(1)}, u32[]{:S(2)}, u32[]{:S(2)}) collective-permute-start(f32[200,384]{1,0:T(8,128)} %get-tuple-element.93), channel_id=1, source_target_pairs={{0,1},{1,0},{2,3},{3,2},{4,5},{5,4},{6,7},{7,6},{8,9},{9,8},{10,11... | collective-permute-start | bytes 921608 | tf_op jit(solution)/shard_map/ppermute | solution.py:595
  124.5 12.7 %collective-permute-start.36 = (f32[200,384]{1,0:T(8,128)S(1)}, f32[200,384]{1,0:T(8,128)S(1)}, u32[]{:S(2)}, u32[]{:S(2)}) collective-permute-start(f32[200,384]{1,0:T(8,128)S(1)} %add.252), channel_id=1, source_target_pairs={{0,24},{8,16},{16,8},{24,0},{1,25},{9,17},{17,9},{25,1},{2,26},{10... | collective-permute-start | bytes 921608 | tf_op jit(solution)/shard_map/ppermute | solution.py:608
  127.0 14.3 %collective-permute-start.34 = (f32[200,384]{1,0:T(8,128)S(1)}, f32[200,384]{1,0:T(8,128)S(1)}, u32[]{:S(2)}, u32[]{:S(2)}) collective-permute-start(f32[200,384]{1,0:T(8,128)S(1)} %add.251), channel_id=1, source_target_pairs={{0,16},{8,24},{16,0},{24,8},{1,17},{9,25},{17,1},{25,9},{2,18},{10... | collective-permute-start | bytes 921608 | tf_op jit(solution)/shard_map/ppermute | solution.py:608
  128.6 12.7 %collective-permute-start.32 = (f32[200,384]{1,0:T(8,128)S(1)}, f32[200,384]{1,0:T(8,128)S(1)}, u32[]{:S(2)}, u32[]{:S(2)}) collective-permute-start(f32[200,384]{1,0:T(8,128)S(1)} %add.250), channel_id=1, source_target_pairs={{0,8},{8,0},{16,24},{24,16},{1,9},{9,1},{17,25},{25,17},{2,10},{10... | collective-permute-start | bytes 921608 | tf_op jit(solution)/shard_map/ppermute | solution.py:608
  135.0 11.4 %collective-permute-start.23 = (f32[400,128]{1,0:T(8,128)}, f32[400,128]{1,0:T(8,128)S(1)}, u32[]{:S(2)}, u32[]{:S(2)}) collective-permute-start(f32[400,128]{1,0:T(8,128)} %get-tuple-element.84), channel_id=1, source_target_pairs={{0,6},{1,7},{2,0},{3,1},{4,2},{5,3},{6,4},{7,5},{8,14},{9,15},{10,... | collective-permute-start | bytes 614408 | tf_op jit(solution)/shard_map/ppermute | solution.py:595
  135.9 17.3 %collective-permute-start.24 = (f32[400,128]{1,0:T(8,128)}, f32[400,128]{1,0:T(8,128)S(1)}, u32[]{:S(2)}, u32[]{:S(2)}) collective-permute-start(f32[400,128]{1,0:T(8,128)} %get-tuple-element.85), channel_id=1, source_target_pairs={{0,7},{1,6},{2,1},{3,0},{4,3},{5,2},{6,5},{7,4},{8,15},{9,14},{10,... | collective-permute-start | bytes 614408 | tf_op jit(solution)/shard_map/ppermute | solution.py:595
  137.2 36.5 %collective-permute-start.25 = (f32[400,128]{1,0:T(8,128)}, f32[400,128]{1,0:T(8,128)S(1)}, u32[]{:S(2)}, u32[]{:S(2)}) collective-permute-start(f32[400,128]{1,0:T(8,128)} %get-tuple-element.86), channel_id=1, source_target_pairs={{0,4},{1,5},{2,6},{3,7},{4,0},{5,1},{6,2},{7,3},{8,12},{9,13},{10,... | collective-permute-start | bytes 614408 | tf_op jit(solution)/shard_map/ppermute | solution.py:595
  144.8 9.1 %collective-permute-start.37 = (f32[56,384]{1,0:T(8,128)}, f32[56,384]{1,0:T(8,128)S(1)}, u32[]{:S(2)}, u32[]{:S(2)}) collective-permute-start(f32[56,384]{1,0:T(8,128)} %get-tuple-element.101), channel_id=1, source_target_pairs={{0,2},{1,3},{2,4},{3,5},{4,6},{5,7},{6,0},{7,1},{8,10},{9,11},{10,... | collective-permute-start | bytes 258056 | tf_op jit(solution)/shard_map/ppermute | solution.py:595
  144.8 24.0 %collective-permute-start.38 = (f32[56,384]{1,0:T(8,128)}, f32[56,384]{1,0:T(8,128)S(1)}, u32[]{:S(2)}, u32[]{:S(2)}) collective-permute-start(f32[56,384]{1,0:T(8,128)} %get-tuple-element.102), channel_id=1, source_target_pairs={{0,4},{1,5},{2,6},{3,7},{4,0},{5,1},{6,2},{7,3},{8,12},{9,13},{10,... | collective-permute-start | bytes 258056 | tf_op jit(solution)/shard_map/ppermute | solution.py:595
  146.5 22.4 %collective-permute-start.39 = (f32[56,384]{1,0:T(8,128)}, f32[56,384]{1,0:T(8,128)S(1)}, u32[]{:S(2)}, u32[]{:S(2)}) collective-permute-start(f32[56,384]{1,0:T(8,128)} %get-tuple-element.103), channel_id=1, source_target_pairs={{0,6},{1,7},{2,0},{3,1},{4,2},{5,3},{6,4},{7,5},{8,14},{9,15},{10,... | collective-permute-start | bytes 258056 | tf_op jit(solution)/shard_map/ppermute | solution.py:595
  153.2 30.9 %collective-permute-start.26 = (f32[400,128]{1,0:T(8,128)S(1)}, f32[400,128]{1,0:T(8,128)S(1)}, u32[]{:S(2)}, u32[]{:S(2)}) collective-permute-start(f32[400,128]{1,0:T(8,128)S(1)} %copy-done.45), channel_id=1, source_target_pairs={{0,5},{1,4},{2,7},{3,6},{4,1},{5,0},{6,3},{7,2},{8,13},{9,12},{10,... | collective-permute-start | bytes 614408 | tf_op jit(solution)/shard_map/ppermute | solution.py:595
  154.0 30.1 %collective-permute-start.27 = (f32[400,128]{1,0:T(8,128)S(1)}, f32[400,128]{1,0:T(8,128)S(1)}, u32[]{:S(2)}, u32[]{:S(2)}) collective-permute-start(f32[400,128]{1,0:T(8,128)S(1)} %copy-done.44), channel_id=1, source_target_pairs={{0,2},{1,3},{2,4},{3,5},{4,6},{5,7},{6,0},{7,1},{8,10},{9,11},{10,... | collective-permute-start | bytes 614408 | tf_op jit(solution)/shard_map/ppermute | solution.py:595
  168.8 16.9 %collective-permute-start.28 = (f32[400,128]{1,0:T(8,128)S(1)}, f32[400,128]{1,0:T(8,128)S(1)}, u32[]{:S(2)}, u32[]{:S(2)}) collective-permute-start(f32[400,128]{1,0:T(8,128)S(1)} %copy-done.43), channel_id=1, source_target_pairs={{0,3},{1,2},{2,5},{3,4},{4,7},{5,6},{6,1},{7,0},{8,11},{9,10},{10,... | collective-permute-start | bytes 614408 | tf_op jit(solution)/shard_map/ppermute | solution.py:595
  168.9 18.5 %collective-permute-start.19 = (f32[400,128]{1,0:T(8,128)}, f32[400,128]{1,0:T(8,128)S(1)}, u32[]{:S(2)}, u32[]{:S(2)}) collective-permute-start(f32[400,128]{1,0:T(8,128)} %get-tuple-element.77), channel_id=1, source_target_pairs={{0,10},{1,11},{2,12},{3,13},{4,14},{5,15},{6,8},{7,9},{8,18},{9,19... | collective-permute-start | bytes 614408 | tf_op jit(solution)/shard_map/ppermute | solution.py:604
  173.7 14.3 %collective-permute-start.40 = (f32[56,384]{1,0:T(8,128)}, f32[56,384]{1,0:T(8,128)S(1)}, u32[]{:S(2)}, u32[]{:S(2)}) collective-permute-start(f32[56,384]{1,0:T(8,128)} %shard_map.146.refs_0_), channel_id=1, source_target_pairs={{0,2},{1,3},{2,4},{3,5},{4,6},{5,7},{6,0},{7,1},{8,10},{9,11},{10,... | collective-permute-start | bytes 258056 | tf_op jit(solution)/shard_map/ppermute | solution.py:595
  184.0 18.8 %collective-permute-start.20 = (f32[400,128]{1,0:T(8,128)}, f32[400,128]{1,0:T(8,128)}, u32[]{:S(2)}, u32[]{:S(2)}) collective-permute-start(f32[400,128]{1,0:T(8,128)} %get-tuple-element.78), channel_id=1, source_target_pairs={{0,11},{1,10},{2,13},{3,12},{4,15},{5,14},{6,9},{7,8},{8,19},{9,18... | collective-permute-start | bytes 614408 | tf_op jit(solution)/shard_map/ppermute | solution.py:604
  184.1 19.5 %collective-permute-start.21 = (f32[400,128]{1,0:T(8,128)}, f32[400,128]{1,0:T(8,128)}, u32[]{:S(2)}, u32[]{:S(2)}) collective-permute-start(f32[400,128]{1,0:T(8,128)} %get-tuple-element.79), channel_id=1, source_target_pairs={{0,9},{1,8},{2,11},{3,10},{4,13},{5,12},{6,15},{7,14},{8,17},{9,16... | collective-permute-start | bytes 614408 | tf_op jit(solution)/shard_map/ppermute | solution.py:604
  185.8 19.1 %collective-permute-start.22 = (f32[400,128]{1,0:T(8,128)}, f32[400,128]{1,0:T(8,128)}, u32[]{:S(2)}, u32[]{:S(2)}) collective-permute-start(f32[400,128]{1,0:T(8,128)} %get-tuple-element.80), channel_id=1, source_target_pairs={{0,8},{1,9},{2,10},{3,11},{4,12},{5,13},{6,14},{7,15},{8,16},{9,17... | collective-permute-start | bytes 614408 | tf_op jit(solution)/shard_map/ppermute | solution.py:604
  187.4 10.8 %collective-permute-start.41 = (f32[56,384]{1,0:T(8,128)}, f32[56,384]{1,0:T(8,128)S(1)}, u32[]{:S(2)}, u32[]{:S(2)}) collective-permute-start(f32[56,384]{1,0:T(8,128)} %shard_map.146.refs_0_), channel_id=1, source_target_pairs={{0,4},{1,5},{2,6},{3,7},{4,0},{5,1},{6,2},{7,3},{8,12},{9,13},{10,... | collective-permute-start | bytes 258056 | tf_op jit(solution)/shard_map/ppermute | solution.py:595
  188.0 12.4 %collective-permute-start.42 = (f32[56,384]{1,0:T(8,128)}, f32[56,384]{1,0:T(8,128)S(1)}, u32[]{:S(2)}, u32[]{:S(2)}) collective-permute-start(f32[56,384]{1,0:T(8,128)} %shard_map.146.refs_0_), channel_id=1, source_target_pairs={{0,6},{1,7},{2,0},{3,1},{4,2},{5,3},{6,4},{7,5},{8,14},{9,15},{10,... | collective-permute-start | bytes 258056 | tf_op jit(solution)/shard_map/ppermute | solution.py:595
  198.1 9.9 %collective-permute-start.15 = (f32[400,128]{1,0:T(8,128)}, f32[400,128]{1,0:T(8,128)S(1)}, u32[]{:S(2)}, u32[]{:S(2)}) collective-permute-start(f32[400,128]{1,0:T(8,128)} %get-tuple-element.73), channel_id=1, source_target_pairs={{0,14},{1,15},{2,8},{3,9},{4,10},{5,11},{6,12},{7,13},{8,22},{9,23... | collective-permute-start | bytes 614408 | tf_op jit(solution)/shard_map/ppermute | solution.py:604
  200.4 10.0 %collective-permute-start.16 = (f32[400,128]{1,0:T(8,128)}, f32[400,128]{1,0:T(8,128)S(1)}, u32[]{:S(2)}, u32[]{:S(2)}) collective-permute-start(f32[400,128]{1,0:T(8,128)} %get-tuple-element.74), channel_id=1, source_target_pairs={{0,15},{1,14},{2,9},{3,8},{4,11},{5,10},{6,13},{7,12},{8,23},{9,22... | collective-permute-start | bytes 614408 | tf_op jit(solution)/shard_map/ppermute | solution.py:604
  202.8 23.7 %collective-permute-start.43 = (f32[200,384]{1,0:T(8,128)}, f32[200,384]{1,0:T(8,128)S(1)}, u32[]{:S(2)}, u32[]{:S(2)}) collective-permute-start(f32[200,384]{1,0:T(8,128)} %shard_map.147.refs_0_), channel_id=1, source_target_pairs={{0,8},{8,0},{16,24},{24,16},{1,9},{9,1},{17,25},{25,17},{2,10},{10... | collective-permute-start | bytes 921608 | tf_op jit(solution)/shard_map/ppermute | solution.py:608
  203.5 23.5 %collective-permute-start.44 = (f32[200,384]{1,0:T(8,128)}, f32[200,384]{1,0:T(8,128)S(1)}, u32[]{:S(2)}, u32[]{:S(2)}) collective-permute-start(f32[200,384]{1,0:T(8,128)} %shard_map.147.refs_0_), channel_id=1, source_target_pairs={{0,16},{8,24},{16,0},{24,8},{1,17},{9,25},{17,1},{25,9},{2,18},{10... | collective-permute-start | bytes 921608 | tf_op jit(solution)/shard_map/ppermute | solution.py:608
  204.9 28.1 %collective-permute-start.45 = (f32[200,384]{1,0:T(8,128)}, f32[200,384]{1,0:T(8,128)S(1)}, u32[]{:S(2)}, u32[]{:S(2)}) collective-permute-start(f32[200,384]{1,0:T(8,128)} %shard_map.147.refs_0_), channel_id=1, source_target_pairs={{0,24},{8,16},{16,8},{24,0},{1,25},{9,17},{17,9},{25,1},{2,26},{10... | collective-permute-start | bytes 921608 | tf_op jit(solution)/shard_map/ppermute | solution.py:608
  208.1 18.4 %collective-permute-start.17 = (f32[400,128]{1,0:T(8,128)}, f32[400,128]{1,0:T(8,128)S(1)}, u32[]{:S(2)}, u32[]{:S(2)}) collective-permute-start(f32[400,128]{1,0:T(8,128)} %get-tuple-element.75), channel_id=1, source_target_pairs={{0,12},{1,13},{2,14},{3,15},{4,8},{5,9},{6,10},{7,11},{8,20},{9,21... | collective-permute-start | bytes 614408 | tf_op jit(solution)/shard_map/ppermute | solution.py:604
  210.4 22.7 %collective-permute-start.18 = (f32[400,128]{1,0:T(8,128)}, f32[400,128]{1,0:T(8,128)S(1)}, u32[]{:S(2)}, u32[]{:S(2)}) collective-permute-start(f32[400,128]{1,0:T(8,128)} %get-tuple-element.76), channel_id=1, source_target_pairs={{0,13},{1,12},{2,15},{3,14},{4,9},{5,8},{6,11},{7,10},{8,21},{9,20... | collective-permute-start | bytes 614408 | tf_op jit(solution)/shard_map/ppermute | solution.py:604
  226.5 23.1 %collective-permute-start.46 = (f32[200,384]{1,0:T(8,128)}, f32[200,384]{1,0:T(8,128)S(1)}, u32[]{:S(2)}, u32[]{:S(2)}) collective-permute-start(f32[200,384]{1,0:T(8,128)} %shard_map.147.refs_0_), channel_id=1, source_target_pairs={{0,1},{1,0},{2,3},{3,2},{4,5},{5,4},{6,7},{7,6},{8,9},{9,8},{10,11... | collective-permute-start | bytes 921608 | tf_op jit(solution)/shard_map/ppermute | solution.py:595
  226.5 23.1 %collective-permute-start.47 = (f32[200,384]{1,0:T(8,128)S(1)}, f32[200,384]{1,0:T(8,128)S(1)}, u32[]{:S(2)}, u32[]{:S(2)}) collective-permute-start(f32[200,384]{1,0:T(8,128)S(1)} %collective-permute-done.43.refs_1_), channel_id=1, source_target_pairs={{0,1},{1,0},{2,3},{3,2},{4,5},{5,4},{6,7},{7,6},{8,9},{9,8},{10,11... | collective-permute-start | bytes 921608 | tf_op jit(solution)/shard_map/ppermute | solution.py:595
  227.0 22.6 %collective-permute-start.48 = (f32[200,384]{1,0:T(8,128)S(1)}, f32[200,384]{1,0:T(8,128)S(1)}, u32[]{:S(2)}, u32[]{:S(2)}) collective-permute-start(f32[200,384]{1,0:T(8,128)S(1)} %collective-permute-done.44.refs_2_), channel_id=1, source_target_pairs={{0,1},{1,0},{2,3},{3,2},{4,5},{5,4},{6,7},{7,6},{8,9},{9,8},{10,11... | collective-permute-start | bytes 921608 | tf_op jit(solution)/shard_map/ppermute | solution.py:595
  233.0 16.6 %collective-permute-start.49 = (f32[200,384]{1,0:T(8,128)S(1)}, f32[200,384]{1,0:T(8,128)S(1)}, u32[]{:S(2)}, u32[]{:S(2)}) collective-permute-start(f32[200,384]{1,0:T(8,128)S(1)} %collective-permute-done.45.refs_3_), channel_id=1, source_target_pairs={{0,1},{1,0},{2,3},{3,2},{4,5},{5,4},{6,7},{7,6},{8,9},{9,8},{10,11... | collective-permute-start | bytes 921608 | tf_op jit(solution)/shard_map/ppermute | solution.py:595
  233.1 12.2 %collective-permute-start.29 = (f32[400,128]{1,0:T(8,128)}, f32[400,128]{1,0:T(8,128)}, u32[]{:S(2)}, u32[]{:S(2)}) collective-permute-start(f32[400,128]{1,0:T(8,128)} %get-tuple-element.90), channel_id=1, source_target_pairs={{0,1},{1,0},{2,3},{3,2},{4,5},{5,4},{6,7},{7,6},{8,9},{9,8},{10,11... | collective-permute-start | bytes 614408 | tf_op jit(solution)/shard_map/ppermute | solution.py:595
  (60 other events, 930.5 us)

commit v3 on v2

--- a/solution.py
+++ b/solution.py
@@ -20,7 +20,7 @@
 F32, BF16, I32 = jnp.float32, jnp.bfloat16, jnp.int32
 VMEM = pl.BlockSpec(memory_space=pltpu.VMEM)
 SMEM = pl.BlockSpec(memory_space=pltpu.SMEM)
-VMEM_LIMIT = 60 << 20
+VMEM_LIMIT = 32 << 20
 
 
 def kernel_call(kernel, outs, flops, moved, **kw):
@@ -434,36 +434,26 @@
     )(me, table, grad, heads, rels, edge_relation)
 
 
-def source_grad_kernel(rows_ref, edge_source_ref, *refs):
-    outs, total = refs[:-1], refs[-1]
+def source_grad_kernel(first, rows_ref, edge_source_ref, *outs):
+    step = pl.program_id(0)
     block = outs[0].shape[1]
-    step = pl.program_id(0)
-
-    @pl.when(step == 0)
-    def _():
-        total[...] = jnp.zeros_like(total)
-
-    hot = columns_hot(edge_source_ref[...], total.shape[1])
-    total[...] += dot(rows_ref[0], hot) + dot(rows_ref[1], hot)
-
-    @pl.when(step == pl.num_programs(0) - 1)
-    def _():
-        for p, ref in enumerate(outs):
-            ref[...] = total[:, p * block:(p + 1) * block]
-
-
-def source_grads(rows, edge_source, peers, block):
+    hot = columns_hot(edge_source_ref[...] - (first * block + step * 2 * block), 2 * block)
+    result = dot(rows_ref[0], hot) + dot(rows_ref[1], hot)
+    for pair in range(len(outs) // 2):
+        @pl.when(step == pair)
+        def _():
+            outs[2 * pair][...] = result[:, :block]
+            outs[2 * pair + 1][...] = result[:, block:]
+
+
+def source_grads(rows, edge_source, block, first, count):
     _, features, edges = rows.shape
     return kernel_call(
-        source_grad_kernel, [shape((features, block))] * peers,
-        4 * features * peers * block * edges, 12 * features * edges,
-        grid=(edges // CHUNK,),
-        in_specs=[
-            pl.BlockSpec((2, features, CHUNK), lambda i: (0, 0, i)),
-            pl.BlockSpec((CHUNK, 1), lambda i: (i, 0)),
-        ],
-        out_specs=[held((features, block))] * peers,
-        scratch_shapes=[pltpu.VMEM((features, peers * block), F32)],
+        functools.partial(source_grad_kernel, first), [shape((features, block))] * count,
+        4 * features * count * block * edges, 4 * features * (edges + count * block),
+        grid=(count // 2,),
+        in_specs=[held((2, features, edges)), held((edges, 1))],
+        out_specs=[held((features, block))] * count,
     )(rows, edge_source)
 
 
@@ -488,7 +478,7 @@
 
 def adagrad(params, state, gradient):
     new_state = state + jnp.mean(gradient * gradient, axis=0, keepdims=True)
-    return params - learn_rate * gradient / jnp.sqrt(new_state)
+    return params - gradient * (learn_rate / jnp.sqrt(new_state))
 
 
 def entity_kernel(other_ref, entity_ref, state_ref, hot_ref, *refs):
@@ -646,9 +636,8 @@
         return places_of(me, slots // block, peers) * block + slots % block
 
     edge_source, edge_target = placed(edge_source), placed(edge_target)
-    first = peers // 2
-    sources = pick_blocks(order[:first], entity_t, src_send[0])
-    sources += pick_blocks(order[first:], entity_t, src_send[0])
+    sources = pick_blocks(order[:2], entity_t, src_send[0])
+    sources += pick_blocks(order[2:], entity_t, src_send[0])
     sources = [
         sent_on(value, hop, peers) if hop != (0, 0) else value
         for value, hop in zip(sources, ways)
@@ -663,21 +652,23 @@
     loss, grad, table = score_spans(
         edge_count, targets, query_lines, counts, edge_target.reshape(-1, 1)
     )
-    table_parts = table_grads(query_columns, grad, block, 0, first)
-    table_parts += table_grads(query_columns, grad, block, first, peers - first)
+    table_parts = table_grads(query_columns, grad, block, 0, 2)
+    table_parts += table_grads(query_columns, grad, block, 2, peers - 2)
     back = [(-hop[0], hop[1]) for hop in ways]
     home = [
         sent_across(value, hop, peers, groups, 1)
-        for value, hop in zip(table_parts[:first], back[:first])
+        for value, hop in zip(table_parts[:2], back[:2])
     ]
     home += [
         sent_across(value, hop, peers, groups, 1)
-        for value, hop in zip(table_parts[first:], back[first:])
+        for value, hop in zip(table_parts[2:], back[2:])
     ]
     source_lines, *halves = relation_grads(
         here, table, grad, heads, rels, edge_relation.reshape(-1, 1), groups, width
     )
-    source_parts = source_grads(source_lines, edge_source.reshape(-1, 1), peers, block)
+    edge_source = edge_source.reshape(-1, 1)
+    source_parts = source_grads(source_lines, edge_source, block, 0, 2)
+    source_parts += source_grads(source_lines, edge_source, block, 2, peers - 2)
     returned = []
     for value, hop, way in zip(source_parts, back, ways):
         returned.append(sent_on(value, hop, peers) if way != (0, 0) else value)

time: 257 us -> 251 us (0.977)
  Pallas kernels: 88.2 us -> 54.4 us
  waiting for transfers between devices: 72.3 us -> 87.7 us
  local copies, waits for them, and re-layouts: 11.8 us -> 25.9 us
  other arithmetic: 7.32 us -> 4.41 us
    unnamed x116 -> x114, local copies, waits for them, and re-layouts: 4.03 us -> 23.4 us
    ppermute x16, waiting for transfers between devices: 31.2 us -> 44.5 us  [sent_across(): return lax.ppermute(value, ('group', 'shard'), pairs)]
    ppermute x6, waiting for transfers between devices: 8.83 us -> 15.1 us  [sent_group(): return lax.ppermute(value, 'group', [(g, g ^ bit) for g in range(groups)])]
    pallas_call x2, Pallas kernels: 8.72 us -> 3.75 us  [table_grads(): kernel_call(table_grad_kernel, [shape((features, block))] * count, 6 * fe...]
    ppermute x28, waiting for transfers between devices: 32.2 us -> 28 us  [sent_on(): lax.ppermute(value, 'shard', [(i, partner(i, hop, peers, 1)) for i in ran...]
    pallas_call x3, Pallas kernels: 9.46 us -> 5.64 us  [pick_blocks(): kernel_call(pick_kernel, [shape((features, block))] * count, 6 * features...]
    pallas_call x1, Pallas kernels: 10.4 us -> 6.87 us  [score_spans(): kernel_call(functools.partial(score_kernel, peers), [shape((edges, 1)), s...]
    pallas_call x2, Pallas kernels: 4.55 us -> 1.57 us  [home_hots(): kernel_call(hot_kernel, shape((peers * block, rows), BF16), 2 * peers * b...]
  transfers between devices with their start and end apart: 50 -> 50, of which waited for: 12 -> 15; matrix products, arithmetic and copies ran while one was open for 6% -> 3% of each run, Pallas kernels for 22% -> 13%
where the time goes in v3:
time: 251 us; the launch traced here: 250 us
  waiting for transfers between devices  87.7 us (35%)
  starting transfers between devices  75.7 us (30%)
  Pallas kernels  54.4 us (22%)
  local copies, waits for them, and re-layouts  25.9 us (10%)
  other arithmetic  4.41 us (2%)
    ppermute x16, waiting for transfers between devices, sent_across(): return lax.ppermute(value, ('group', 'shard'), pairs)  44.5 us
    ppermute x28, starting transfers between devices, sent_on(): lax.ppermute(value, 'shard', [(i, partner(i, hop, peers, 1)) for i in ran...  35.4 us
    ppermute x16, starting transfers between devices, sent_across(): return lax.ppermute(value, ('group', 'shard'), pairs)  33.2 us
    ppermute x28, waiting for transfers between devices, sent_on(): lax.ppermute(value, 'shard', [(i, partner(i, hop, peers, 1)) for i in ran...  28 us
    unnamed x114, local copies, waits for them, and re-layouts  23.4 us
    ppermute x6, waiting for transfers between devices, sent_group(): return lax.ppermute(value, 'group', [(g, g ^ bit) for g in range(groups)])  15.1 us
    pallas_call x1, Pallas kernels, relation_grads(): kernel_call(functools.partial(relation_grad_kernel, steps), [shape((2, fe...  9.92 us
    pallas_call x1, Pallas kernels, query_rows(): kernel_call(query_kernel, [shape((features, edges)), shape((2, features,...  7.26 us
  transfers between devices with their start and end apart: 50, of which 15 were waited for; matrix products, arithmetic and copies ran while one was open for 3% of the time, Pallas kernels for 13%

profile of v3, /device:TPU:0, one launch (start us, length us, event | category | flops | bytes accessed | tf_op | source)
XLA Modules:
  0.0 250.1 jit_solution(2814814831787553121)
XLA Ops:
  0.8 1.1 copy-done.7
  2.7 2.6 %shard_map.133 = (f32[400,128]{1,0:T(8,128)}, f32[400,128]{1,0:T(8,128)}, f32[400,128]{1,0:T(8,128)}, f32[400,128]{1,0:T(8,128)}, f32[400,128]{1,0:T(8,128)}, /*index=5*/f32[400,128]{1,0:T(8,128)S(1)}) custom-call(s32[6]{0:T(128)S(1)} %stack.50.order_ref, f32[400,512]{1,0:T(8,128)S(1)} %bitcast.28, s32[8,128]{1,0:T(8,128)S(1)} %bitcast.38), custom_call_target="tpu_custom_call" | custom-call | flops 943718400 | bytes 2457600 | tf_op jit(solution)/shard_map/pallas_call | solution.py:126
  5.9 4.1 %collective-permute-start.2 = (f32[400,128]{1,0:T(8,128)}, f32[400,128]{1,0:T(8,128)}, u32[]{:S(2)}, u32[]{:S(2)}) collective-permute-start(f32[400,128]{1,0:T(8,128)} %get-tuple-element.56), channel_id=1, source_target_pairs={{0,4},{1,5},{2,6},{3,7},{4,0},{5,1},{6,2},{7,3},{8,12},{9,13},{10,... | collective-permute-start | bytes 614408 | tf_op jit(solution)/shard_map/ppermute | solution.py:585
  10.0 3.1 %collective-permute-start.4 = (f32[400,128]{1,0:T(8,128)}, f32[400,128]{1,0:T(8,128)}, u32[]{:S(2)}, u32[]{:S(2)}) collective-permute-start(f32[400,128]{1,0:T(8,128)} %get-tuple-element.58), channel_id=1, source_target_pairs={{0,6},{1,7},{2,0},{3,1},{4,2},{5,3},{6,4},{7,5},{8,14},{9,15},{10,... | collective-permute-start | bytes 614408 | tf_op jit(solution)/shard_map/ppermute | solution.py:585
  19.9 5.3 %shard_map.131.refs_1_.rels_ref = f32[400,1024]{1,0:T(8,128)S(1)} custom-call(f32[400,1345]{1,0:T(8,128)S(1)} %bitcast.26, s32[1,1024]{1,0:T(1,128)S(1)} %bitcast.35), custom_call_target="tpu_custom_call" | custom-call | flops 3460300800 | bytes 3276800 | tf_op jit(solution)/shard_map/pallas_call | solution.py:153
  25.3 2.0 shard_map.136
  27.3 6.4 %collective-permute-start = (f32[400,128]{1,0:T(8,128)S(1)}, f32[400,128]{1,0:T(8,128)S(1)}, u32[]{:S(2)}, u32[]{:S(2)}) collective-permute-start(f32[400,128]{1,0:T(8,128)S(1)} %copy-done.50), channel_id=1, source_target_pairs={{0,2},{1,3},{2,4},{3,5},{4,6},{5,7},{6,0},{7,1},{8,10},{9,11},{10,... | collective-permute-start | bytes 614408 | tf_op jit(solution)/shard_map/ppermute | solution.py:585
  33.7 3.9 %collective-permute-start.1 = (f32[400,128]{1,0:T(8,128)S(1)}, f32[400,128]{1,0:T(8,128)S(1)}, u32[]{:S(2)}, u32[]{:S(2)}) collective-permute-start(f32[400,128]{1,0:T(8,128)S(1)} %copy-done.48), channel_id=1, source_target_pairs={{0,3},{1,2},{2,5},{3,4},{4,7},{5,6},{6,1},{7,0},{8,11},{9,10},{10,... | collective-permute-start | bytes 614408 | tf_op jit(solution)/shard_map/ppermute | solution.py:585
  37.7 5.4 %collective-permute-start.10 = (f32[400,128]{1,0:T(8,128)S(1)}, f32[400,128]{1,0:T(8,128)S(1)}, u32[]{:S(2)}, u32[]{:S(2)}) collective-permute-start(f32[400,128]{1,0:T(8,128)S(1)} %get-tuple-element.67), channel_id=1, source_target_pairs={{0,29},{1,28},{2,31},{3,30},{4,25},{5,24},{6,27},{7,26},{8,5},{9,4... | collective-permute-start | bytes 614408 | tf_op jit(solution)/shard_map/ppermute | solution.py:594
  43.0 1.2 collective-permute-start.12
  44.3 1.4 collective-permute-start.13
  45.7 2.4 collective-permute-start.14
  48.1 7.9 %collective-permute-done.10.refs_7_ = f32[400,128]{1,0:T(8,128)S(1)} collective-permute-done((f32[400,128]{1,0:T(8,128)S(1)}, f32[400,128]{1,0:T(8,128)S(1)}, u32[]{:S(2)}, u32[]{:S(2)}) %collective-permute-start.10) | collective-permute-done | bytes 204832 | tf_op jit(solution)/shard_map/ppermute | solution.py:594
  56.0 10.2 %collective-permute-start.7 = (f32[400,128]{1,0:T(8,128)S(1)}, f32[400,128]{1,0:T(8,128)S(1)}, u32[]{:S(2)}, u32[]{:S(2)}) collective-permute-start(f32[400,128]{1,0:T(8,128)S(1)} %get-tuple-element.64), channel_id=1, source_target_pairs={{0,26},{1,27},{2,28},{3,29},{4,30},{5,31},{6,24},{7,25},{8,2},{9,3... | collective-permute-start | bytes 614408 | tf_op jit(solution)/shard_map/ppermute | solution.py:594
  66.2 4.5 %collective-permute-start.9 = (f32[400,128]{1,0:T(8,128)S(1)}, f32[400,128]{1,0:T(8,128)S(1)}, u32[]{:S(2)}, u32[]{:S(2)}) collective-permute-start(f32[400,128]{1,0:T(8,128)S(1)} %get-tuple-element.66), channel_id=1, source_target_pairs={{0,28},{1,29},{2,30},{3,31},{4,24},{5,25},{6,26},{7,27},{8,4},{9,5... | collective-permute-start | bytes 614408 | tf_op jit(solution)/shard_map/ppermute | solution.py:594
  70.7 7.3 %shard_map.134 = (f32[400,1024]{1,0:T(8,128)S(1)}, bf16[2,400,1024]{2,1,0:T(8,128)(2,1)S(1)}, bf16[1024,1200]{1,0:T(8,128)(2,1)S(1)}) custom-call(s32[1,1024]{1,0:T(1,128)S(1)} %bitcast.32, f32[400,1024]{1,0:T(8,128)S(1)} %shard_map.131.refs_1_.rels_ref, f32[400,128]{1,0:T(8,128)S(1)} %collective-permute-done.refs_2_, ...), custom_call_target="tpu_custom_call" | custom-call | flops 2516582400 | bytes 8192000 | tf_op jit(solution)/shard_map/pallas_call | solution.py:221
  78.0 9.4 %collective-permute-done.9.refs_6_ = f32[400,128]{1,0:T(8,128)S(1)} collective-permute-done((f32[400,128]{1,0:T(8,128)S(1)}, f32[400,128]{1,0:T(8,128)S(1)}, u32[]{:S(2)}, u32[]{:S(2)}) %collective-permute-start.9) | collective-permute-done | bytes 204832 | tf_op jit(solution)/shard_map/ppermute | solution.py:594
  87.4 6.9 %shard_map.137 = (f32[1024,1]{1,0:T(8,128)S(1)}, bf16[2,1024,1024]{2,1,0:T(8,128)(2,1)S(1)}, bf16[1200,1024]{1,0:T(8,128)(2,1)S(1)}) custom-call(s32[1]{0:T(128)S(6)} %copy.21.refs_0_, bf16[1024,1200]{1,0:T(8,128)(2,1)S(1)} %get-tuple-element.63.refs_1_, f32[2,1,1024]{2,1,0:T(1,128)S(1)} %shard_map.135.refs_2_, s32[1024,1]{1,0:T(8,128)S(1)} %copy-done.11, ...), custom_call_target="tpu_custom_call" | custom-call | flops 2516582400 | bytes 12288000 | tf_op jit(solution)/shard_map/pallas_call | solution.py:311
  94.3 9.9 %shard_map.142 = (bf16[2,400,1024]{2,1,0:T(8,128)(2,1)S(1)}, f32[200,384]{1,0:T(8,128)S(1)}, f32[200,384]{1,0:T(8,128)S(1)}, f32[200,384]{1,0:T(8,128)S(1)}, f32...) custom-call(s32[2]{0:T(128)S(1)} %pad_add_fusion.1.me_ref, ...), custom_call_target="tpu_custom_call" | custom-call | flops 4194304000 | bytes 12288000 | tf_op jit(solution)/shard_map/pallas_call | solution.py:415
  106.5 1.4 collective-permute-start.36
  108.7 1.5 collective-permute-start.34
  111.8 1.4 copy-done.5
  113.2 2.1 shard_map.144
  115.4 1.5 collective-permute-start.26
  118.0 5.7 %collective-permute-done.34.refs_2_ = f32[200,384]{1,0:T(8,128)} collective-permute-done((f32[200,384]{1,0:T(8,128)}, f32[200,384]{1,0:T(8,128)}, u32[]{:S(2)}, u32[]{:S(2)}) %collective-permute-start.34) | collective-permute-done | bytes 307232 | tf_op jit(solution)/shard_map/ppermute | solution.py:598
  123.7 1.2 shard_map.146
  125.4 3.9 %collective-permute-start.27 = (f32[400,128]{1,0:T(8,128)S(1)}, f32[400,128]{1,0:T(8,128)S(1)}, u32[]{:S(2)}, u32[]{:S(2)}) collective-permute-start(f32[400,128]{1,0:T(8,128)S(1)} %get-tuple-element.88), channel_id=1, source_target_pairs={{0,2},{1,3},{2,4},{3,5},{4,6},{5,7},{6,0},{7,1},{8,10},{9,11},{10,... | collective-permute-start | bytes 614408 | tf_op jit(solution)/shard_map/ppermute | solution.py:585
  129.3 1.3 shard_map.143
  130.6 14.7 %collective-permute-done.26.refs_3_ = f32[400,128]{1,0:T(8,128)S(1)} collective-permute-done((f32[400,128]{1,0:T(8,128)S(1)}, f32[400,128]{1,0:T(8,128)S(1)}, u32[]{:S(2)}, u32[]{:S(2)}) %collective-permute-start.26) | collective-permute-done | bytes 204832 | tf_op jit(solution)/shard_map/ppermute | solution.py:585
  145.5 1.9 collective-permute-done.38.refs_2_
  147.4 2.9 %shard_map.139 = (f32[400,128]{1,0:T(8,128)S(1)}, f32[400,128]{1,0:T(8,128)S(1)}, f32[400,128]{1,0:T(8,128)S(1)}, f32[400,128]{1,0:T(8,128)S(1)}, f32[400,128]{1,0:T(8,128)S(1)}, /*index=5*/f32[400,128]{1,0:T(8,128)S(1)}) custom-call(bf16[2,400,1024]{2,1,0:T(8,128)(2,1)S(1)} %get-tuple-element.62.columns_ref, bf16[2,1024,1024]{2,1,0:T(8,128)(2,1)S(1)} %copy-done.1), custom_call_target="tpu_custom_call" | custom-call | flops 1887436800 | bytes 4784128 | tf_op jit(solution)/shard_map/pallas_call | solution.py:352
  150.4 4.3 %collective-permute-done.39.refs_3_ = f32[56,384]{1,0:T(8,128)S(1)} collective-permute-done((f32[56,384]{1,0:T(8,128)S(1)}, f32[56,384]{1,0:T(8,128)S(1)}, u32[]{:S(2)}, u32[]{:S(2)}) %collective-permute-start.39) | collective-permute-done | bytes 86048 | tf_op jit(solution)/shard_map/ppermute | solution.py:585
  155.4 3.0 %collective-permute-start.40 = (f32[56,384]{1,0:T(8,128)S(1)}, f32[56,384]{1,0:T(8,128)S(1)}, u32[]{:S(2)}, u32[]{:S(2)}) collective-permute-start(f32[56,384]{1,0:T(8,128)S(1)} %shard_map.147.refs_0_), channel_id=1, source_target_pairs={{0,2},{1,3},{2,4},{3,5},{4,6},{5,7},{6,0},{7,1},{8,10},{9,11},{10,... | collective-permute-start | bytes 258056 | tf_op jit(solution)/shard_map/ppermute | solution.py:585
  160.9 3.6 %collective-permute-start.20 = (f32[400,128]{1,0:T(8,128)S(1)}, f32[400,128]{1,0:T(8,128)S(1)}, u32[]{:S(2)}, u32[]{:S(2)}) collective-permute-start(f32[400,128]{1,0:T(8,128)S(1)} %get-tuple-element.78), channel_id=1, source_target_pairs={{0,11},{1,10},{2,13},{3,12},{4,15},{5,14},{6,9},{7,8},{8,19},{9,18... | collective-permute-start | bytes 614408 | tf_op jit(solution)/shard_map/ppermute | solution.py:594
  164.5 20.1 %collective-permute-done.17.refs_2_ = f32[400,128]{1,0:T(8,128)S(1)} collective-permute-done((f32[400,128]{1,0:T(8,128)S(1)}, f32[400,128]{1,0:T(8,128)S(1)}, u32[]{:S(2)}, u32[]{:S(2)}) %collective-permute-start.17) | collective-permute-done | bytes 204832 | tf_op jit(solution)/shard_map/ppermute | solution.py:594
  185.3 6.2 %collective-permute-done.41.refs_2_ = f32[56,384]{1,0:T(8,128)S(1)} collective-permute-done((f32[56,384]{1,0:T(8,128)S(1)}, f32[56,384]{1,0:T(8,128)S(1)}, u32[]{:S(2)}, u32[]{:S(2)}) %collective-permute-start.41) | collective-permute-done | bytes 86048 | tf_op jit(solution)/shard_map/ppermute | solution.py:585
  191.7 1.6 collective-permute-start.22
  193.9 1.5 collective-permute-start.43
  195.9 1.6 collective-permute-start.45
  198.3 1.5 collective-permute-done.21.refs_6_
  200.5 1.3 collective-permute-start.15
  203.4 4.8 %collective-permute-done.15.refs_0_ = f32[400,128]{1,0:T(8,128)S(1)} collective-permute-done((f32[400,128]{1,0:T(8,128)S(1)}, f32[400,128]{1,0:T(8,128)S(1)}, u32[]{:S(2)}, u32[]{:S(2)}) %collective-permute-start.15) | collective-permute-done | bytes 204832 | tf_op jit(solution)/shard_map/ppermute | solution.py:594
  208.8 3.1 %collective-permute-start.46 = (f32[200,384]{1,0:T(8,128)S(1)}, f32[200,384]{1,0:T(8,128)}, u32[]{:S(2)}, u32[]{:S(2)}) collective-permute-start(f32[200,384]{1,0:T(8,128)S(1)} %shard_map.148.refs_0_), channel_id=1, source_target_pairs={{0,1},{1,0},{2,3},{3,2},{4,5},{5,4},{6,7},{7,6},{8,9},{9,8},{10,11... | collective-permute-start | bytes 921608 | tf_op jit(solution)/shard_map/ppermute | solution.py:585
  211.9 4.6 %collective-permute-done.43.refs_1_ = f32[200,384]{1,0:T(8,128)} collective-permute-done((f32[200,384]{1,0:T(8,128)S(1)}, f32[200,384]{1,0:T(8,128)}, u32[]{:S(2)}, u32[]{:S(2)}) %collective-permute-start.43) | collective-permute-done | bytes 307232 | tf_op jit(solution)/shard_map/ppermute | solution.py:598
  216.5 3.3 %collective-permute-start.47 = (f32[200,384]{1,0:T(8,128)}, f32[200,384]{1,0:T(8,128)}, u32[]{:S(2)}, u32[]{:S(2)}) collective-permute-start(f32[200,384]{1,0:T(8,128)} %collective-permute-done.43.refs_1_), channel_id=1, source_target_pairs={{0,1},{1,0},{2,3},{3,2},{4,5},{5,4},{6,7},{7,6},{8,9},{9,8},{10,11... | collective-permute-start | bytes 921608 | tf_op jit(solution)/shard_map/ppermute | solution.py:585
  219.9 4.8 %collective-permute-done.45.refs_3_ = f32[200,384]{1,0:T(8,128)} collective-permute-done((f32[200,384]{1,0:T(8,128)S(1)}, f32[200,384]{1,0:T(8,128)}, u32[]{:S(2)}, u32[]{:S(2)}) %collective-permute-start.45) | collective-permute-done | bytes 307232 | tf_op jit(solution)/shard_map/ppermute | solution.py:598
  243.2 3.2 %shard_map.145 = f32[400,512]{1,0:T(8,128)} custom-call(f32[400,512]{1,0:T(8,128)S(1)} %shard_map.140.other_ref, f32[400,512]{1,0:T(8,128)S(1)} %bitcast.31, f32[1,512]{1,0:T(1,128)S(1)} %bitcast.41, bf16[1024,512]{1,0:T(8,128)(2,1)S(1)} %shard_map.141.hot_ref, f32[400,128]{1,0:T(8,128)S(1)} %copy-done.25, f32[400,128]{1,0:T(8,128)} %collective-permute-done.24.refs_1_, ...), custom_call_target="tpu_custom_call" | custom-call | flops 838860800 | bytes 3276800 | tf_op jit(solution)/shard_map/pallas_call | solution.py:491
  246.4 3.7 %shard_map.149 = f32[400,1345]{1,0:T(8,128)} custom-call(s32[2]{0:T(128)S(1)} %pad_add_fusion.1.me_ref, f32[400,1345]{1,0:T(8,128)S(1)} %bitcast.27, f32[1,1345]{1,0:T(1,128)S(1)} %reshape.36.state_ref, f32[200,384]{1,0:T(8,128)S(1)} %shard_map.148.refs_0_, f32[200,384]{1,0:T(8,128)} %collective-permute-done.43.refs_1_, ...), custom_call_target="tpu_custom_call" | custom-call | flops 4304000 | bytes 6456000 | tf_op jit(solution)/shard_map/pallas_call | solution.py:576
  (207 shorter events, 41.4 us)
Async XLA Ops:
  5.9 21.4 %collective-permute-start.2 = (f32[400,128]{1,0:T(8,128)}, f32[400,128]{1,0:T(8,128)}, u32[]{:S(2)}, u32[]{:S(2)}) collective-permute-start(f32[400,128]{1,0:T(8,128)} %get-tuple-element.56), channel_id=1, source_target_pairs={{0,4},{1,5},{2,6},{3,7},{4,0},{5,1},{6,2},{7,3},{8,12},{9,13},{10,... | collective-permute-start | bytes 614408 | tf_op jit(solution)/shard_map/ppermute | solution.py:585
  10.0 23.8 %collective-permute-start.3 = (f32[400,128]{1,0:T(8,128)}, f32[400,128]{1,0:T(8,128)}, u32[]{:S(2)}, u32[]{:S(2)}) collective-permute-start(f32[400,128]{1,0:T(8,128)} %get-tuple-element.57), channel_id=1, source_target_pairs={{0,5},{1,4},{2,7},{3,6},{4,1},{5,0},{6,3},{7,2},{8,13},{9,12},{10,... | collective-permute-start | bytes 614408 | tf_op jit(solution)/shard_map/ppermute | solution.py:585
  10.0 27.7 %collective-permute-start.4 = (f32[400,128]{1,0:T(8,128)}, f32[400,128]{1,0:T(8,128)}, u32[]{:S(2)}, u32[]{:S(2)}) collective-permute-start(f32[400,128]{1,0:T(8,128)} %get-tuple-element.58), channel_id=1, source_target_pairs={{0,6},{1,7},{2,0},{3,1},{4,2},{5,3},{6,4},{7,5},{8,14},{9,15},{10,... | collective-permute-start | bytes 614408 | tf_op jit(solution)/shard_map/ppermute | solution.py:585
  13.1 30.0 %collective-permute-start.5 = (f32[400,128]{1,0:T(8,128)}, f32[400,128]{1,0:T(8,128)}, u32[]{:S(2)}, u32[]{:S(2)}) collective-permute-start(f32[400,128]{1,0:T(8,128)} %get-tuple-element.59), channel_id=1, source_target_pairs={{0,7},{1,6},{2,1},{3,0},{4,3},{5,2},{6,5},{7,4},{8,15},{9,14},{10,... | collective-permute-start | bytes 614408 | tf_op jit(solution)/shard_map/ppermute | solution.py:585
  13.8 29.2 %collective-permute-start.6 = (f32[400,128]{1,0:T(8,128)}, f32[400,128]{1,0:T(8,128)}, u32[]{:S(2)}, u32[]{:S(2)}) collective-permute-start(f32[400,128]{1,0:T(8,128)} %get-tuple-element.60), channel_id=1, source_target_pairs={{0,1},{1,0},{2,3},{3,2},{4,5},{5,4},{6,7},{7,6},{8,9},{9,8},{10,11... | collective-permute-start | bytes 614408 | tf_op jit(solution)/shard_map/ppermute | solution.py:585
  27.3 17.0 %collective-permute-start = (f32[400,128]{1,0:T(8,128)S(1)}, f32[400,128]{1,0:T(8,128)S(1)}, u32[]{:S(2)}, u32[]{:S(2)}) collective-permute-start(f32[400,128]{1,0:T(8,128)S(1)} %copy-done.50), channel_id=1, source_target_pairs={{0,2},{1,3},{2,4},{3,5},{4,6},{5,7},{6,0},{7,1},{8,10},{9,11},{10,... | collective-permute-start | bytes 614408 | tf_op jit(solution)/shard_map/ppermute | solution.py:585
  33.7 11.9 %collective-permute-start.1 = (f32[400,128]{1,0:T(8,128)S(1)}, f32[400,128]{1,0:T(8,128)S(1)}, u32[]{:S(2)}, u32[]{:S(2)}) collective-permute-start(f32[400,128]{1,0:T(8,128)S(1)} %copy-done.48), channel_id=1, source_target_pairs={{0,3},{1,2},{2,5},{3,4},{4,7},{5,6},{6,1},{7,0},{8,11},{9,10},{10,... | collective-permute-start | bytes 614408 | tf_op jit(solution)/shard_map/ppermute | solution.py:585
  37.7 18.3 %collective-permute-start.10 = (f32[400,128]{1,0:T(8,128)S(1)}, f32[400,128]{1,0:T(8,128)S(1)}, u32[]{:S(2)}, u32[]{:S(2)}) collective-permute-start(f32[400,128]{1,0:T(8,128)S(1)} %get-tuple-element.67), channel_id=1, source_target_pairs={{0,29},{1,28},{2,31},{3,30},{4,25},{5,24},{6,27},{7,26},{8,5},{9,4... | collective-permute-start | bytes 614408 | tf_op jit(solution)/shard_map/ppermute | solution.py:594
  43.0 23.1 %collective-permute-start.11 = (f32[400,128]{1,0:T(8,128)S(1)}, f32[400,128]{1,0:T(8,128)S(1)}, u32[]{:S(2)}, u32[]{:S(2)}) collective-permute-start(f32[400,128]{1,0:T(8,128)S(1)} %get-tuple-element.68), channel_id=1, source_target_pairs={{0,30},{1,31},{2,24},{3,25},{4,26},{5,27},{6,28},{7,29},{8,6},{9,7... | collective-permute-start | bytes 614408 | tf_op jit(solution)/shard_map/ppermute | solution.py:594
  43.0 23.1 %collective-permute-start.12 = (f32[400,128]{1,0:T(8,128)S(1)}, f32[400,128]{1,0:T(8,128)S(1)}, u32[]{:S(2)}, u32[]{:S(2)}) collective-permute-start(f32[400,128]{1,0:T(8,128)S(1)} %get-tuple-element.69), channel_id=1, source_target_pairs={{0,31},{1,30},{2,25},{3,24},{4,27},{5,26},{6,29},{7,28},{8,7},{9,6... | collective-permute-start | bytes 614408 | tf_op jit(solution)/shard_map/ppermute | solution.py:594
  44.3 33.7 %collective-permute-start.13 = (f32[400,128]{1,0:T(8,128)S(1)}, f32[400,128]{1,0:T(8,128)S(1)}, u32[]{:S(2)}, u32[]{:S(2)}) collective-permute-start(f32[400,128]{1,0:T(8,128)S(1)} %get-tuple-element.70), channel_id=1, source_target_pairs={{0,25},{1,24},{2,27},{3,26},{4,29},{5,28},{6,31},{7,30},{8,1},{9,0... | collective-permute-start | bytes 614408 | tf_op jit(solution)/shard_map/ppermute | solution.py:594
  45.7 32.3 %collective-permute-start.14 = (f32[400,128]{1,0:T(8,128)S(1)}, f32[400,128]{1,0:T(8,128)S(1)}, u32[]{:S(2)}, u32[]{:S(2)}) collective-permute-start(f32[400,128]{1,0:T(8,128)S(1)} %get-tuple-element.71), channel_id=1, source_target_pairs={{0,24},{1,25},{2,26},{3,27},{4,28},{5,29},{6,30},{7,31},{8,0},{9,1... | collective-permute-start | bytes 614408 | tf_op jit(solution)/shard_map/ppermute | solution.py:594
  56.0 22.0 %collective-permute-start.7 = (f32[400,128]{1,0:T(8,128)S(1)}, f32[400,128]{1,0:T(8,128)S(1)}, u32[]{:S(2)}, u32[]{:S(2)}) collective-permute-start(f32[400,128]{1,0:T(8,128)S(1)} %get-tuple-element.64), channel_id=1, source_target_pairs={{0,26},{1,27},{2,28},{3,29},{4,30},{5,31},{6,24},{7,25},{8,2},{9,3... | collective-permute-start | bytes 614408 | tf_op jit(solution)/shard_map/ppermute | solution.py:594
  66.2 11.9 %collective-permute-start.8 = (f32[400,128]{1,0:T(8,128)S(1)}, f32[400,128]{1,0:T(8,128)S(1)}, u32[]{:S(2)}, u32[]{:S(2)}) collective-permute-start(f32[400,128]{1,0:T(8,128)S(1)} %get-tuple-element.65), channel_id=1, source_target_pairs={{0,27},{1,26},{2,29},{3,28},{4,31},{5,30},{6,25},{7,24},{8,3},{9,2... | collective-permute-start | bytes 614408 | tf_op jit(solution)/shard_map/ppermute | solution.py:594
  66.2 21.2 %collective-permute-start.9 = (f32[400,128]{1,0:T(8,128)S(1)}, f32[400,128]{1,0:T(8,128)S(1)}, u32[]{:S(2)}, u32[]{:S(2)}) collective-permute-start(f32[400,128]{1,0:T(8,128)S(1)} %get-tuple-element.66), channel_id=1, source_target_pairs={{0,28},{1,29},{2,30},{3,31},{4,24},{5,25},{6,26},{7,27},{8,4},{9,5... | collective-permute-start | bytes 614408 | tf_op jit(solution)/shard_map/ppermute | solution.py:594
  104.7 5.6 %collective-permute-start.31 = (f32[200,384]{1,0:T(8,128)S(1)}, f32[200,384]{1,0:T(8,128)S(1)}, u32[]{:S(2)}, u32[]{:S(2)}) collective-permute-start(f32[200,384]{1,0:T(8,128)S(1)} %get-tuple-element.95), channel_id=1, source_target_pairs={{0,1},{1,0},{2,3},{3,2},{4,5},{5,4},{6,7},{7,6},{8,9},{9,8},{10,11... | collective-permute-start | bytes 921608 | tf_op jit(solution)/shard_map/ppermute | solution.py:585
  104.8 10.7 %collective-permute-start.30 = (f32[200,384]{1,0:T(8,128)}, f32[200,384]{1,0:T(8,128)}, u32[]{:S(2)}, u32[]{:S(2)}) collective-permute-start(f32[200,384]{1,0:T(8,128)} %get-tuple-element.93), channel_id=1, source_target_pairs={{0,1},{1,0},{2,3},{3,2},{4,5},{5,4},{6,7},{7,6},{8,9},{9,8},{10,11... | collective-permute-start | bytes 921608 | tf_op jit(solution)/shard_map/ppermute | solution.py:585
  106.5 11.4 %collective-permute-start.36 = (f32[200,384]{1,0:T(8,128)}, f32[200,384]{1,0:T(8,128)}, u32[]{:S(2)}, u32[]{:S(2)}) collective-permute-start(f32[200,384]{1,0:T(8,128)} %add.252), channel_id=1, source_target_pairs={{0,24},{8,16},{16,8},{24,0},{1,25},{9,17},{17,9},{25,1},{2,26},{10... | collective-permute-start | bytes 921608 | tf_op jit(solution)/shard_map/ppermute | solution.py:598
  108.7 14.9 %collective-permute-start.34 = (f32[200,384]{1,0:T(8,128)}, f32[200,384]{1,0:T(8,128)}, u32[]{:S(2)}, u32[]{:S(2)}) collective-permute-start(f32[200,384]{1,0:T(8,128)} %add.251), channel_id=1, source_target_pairs={{0,16},{8,24},{16,0},{24,8},{1,17},{9,25},{17,1},{25,9},{2,18},{10... | collective-permute-start | bytes 921608 | tf_op jit(solution)/shard_map/ppermute | solution.py:598
  111.0 12.7 %collective-permute-start.32 = (f32[200,384]{1,0:T(8,128)}, f32[200,384]{1,0:T(8,128)S(1)}, u32[]{:S(2)}, u32[]{:S(2)}) collective-permute-start(f32[200,384]{1,0:T(8,128)} %add.250), channel_id=1, source_target_pairs={{0,8},{8,0},{16,24},{24,16},{1,9},{9,1},{17,25},{25,17},{2,10},{10... | collective-permute-start | bytes 921608 | tf_op jit(solution)/shard_map/ppermute | solution.py:598
  115.3 15.3 %collective-permute-start.25 = (f32[400,128]{1,0:T(8,128)S(1)}, f32[400,128]{1,0:T(8,128)S(1)}, u32[]{:S(2)}, u32[]{:S(2)}) collective-permute-start(f32[400,128]{1,0:T(8,128)S(1)} %get-tuple-element.86), channel_id=1, source_target_pairs={{0,4},{1,5},{2,6},{3,7},{4,0},{5,1},{6,2},{7,3},{8,12},{9,13},{10,... | collective-permute-start | bytes 614408 | tf_op jit(solution)/shard_map/ppermute | solution.py:585
  115.4 30.0 %collective-permute-start.26 = (f32[400,128]{1,0:T(8,128)S(1)}, f32[400,128]{1,0:T(8,128)S(1)}, u32[]{:S(2)}, u32[]{:S(2)}) collective-permute-start(f32[400,128]{1,0:T(8,128)S(1)} %get-tuple-element.87), channel_id=1, source_target_pairs={{0,5},{1,4},{2,7},{3,6},{4,1},{5,0},{6,3},{7,2},{8,13},{9,12},{10,... | collective-permute-start | bytes 614408 | tf_op jit(solution)/shard_map/ppermute | solution.py:585
  124.8 20.7 %collective-permute-start.37 = (f32[56,384]{1,0:T(8,128)S(1)}, f32[56,384]{1,0:T(8,128)S(1)}, u32[]{:S(2)}, u32[]{:S(2)}) collective-permute-start(f32[56,384]{1,0:T(8,128)S(1)} %get-tuple-element.101), channel_id=1, source_target_pairs={{0,2},{1,3},{2,4},{3,5},{4,6},{5,7},{6,0},{7,1},{8,10},{9,11},{10,... | collective-permute-start | bytes 258056 | tf_op jit(solution)/shard_map/ppermute | solution.py:585
  124.9 22.5 %collective-permute-start.38 = (f32[56,384]{1,0:T(8,128)S(1)}, f32[56,384]{1,0:T(8,128)S(1)}, u32[]{:S(2)}, u32[]{:S(2)}) collective-permute-start(f32[56,384]{1,0:T(8,128)S(1)} %get-tuple-element.102), channel_id=1, source_target_pairs={{0,4},{1,5},{2,6},{3,7},{4,0},{5,1},{6,2},{7,3},{8,12},{9,13},{10,... | collective-permute-start | bytes 258056 | tf_op jit(solution)/shard_map/ppermute | solution.py:585
  125.4 30.0 %collective-permute-start.27 = (f32[400,128]{1,0:T(8,128)S(1)}, f32[400,128]{1,0:T(8,128)S(1)}, u32[]{:S(2)}, u32[]{:S(2)}) collective-permute-start(f32[400,128]{1,0:T(8,128)S(1)} %get-tuple-element.88), channel_id=1, source_target_pairs={{0,2},{1,3},{2,4},{3,5},{4,6},{5,7},{6,0},{7,1},{8,10},{9,11},{10,... | collective-permute-start | bytes 614408 | tf_op jit(solution)/shard_map/ppermute | solution.py:585
  130.6 27.8 %collective-permute-start.28 = (f32[400,128]{1,0:T(8,128)S(1)}, f32[400,128]{1,0:T(8,128)S(1)}, u32[]{:S(2)}, u32[]{:S(2)}) collective-permute-start(f32[400,128]{1,0:T(8,128)S(1)} %get-tuple-element.89), channel_id=1, source_target_pairs={{0,3},{1,2},{2,5},{3,4},{4,7},{5,6},{6,1},{7,0},{8,11},{9,10},{10,... | collective-permute-start | bytes 614408 | tf_op jit(solution)/shard_map/ppermute | solution.py:585
  145.4 13.0 %collective-permute-start.29 = (f32[400,128]{1,0:T(8,128)S(1)}, f32[400,128]{1,0:T(8,128)S(1)}, u32[]{:S(2)}, u32[]{:S(2)}) collective-permute-start(f32[400,128]{1,0:T(8,128)S(1)} %get-tuple-element.90), channel_id=1, source_target_pairs={{0,1},{1,0},{2,3},{3,2},{4,5},{5,4},{6,7},{7,6},{8,9},{9,8},{10,11... | collective-permute-start | bytes 614408 | tf_op jit(solution)/shard_map/ppermute | solution.py:585
  145.5 14.6 %collective-permute-start.23 = (f32[400,128]{1,0:T(8,128)S(1)}, f32[400,128]{1,0:T(8,128)S(1)}, u32[]{:S(2)}, u32[]{:S(2)}) collective-permute-start(f32[400,128]{1,0:T(8,128)S(1)} %get-tuple-element.84), channel_id=1, source_target_pairs={{0,6},{1,7},{2,0},{3,1},{4,2},{5,3},{6,4},{7,5},{8,14},{9,15},{10,... | collective-permute-start | bytes 614408 | tf_op jit(solution)/shard_map/ppermute | solution.py:585
  147.4 7.3 %collective-permute-start.39 = (f32[56,384]{1,0:T(8,128)S(1)}, f32[56,384]{1,0:T(8,128)S(1)}, u32[]{:S(2)}, u32[]{:S(2)}) collective-permute-start(f32[56,384]{1,0:T(8,128)S(1)} %get-tuple-element.103), channel_id=1, source_target_pairs={{0,6},{1,7},{2,0},{3,1},{4,2},{5,3},{6,4},{7,5},{8,14},{9,15},{10,... | collective-permute-start | bytes 258056 | tf_op jit(solution)/shard_map/ppermute | solution.py:585
  154.7 29.9 %collective-permute-start.17 = (f32[400,128]{1,0:T(8,128)S(1)}, f32[400,128]{1,0:T(8,128)S(1)}, u32[]{:S(2)}, u32[]{:S(2)}) collective-permute-start(f32[400,128]{1,0:T(8,128)S(1)} %get-tuple-element.75), channel_id=1, source_target_pairs={{0,12},{1,13},{2,14},{3,15},{4,8},{5,9},{6,10},{7,11},{8,20},{9,21... | collective-permute-start | bytes 614408 | tf_op jit(solution)/shard_map/ppermute | solution.py:594
  155.4 29.8 %collective-permute-start.40 = (f32[56,384]{1,0:T(8,128)S(1)}, f32[56,384]{1,0:T(8,128)S(1)}, u32[]{:S(2)}, u32[]{:S(2)}) collective-permute-start(f32[56,384]{1,0:T(8,128)S(1)} %shard_map.147.refs_0_), channel_id=1, source_target_pairs={{0,2},{1,3},{2,4},{3,5},{4,6},{5,7},{6,0},{7,1},{8,10},{9,11},{10,... | collective-permute-start | bytes 258056 | tf_op jit(solution)/shard_map/ppermute | solution.py:585
  158.4 35.5 %collective-permute-start.18 = (f32[400,128]{1,0:T(8,128)S(1)}, f32[400,128]{1,0:T(8,128)S(1)}, u32[]{:S(2)}, u32[]{:S(2)}) collective-permute-start(f32[400,128]{1,0:T(8,128)S(1)} %get-tuple-element.76), channel_id=1, source_target_pairs={{0,13},{1,12},{2,15},{3,14},{4,9},{5,8},{6,11},{7,10},{8,21},{9,20... | collective-permute-start | bytes 614408 | tf_op jit(solution)/shard_map/ppermute | solution.py:594
  159.1 36.3 %collective-permute-start.19 = (f32[400,128]{1,0:T(8,128)S(1)}, f32[400,128]{1,0:T(8,128)S(1)}, u32[]{:S(2)}, u32[]{:S(2)}) collective-permute-start(f32[400,128]{1,0:T(8,128)S(1)} %get-tuple-element.77), channel_id=1, source_target_pairs={{0,10},{1,11},{2,12},{3,13},{4,14},{5,15},{6,8},{7,9},{8,18},{9,19... | collective-permute-start | bytes 614408 | tf_op jit(solution)/shard_map/ppermute | solution.py:594
  160.9 35.1 %collective-permute-start.20 = (f32[400,128]{1,0:T(8,128)S(1)}, f32[400,128]{1,0:T(8,128)S(1)}, u32[]{:S(2)}, u32[]{:S(2)}) collective-permute-start(f32[400,128]{1,0:T(8,128)S(1)} %get-tuple-element.78), channel_id=1, source_target_pairs={{0,11},{1,10},{2,13},{3,12},{4,15},{5,14},{6,9},{7,8},{8,19},{9,18... | collective-permute-start | bytes 614408 | tf_op jit(solution)/shard_map/ppermute | solution.py:594
  185.3 6.2 %collective-permute-start.41 = (f32[56,384]{1,0:T(8,128)S(1)}, f32[56,384]{1,0:T(8,128)S(1)}, u32[]{:S(2)}, u32[]{:S(2)}) collective-permute-start(f32[56,384]{1,0:T(8,128)S(1)} %shard_map.147.refs_0_), channel_id=1, source_target_pairs={{0,4},{1,5},{2,6},{3,7},{4,0},{5,1},{6,2},{7,3},{8,12},{9,13},{10,... | collective-permute-start | bytes 258056 | tf_op jit(solution)/shard_map/ppermute | solution.py:585
  185.3 6.4 %collective-permute-start.42 = (f32[56,384]{1,0:T(8,128)S(1)}, f32[56,384]{1,0:T(8,128)S(1)}, u32[]{:S(2)}, u32[]{:S(2)}) collective-permute-start(f32[56,384]{1,0:T(8,128)S(1)} %shard_map.147.refs_0_), channel_id=1, source_target_pairs={{0,6},{1,7},{2,0},{3,1},{4,2},{5,3},{6,4},{7,5},{8,14},{9,15},{10,... | collective-permute-start | bytes 258056 | tf_op jit(solution)/shard_map/ppermute | solution.py:585
  191.5 8.4 %collective-permute-start.21 = (f32[400,128]{1,0:T(8,128)S(1)}, f32[400,128]{1,0:T(8,128)S(1)}, u32[]{:S(2)}, u32[]{:S(2)}) collective-permute-start(f32[400,128]{1,0:T(8,128)S(1)} %get-tuple-element.79), channel_id=1, source_target_pairs={{0,9},{1,8},{2,11},{3,10},{4,13},{5,12},{6,15},{7,14},{8,17},{9,16... | collective-permute-start | bytes 614408 | tf_op jit(solution)/shard_map/ppermute | solution.py:594
  191.7 11.0 %collective-permute-start.22 = (f32[400,128]{1,0:T(8,128)S(1)}, f32[400,128]{1,0:T(8,128)S(1)}, u32[]{:S(2)}, u32[]{:S(2)}) collective-permute-start(f32[400,128]{1,0:T(8,128)S(1)} %get-tuple-element.80), channel_id=1, source_target_pairs={{0,8},{1,9},{2,10},{3,11},{4,12},{5,13},{6,14},{7,15},{8,16},{9,17... | collective-permute-start | bytes 614408 | tf_op jit(solution)/shard_map/ppermute | solution.py:594
  193.9 22.7 %collective-permute-start.43 = (f32[200,384]{1,0:T(8,128)S(1)}, f32[200,384]{1,0:T(8,128)}, u32[]{:S(2)}, u32[]{:S(2)}) collective-permute-start(f32[200,384]{1,0:T(8,128)S(1)} %shard_map.148.refs_0_), channel_id=1, source_target_pairs={{0,8},{8,0},{16,24},{24,16},{1,9},{9,1},{17,25},{25,17},{2,10},{10... | collective-permute-start | bytes 921608 | tf_op jit(solution)/shard_map/ppermute | solution.py:598
  195.4 24.4 %collective-permute-start.44 = (f32[200,384]{1,0:T(8,128)S(1)}, f32[200,384]{1,0:T(8,128)}, u32[]{:S(2)}, u32[]{:S(2)}) collective-permute-start(f32[200,384]{1,0:T(8,128)S(1)} %shard_map.148.refs_0_), channel_id=1, source_target_pairs={{0,16},{8,24},{16,0},{24,8},{1,17},{9,25},{17,1},{25,9},{2,18},{10... | collective-permute-start | bytes 921608 | tf_op jit(solution)/shard_map/ppermute | solution.py:598
  195.9 28.8 %collective-permute-start.45 = (f32[200,384]{1,0:T(8,128)S(1)}, f32[200,384]{1,0:T(8,128)}, u32[]{:S(2)}, u32[]{:S(2)}) collective-permute-start(f32[200,384]{1,0:T(8,128)S(1)} %shard_map.148.refs_0_), channel_id=1, source_target_pairs={{0,24},{8,16},{16,8},{24,0},{1,25},{9,17},{17,9},{25,1},{2,26},{10... | collective-permute-start | bytes 921608 | tf_op jit(solution)/shard_map/ppermute | solution.py:598
  200.5 7.6 %collective-permute-start.15 = (f32[400,128]{1,0:T(8,128)S(1)}, f32[400,128]{1,0:T(8,128)S(1)}, u32[]{:S(2)}, u32[]{:S(2)}) collective-permute-start(f32[400,128]{1,0:T(8,128)S(1)} %get-tuple-element.73), channel_id=1, source_target_pairs={{0,14},{1,15},{2,8},{3,9},{4,10},{5,11},{6,12},{7,13},{8,22},{9,23... | collective-permute-start | bytes 614408 | tf_op jit(solution)/shard_map/ppermute | solution.py:594
  203.4 21.9 %collective-permute-start.16 = (f32[400,128]{1,0:T(8,128)S(1)}, f32[400,128]{1,0:T(8,128)S(1)}, u32[]{:S(2)}, u32[]{:S(2)}) collective-permute-start(f32[400,128]{1,0:T(8,128)S(1)} %get-tuple-element.74), channel_id=1, source_target_pairs={{0,15},{1,14},{2,9},{3,8},{4,11},{5,10},{6,13},{7,12},{8,23},{9,22... | collective-permute-start | bytes 614408 | tf_op jit(solution)/shard_map/ppermute | solution.py:594
  208.8 37.5 %collective-permute-start.46 = (f32[200,384]{1,0:T(8,128)S(1)}, f32[200,384]{1,0:T(8,128)}, u32[]{:S(2)}, u32[]{:S(2)}) collective-permute-start(f32[200,384]{1,0:T(8,128)S(1)} %shard_map.148.refs_0_), channel_id=1, source_target_pairs={{0,1},{1,0},{2,3},{3,2},{4,5},{5,4},{6,7},{7,6},{8,9},{9,8},{10,11... | collective-permute-start | bytes 921608 | tf_op jit(solution)/shard_map/ppermute | solution.py:585
  216.5 29.8 %collective-permute-start.47 = (f32[200,384]{1,0:T(8,128)}, f32[200,384]{1,0:T(8,128)}, u32[]{:S(2)}, u32[]{:S(2)}) collective-permute-start(f32[200,384]{1,0:T(8,128)} %collective-permute-done.43.refs_1_), channel_id=1, source_target_pairs={{0,1},{1,0},{2,3},{3,2},{4,5},{5,4},{6,7},{7,6},{8,9},{9,8},{10,11... | collective-permute-start | bytes 921608 | tf_op jit(solution)/shard_map/ppermute | solution.py:585
  219.9 26.5 %collective-permute-start.48 = (f32[200,384]{1,0:T(8,128)}, f32[200,384]{1,0:T(8,128)}, u32[]{:S(2)}, u32[]{:S(2)}) collective-permute-start(f32[200,384]{1,0:T(8,128)} %collective-permute-done.44.refs_2_), channel_id=1, source_target_pairs={{0,1},{1,0},{2,3},{3,2},{4,5},{5,4},{6,7},{7,6},{8,9},{9,8},{10,11... | collective-permute-start | bytes 921608 | tf_op jit(solution)/shard_map/ppermute | solution.py:585
  224.7 21.7 %collective-permute-start.49 = (f32[200,384]{1,0:T(8,128)}, f32[200,384]{1,0:T(8,128)}, u32[]{:S(2)}, u32[]{:S(2)}) collective-permute-start(f32[200,384]{1,0:T(8,128)} %collective-permute-done.45.refs_3_), channel_id=1, source_target_pairs={{0,1},{1,0},{2,3},{3,2},{4,5},{5,4},{6,7},{7,6},{8,9},{9,8},{10,11... | collective-permute-start | bytes 921608 | tf_op jit(solution)/shard_map/ppermute | solution.py:585
  226.0 11.4 %collective-permute-start.24 = (f32[400,128]{1,0:T(8,128)}, f32[400,128]{1,0:T(8,128)}, u32[]{:S(2)}, u32[]{:S(2)}) collective-permute-start(f32[400,128]{1,0:T(8,128)} %get-tuple-element.85), channel_id=1, source_target_pairs={{0,7},{1,6},{2,1},{3,0},{4,3},{5,2},{6,5},{7,4},{8,15},{9,14},{10,... | collective-permute-start | bytes 614408 | tf_op jit(solution)/shard_map/ppermute | solution.py:585
  (59 other events, 490.1 us)

commit v4 on v3

--- a/solution.py
+++ b/solution.py
@@ -20,7 +20,7 @@
 F32, BF16, I32 = jnp.float32, jnp.bfloat16, jnp.int32
 VMEM = pl.BlockSpec(memory_space=pltpu.VMEM)
 SMEM = pl.BlockSpec(memory_space=pltpu.SMEM)
-VMEM_LIMIT = 32 << 20
+VMEM_LIMIT = 24 << 20
 
 
 def kernel_call(kernel, outs, flops, moved, **kw):
@@ -636,6 +636,7 @@
         return places_of(me, slots // block, peers) * block + slots % block
 
     edge_source, edge_target = placed(edge_source), placed(edge_target)
+    early = peers // 2
     sources = pick_blocks(order[:2], entity_t, src_send[0])
     sources += pick_blocks(order[2:], entity_t, src_send[0])
     sources = [
@@ -652,16 +653,16 @@
     loss, grad, table = score_spans(
         edge_count, targets, query_lines, counts, edge_target.reshape(-1, 1)
     )
-    table_parts = table_grads(query_columns, grad, block, 0, 2)
-    table_parts += table_grads(query_columns, grad, block, 2, peers - 2)
+    table_parts = table_grads(query_columns, grad, block, 0, early)
+    table_parts += table_grads(query_columns, grad, block, early, peers - early)
     back = [(-hop[0], hop[1]) for hop in ways]
     home = [
         sent_across(value, hop, peers, groups, 1)
-        for value, hop in zip(table_parts[:2], back[:2])
+        for value, hop in zip(table_parts[:early], back[:early])
     ]
     home += [
         sent_across(value, hop, peers, groups, 1)
-        for value, hop in zip(table_parts[2:], back[2:])
+        for value, hop in zip(table_parts[early:], back[early:])
     ]
     source_lines, *halves = relation_grads(
         here, table, grad, heads, rels, edge_relation.reshape(-1, 1), groups, width

time: 251 us -> 233 us (0.928)
  waiting for transfers between devices: 87.7 us -> 69.6 us
    ppermute x6, waiting for transfers between devices: 15.1 us -> 4.3 us  [sent_group(): return lax.ppermute(value, 'group', [(g, g ^ bit) for g in range(groups)])]
    ppermute x28, waiting for transfers between devices: 28 us -> 19.9 us  [sent_on(): lax.ppermute(value, 'shard', [(i, partner(i, hop, peers, 1)) for i in ran...]
    ppermute x16, starting transfers between devices: 33.2 us -> 37.1 us  [sent_across(): return lax.ppermute(value, ('group', 'shard'), pairs)]
    ppermute x28, starting transfers between devices: 35.4 us -> 32.5 us  [sent_on(): lax.ppermute(value, 'shard', [(i, partner(i, hop, peers, 1)) for i in ran...]
    unnamed x114 -> x122, local copies, waits for them, and re-layouts: 23.4 us -> 22.1 us
  transfers between devices with their start and end apart: 50 -> 50, of which waited for: 15 -> 13; matrix products, arithmetic and copies ran while one was open for 3% -> 4% of each run, Pallas kernels for 13% -> 13%
where the time goes in v4:
time: 233 us; the launch traced here: 232 us
  starting transfers between devices  75.3 us (32%)
  waiting for transfers between devices  69.6 us (30%)
  Pallas kernels  54.3 us (23%)
  local copies, waits for them, and re-layouts  25.4 us (11%)
  other arithmetic  5.33 us (2%)
    ppermute x16, waiting for transfers between devices, sent_across(): return lax.ppermute(value, ('group', 'shard'), pairs)  45.5 us
    ppermute x16, starting transfers between devices, sent_across(): return lax.ppermute(value, ('group', 'shard'), pairs)  37.1 us
    ppermute x28, starting transfers between devices, sent_on(): lax.ppermute(value, 'shard', [(i, partner(i, hop, peers, 1)) for i in ran...  32.5 us
    unnamed x122, local copies, waits for them, and re-layouts  22.1 us
    ppermute x28, waiting for transfers between devices, sent_on(): lax.ppermute(value, 'shard', [(i, partner(i, hop, peers, 1)) for i in ran...  19.9 us
    pallas_call x1, Pallas kernels, relation_grads(): kernel_call(functools.partial(relation_grad_kernel, steps), [shape((2, fe...  10.2 us
    pallas_call x1, Pallas kernels, query_rows(): kernel_call(query_kernel, [shape((features, edges)), shape((2, features,...  7.26 us
    pallas_call x1, Pallas kernels, score_spans(): kernel_call(functools.partial(score_kernel, peers), [shape((edges, 1)), s...  6.87 us
  transfers between devices with their start and end apart: 50, of which 13 were waited for; matrix products, arithmetic and copies ran while one was open for 4% of the time, Pallas kernels for 13%

profile of v4, /device:TPU:0, one launch (start us, length us, event | category | flops | bytes accessed | tf_op | source)
XLA Modules:
  0.0 232.0 jit_solution(12445072378409647443)
XLA Ops:
  0.8 1.1 copy-done.6
  2.7 2.6 %shard_map.133 = (f32[400,128]{1,0:T(8,128)}, f32[400,128]{1,0:T(8,128)}, f32[400,128]{1,0:T(8,128)}, f32[400,128]{1,0:T(8,128)}, f32[400,128]{1,0:T(8,128)}, /*index=5*/f32[400,128]{1,0:T(8,128)S(1)}) custom-call(s32[6]{0:T(128)S(1)} %stack.50.order_ref, f32[400,512]{1,0:T(8,128)S(1)} %bitcast.28, s32[8,128]{1,0:T(8,128)S(1)} %bitcast.38), custom_call_target="tpu_custom_call" | custom-call | flops 943718400 | bytes 2457600 | tf_op jit(solution)/shard_map/pallas_call | solution.py:126
  5.9 4.1 %collective-permute-start.2 = (f32[400,128]{1,0:T(8,128)}, f32[400,128]{1,0:T(8,128)}, u32[]{:S(2)}, u32[]{:S(2)}) collective-permute-start(f32[400,128]{1,0:T(8,128)} %get-tuple-element.56), channel_id=1, source_target_pairs={{0,4},{1,5},{2,6},{3,7},{4,0},{5,1},{6,2},{7,3},{8,12},{9,13},{10,... | collective-permute-start | bytes 614408 | tf_op jit(solution)/shard_map/ppermute | solution.py:585
  10.0 3.1 %collective-permute-start.4 = (f32[400,128]{1,0:T(8,128)}, f32[400,128]{1,0:T(8,128)}, u32[]{:S(2)}, u32[]{:S(2)}) collective-permute-start(f32[400,128]{1,0:T(8,128)} %get-tuple-element.58), channel_id=1, source_target_pairs={{0,6},{1,7},{2,0},{3,1},{4,2},{5,3},{6,4},{7,5},{8,14},{9,15},{10,... | collective-permute-start | bytes 614408 | tf_op jit(solution)/shard_map/ppermute | solution.py:585
  20.7 5.2 %shard_map.131.refs_1_.rels_ref = f32[400,1024]{1,0:T(8,128)S(1)} custom-call(f32[400,1345]{1,0:T(8,128)S(1)} %bitcast.26, s32[1,1024]{1,0:T(1,128)S(1)} %bitcast.35), custom_call_target="tpu_custom_call" | custom-call | flops 3460300800 | bytes 3276800 | tf_op jit(solution)/shard_map/pallas_call | solution.py:153
  26.0 2.0 shard_map.136
  28.1 5.7 %collective-permute-start = (f32[400,128]{1,0:T(8,128)S(1)}, f32[400,128]{1,0:T(8,128)S(1)}, u32[]{:S(2)}, u32[]{:S(2)}) collective-permute-start(f32[400,128]{1,0:T(8,128)S(1)} %copy-done.54), channel_id=1, source_target_pairs={{0,2},{1,3},{2,4},{3,5},{4,6},{5,7},{6,0},{7,1},{8,10},{9,11},{10,... | collective-permute-start | bytes 614408 | tf_op jit(solution)/shard_map/ppermute | solution.py:585
  33.8 3.9 %collective-permute-start.1 = (f32[400,128]{1,0:T(8,128)S(1)}, f32[400,128]{1,0:T(8,128)S(1)}, u32[]{:S(2)}, u32[]{:S(2)}) collective-permute-start(f32[400,128]{1,0:T(8,128)S(1)} %copy-done.52), channel_id=1, source_target_pairs={{0,3},{1,2},{2,5},{3,4},{4,7},{5,6},{6,1},{7,0},{8,11},{9,10},{10,... | collective-permute-start | bytes 614408 | tf_op jit(solution)/shard_map/ppermute | solution.py:585
  37.7 5.4 %collective-permute-start.10 = (f32[400,128]{1,0:T(8,128)S(1)}, f32[400,128]{1,0:T(8,128)S(1)}, u32[]{:S(2)}, u32[]{:S(2)}) collective-permute-start(f32[400,128]{1,0:T(8,128)S(1)} %get-tuple-element.67), channel_id=1, source_target_pairs={{0,29},{1,28},{2,31},{3,30},{4,25},{5,24},{6,27},{7,26},{8,5},{9,4... | collective-permute-start | bytes 614408 | tf_op jit(solution)/shard_map/ppermute | solution.py:594
  43.0 1.2 collective-permute-start.12
  44.3 1.4 collective-permute-start.13
  45.7 2.4 %collective-permute-start.14 = (f32[400,128]{1,0:T(8,128)S(1)}, f32[400,128]{1,0:T(8,128)S(1)}, u32[]{:S(2)}, u32[]{:S(2)}) collective-permute-start(f32[400,128]{1,0:T(8,128)S(1)} %get-tuple-element.71), channel_id=1, source_target_pairs={{0,24},{1,25},{2,26},{3,27},{4,28},{5,29},{6,30},{7,31},{8,0},{9,1... | collective-permute-start | bytes 614408 | tf_op jit(solution)/shard_map/ppermute | solution.py:594
  48.1 7.9 %collective-permute-done.10.refs_7_ = f32[400,128]{1,0:T(8,128)S(1)} collective-permute-done((f32[400,128]{1,0:T(8,128)S(1)}, f32[400,128]{1,0:T(8,128)S(1)}, u32[]{:S(2)}, u32[]{:S(2)}) %collective-permute-start.10) | collective-permute-done | bytes 204832 | tf_op jit(solution)/shard_map/ppermute | solution.py:594
  56.0 10.2 %collective-permute-start.7 = (f32[400,128]{1,0:T(8,128)S(1)}, f32[400,128]{1,0:T(8,128)S(1)}, u32[]{:S(2)}, u32[]{:S(2)}) collective-permute-start(f32[400,128]{1,0:T(8,128)S(1)} %get-tuple-element.64), channel_id=1, source_target_pairs={{0,26},{1,27},{2,28},{3,29},{4,30},{5,31},{6,24},{7,25},{8,2},{9,3... | collective-permute-start | bytes 614408 | tf_op jit(solution)/shard_map/ppermute | solution.py:594
  66.2 4.5 %collective-permute-start.9 = (f32[400,128]{1,0:T(8,128)S(1)}, f32[400,128]{1,0:T(8,128)S(1)}, u32[]{:S(2)}, u32[]{:S(2)}) collective-permute-start(f32[400,128]{1,0:T(8,128)S(1)} %get-tuple-element.66), channel_id=1, source_target_pairs={{0,28},{1,29},{2,30},{3,31},{4,24},{5,25},{6,26},{7,27},{8,4},{9,5... | collective-permute-start | bytes 614408 | tf_op jit(solution)/shard_map/ppermute | solution.py:594
  70.7 7.3 %shard_map.134 = (f32[400,1024]{1,0:T(8,128)S(1)}, bf16[2,400,1024]{2,1,0:T(8,128)(2,1)S(1)}, bf16[1024,1200]{1,0:T(8,128)(2,1)S(1)}) custom-call(s32[1,1024]{1,0:T(1,128)S(1)} %bitcast.32, f32[400,1024]{1,0:T(8,128)S(1)} %shard_map.131.refs_1_.rels_ref, f32[400,128]{1,0:T(8,128)S(1)} %collective-permute-done.refs_2_, ...), custom_call_target="tpu_custom_call" | custom-call | flops 2516582400 | bytes 8192000 | tf_op jit(solution)/shard_map/pallas_call | solution.py:221
  78.0 9.4 %collective-permute-done.9.refs_6_ = f32[400,128]{1,0:T(8,128)S(1)} collective-permute-done((f32[400,128]{1,0:T(8,128)S(1)}, f32[400,128]{1,0:T(8,128)S(1)}, u32[]{:S(2)}, u32[]{:S(2)}) %collective-permute-start.9) | collective-permute-done | bytes 204832 | tf_op jit(solution)/shard_map/ppermute | solution.py:594
  87.4 6.9 %shard_map.137 = (f32[1024,1]{1,0:T(8,128)S(1)}, bf16[2,1024,1024]{2,1,0:T(8,128)(2,1)S(1)}, bf16[1200,1024]{1,0:T(8,128)(2,1)S(1)}) custom-call(s32[1]{0:T(128)S(6)} %copy.21.refs_0_, bf16[1024,1200]{1,0:T(8,128)(2,1)S(1)} %get-tuple-element.63.refs_1_, f32[2,1,1024]{2,1,0:T(1,128)S(1)} %shard_map.135.refs_2_, s32[1024,1]{1,0:T(8,128)S(1)} %copy-done.11, ...), custom_call_target="tpu_custom_call" | custom-call | flops 2516582400 | bytes 12288000 | tf_op jit(solution)/shard_map/pallas_call | solution.py:311
  94.3 10.2 %shard_map.142 = (bf16[2,400,1024]{2,1,0:T(8,128)(2,1)S(1)}, f32[200,384]{1,0:T(8,128)S(1)}, f32[200,384]{1,0:T(8,128)S(1)}, f32[200,384]{1,0:T(8,128)S(1)}, f32...) custom-call(s32[2]{0:T(128)S(1)} %pad_add_fusion.1.me_ref, ...), custom_call_target="tpu_custom_call" | custom-call | flops 4194304000 | bytes 12288000 | tf_op jit(solution)/shard_map/pallas_call | solution.py:415
  104.5 1.2 copy-done.4
  110.2 1.5 collective-permute-start.36
  111.7 1.1 add.251
  112.8 1.6 collective-permute-start.34
  116.0 2.1 shard_map.144
  118.8 1.5 collective-permute-start.26
  120.3 1.4 shard_map.143
  122.8 4.3 %collective-permute-done.34.refs_2_ = f32[200,384]{1,0:T(8,128)S(1)} collective-permute-done((f32[200,384]{1,0:T(8,128)S(1)}, f32[200,384]{1,0:T(8,128)S(1)}, u32[]{:S(2)}, u32[]{:S(2)}) %collective-permute-start.34) | collective-permute-done | bytes 307232 | tf_op jit(solution)/shard_map/ppermute | solution.py:598
  128.3 11.8 %collective-permute-done.25.refs_2_ = f32[400,128]{1,0:T(8,128)S(1)} collective-permute-done((f32[400,128]{1,0:T(8,128)S(1)}, f32[400,128]{1,0:T(8,128)S(1)}, u32[]{:S(2)}, u32[]{:S(2)}) %collective-permute-start.25) | collective-permute-done | bytes 204832 | tf_op jit(solution)/shard_map/ppermute | solution.py:585
  140.2 2.0 shard_map.139
  142.2 2.3 collective-permute-done.26.refs_3_
  144.6 1.9 collective-permute-done.38.refs_2_
  146.4 5.8 %collective-permute-start.23 = (f32[400,128]{1,0:T(8,128)S(1)}, f32[400,128]{1,0:T(8,128)S(1)}, u32[]{:S(2)}, u32[]{:S(2)}) collective-permute-start(f32[400,128]{1,0:T(8,128)S(1)} %get-tuple-element.84), channel_id=1, source_target_pairs={{0,6},{1,7},{2,0},{3,1},{4,2},{5,3},{6,4},{7,5},{8,14},{9,15},{10,... | collective-permute-start | bytes 614408 | tf_op jit(solution)/shard_map/ppermute | solution.py:585
  154.2 4.3 %collective-permute-start.21 = (f32[400,128]{1,0:T(8,128)S(1)}, f32[400,128]{1,0:T(8,128)S(1)}, u32[]{:S(2)}, u32[]{:S(2)}) collective-permute-start(f32[400,128]{1,0:T(8,128)S(1)} %get-tuple-element.79), channel_id=1, source_target_pairs={{0,9},{1,8},{2,11},{3,10},{4,13},{5,12},{6,15},{7,14},{8,17},{9,16... | collective-permute-start | bytes 614408 | tf_op jit(solution)/shard_map/ppermute | solution.py:594
  158.6 1.5 collective-permute-start.22
  160.0 4.6 %collective-permute-done.19.refs_4_ = f32[400,128]{1,0:T(8,128)S(1)} collective-permute-done((f32[400,128]{1,0:T(8,128)S(1)}, f32[400,128]{1,0:T(8,128)S(1)}, u32[]{:S(2)}, u32[]{:S(2)}) %collective-permute-start.19) | collective-permute-done | bytes 204832 | tf_op jit(solution)/shard_map/ppermute | solution.py:594
  165.4 2.5 %collective-permute-start.42 = (f32[56,384]{1,0:T(8,128)S(1)}, f32[56,384]{1,0:T(8,128)S(1)}, u32[]{:S(2)}, u32[]{:S(2)}) collective-permute-start(f32[56,384]{1,0:T(8,128)S(1)} %shard_map.147.refs_0_), channel_id=1, source_target_pairs={{0,6},{1,7},{2,0},{3,1},{4,2},{5,3},{6,4},{7,5},{8,14},{9,15},{10,... | collective-permute-start | bytes 258056 | tf_op jit(solution)/shard_map/ppermute | solution.py:585
  167.9 2.0 shard_map.138
  169.9 2.7 %collective-permute-done.41.refs_2_ = f32[56,384]{1,0:T(8,128)S(1)} collective-permute-done((f32[56,384]{1,0:T(8,128)S(1)}, f32[56,384]{1,0:T(8,128)S(1)}, u32[]{:S(2)}, u32[]{:S(2)}) %collective-permute-start.41) | collective-permute-done | bytes 86048 | tf_op jit(solution)/shard_map/ppermute | solution.py:585
  172.6 4.1 %collective-permute-start.15 = (f32[400,128]{1,0:T(8,128)S(1)}, f32[400,128]{1,0:T(8,128)S(1)}, u32[]{:S(2)}, u32[]{:S(2)}) collective-permute-start(f32[400,128]{1,0:T(8,128)S(1)} %get-tuple-element.73), channel_id=1, source_target_pairs={{0,14},{1,15},{2,8},{3,9},{4,10},{5,11},{6,12},{7,13},{8,22},{9,23... | collective-permute-start | bytes 614408 | tf_op jit(solution)/shard_map/ppermute | solution.py:594
  178.0 1.6 collective-permute-start.43
  180.7 5.7 %collective-permute-done.22.refs_7_ = f32[400,128]{1,0:T(8,128)S(1)} collective-permute-done((f32[400,128]{1,0:T(8,128)S(1)}, f32[400,128]{1,0:T(8,128)S(1)}, u32[]{:S(2)}, u32[]{:S(2)}) %collective-permute-start.22) | collective-permute-done | bytes 204832 | tf_op jit(solution)/shard_map/ppermute | solution.py:594
  187.8 2.2 collective-permute-start.17
  190.7 15.4 %collective-permute-done.17.refs_2_ = f32[400,128]{1,0:T(8,128)S(1)} collective-permute-done((f32[400,128]{1,0:T(8,128)S(1)}, f32[400,128]{1,0:T(8,128)S(1)}, u32[]{:S(2)}, u32[]{:S(2)}) %collective-permute-start.17) | collective-permute-done | bytes 204832 | tf_op jit(solution)/shard_map/ppermute | solution.py:594
  207.8 2.5 %collective-permute-done.18.refs_3_ = f32[400,128]{1,0:T(8,128)S(1)} collective-permute-done((f32[400,128]{1,0:T(8,128)S(1)}, f32[400,128]{1,0:T(8,128)S(1)}, u32[]{:S(2)}, u32[]{:S(2)}) %collective-permute-start.18) | collective-permute-done | bytes 204832 | tf_op jit(solution)/shard_map/ppermute | solution.py:594
  211.0 1.5 collective-permute-start.24
  224.0 1.1 copy-done.9
  225.1 3.2 %shard_map.145 = f32[400,512]{1,0:T(8,128)} custom-call(f32[400,512]{1,0:T(8,128)S(1)} %shard_map.140.other_ref, f32[400,512]{1,0:T(8,128)S(1)} %bitcast.31, f32[1,512]{1,0:T(1,128)S(1)} %bitcast.41, bf16[1024,512]{1,0:T(8,128)(2,1)S(1)} %shard_map.141.hot_ref, f32[400,128]{1,0:T(8,128)S(1)} %copy-done.27, f32[400,128]{1,0:T(8,128)} %collective-permute-done.24.refs_1_, ...), custom_call_target="tpu_custom_call" | custom-call | flops 838860800 | bytes 3276800 | tf_op jit(solution)/shard_map/pallas_call | solution.py:491
  228.3 3.7 %shard_map.149 = f32[400,1345]{1,0:T(8,128)} custom-call(s32[2]{0:T(128)S(1)} %copy-done.50, f32[400,1345]{1,0:T(8,128)S(1)} %bitcast.27, f32[1,1345]{1,0:T(1,128)S(1)} %reshape.36.state_ref, f32[200,384]{1,0:T(8,128)S(1)} %shard_map.148.refs_0_, f32[200,384]{1,0:T(8,128)} %collective-permute-done.43.refs_1_, f32[200,384]{1,0:T(8,128)} %collective-permute-done.44.refs_2_, ...), custom_call_target="tpu_custom_call" | custom-call | flops 4304000 | bytes 6456000 | tf_op jit(solution)/shard_map/pallas_call | solution.py:576
  (215 shorter events, 38.9 us)
Async XLA Ops:
  5.9 22.1 %collective-permute-start.2 = (f32[400,128]{1,0:T(8,128)}, f32[400,128]{1,0:T(8,128)}, u32[]{:S(2)}, u32[]{:S(2)}) collective-permute-start(f32[400,128]{1,0:T(8,128)} %get-tuple-element.56), channel_id=1, source_target_pairs={{0,4},{1,5},{2,6},{3,7},{4,0},{5,1},{6,2},{7,3},{8,12},{9,13},{10,... | collective-permute-start | bytes 614408 | tf_op jit(solution)/shard_map/ppermute | solution.py:585
  10.0 23.8 %collective-permute-start.3 = (f32[400,128]{1,0:T(8,128)}, f32[400,128]{1,0:T(8,128)}, u32[]{:S(2)}, u32[]{:S(2)}) collective-permute-start(f32[400,128]{1,0:T(8,128)} %get-tuple-element.57), channel_id=1, source_target_pairs={{0,5},{1,4},{2,7},{3,6},{4,1},{5,0},{6,3},{7,2},{8,13},{9,12},{10,... | collective-permute-start | bytes 614408 | tf_op jit(solution)/shard_map/ppermute | solution.py:585
  10.0 27.7 %collective-permute-start.4 = (f32[400,128]{1,0:T(8,128)}, f32[400,128]{1,0:T(8,128)}, u32[]{:S(2)}, u32[]{:S(2)}) collective-permute-start(f32[400,128]{1,0:T(8,128)} %get-tuple-element.58), channel_id=1, source_target_pairs={{0,6},{1,7},{2,0},{3,1},{4,2},{5,3},{6,4},{7,5},{8,14},{9,15},{10,... | collective-permute-start | bytes 614408 | tf_op jit(solution)/shard_map/ppermute | solution.py:585
  13.1 30.0 %collective-permute-start.5 = (f32[400,128]{1,0:T(8,128)}, f32[400,128]{1,0:T(8,128)}, u32[]{:S(2)}, u32[]{:S(2)}) collective-permute-start(f32[400,128]{1,0:T(8,128)} %get-tuple-element.59), channel_id=1, source_target_pairs={{0,7},{1,6},{2,1},{3,0},{4,3},{5,2},{6,5},{7,4},{8,15},{9,14},{10,... | collective-permute-start | bytes 614408 | tf_op jit(solution)/shard_map/ppermute | solution.py:585
  13.8 29.2 %collective-permute-start.6 = (f32[400,128]{1,0:T(8,128)}, f32[400,128]{1,0:T(8,128)}, u32[]{:S(2)}, u32[]{:S(2)}) collective-permute-start(f32[400,128]{1,0:T(8,128)} %get-tuple-element.60), channel_id=1, source_target_pairs={{0,1},{1,0},{2,3},{3,2},{4,5},{5,4},{6,7},{7,6},{8,9},{9,8},{10,11... | collective-permute-start | bytes 614408 | tf_op jit(solution)/shard_map/ppermute | solution.py:585
  28.1 16.2 %collective-permute-start = (f32[400,128]{1,0:T(8,128)S(1)}, f32[400,128]{1,0:T(8,128)S(1)}, u32[]{:S(2)}, u32[]{:S(2)}) collective-permute-start(f32[400,128]{1,0:T(8,128)S(1)} %copy-done.54), channel_id=1, source_target_pairs={{0,2},{1,3},{2,4},{3,5},{4,6},{5,7},{6,0},{7,1},{8,10},{9,11},{10,... | collective-permute-start | bytes 614408 | tf_op jit(solution)/shard_map/ppermute | solution.py:585
  33.8 11.9 %collective-permute-start.1 = (f32[400,128]{1,0:T(8,128)S(1)}, f32[400,128]{1,0:T(8,128)S(1)}, u32[]{:S(2)}, u32[]{:S(2)}) collective-permute-start(f32[400,128]{1,0:T(8,128)S(1)} %copy-done.52), channel_id=1, source_target_pairs={{0,3},{1,2},{2,5},{3,4},{4,7},{5,6},{6,1},{7,0},{8,11},{9,10},{10,... | collective-permute-start | bytes 614408 | tf_op jit(solution)/shard_map/ppermute | solution.py:585
  37.7 18.3 %collective-permute-start.10 = (f32[400,128]{1,0:T(8,128)S(1)}, f32[400,128]{1,0:T(8,128)S(1)}, u32[]{:S(2)}, u32[]{:S(2)}) collective-permute-start(f32[400,128]{1,0:T(8,128)S(1)} %get-tuple-element.67), channel_id=1, source_target_pairs={{0,29},{1,28},{2,31},{3,30},{4,25},{5,24},{6,27},{7,26},{8,5},{9,4... | collective-permute-start | bytes 614408 | tf_op jit(solution)/shard_map/ppermute | solution.py:594
  43.0 23.1 %collective-permute-start.11 = (f32[400,128]{1,0:T(8,128)S(1)}, f32[400,128]{1,0:T(8,128)S(1)}, u32[]{:S(2)}, u32[]{:S(2)}) collective-permute-start(f32[400,128]{1,0:T(8,128)S(1)} %get-tuple-element.68), channel_id=1, source_target_pairs={{0,30},{1,31},{2,24},{3,25},{4,26},{5,27},{6,28},{7,29},{8,6},{9,7... | collective-permute-start | bytes 614408 | tf_op jit(solution)/shard_map/ppermute | solution.py:594
  43.0 23.1 %collective-permute-start.12 = (f32[400,128]{1,0:T(8,128)S(1)}, f32[400,128]{1,0:T(8,128)S(1)}, u32[]{:S(2)}, u32[]{:S(2)}) collective-permute-start(f32[400,128]{1,0:T(8,128)S(1)} %get-tuple-element.69), channel_id=1, source_target_pairs={{0,31},{1,30},{2,25},{3,24},{4,27},{5,26},{6,29},{7,28},{8,7},{9,6... | collective-permute-start | bytes 614408 | tf_op jit(solution)/shard_map/ppermute | solution.py:594
  44.3 33.7 %collective-permute-start.13 = (f32[400,128]{1,0:T(8,128)S(1)}, f32[400,128]{1,0:T(8,128)S(1)}, u32[]{:S(2)}, u32[]{:S(2)}) collective-permute-start(f32[400,128]{1,0:T(8,128)S(1)} %get-tuple-element.70), channel_id=1, source_target_pairs={{0,25},{1,24},{2,27},{3,26},{4,29},{5,28},{6,31},{7,30},{8,1},{9,0... | collective-permute-start | bytes 614408 | tf_op jit(solution)/shard_map/ppermute | solution.py:594
  45.7 32.3 %collective-permute-start.14 = (f32[400,128]{1,0:T(8,128)S(1)}, f32[400,128]{1,0:T(8,128)S(1)}, u32[]{:S(2)}, u32[]{:S(2)}) collective-permute-start(f32[400,128]{1,0:T(8,128)S(1)} %get-tuple-element.71), channel_id=1, source_target_pairs={{0,24},{1,25},{2,26},{3,27},{4,28},{5,29},{6,30},{7,31},{8,0},{9,1... | collective-permute-start | bytes 614408 | tf_op jit(solution)/shard_map/ppermute | solution.py:594
  56.0 22.0 %collective-permute-start.7 = (f32[400,128]{1,0:T(8,128)S(1)}, f32[400,128]{1,0:T(8,128)S(1)}, u32[]{:S(2)}, u32[]{:S(2)}) collective-permute-start(f32[400,128]{1,0:T(8,128)S(1)} %get-tuple-element.64), channel_id=1, source_target_pairs={{0,26},{1,27},{2,28},{3,29},{4,30},{5,31},{6,24},{7,25},{8,2},{9,3... | collective-permute-start | bytes 614408 | tf_op jit(solution)/shard_map/ppermute | solution.py:594
  66.2 11.9 %collective-permute-start.8 = (f32[400,128]{1,0:T(8,128)S(1)}, f32[400,128]{1,0:T(8,128)S(1)}, u32[]{:S(2)}, u32[]{:S(2)}) collective-permute-start(f32[400,128]{1,0:T(8,128)S(1)} %get-tuple-element.65), channel_id=1, source_target_pairs={{0,27},{1,26},{2,29},{3,28},{4,31},{5,30},{6,25},{7,24},{8,3},{9,2... | collective-permute-start | bytes 614408 | tf_op jit(solution)/shard_map/ppermute | solution.py:594
  66.2 21.2 %collective-permute-start.9 = (f32[400,128]{1,0:T(8,128)S(1)}, f32[400,128]{1,0:T(8,128)S(1)}, u32[]{:S(2)}, u32[]{:S(2)}) collective-permute-start(f32[400,128]{1,0:T(8,128)S(1)} %get-tuple-element.66), channel_id=1, source_target_pairs={{0,28},{1,29},{2,30},{3,31},{4,24},{5,25},{6,26},{7,27},{8,4},{9,5... | collective-permute-start | bytes 614408 | tf_op jit(solution)/shard_map/ppermute | solution.py:594
  107.7 6.7 %collective-permute-start.31 = (f32[200,384]{1,0:T(8,128)}, f32[200,384]{1,0:T(8,128)}, u32[]{:S(2)}, u32[]{:S(2)}) collective-permute-start(f32[200,384]{1,0:T(8,128)} %get-tuple-element.95), channel_id=1, source_target_pairs={{0,1},{1,0},{2,3},{3,2},{4,5},{5,4},{6,7},{7,6},{8,9},{9,8},{10,11... | collective-permute-start | bytes 921608 | tf_op jit(solution)/shard_map/ppermute | solution.py:585
  107.7 11.1 %collective-permute-start.30 = (f32[200,384]{1,0:T(8,128)}, f32[200,384]{1,0:T(8,128)}, u32[]{:S(2)}, u32[]{:S(2)}) collective-permute-start(f32[200,384]{1,0:T(8,128)} %get-tuple-element.93), channel_id=1, source_target_pairs={{0,1},{1,0},{2,3},{3,2},{4,5},{5,4},{6,7},{7,6},{8,9},{9,8},{10,11... | collective-permute-start | bytes 921608 | tf_op jit(solution)/shard_map/ppermute | solution.py:585
  110.2 12.5 %collective-permute-start.36 = (f32[200,384]{1,0:T(8,128)S(1)}, f32[200,384]{1,0:T(8,128)S(1)}, u32[]{:S(2)}, u32[]{:S(2)}) collective-permute-start(f32[200,384]{1,0:T(8,128)S(1)} %add.252), channel_id=1, source_target_pairs={{0,24},{8,16},{16,8},{24,0},{1,25},{9,17},{17,9},{25,1},{2,26},{10... | collective-permute-start | bytes 921608 | tf_op jit(solution)/shard_map/ppermute | solution.py:598
  112.8 14.3 %collective-permute-start.34 = (f32[200,384]{1,0:T(8,128)S(1)}, f32[200,384]{1,0:T(8,128)S(1)}, u32[]{:S(2)}, u32[]{:S(2)}) collective-permute-start(f32[200,384]{1,0:T(8,128)S(1)} %add.251), channel_id=1, source_target_pairs={{0,16},{8,24},{16,0},{24,8},{1,17},{9,25},{17,1},{25,9},{2,18},{10... | collective-permute-start | bytes 921608 | tf_op jit(solution)/shard_map/ppermute | solution.py:598
  115.4 11.7 %collective-permute-start.32 = (f32[200,384]{1,0:T(8,128)S(1)}, f32[200,384]{1,0:T(8,128)S(1)}, u32[]{:S(2)}, u32[]{:S(2)}) collective-permute-start(f32[200,384]{1,0:T(8,128)S(1)} %add.250), channel_id=1, source_target_pairs={{0,8},{8,0},{16,24},{24,16},{1,9},{9,1},{17,25},{25,17},{2,10},{10... | collective-permute-start | bytes 921608 | tf_op jit(solution)/shard_map/ppermute | solution.py:598
  118.8 21.4 %collective-permute-start.25 = (f32[400,128]{1,0:T(8,128)S(1)}, f32[400,128]{1,0:T(8,128)S(1)}, u32[]{:S(2)}, u32[]{:S(2)}) collective-permute-start(f32[400,128]{1,0:T(8,128)S(1)} %get-tuple-element.86), channel_id=1, source_target_pairs={{0,4},{1,5},{2,6},{3,7},{4,0},{5,1},{6,2},{7,3},{8,12},{9,13},{10,... | collective-permute-start | bytes 614408 | tf_op jit(solution)/shard_map/ppermute | solution.py:585
  118.8 25.7 %collective-permute-start.26 = (f32[400,128]{1,0:T(8,128)S(1)}, f32[400,128]{1,0:T(8,128)S(1)}, u32[]{:S(2)}, u32[]{:S(2)}) collective-permute-start(f32[400,128]{1,0:T(8,128)S(1)} %get-tuple-element.87), channel_id=1, source_target_pairs={{0,5},{1,4},{2,7},{3,6},{4,1},{5,0},{6,3},{7,2},{8,13},{9,12},{10,... | collective-permute-start | bytes 614408 | tf_op jit(solution)/shard_map/ppermute | solution.py:585
  122.7 29.5 %collective-permute-start.27 = (f32[400,128]{1,0:T(8,128)S(1)}, f32[400,128]{1,0:T(8,128)S(1)}, u32[]{:S(2)}, u32[]{:S(2)}) collective-permute-start(f32[400,128]{1,0:T(8,128)S(1)} %get-tuple-element.88), channel_id=1, source_target_pairs={{0,2},{1,3},{2,4},{3,5},{4,6},{5,7},{6,0},{7,1},{8,10},{9,11},{10,... | collective-permute-start | bytes 614408 | tf_op jit(solution)/shard_map/ppermute | solution.py:585
  127.7 16.7 %collective-permute-start.37 = (f32[56,384]{1,0:T(8,128)S(1)}, f32[56,384]{1,0:T(8,128)S(1)}, u32[]{:S(2)}, u32[]{:S(2)}) collective-permute-start(f32[56,384]{1,0:T(8,128)S(1)} %get-tuple-element.101), channel_id=1, source_target_pairs={{0,2},{1,3},{2,4},{3,5},{4,6},{5,7},{6,0},{7,1},{8,10},{9,11},{10,... | collective-permute-start | bytes 258056 | tf_op jit(solution)/shard_map/ppermute | solution.py:585
  127.8 18.6 %collective-permute-start.38 = (f32[56,384]{1,0:T(8,128)S(1)}, f32[56,384]{1,0:T(8,128)S(1)}, u32[]{:S(2)}, u32[]{:S(2)}) collective-permute-start(f32[56,384]{1,0:T(8,128)S(1)} %get-tuple-element.102), channel_id=1, source_target_pairs={{0,4},{1,5},{2,6},{3,7},{4,0},{5,1},{6,2},{7,3},{8,12},{9,13},{10,... | collective-permute-start | bytes 258056 | tf_op jit(solution)/shard_map/ppermute | solution.py:585
  140.2 12.0 %collective-permute-start.39 = (f32[56,384]{1,0:T(8,128)S(1)}, f32[56,384]{1,0:T(8,128)S(1)}, u32[]{:S(2)}, u32[]{:S(2)}) collective-permute-start(f32[56,384]{1,0:T(8,128)S(1)} %get-tuple-element.103), channel_id=1, source_target_pairs={{0,6},{1,7},{2,0},{3,1},{4,2},{5,3},{6,4},{7,5},{8,14},{9,15},{10,... | collective-permute-start | bytes 258056 | tf_op jit(solution)/shard_map/ppermute | solution.py:585
  144.5 9.1 %collective-permute-start.28 = (f32[400,128]{1,0:T(8,128)S(1)}, f32[400,128]{1,0:T(8,128)S(1)}, u32[]{:S(2)}, u32[]{:S(2)}) collective-permute-start(f32[400,128]{1,0:T(8,128)S(1)} %get-tuple-element.89), channel_id=1, source_target_pairs={{0,3},{1,2},{2,5},{3,4},{4,7},{5,6},{6,1},{7,0},{8,11},{9,10},{10,... | collective-permute-start | bytes 614408 | tf_op jit(solution)/shard_map/ppermute | solution.py:585
  144.5 9.8 %collective-permute-start.29 = (f32[400,128]{1,0:T(8,128)S(1)}, f32[400,128]{1,0:T(8,128)S(1)}, u32[]{:S(2)}, u32[]{:S(2)}) collective-permute-start(f32[400,128]{1,0:T(8,128)S(1)} %get-tuple-element.90), channel_id=1, source_target_pairs={{0,1},{1,0},{2,3},{3,2},{4,5},{5,4},{6,7},{7,6},{8,9},{9,8},{10,11... | collective-permute-start | bytes 614408 | tf_op jit(solution)/shard_map/ppermute | solution.py:585
  146.4 12.1 %collective-permute-start.23 = (f32[400,128]{1,0:T(8,128)S(1)}, f32[400,128]{1,0:T(8,128)S(1)}, u32[]{:S(2)}, u32[]{:S(2)}) collective-permute-start(f32[400,128]{1,0:T(8,128)S(1)} %get-tuple-element.84), channel_id=1, source_target_pairs={{0,6},{1,7},{2,0},{3,1},{4,2},{5,3},{6,4},{7,5},{8,14},{9,15},{10,... | collective-permute-start | bytes 614408 | tf_op jit(solution)/shard_map/ppermute | solution.py:585
  152.2 12.4 %collective-permute-start.19 = (f32[400,128]{1,0:T(8,128)S(1)}, f32[400,128]{1,0:T(8,128)S(1)}, u32[]{:S(2)}, u32[]{:S(2)}) collective-permute-start(f32[400,128]{1,0:T(8,128)S(1)} %get-tuple-element.77), channel_id=1, source_target_pairs={{0,10},{1,11},{2,12},{3,13},{4,14},{5,15},{6,8},{7,9},{8,18},{9,19... | collective-permute-start | bytes 614408 | tf_op jit(solution)/shard_map/ppermute | solution.py:594
  152.9 12.5 %collective-permute-start.40 = (f32[56,384]{1,0:T(8,128)S(1)}, f32[56,384]{1,0:T(8,128)S(1)}, u32[]{:S(2)}, u32[]{:S(2)}) collective-permute-start(f32[56,384]{1,0:T(8,128)S(1)} %shard_map.147.refs_0_), channel_id=1, source_target_pairs={{0,2},{1,3},{2,4},{3,5},{4,6},{5,7},{6,0},{7,1},{8,10},{9,11},{10,... | collective-permute-start | bytes 258056 | tf_op jit(solution)/shard_map/ppermute | solution.py:585
  154.2 23.1 %collective-permute-start.20 = (f32[400,128]{1,0:T(8,128)S(1)}, f32[400,128]{1,0:T(8,128)S(1)}, u32[]{:S(2)}, u32[]{:S(2)}) collective-permute-start(f32[400,128]{1,0:T(8,128)S(1)} %get-tuple-element.78), channel_id=1, source_target_pairs={{0,11},{1,10},{2,13},{3,12},{4,15},{5,14},{6,9},{7,8},{8,19},{9,18... | collective-permute-start | bytes 614408 | tf_op jit(solution)/shard_map/ppermute | solution.py:594
  154.2 25.4 %collective-permute-start.21 = (f32[400,128]{1,0:T(8,128)S(1)}, f32[400,128]{1,0:T(8,128)S(1)}, u32[]{:S(2)}, u32[]{:S(2)}) collective-permute-start(f32[400,128]{1,0:T(8,128)S(1)} %get-tuple-element.79), channel_id=1, source_target_pairs={{0,9},{1,8},{2,11},{3,10},{4,13},{5,12},{6,15},{7,14},{8,17},{9,16... | collective-permute-start | bytes 614408 | tf_op jit(solution)/shard_map/ppermute | solution.py:594
  158.6 27.9 %collective-permute-start.22 = (f32[400,128]{1,0:T(8,128)S(1)}, f32[400,128]{1,0:T(8,128)S(1)}, u32[]{:S(2)}, u32[]{:S(2)}) collective-permute-start(f32[400,128]{1,0:T(8,128)S(1)} %get-tuple-element.80), channel_id=1, source_target_pairs={{0,8},{1,9},{2,10},{3,11},{4,12},{5,13},{6,14},{7,15},{8,16},{9,17... | collective-permute-start | bytes 614408 | tf_op jit(solution)/shard_map/ppermute | solution.py:594
  164.6 8.0 %collective-permute-start.41 = (f32[56,384]{1,0:T(8,128)S(1)}, f32[56,384]{1,0:T(8,128)S(1)}, u32[]{:S(2)}, u32[]{:S(2)}) collective-permute-start(f32[56,384]{1,0:T(8,128)S(1)} %shard_map.147.refs_0_), channel_id=1, source_target_pairs={{0,4},{1,5},{2,6},{3,7},{4,0},{5,1},{6,2},{7,3},{8,12},{9,13},{10,... | collective-permute-start | bytes 258056 | tf_op jit(solution)/shard_map/ppermute | solution.py:585
  165.4 11.3 %collective-permute-start.42 = (f32[56,384]{1,0:T(8,128)S(1)}, f32[56,384]{1,0:T(8,128)S(1)}, u32[]{:S(2)}, u32[]{:S(2)}) collective-permute-start(f32[56,384]{1,0:T(8,128)S(1)} %shard_map.147.refs_0_), channel_id=1, source_target_pairs={{0,6},{1,7},{2,0},{3,1},{4,2},{5,3},{6,4},{7,5},{8,14},{9,15},{10,... | collective-permute-start | bytes 258056 | tf_op jit(solution)/shard_map/ppermute | solution.py:585
  172.6 14.5 %collective-permute-start.15 = (f32[400,128]{1,0:T(8,128)S(1)}, f32[400,128]{1,0:T(8,128)S(1)}, u32[]{:S(2)}, u32[]{:S(2)}) collective-permute-start(f32[400,128]{1,0:T(8,128)S(1)} %get-tuple-element.73), channel_id=1, source_target_pairs={{0,14},{1,15},{2,8},{3,9},{4,10},{5,11},{6,12},{7,13},{8,22},{9,23... | collective-permute-start | bytes 614408 | tf_op jit(solution)/shard_map/ppermute | solution.py:594
  176.7 13.3 %collective-permute-start.16 = (f32[400,128]{1,0:T(8,128)S(1)}, f32[400,128]{1,0:T(8,128)S(1)}, u32[]{:S(2)}, u32[]{:S(2)}) collective-permute-start(f32[400,128]{1,0:T(8,128)S(1)} %get-tuple-element.74), channel_id=1, source_target_pairs={{0,15},{1,14},{2,9},{3,8},{4,11},{5,10},{6,13},{7,12},{8,23},{9,22... | collective-permute-start | bytes 614408 | tf_op jit(solution)/shard_map/ppermute | solution.py:594
  178.0 28.8 %collective-permute-start.43 = (f32[200,384]{1,0:T(8,128)S(1)}, f32[200,384]{1,0:T(8,128)}, u32[]{:S(2)}, u32[]{:S(2)}) collective-permute-start(f32[200,384]{1,0:T(8,128)S(1)} %shard_map.148.refs_0_), channel_id=1, source_target_pairs={{0,8},{8,0},{16,24},{24,16},{1,9},{9,1},{17,25},{25,17},{2,10},{10... | collective-permute-start | bytes 921608 | tf_op jit(solution)/shard_map/ppermute | solution.py:598
  180.3 26.9 %collective-permute-start.44 = (f32[200,384]{1,0:T(8,128)S(1)}, f32[200,384]{1,0:T(8,128)}, u32[]{:S(2)}, u32[]{:S(2)}) collective-permute-start(f32[200,384]{1,0:T(8,128)S(1)} %shard_map.148.refs_0_), channel_id=1, source_target_pairs={{0,16},{8,24},{16,0},{24,8},{1,17},{9,25},{17,1},{25,9},{2,18},{10... | collective-permute-start | bytes 921608 | tf_op jit(solution)/shard_map/ppermute | solution.py:598
  187.1 20.2 %collective-permute-start.45 = (f32[200,384]{1,0:T(8,128)S(1)}, f32[200,384]{1,0:T(8,128)}, u32[]{:S(2)}, u32[]{:S(2)}) collective-permute-start(f32[200,384]{1,0:T(8,128)S(1)} %shard_map.148.refs_0_), channel_id=1, source_target_pairs={{0,24},{8,16},{16,8},{24,0},{1,25},{9,17},{17,9},{25,1},{2,26},{10... | collective-permute-start | bytes 921608 | tf_op jit(solution)/shard_map/ppermute | solution.py:598
  187.8 18.3 %collective-permute-start.17 = (f32[400,128]{1,0:T(8,128)S(1)}, f32[400,128]{1,0:T(8,128)S(1)}, u32[]{:S(2)}, u32[]{:S(2)}) collective-permute-start(f32[400,128]{1,0:T(8,128)S(1)} %get-tuple-element.75), channel_id=1, source_target_pairs={{0,12},{1,13},{2,14},{3,15},{4,8},{5,9},{6,10},{7,11},{8,20},{9,21... | collective-permute-start | bytes 614408 | tf_op jit(solution)/shard_map/ppermute | solution.py:594
  190.7 19.6 %collective-permute-start.18 = (f32[400,128]{1,0:T(8,128)S(1)}, f32[400,128]{1,0:T(8,128)S(1)}, u32[]{:S(2)}, u32[]{:S(2)}) collective-permute-start(f32[400,128]{1,0:T(8,128)S(1)} %get-tuple-element.76), channel_id=1, source_target_pairs={{0,13},{1,12},{2,15},{3,14},{4,9},{5,8},{6,11},{7,10},{8,21},{9,20... | collective-permute-start | bytes 614408 | tf_op jit(solution)/shard_map/ppermute | solution.py:594
  206.7 21.6 %collective-permute-start.46 = (f32[200,384]{1,0:T(8,128)S(1)}, f32[200,384]{1,0:T(8,128)}, u32[]{:S(2)}, u32[]{:S(2)}) collective-permute-start(f32[200,384]{1,0:T(8,128)S(1)} %shard_map.148.refs_0_), channel_id=1, source_target_pairs={{0,1},{1,0},{2,3},{3,2},{4,5},{5,4},{6,7},{7,6},{8,9},{9,8},{10,11... | collective-permute-start | bytes 921608 | tf_op jit(solution)/shard_map/ppermute | solution.py:585
  206.8 21.6 %collective-permute-start.47 = (f32[200,384]{1,0:T(8,128)}, f32[200,384]{1,0:T(8,128)}, u32[]{:S(2)}, u32[]{:S(2)}) collective-permute-start(f32[200,384]{1,0:T(8,128)} %collective-permute-done.43.refs_1_), channel_id=1, source_target_pairs={{0,1},{1,0},{2,3},{3,2},{4,5},{5,4},{6,7},{7,6},{8,9},{9,8},{10,11... | collective-permute-start | bytes 921608 | tf_op jit(solution)/shard_map/ppermute | solution.py:585
  207.3 21.1 %collective-permute-start.48 = (f32[200,384]{1,0:T(8,128)}, f32[200,384]{1,0:T(8,128)}, u32[]{:S(2)}, u32[]{:S(2)}) collective-permute-start(f32[200,384]{1,0:T(8,128)} %collective-permute-done.44.refs_2_), channel_id=1, source_target_pairs={{0,1},{1,0},{2,3},{3,2},{4,5},{5,4},{6,7},{7,6},{8,9},{9,8},{10,11... | collective-permute-start | bytes 921608 | tf_op jit(solution)/shard_map/ppermute | solution.py:585
  207.3 21.0 %collective-permute-start.49 = (f32[200,384]{1,0:T(8,128)}, f32[200,384]{1,0:T(8,128)}, u32[]{:S(2)}, u32[]{:S(2)}) collective-permute-start(f32[200,384]{1,0:T(8,128)} %collective-permute-done.45.refs_3_), channel_id=1, source_target_pairs={{0,1},{1,0},{2,3},{3,2},{4,5},{5,4},{6,7},{7,6},{8,9},{9,8},{10,11... | collective-permute-start | bytes 921608 | tf_op jit(solution)/shard_map/ppermute | solution.py:585
  211.0 12.8 %collective-permute-start.24 = (f32[400,128]{1,0:T(8,128)}, f32[400,128]{1,0:T(8,128)}, u32[]{:S(2)}, u32[]{:S(2)}) collective-permute-start(f32[400,128]{1,0:T(8,128)} %get-tuple-element.85), channel_id=1, source_target_pairs={{0,7},{1,6},{2,1},{3,0},{4,3},{5,2},{6,5},{7,4},{8,15},{9,14},{10,... | collective-permute-start | bytes 614408 | tf_op jit(solution)/shard_map/ppermute | solution.py:585
  (63 other events, 484.5 us)

commit v5 on v4

--- a/solution.py
+++ b/solution.py
@@ -246,7 +246,8 @@
     sum_all = pos_weight + jnp.sum(weight, axis=1, keepdims=True)
     edge = step * score.shape[0] + lax.broadcasted_iota(I32, pos.shape, 0)
     is_live = jnp.where(edge < live, 1.0, 0.0)
-    loss_ref[...] = (peak - pos + jnp.log(sum_all)) * is_live
+    loss = (peak - pos + jnp.log(sum_all)) * is_live
+    loss_ref[...] = jnp.broadcast_to(loss, (loss.shape[0], LANES)).T[:1]
     scale = is_live / sum_all
     pos_grad = pos_weight * scale - is_live
     grad = weight * scale + jnp.where(own, pos_grad, 0.0)
@@ -311,7 +312,7 @@
     return kernel_call(
         functools.partial(score_kernel, peers),
         [
-            shape((edges, 1)),
+            shape((1, edges)),
             shape((2, edges, table_rows), BF16),
             shape((3 * features, table_rows), BF16),
         ],
@@ -324,7 +325,7 @@
             pl.BlockSpec((chunk, 1), lambda i: (before(i), 0)),
         ] + [held((features, block))] * peers,
         out_specs=[
-            pl.BlockSpec((chunk, 1), lambda i: (before(i), 0)),
+            pl.BlockSpec((1, chunk), lambda i: (0, before(i))),
             pl.BlockSpec((2, chunk, table_rows), lambda i: (0, before(i), 0)),
             held((3 * features, table_rows)),
         ],
@@ -457,23 +458,26 @@
     )(rows, edge_source)
 
 
-def put_back(blocks, hot_ref):
+def put_back(blocks, hot):
     hi, lo = split2(jnp.concatenate([ref[...] for ref in blocks], axis=1))
-    return dot(hi, hot_ref[...]) + dot(lo, hot_ref[...])
-
-
-def target_home_kernel(hot_ref, *refs):
-    refs[-1][...] = put_back(refs[:-1], hot_ref)
-
-
-def target_home(hots, blocks):
-    features = blocks[0].shape[0]
-    rows = hots.shape[1]
-    return kernel_call(
-        target_home_kernel, shape((features, rows)),
+    return dot(hi, hot) + dot(lo, hot)
+
+
+def target_home_kernel(hot_ref, source_hot_ref, own_ref, entity_ref, *refs):
+    blocks, out_ref, entity_out_ref = refs[:-2], refs[-2], refs[-1]
+    block = own_ref.shape[1]
+    own_hot = source_hot_ref[source_hot_ref.shape[0] - block:, :]
+    out_ref[...] = put_back(blocks, hot_ref[...]) + put_back([own_ref], own_hot)
+    entity_out_ref[...] = entity_ref[...]
+
+
+def target_home(hots, source_hots, own, entity, blocks):
+    features, rows = entity.shape
+    return kernel_call(
+        target_home_kernel, [shape((features, rows))] * 2,
         4 * features * rows * hots.shape[0], 8 * features * hots.shape[0],
-        in_specs=[VMEM] * (1 + len(blocks)), out_specs=VMEM,
-    )(hots, *blocks)
+        in_specs=[VMEM] * (4 + len(blocks)), out_specs=[VMEM] * 2,
+    )(hots, source_hots, own, entity, *blocks)
 
 
 def adagrad(params, state, gradient):
@@ -482,7 +486,9 @@
 
 
 def entity_kernel(other_ref, entity_ref, state_ref, hot_ref, *refs):
-    gradient = other_ref[...] + put_back(refs[:-1], hot_ref)
+    blocks = refs[:-1]
+    here = len(blocks) * blocks[0].shape[1]
+    gradient = other_ref[...] + put_back(blocks, hot_ref[:here, :])
     refs[-1][...] = adagrad(entity_ref[...], state_ref[...], gradient)
 
 
@@ -493,6 +499,22 @@
         4 * features * rows * hots.shape[0], 8 * features * hots.shape[0],
         in_specs=[VMEM] * (4 + len(blocks)), out_specs=VMEM,
     )(other, entity, state, hots, *blocks)
+
+
+def add_kernel(*refs):
+    count = len(refs) // 3
+    for i in range(count):
+        refs[2 * count + i][...] = refs[i][...] + refs[count + i][...]
+
+
+def added(ours, theirs):
+    count = len(ours)
+    dims = ours[0].shape
+    return kernel_call(
+        add_kernel, [shape(dims)] * count,
+        count * dims[0] * dims[1], 12 * count * dims[0] * dims[1],
+        in_specs=[VMEM] * (2 * count), out_specs=[VMEM] * count,
+    )(*ours, *theirs)
 
 
 def cut_kernel(me_ref, *refs):
@@ -603,7 +625,7 @@
     half = kept[0].shape[0]
     other_core = (0, 1)
     sent = [sent_on(b, other_core, peers) for b in sent]
-    mine = [a + b for a, b in zip(kept, sent)]
+    mine = added(kept, sent)
     terms = [mine[0]] + [sent_group(mine[j], j, groups) for j in range(1, groups)]
     ahead = (chip + jnp.arange(chips, dtype=I32)) % chips
     behind = (chip - jnp.arange(chips, dtype=I32)) % chips
@@ -675,9 +697,9 @@
         returned.append(sent_on(value, hop, peers) if way != (0, 0) else value)
     parts = relation_sum(halves[:groups], halves[groups:], peers, groups, me // 2)
     relation_new = relation_update(here, relation_t, relation_state.reshape(1, -1), parts)
-    target_part = target_home(target_hots, home)
+    target_part, entity_t = target_home(target_hots, source_hots, returned[-1], entity_t, home)
     entity_new = entity_update(
-        source_hots, returned, target_part, entity_t, entity_state.reshape(1, -1)
+        source_hots, returned[:-1], target_part, entity_t, entity_state.reshape(1, -1)
     )
     return entity_new.T, relation_new.T, loss.reshape(-1)
 

time: 233 us -> 240 us (1.030)
  waiting for transfers between devices: 69.6 us -> 86 us
  local copies, waits for them, and re-layouts: 25.4 us -> 17.4 us
  other arithmetic: 5.33 us -> 0.35 us
  Pallas kernels: 54.3 us -> 57.1 us
    ppermute x6, waiting for transfers between devices: 4.3 us -> 27.1 us  [sent_group(): return lax.ppermute(value, 'group', [(g, g ^ bit) for g in range(groups)])]
    ppermute x16, waiting for transfers between devices: 45.5 us -> 34.9 us  [sent_across(): return lax.ppermute(value, ('group', 'shard'), pairs)]
    unnamed x122 -> x102, local copies, waits for them, and re-layouts: 22.1 us -> 14.1 us
    ppermute x16, starting transfers between devices: 37.1 us -> 29.3 us  [sent_across(): return lax.ppermute(value, ('group', 'shard'), pairs)]
    ppermute x28, starting transfers between devices: 32.5 us -> 40.2 us  [sent_on(): lax.ppermute(value, 'shard', [(i, partner(i, hop, peers, 1)) for i in ran...]
    add x4 -> x0, other arithmetic: 4.18 us -> none  [relation_sum(): mine = [a + b for a, b in zip(kept, sent)]]
    ppermute x28, waiting for transfers between devices: 19.9 us -> 24 us  [sent_on(): lax.ppermute(value, 'shard', [(i, partner(i, hop, peers, 1)) for i in ran...]
    pallas_call x2 -> x3, Pallas kernels: 7.9 us -> 10.3 us  [the longest x1 7.54 us: score_spans(): kernel_call(functools.partial(score_kernel, peers), [shape((1, edges)), s...]
  transfers between devices with their start and end apart: 50 -> 50, of which waited for: 13 -> 17; matrix products, arithmetic and copies ran while one was open for 4% -> 1% of each run, Pallas kernels for 13% -> 14%
where the time goes in v5:
time: 240 us; the launch traced here: 239 us
  waiting for transfers between devices  86 us (36%)
  starting transfers between devices  76.6 us (32%)
  Pallas kernels  57.1 us (24%)
  local copies, waits for them, and re-layouts  17.4 us (7%)
    ppermute x28, starting transfers between devices, sent_on(): lax.ppermute(value, 'shard', [(i, partner(i, hop, peers, 1)) for i in ran...  40.2 us
    ppermute x16, waiting for transfers between devices, sent_across(): return lax.ppermute(value, ('group', 'shard'), pairs)  34.9 us
    ppermute x16, starting transfers between devices, sent_across(): return lax.ppermute(value, ('group', 'shard'), pairs)  29.3 us
    ppermute x6, waiting for transfers between devices, sent_group(): return lax.ppermute(value, 'group', [(g, g ^ bit) for g in range(groups)])  27.1 us
    ppermute x28, waiting for transfers between devices, sent_on(): lax.ppermute(value, 'shard', [(i, partner(i, hop, peers, 1)) for i in ran...  24 us
    unnamed x102, local copies, waits for them, and re-layouts  14.1 us
    pallas_call x1, Pallas kernels, relation_grads(): kernel_call(functools.partial(relation_grad_kernel, steps), [shape((2, fe...  9.16 us
    pallas_call x1, Pallas kernels, score_spans(): kernel_call(functools.partial(score_kernel, peers), [shape((1, edges)), s...  7.54 us
  transfers between devices with their start and end apart: 50, of which 17 were waited for; matrix products, arithmetic and copies ran while one was open for 1% of the time, Pallas kernels for 14%

profile of v5, /device:TPU:0, one launch (start us, length us, event | category | flops | bytes accessed | tf_op | source)
XLA Modules:
  0.0 239.5 jit_solution(610281069174172533)
XLA Ops:
  0.8 1.1 copy-done.5
  2.7 2.6 %shard_map.134 = (f32[400,128]{1,0:T(8,128)}, f32[400,128]{1,0:T(8,128)}, f32[400,128]{1,0:T(8,128)}, f32[400,128]{1,0:T(8,128)}, f32[400,128]{1,0:T(8,128)}, /*index=5*/f32[400,128]{1,0:T(8,128)S(1)}) custom-call(s32[6]{0:T(128)S(1)} %stack.53.order_ref, f32[400,512]{1,0:T(8,128)S(1)} %bitcast.29, s32[8,128]{1,0:T(8,128)S(1)} %bitcast.39), custom_call_target="tpu_custom_call" | custom-call | flops 943718400 | bytes 2457600 | tf_op jit(solution)/shard_map/pallas_call | solution.py:126
  5.9 4.1 %collective-permute-start.2 = (f32[400,128]{1,0:T(8,128)}, f32[400,128]{1,0:T(8,128)}, u32[]{:S(2)}, u32[]{:S(2)}) collective-permute-start(f32[400,128]{1,0:T(8,128)} %get-tuple-element.62), channel_id=1, source_target_pairs={{0,4},{1,5},{2,6},{3,7},{4,0},{5,1},{6,2},{7,3},{8,12},{9,13},{10,... | collective-permute-start | bytes 614408 | tf_op jit(solution)/shard_map/ppermute | solution.py:607
  10.0 3.1 %collective-permute-start.4 = (f32[400,128]{1,0:T(8,128)}, f32[400,128]{1,0:T(8,128)}, u32[]{:S(2)}, u32[]{:S(2)}) collective-permute-start(f32[400,128]{1,0:T(8,128)} %get-tuple-element.64), channel_id=1, source_target_pairs={{0,6},{1,7},{2,0},{3,1},{4,2},{5,3},{6,4},{7,5},{8,14},{9,15},{10,... | collective-permute-start | bytes 614408 | tf_op jit(solution)/shard_map/ppermute | solution.py:607
  14.0 1.0 shard_map.133
  19.9 5.3 %shard_map.132.refs_1_.rels_ref = f32[400,1024]{1,0:T(8,128)S(1)} custom-call(f32[400,1345]{1,0:T(8,128)S(1)} %bitcast.27, s32[1,1024]{1,0:T(1,128)S(1)} %bitcast.36), custom_call_target="tpu_custom_call" | custom-call | flops 3460300800 | bytes 3276800 | tf_op jit(solution)/shard_map/pallas_call | solution.py:153
  25.3 2.0 shard_map.137
  27.3 6.4 %collective-permute-start = (f32[400,128]{1,0:T(8,128)S(1)}, f32[400,128]{1,0:T(8,128)S(1)}, u32[]{:S(2)}, u32[]{:S(2)}) collective-permute-start(f32[400,128]{1,0:T(8,128)S(1)} %copy-done.44), channel_id=1, source_target_pairs={{0,2},{1,3},{2,4},{3,5},{4,6},{5,7},{6,0},{7,1},{8,10},{9,11},{10,... | collective-permute-start | bytes 614408 | tf_op jit(solution)/shard_map/ppermute | solution.py:607
  33.8 3.9 %collective-permute-start.1 = (f32[400,128]{1,0:T(8,128)S(1)}, f32[400,128]{1,0:T(8,128)S(1)}, u32[]{:S(2)}, u32[]{:S(2)}) collective-permute-start(f32[400,128]{1,0:T(8,128)S(1)} %copy-done.42), channel_id=1, source_target_pairs={{0,3},{1,2},{2,5},{3,4},{4,7},{5,6},{6,1},{7,0},{8,11},{9,10},{10,... | collective-permute-start | bytes 614408 | tf_op jit(solution)/shard_map/ppermute | solution.py:607
  37.7 5.4 %collective-permute-start.10 = (f32[400,128]{1,0:T(8,128)S(1)}, f32[400,128]{1,0:T(8,128)S(1)}, u32[]{:S(2)}, u32[]{:S(2)}) collective-permute-start(f32[400,128]{1,0:T(8,128)S(1)} %get-tuple-element.72), channel_id=1, source_target_pairs={{0,29},{1,28},{2,31},{3,30},{4,25},{5,24},{6,27},{7,26},{8,5},{9,4... | collective-permute-start | bytes 614408 | tf_op jit(solution)/shard_map/ppermute | solution.py:616
  43.0 1.2 collective-permute-start.12
  44.3 1.4 collective-permute-start.13
  45.7 2.4 %collective-permute-start.14 = (f32[400,128]{1,0:T(8,128)S(1)}, f32[400,128]{1,0:T(8,128)S(1)}, u32[]{:S(2)}, u32[]{:S(2)}) collective-permute-start(f32[400,128]{1,0:T(8,128)S(1)} %get-tuple-element.76), channel_id=1, source_target_pairs={{0,24},{1,25},{2,26},{3,27},{4,28},{5,29},{6,30},{7,31},{8,0},{9,1... | collective-permute-start | bytes 614408 | tf_op jit(solution)/shard_map/ppermute | solution.py:616
  48.1 7.9 %collective-permute-done.10.refs_7_ = f32[400,128]{1,0:T(8,128)S(1)} collective-permute-done((f32[400,128]{1,0:T(8,128)S(1)}, f32[400,128]{1,0:T(8,128)S(1)}, u32[]{:S(2)}, u32[]{:S(2)}) %collective-permute-start.10) | collective-permute-done | bytes 204832 | tf_op jit(solution)/shard_map/ppermute | solution.py:616
  56.0 10.2 %collective-permute-start.7 = (f32[400,128]{1,0:T(8,128)S(1)}, f32[400,128]{1,0:T(8,128)S(1)}, u32[]{:S(2)}, u32[]{:S(2)}) collective-permute-start(f32[400,128]{1,0:T(8,128)S(1)} %get-tuple-element.69), channel_id=1, source_target_pairs={{0,26},{1,27},{2,28},{3,29},{4,30},{5,31},{6,24},{7,25},{8,2},{9,3... | collective-permute-start | bytes 614408 | tf_op jit(solution)/shard_map/ppermute | solution.py:616
  66.2 4.5 %collective-permute-start.9 = (f32[400,128]{1,0:T(8,128)S(1)}, f32[400,128]{1,0:T(8,128)S(1)}, u32[]{:S(2)}, u32[]{:S(2)}) collective-permute-start(f32[400,128]{1,0:T(8,128)S(1)} %get-tuple-element.71), channel_id=1, source_target_pairs={{0,28},{1,29},{2,30},{3,31},{4,24},{5,25},{6,26},{7,27},{8,4},{9,5... | collective-permute-start | bytes 614408 | tf_op jit(solution)/shard_map/ppermute | solution.py:616
  70.7 7.3 %shard_map.135 = (f32[400,1024]{1,0:T(8,128)S(1)}, bf16[2,400,1024]{2,1,0:T(8,128)(2,1)S(1)}, bf16[1024,1200]{1,0:T(8,128)(2,1)S(1)}) custom-call(s32[1,1024]{1,0:T(1,128)S(1)} %bitcast.33, f32[400,1024]{1,0:T(8,128)S(1)} %shard_map.132.refs_1_.rels_ref, f32[400,128]{1,0:T(8,128)S(1)} %collective-permute-done.refs_2_, ...), custom_call_target="tpu_custom_call" | custom-call | flops 2516582400 | bytes 8192000 | tf_op jit(solution)/shard_map/pallas_call | solution.py:221
  78.0 9.4 %collective-permute-done.9.refs_6_ = f32[400,128]{1,0:T(8,128)S(1)} collective-permute-done((f32[400,128]{1,0:T(8,128)S(1)}, f32[400,128]{1,0:T(8,128)S(1)}, u32[]{:S(2)}, u32[]{:S(2)}) %collective-permute-start.9) | collective-permute-done | bytes 204832 | tf_op jit(solution)/shard_map/ppermute | solution.py:616
  87.4 7.5 %shard_map.138 = (f32[1,1024]{1,0:T(1,128)}, bf16[2,1024,1024]{2,1,0:T(8,128)(2,1)S(1)}, bf16[1200,1024]{1,0:T(8,128)(2,1)S(1)}) custom-call(s32[1]{0:T(128)S(6)} %copy.21.refs_0_, bf16[1024,1200]{1,0:T(8,128)(2,1)S(1)} %get-tuple-element.68.refs_1_, f32[2,1,1024]{2,1,0:T(1,128)S(1)} %shard_map.136.refs_2_, s32[1024,1]{1,0:T(8,128)S(1)} %copy-done.9, ...), custom_call_target="tpu_custom_call" | custom-call | flops 2516582400 | bytes 12288000 | tf_op jit(solution)/shard_map/pallas_call | solution.py:312
  94.9 9.2 %shard_map.139 = (bf16[2,400,1024]{2,1,0:T(8,128)(2,1)S(1)}, f32[200,384]{1,0:T(8,128)S(1)}, f32[200,384]{1,0:T(8,128)S(1)}, f32[200,384]{1,0:T(8,128)S(1)}, f32...) custom-call(s32[2]{0:T(128)S(1)} %pad_add_fusion.me_ref, ...), custom_call_target="tpu_custom_call" | custom-call | flops 4194304000 | bytes 12288000 | tf_op jit(solution)/shard_map/pallas_call | solution.py:416
  107.2 1.5 collective-permute-start.34
  109.3 1.5 collective-permute-start.36
  110.8 2.7 %shard_map.142 = (f32[400,128]{1,0:T(8,128)S(1)}, f32[400,128]{1,0:T(8,128)S(1)}, f32[400,128]{1,0:T(8,128)}, f32[400,128]{1,0:T(8,128)}) custom-call(bf16[2,400,1024]{2,1,0:T(8,128)(2,1)S(1)} %get-tuple-element.82.columns_ref, bf16[2,1024,1024]{2,1,0:T(8,128)(2,1)S(1)} %get-tuple-element.78.grad_ref), custom_call_target="tpu_custom_call" | custom-call | flops 1258291200 | bytes 3735552 | tf_op jit(solution)/shard_map/pallas_call | solution.py:353
  113.5 3.9 %collective-permute-done.34.refs_1_ = f32[200,384]{1,0:T(8,128)S(1)} collective-permute-done((f32[200,384]{1,0:T(8,128)S(1)}, f32[200,384]{1,0:T(8,128)S(1)}, u32[]{:S(2)}, u32[]{:S(2)}) %collective-permute-start.34) | collective-permute-done | bytes 307232 | tf_op jit(solution)/shard_map/ppermute | solution.py:620
  117.4 20.1 %collective-permute-done.35.refs_2_ = f32[200,384]{1,0:T(8,128)S(1)} collective-permute-done((f32[200,384]{1,0:T(8,128)S(1)}, f32[200,384]{1,0:T(8,128)S(1)}, u32[]{:S(2)}, u32[]{:S(2)}) %collective-permute-start.35) | collective-permute-done | bytes 307232 | tf_op jit(solution)/shard_map/ppermute | solution.py:620
  138.7 3.3 %collective-permute-start.39 = (f32[56,384]{1,0:T(8,128)S(1)}, f32[56,384]{1,0:T(8,128)S(1)}, u32[]{:S(2)}, u32[]{:S(2)}) collective-permute-start(f32[56,384]{1,0:T(8,128)S(1)} %get-tuple-element.115), channel_id=1, source_target_pairs={{0,6},{1,7},{2,0},{3,1},{4,2},{5,3},{6,4},{7,5},{8,14},{9,15},{10,... | collective-permute-start | bytes 258056 | tf_op jit(solution)/shard_map/ppermute | solution.py:607
  142.1 2.8 %shard_map.141 = (f32[400,128]{1,0:T(8,128)}, f32[400,128]{1,0:T(8,128)}, f32[400,128]{1,0:T(8,128)}, f32[400,128]{1,0:T(8,128)S(1)}) custom-call(bf16[2,400,1024]{2,1,0:T(8,128)(2,1)S(1)} %get-tuple-element.82.columns_ref, bf16[2,1024,1024]{2,1,0:T(8,128)(2,1)S(1)} %get-tuple-element.78.grad_ref), custom_call_target="tpu_custom_call" | custom-call | flops 1258291200 | bytes 3735552 | tf_op jit(solution)/shard_map/pallas_call | solution.py:353
  146.2 2.0 collective-permute-start.15
  149.0 2.1 collective-permute-start.17
  153.9 1.4 copy-done.3
  155.4 2.1 shard_map.140
  157.5 5.2 %collective-permute-done.22.refs_7_ = f32[400,128]{1,0:T(8,128)} collective-permute-done((f32[400,128]{1,0:T(8,128)}, f32[400,128]{1,0:T(8,128)}, u32[]{:S(2)}, u32[]{:S(2)}) %collective-permute-start.22) | collective-permute-done | bytes 204832 | tf_op jit(solution)/shard_map/ppermute | solution.py:616
  162.7 5.2 %collective-permute-start.25 = (f32[400,128]{1,0:T(8,128)S(1)}, f32[400,128]{1,0:T(8,128)S(1)}, u32[]{:S(2)}, u32[]{:S(2)}) collective-permute-start(f32[400,128]{1,0:T(8,128)S(1)} %get-tuple-element.95), channel_id=1, source_target_pairs={{0,4},{1,5},{2,6},{3,7},{4,0},{5,1},{6,2},{7,3},{8,12},{9,13},{10,... | collective-permute-start | bytes 614408 | tf_op jit(solution)/shard_map/ppermute | solution.py:607
  168.8 12.4 %collective-permute-done.17.refs_2_ = f32[400,128]{1,0:T(8,128)} collective-permute-done((f32[400,128]{1,0:T(8,128)}, f32[400,128]{1,0:T(8,128)}, u32[]{:S(2)}, u32[]{:S(2)}) %collective-permute-start.17) | collective-permute-done | bytes 204832 | tf_op jit(solution)/shard_map/ppermute | solution.py:616
  181.2 3.3 %collective-permute-start.41 = (f32[56,384]{1,0:T(8,128)S(1)}, f32[56,384]{1,0:T(8,128)S(1)}, u32[]{:S(2)}, u32[]{:S(2)}) collective-permute-start(f32[56,384]{1,0:T(8,128)S(1)} %shard_map.148.refs_0_), channel_id=1, source_target_pairs={{0,4},{1,5},{2,6},{3,7},{4,0},{5,1},{6,2},{7,3},{8,12},{9,13},{10,... | collective-permute-start | bytes 258056 | tf_op jit(solution)/shard_map/ppermute | solution.py:607
  184.5 15.1 %collective-permute-done.41.refs_2_ = f32[56,384]{1,0:T(8,128)S(1)} collective-permute-done((f32[56,384]{1,0:T(8,128)S(1)}, f32[56,384]{1,0:T(8,128)S(1)}, u32[]{:S(2)}, u32[]{:S(2)}) %collective-permute-start.41) | collective-permute-done | bytes 86048 | tf_op jit(solution)/shard_map/ppermute | solution.py:607
  201.8 1.3 collective-permute-start.44
  203.2 1.6 collective-permute-start.45
  204.7 4.7 %collective-permute-done.27.refs_4_ = f32[400,128]{1,0:T(8,128)S(1)} collective-permute-done((f32[400,128]{1,0:T(8,128)S(1)}, f32[400,128]{1,0:T(8,128)S(1)}, u32[]{:S(2)}, u32[]{:S(2)}) %collective-permute-start.27) | collective-permute-done | bytes 204832 | tf_op jit(solution)/shard_map/ppermute | solution.py:607
  209.4 1.3 shard_map.144
  212.0 2.1 collective-permute-start.23
  215.6 1.4 collective-permute-done.44.refs_2_
  217.1 1.7 collective-permute-done.45.refs_3_
  218.8 1.1 collective-permute-done.23.refs_0_
  220.6 3.6 %collective-permute-start.24 = (f32[400,128]{1,0:T(8,128)}, f32[400,128]{1,0:T(8,128)}, u32[]{:S(2)}, u32[]{:S(2)}) collective-permute-start(f32[400,128]{1,0:T(8,128)} %get-tuple-element.94), channel_id=1, source_target_pairs={{0,7},{1,6},{2,1},{3,0},{4,3},{5,2},{6,5},{7,4},{8,15},{9,14},{10,... | collective-permute-start | bytes 614408 | tf_op jit(solution)/shard_map/ppermute | solution.py:607
  230.0 2.6 %shard_map.143 = (f32[400,512]{1,0:T(8,128)S(1)}, f32[400,512]{1,0:T(8,128)S(1)}) custom-call(bf16[1024,512]{1,0:T(8,128)(2,1)S(1)} %shard_map.130.hot_ref, bf16[1024,512]{1,0:T(8,128)(2,1)S(1)} %shard_map.131.source_hot_ref.hot_ref, f32[400,128]{1,0:T(8,128)S(1)} %copy-done.15, f32[400,512]{1,0:T(8,128)S(1)} %bitcast.32, ...), custom_call_target="tpu_custom_call" | custom-call | flops 838860800 | bytes 3276800 | tf_op jit(solution)/shard_map/pallas_call | solution.py:476
  232.7 3.0 %shard_map.145 = f32[400,512]{1,0:T(8,128)} custom-call(f32[400,512]{1,0:T(8,128)S(1)} %get-tuple-element.91.other_ref, f32[400,512]{1,0:T(8,128)S(1)} %get-tuple-element.92.entity_ref, f32[1,512]{1,0:T(1,128)S(1)} %bitcast.42, bf16[1024,512]{1,0:T(8,128)(2,1)S(1)} %shard_map.131.source_hot_ref.hot_ref, f32[400,128]{1,0:T(8,128)S(1)} %copy-done.29, ...), custom_call_target="tpu_custom_call" | custom-call | flops 838860800 | bytes 3276800 | tf_op jit(solution)/shard_map/pallas_call | solution.py:497
  235.8 3.7 %shard_map.150 = f32[400,1345]{1,0:T(8,128)} custom-call(s32[2]{0:T(128)S(1)} %pad_add_fusion.me_ref, f32[400,1345]{1,0:T(8,128)S(1)} %bitcast.28, f32[1,1345]{1,0:T(1,128)S(1)} %reshape.36.state_ref, f32[200,384]{1,0:T(8,128)S(1)} %shard_map.149.refs_0_, f32[200,384]{1,0:T(8,128)} %collective-permute-done.43.refs_1_, ...), custom_call_target="tpu_custom_call" | custom-call | flops 4304000 | bytes 6456000 | tf_op jit(solution)/shard_map/pallas_call | solution.py:598
  (191 shorter events, 28.6 us)
Async XLA Ops:
  5.9 21.4 %collective-permute-start.2 = (f32[400,128]{1,0:T(8,128)}, f32[400,128]{1,0:T(8,128)}, u32[]{:S(2)}, u32[]{:S(2)}) collective-permute-start(f32[400,128]{1,0:T(8,128)} %get-tuple-element.62), channel_id=1, source_target_pairs={{0,4},{1,5},{2,6},{3,7},{4,0},{5,1},{6,2},{7,3},{8,12},{9,13},{10,... | collective-permute-start | bytes 614408 | tf_op jit(solution)/shard_map/ppermute | solution.py:607
  10.0 23.8 %collective-permute-start.3 = (f32[400,128]{1,0:T(8,128)}, f32[400,128]{1,0:T(8,128)}, u32[]{:S(2)}, u32[]{:S(2)}) collective-permute-start(f32[400,128]{1,0:T(8,128)} %get-tuple-element.63), channel_id=1, source_target_pairs={{0,5},{1,4},{2,7},{3,6},{4,1},{5,0},{6,3},{7,2},{8,13},{9,12},{10,... | collective-permute-start | bytes 614408 | tf_op jit(solution)/shard_map/ppermute | solution.py:607
  10.0 27.7 %collective-permute-start.4 = (f32[400,128]{1,0:T(8,128)}, f32[400,128]{1,0:T(8,128)}, u32[]{:S(2)}, u32[]{:S(2)}) collective-permute-start(f32[400,128]{1,0:T(8,128)} %get-tuple-element.64), channel_id=1, source_target_pairs={{0,6},{1,7},{2,0},{3,1},{4,2},{5,3},{6,4},{7,5},{8,14},{9,15},{10,... | collective-permute-start | bytes 614408 | tf_op jit(solution)/shard_map/ppermute | solution.py:607
  13.1 30.0 %collective-permute-start.5 = (f32[400,128]{1,0:T(8,128)}, f32[400,128]{1,0:T(8,128)}, u32[]{:S(2)}, u32[]{:S(2)}) collective-permute-start(f32[400,128]{1,0:T(8,128)} %get-tuple-element.65), channel_id=1, source_target_pairs={{0,7},{1,6},{2,1},{3,0},{4,3},{5,2},{6,5},{7,4},{8,15},{9,14},{10,... | collective-permute-start | bytes 614408 | tf_op jit(solution)/shard_map/ppermute | solution.py:607
  13.8 29.2 %collective-permute-start.6 = (f32[400,128]{1,0:T(8,128)}, f32[400,128]{1,0:T(8,128)}, u32[]{:S(2)}, u32[]{:S(2)}) collective-permute-start(f32[400,128]{1,0:T(8,128)} %get-tuple-element.66), channel_id=1, source_target_pairs={{0,1},{1,0},{2,3},{3,2},{4,5},{5,4},{6,7},{7,6},{8,9},{9,8},{10,11... | collective-permute-start | bytes 614408 | tf_op jit(solution)/shard_map/ppermute | solution.py:607
  27.3 17.0 %collective-permute-start = (f32[400,128]{1,0:T(8,128)S(1)}, f32[400,128]{1,0:T(8,128)S(1)}, u32[]{:S(2)}, u32[]{:S(2)}) collective-permute-start(f32[400,128]{1,0:T(8,128)S(1)} %copy-done.44), channel_id=1, source_target_pairs={{0,2},{1,3},{2,4},{3,5},{4,6},{5,7},{6,0},{7,1},{8,10},{9,11},{10,... | collective-permute-start | bytes 614408 | tf_op jit(solution)/shard_map/ppermute | solution.py:607
  33.8 11.9 %collective-permute-start.1 = (f32[400,128]{1,0:T(8,128)S(1)}, f32[400,128]{1,0:T(8,128)S(1)}, u32[]{:S(2)}, u32[]{:S(2)}) collective-permute-start(f32[400,128]{1,0:T(8,128)S(1)} %copy-done.42), channel_id=1, source_target_pairs={{0,3},{1,2},{2,5},{3,4},{4,7},{5,6},{6,1},{7,0},{8,11},{9,10},{10,... | collective-permute-start | bytes 614408 | tf_op jit(solution)/shard_map/ppermute | solution.py:607
  37.7 18.3 %collective-permute-start.10 = (f32[400,128]{1,0:T(8,128)S(1)}, f32[400,128]{1,0:T(8,128)S(1)}, u32[]{:S(2)}, u32[]{:S(2)}) collective-permute-start(f32[400,128]{1,0:T(8,128)S(1)} %get-tuple-element.72), channel_id=1, source_target_pairs={{0,29},{1,28},{2,31},{3,30},{4,25},{5,24},{6,27},{7,26},{8,5},{9,4... | collective-permute-start | bytes 614408 | tf_op jit(solution)/shard_map/ppermute | solution.py:616
  43.0 23.1 %collective-permute-start.11 = (f32[400,128]{1,0:T(8,128)S(1)}, f32[400,128]{1,0:T(8,128)S(1)}, u32[]{:S(2)}, u32[]{:S(2)}) collective-permute-start(f32[400,128]{1,0:T(8,128)S(1)} %get-tuple-element.73), channel_id=1, source_target_pairs={{0,30},{1,31},{2,24},{3,25},{4,26},{5,27},{6,28},{7,29},{8,6},{9,7... | collective-permute-start | bytes 614408 | tf_op jit(solution)/shard_map/ppermute | solution.py:616
  43.0 23.1 %collective-permute-start.12 = (f32[400,128]{1,0:T(8,128)S(1)}, f32[400,128]{1,0:T(8,128)S(1)}, u32[]{:S(2)}, u32[]{:S(2)}) collective-permute-start(f32[400,128]{1,0:T(8,128)S(1)} %get-tuple-element.74), channel_id=1, source_target_pairs={{0,31},{1,30},{2,25},{3,24},{4,27},{5,26},{6,29},{7,28},{8,7},{9,6... | collective-permute-start | bytes 614408 | tf_op jit(solution)/shard_map/ppermute | solution.py:616
  44.3 33.7 %collective-permute-start.13 = (f32[400,128]{1,0:T(8,128)S(1)}, f32[400,128]{1,0:T(8,128)S(1)}, u32[]{:S(2)}, u32[]{:S(2)}) collective-permute-start(f32[400,128]{1,0:T(8,128)S(1)} %get-tuple-element.75), channel_id=1, source_target_pairs={{0,25},{1,24},{2,27},{3,26},{4,29},{5,28},{6,31},{7,30},{8,1},{9,0... | collective-permute-start | bytes 614408 | tf_op jit(solution)/shard_map/ppermute | solution.py:616
  45.7 32.3 %collective-permute-start.14 = (f32[400,128]{1,0:T(8,128)S(1)}, f32[400,128]{1,0:T(8,128)S(1)}, u32[]{:S(2)}, u32[]{:S(2)}) collective-permute-start(f32[400,128]{1,0:T(8,128)S(1)} %get-tuple-element.76), channel_id=1, source_target_pairs={{0,24},{1,25},{2,26},{3,27},{4,28},{5,29},{6,30},{7,31},{8,0},{9,1... | collective-permute-start | bytes 614408 | tf_op jit(solution)/shard_map/ppermute | solution.py:616
  56.0 22.0 %collective-permute-start.7 = (f32[400,128]{1,0:T(8,128)S(1)}, f32[400,128]{1,0:T(8,128)S(1)}, u32[]{:S(2)}, u32[]{:S(2)}) collective-permute-start(f32[400,128]{1,0:T(8,128)S(1)} %get-tuple-element.69), channel_id=1, source_target_pairs={{0,26},{1,27},{2,28},{3,29},{4,30},{5,31},{6,24},{7,25},{8,2},{9,3... | collective-permute-start | bytes 614408 | tf_op jit(solution)/shard_map/ppermute | solution.py:616
  66.2 11.9 %collective-permute-start.8 = (f32[400,128]{1,0:T(8,128)S(1)}, f32[400,128]{1,0:T(8,128)S(1)}, u32[]{:S(2)}, u32[]{:S(2)}) collective-permute-start(f32[400,128]{1,0:T(8,128)S(1)} %get-tuple-element.70), channel_id=1, source_target_pairs={{0,27},{1,26},{2,29},{3,28},{4,31},{5,30},{6,25},{7,24},{8,3},{9,2... | collective-permute-start | bytes 614408 | tf_op jit(solution)/shard_map/ppermute | solution.py:616
  66.2 21.2 %collective-permute-start.9 = (f32[400,128]{1,0:T(8,128)S(1)}, f32[400,128]{1,0:T(8,128)S(1)}, u32[]{:S(2)}, u32[]{:S(2)}) collective-permute-start(f32[400,128]{1,0:T(8,128)S(1)} %get-tuple-element.71), channel_id=1, source_target_pairs={{0,28},{1,29},{2,30},{3,31},{4,24},{5,25},{6,26},{7,27},{8,4},{9,5... | collective-permute-start | bytes 614408 | tf_op jit(solution)/shard_map/ppermute | solution.py:616
  104.2 2.0 collective-permute-start.31
  104.8 2.3 collective-permute-start.33
  107.2 10.2 %collective-permute-start.34 = (f32[200,384]{1,0:T(8,128)S(1)}, f32[200,384]{1,0:T(8,128)S(1)}, u32[]{:S(2)}, u32[]{:S(2)}) collective-permute-start(f32[200,384]{1,0:T(8,128)S(1)} %get-tuple-element.109), channel_id=1, source_target_pairs={{0,8},{8,0},{16,24},{24,16},{1,9},{9,1},{17,25},{25,17},{2,10},{10... | collective-permute-start | bytes 921608 | tf_op jit(solution)/shard_map/ppermute | solution.py:620
  108.8 28.8 %collective-permute-start.35 = (f32[200,384]{1,0:T(8,128)S(1)}, f32[200,384]{1,0:T(8,128)S(1)}, u32[]{:S(2)}, u32[]{:S(2)}) collective-permute-start(f32[200,384]{1,0:T(8,128)S(1)} %get-tuple-element.110), channel_id=1, source_target_pairs={{0,16},{8,24},{16,0},{24,8},{1,17},{9,25},{17,1},{25,9},{2,18},{10... | collective-permute-start | bytes 921608 | tf_op jit(solution)/shard_map/ppermute | solution.py:620
  109.3 28.3 %collective-permute-start.36 = (f32[200,384]{1,0:T(8,128)S(1)}, f32[200,384]{1,0:T(8,128)S(1)}, u32[]{:S(2)}, u32[]{:S(2)}) collective-permute-start(f32[200,384]{1,0:T(8,128)S(1)} %get-tuple-element.111), channel_id=1, source_target_pairs={{0,24},{8,16},{16,8},{24,0},{1,25},{9,17},{17,9},{25,1},{2,26},{10... | collective-permute-start | bytes 921608 | tf_op jit(solution)/shard_map/ppermute | solution.py:620
  113.5 25.2 %collective-permute-start.19 = (f32[400,128]{1,0:T(8,128)S(1)}, f32[400,128]{1,0:T(8,128)S(1)}, u32[]{:S(2)}, u32[]{:S(2)}) collective-permute-start(f32[400,128]{1,0:T(8,128)S(1)} %get-tuple-element.87), channel_id=1, source_target_pairs={{0,10},{1,11},{2,12},{3,13},{4,14},{5,15},{6,8},{7,9},{8,18},{9,19... | collective-permute-start | bytes 614408 | tf_op jit(solution)/shard_map/ppermute | solution.py:616
  113.5 32.0 %collective-permute-start.20 = (f32[400,128]{1,0:T(8,128)S(1)}, f32[400,128]{1,0:T(8,128)S(1)}, u32[]{:S(2)}, u32[]{:S(2)}) collective-permute-start(f32[400,128]{1,0:T(8,128)S(1)} %get-tuple-element.88), channel_id=1, source_target_pairs={{0,11},{1,10},{2,13},{3,12},{4,15},{5,14},{6,9},{7,8},{8,19},{9,18... | collective-permute-start | bytes 614408 | tf_op jit(solution)/shard_map/ppermute | solution.py:616
  117.4 35.7 %collective-permute-start.21 = (f32[400,128]{1,0:T(8,128)}, f32[400,128]{1,0:T(8,128)S(1)}, u32[]{:S(2)}, u32[]{:S(2)}) collective-permute-start(f32[400,128]{1,0:T(8,128)} %get-tuple-element.89), channel_id=1, source_target_pairs={{0,9},{1,8},{2,11},{3,10},{4,13},{5,12},{6,15},{7,14},{8,17},{9,16... | collective-permute-start | bytes 614408 | tf_op jit(solution)/shard_map/ppermute | solution.py:616
  138.2 8.1 %collective-permute-start.37 = (f32[56,384]{1,0:T(8,128)S(1)}, f32[56,384]{1,0:T(8,128)S(1)}, u32[]{:S(2)}, u32[]{:S(2)}) collective-permute-start(f32[56,384]{1,0:T(8,128)S(1)} %get-tuple-element.113), channel_id=1, source_target_pairs={{0,2},{1,3},{2,4},{3,5},{4,6},{5,7},{6,0},{7,1},{8,10},{9,11},{10,... | collective-permute-start | bytes 258056 | tf_op jit(solution)/shard_map/ppermute | solution.py:607
  138.3 10.0 %collective-permute-start.38 = (f32[56,384]{1,0:T(8,128)S(1)}, f32[56,384]{1,0:T(8,128)S(1)}, u32[]{:S(2)}, u32[]{:S(2)}) collective-permute-start(f32[56,384]{1,0:T(8,128)S(1)} %get-tuple-element.114), channel_id=1, source_target_pairs={{0,4},{1,5},{2,6},{3,7},{4,0},{5,1},{6,2},{7,3},{8,12},{9,13},{10,... | collective-permute-start | bytes 258056 | tf_op jit(solution)/shard_map/ppermute | solution.py:607
  138.7 9.6 %collective-permute-start.39 = (f32[56,384]{1,0:T(8,128)S(1)}, f32[56,384]{1,0:T(8,128)S(1)}, u32[]{:S(2)}, u32[]{:S(2)}) collective-permute-start(f32[56,384]{1,0:T(8,128)S(1)} %get-tuple-element.115), channel_id=1, source_target_pairs={{0,6},{1,7},{2,0},{3,1},{4,2},{5,3},{6,4},{7,5},{8,14},{9,15},{10,... | collective-permute-start | bytes 258056 | tf_op jit(solution)/shard_map/ppermute | solution.py:607
  146.2 16.4 %collective-permute-start.22 = (f32[400,128]{1,0:T(8,128)}, f32[400,128]{1,0:T(8,128)}, u32[]{:S(2)}, u32[]{:S(2)}) collective-permute-start(f32[400,128]{1,0:T(8,128)} %get-tuple-element.90), channel_id=1, source_target_pairs={{0,8},{1,9},{2,10},{3,11},{4,12},{5,13},{6,14},{7,15},{8,16},{9,17... | collective-permute-start | bytes 614408 | tf_op jit(solution)/shard_map/ppermute | solution.py:616
  146.2 16.4 %collective-permute-start.15 = (f32[400,128]{1,0:T(8,128)}, f32[400,128]{1,0:T(8,128)}, u32[]{:S(2)}, u32[]{:S(2)}) collective-permute-start(f32[400,128]{1,0:T(8,128)} %get-tuple-element.83), channel_id=1, source_target_pairs={{0,14},{1,15},{2,8},{3,9},{4,10},{5,11},{6,12},{7,13},{8,22},{9,23... | collective-permute-start | bytes 614408 | tf_op jit(solution)/shard_map/ppermute | solution.py:616
  148.3 19.6 %collective-permute-start.16 = (f32[400,128]{1,0:T(8,128)}, f32[400,128]{1,0:T(8,128)}, u32[]{:S(2)}, u32[]{:S(2)}) collective-permute-start(f32[400,128]{1,0:T(8,128)} %get-tuple-element.84), channel_id=1, source_target_pairs={{0,15},{1,14},{2,9},{3,8},{4,11},{5,10},{6,13},{7,12},{8,23},{9,22... | collective-permute-start | bytes 614408 | tf_op jit(solution)/shard_map/ppermute | solution.py:616
  149.0 32.2 %collective-permute-start.17 = (f32[400,128]{1,0:T(8,128)}, f32[400,128]{1,0:T(8,128)}, u32[]{:S(2)}, u32[]{:S(2)}) collective-permute-start(f32[400,128]{1,0:T(8,128)} %get-tuple-element.85), channel_id=1, source_target_pairs={{0,12},{1,13},{2,14},{3,15},{4,8},{5,9},{6,10},{7,11},{8,20},{9,21... | collective-permute-start | bytes 614408 | tf_op jit(solution)/shard_map/ppermute | solution.py:616
  153.2 31.3 %collective-permute-start.40 = (f32[56,384]{1,0:T(8,128)S(1)}, f32[56,384]{1,0:T(8,128)S(1)}, u32[]{:S(2)}, u32[]{:S(2)}) collective-permute-start(f32[56,384]{1,0:T(8,128)S(1)} %shard_map.148.refs_0_), channel_id=1, source_target_pairs={{0,2},{1,3},{2,4},{3,5},{4,6},{5,7},{6,0},{7,1},{8,10},{9,11},{10,... | collective-permute-start | bytes 258056 | tf_op jit(solution)/shard_map/ppermute | solution.py:607
  162.7 38.5 %collective-permute-start.18 = (f32[400,128]{1,0:T(8,128)S(1)}, f32[400,128]{1,0:T(8,128)S(1)}, u32[]{:S(2)}, u32[]{:S(2)}) collective-permute-start(f32[400,128]{1,0:T(8,128)S(1)} %copy-done.40), channel_id=1, source_target_pairs={{0,13},{1,12},{2,15},{3,14},{4,9},{5,8},{6,11},{7,10},{8,21},{9,20... | collective-permute-start | bytes 614408 | tf_op jit(solution)/shard_map/ppermute | solution.py:616
  162.7 39.2 %collective-permute-start.25 = (f32[400,128]{1,0:T(8,128)S(1)}, f32[400,128]{1,0:T(8,128)S(1)}, u32[]{:S(2)}, u32[]{:S(2)}) collective-permute-start(f32[400,128]{1,0:T(8,128)S(1)} %get-tuple-element.95), channel_id=1, source_target_pairs={{0,4},{1,5},{2,6},{3,7},{4,0},{5,1},{6,2},{7,3},{8,12},{9,13},{10,... | collective-permute-start | bytes 614408 | tf_op jit(solution)/shard_map/ppermute | solution.py:607
  167.9 35.3 %collective-permute-start.26 = (f32[400,128]{1,0:T(8,128)S(1)}, f32[400,128]{1,0:T(8,128)S(1)}, u32[]{:S(2)}, u32[]{:S(2)}) collective-permute-start(f32[400,128]{1,0:T(8,128)S(1)} %get-tuple-element.96), channel_id=1, source_target_pairs={{0,5},{1,4},{2,7},{3,6},{4,1},{5,0},{6,3},{7,2},{8,13},{9,12},{10,... | collective-permute-start | bytes 614408 | tf_op jit(solution)/shard_map/ppermute | solution.py:607
  181.2 18.5 %collective-permute-start.41 = (f32[56,384]{1,0:T(8,128)S(1)}, f32[56,384]{1,0:T(8,128)S(1)}, u32[]{:S(2)}, u32[]{:S(2)}) collective-permute-start(f32[56,384]{1,0:T(8,128)S(1)} %shard_map.148.refs_0_), channel_id=1, source_target_pairs={{0,4},{1,5},{2,6},{3,7},{4,0},{5,1},{6,2},{7,3},{8,12},{9,13},{10,... | collective-permute-start | bytes 258056 | tf_op jit(solution)/shard_map/ppermute | solution.py:607
  184.5 16.0 %collective-permute-start.42 = (f32[56,384]{1,0:T(8,128)S(1)}, f32[56,384]{1,0:T(8,128)S(1)}, u32[]{:S(2)}, u32[]{:S(2)}) collective-permute-start(f32[56,384]{1,0:T(8,128)S(1)} %shard_map.148.refs_0_), channel_id=1, source_target_pairs={{0,6},{1,7},{2,0},{3,1},{4,2},{5,3},{6,4},{7,5},{8,14},{9,15},{10,... | collective-permute-start | bytes 258056 | tf_op jit(solution)/shard_map/ppermute | solution.py:607
  199.7 9.7 %collective-permute-start.27 = (f32[400,128]{1,0:T(8,128)S(1)}, f32[400,128]{1,0:T(8,128)S(1)}, u32[]{:S(2)}, u32[]{:S(2)}) collective-permute-start(f32[400,128]{1,0:T(8,128)S(1)} %get-tuple-element.97), channel_id=1, source_target_pairs={{0,2},{1,3},{2,4},{3,5},{4,6},{5,7},{6,0},{7,1},{8,10},{9,11},{10,... | collective-permute-start | bytes 614408 | tf_op jit(solution)/shard_map/ppermute | solution.py:607
  200.5 10.8 %collective-permute-start.28 = (f32[400,128]{1,0:T(8,128)S(1)}, f32[400,128]{1,0:T(8,128)S(1)}, u32[]{:S(2)}, u32[]{:S(2)}) collective-permute-start(f32[400,128]{1,0:T(8,128)S(1)} %get-tuple-element.98), channel_id=1, source_target_pairs={{0,3},{1,2},{2,5},{3,4},{4,7},{5,6},{6,1},{7,0},{8,11},{9,10},{10,... | collective-permute-start | bytes 614408 | tf_op jit(solution)/shard_map/ppermute | solution.py:607
  201.2 14.5 %collective-permute-start.43 = (f32[200,384]{1,0:T(8,128)S(1)}, f32[200,384]{1,0:T(8,128)}, u32[]{:S(2)}, u32[]{:S(2)}) collective-permute-start(f32[200,384]{1,0:T(8,128)S(1)} %shard_map.149.refs_0_), channel_id=1, source_target_pairs={{0,8},{8,0},{16,24},{24,16},{1,9},{9,1},{17,25},{25,17},{2,10},{10... | collective-permute-start | bytes 921608 | tf_op jit(solution)/shard_map/ppermute | solution.py:620
  201.8 15.2 %collective-permute-start.44 = (f32[200,384]{1,0:T(8,128)S(1)}, f32[200,384]{1,0:T(8,128)}, u32[]{:S(2)}, u32[]{:S(2)}) collective-permute-start(f32[200,384]{1,0:T(8,128)S(1)} %shard_map.149.refs_0_), channel_id=1, source_target_pairs={{0,16},{8,24},{16,0},{24,8},{1,17},{9,25},{17,1},{25,9},{2,18},{10... | collective-permute-start | bytes 921608 | tf_op jit(solution)/shard_map/ppermute | solution.py:620
  203.2 15.6 %collective-permute-start.45 = (f32[200,384]{1,0:T(8,128)S(1)}, f32[200,384]{1,0:T(8,128)}, u32[]{:S(2)}, u32[]{:S(2)}) collective-permute-start(f32[200,384]{1,0:T(8,128)S(1)} %shard_map.149.refs_0_), channel_id=1, source_target_pairs={{0,24},{8,16},{16,8},{24,0},{1,25},{9,17},{17,9},{25,1},{2,26},{10... | collective-permute-start | bytes 921608 | tf_op jit(solution)/shard_map/ppermute | solution.py:620
  209.4 4.7 %collective-permute-start.29 = (f32[400,128]{1,0:T(8,128)S(1)}, f32[400,128]{1,0:T(8,128)S(1)}, u32[]{:S(2)}, u32[]{:S(2)}) collective-permute-start(f32[400,128]{1,0:T(8,128)S(1)} %get-tuple-element.99), channel_id=1, source_target_pairs={{0,1},{1,0},{2,3},{3,2},{4,5},{5,4},{6,7},{7,6},{8,9},{9,8},{10,11... | collective-permute-start | bytes 614408 | tf_op jit(solution)/shard_map/ppermute | solution.py:607
  212.0 7.9 %collective-permute-start.23 = (f32[400,128]{1,0:T(8,128)S(1)}, f32[400,128]{1,0:T(8,128)S(1)}, u32[]{:S(2)}, u32[]{:S(2)}) collective-permute-start(f32[400,128]{1,0:T(8,128)S(1)} %get-tuple-element.93), channel_id=1, source_target_pairs={{0,6},{1,7},{2,0},{3,1},{4,2},{5,3},{6,4},{7,5},{8,14},{9,15},{10,... | collective-permute-start | bytes 614408 | tf_op jit(solution)/shard_map/ppermute | solution.py:607
  214.8 20.9 %collective-permute-start.46 = (f32[200,384]{1,0:T(8,128)S(1)}, f32[200,384]{1,0:T(8,128)}, u32[]{:S(2)}, u32[]{:S(2)}) collective-permute-start(f32[200,384]{1,0:T(8,128)S(1)} %shard_map.149.refs_0_), channel_id=1, source_target_pairs={{0,1},{1,0},{2,3},{3,2},{4,5},{5,4},{6,7},{7,6},{8,9},{9,8},{10,11... | collective-permute-start | bytes 921608 | tf_op jit(solution)/shard_map/ppermute | solution.py:607
  215.6 20.1 %collective-permute-start.47 = (f32[200,384]{1,0:T(8,128)}, f32[200,384]{1,0:T(8,128)}, u32[]{:S(2)}, u32[]{:S(2)}) collective-permute-start(f32[200,384]{1,0:T(8,128)} %collective-permute-done.43.refs_1_), channel_id=1, source_target_pairs={{0,1},{1,0},{2,3},{3,2},{4,5},{5,4},{6,7},{7,6},{8,9},{9,8},{10,11... | collective-permute-start | bytes 921608 | tf_op jit(solution)/shard_map/ppermute | solution.py:607
  217.1 18.7 %collective-permute-start.48 = (f32[200,384]{1,0:T(8,128)}, f32[200,384]{1,0:T(8,128)}, u32[]{:S(2)}, u32[]{:S(2)}) collective-permute-start(f32[200,384]{1,0:T(8,128)} %collective-permute-done.44.refs_2_), channel_id=1, source_target_pairs={{0,1},{1,0},{2,3},{3,2},{4,5},{5,4},{6,7},{7,6},{8,9},{9,8},{10,11... | collective-permute-start | bytes 921608 | tf_op jit(solution)/shard_map/ppermute | solution.py:607
  218.8 17.0 %collective-permute-start.49 = (f32[200,384]{1,0:T(8,128)}, f32[200,384]{1,0:T(8,128)}, u32[]{:S(2)}, u32[]{:S(2)}) collective-permute-start(f32[200,384]{1,0:T(8,128)} %collective-permute-done.45.refs_3_), channel_id=1, source_target_pairs={{0,1},{1,0},{2,3},{3,2},{4,5},{5,4},{6,7},{7,6},{8,9},{9,8},{10,11... | collective-permute-start | bytes 921608 | tf_op jit(solution)/shard_map/ppermute | solution.py:607
  220.6 12.1 %collective-permute-start.24 = (f32[400,128]{1,0:T(8,128)}, f32[400,128]{1,0:T(8,128)}, u32[]{:S(2)}, u32[]{:S(2)}) collective-permute-start(f32[400,128]{1,0:T(8,128)} %get-tuple-element.94), channel_id=1, source_target_pairs={{0,7},{1,6},{2,1},{3,0},{4,3},{5,2},{6,5},{7,4},{8,15},{9,14},{10,... | collective-permute-start | bytes 614408 | tf_op jit(solution)/shard_map/ppermute | solution.py:607
  (53 other events, 495.9 us)

commit v6 on v5

--- a/solution.py
+++ b/solution.py
@@ -678,14 +678,9 @@
     table_parts = table_grads(query_columns, grad, block, 0, early)
     table_parts += table_grads(query_columns, grad, block, early, peers - early)
     back = [(-hop[0], hop[1]) for hop in ways]
-    home = [
-        sent_across(value, hop, peers, groups, 1)
-        for value, hop in zip(table_parts[:early], back[:early])
-    ]
-    home += [
-        sent_across(value, hop, peers, groups, 1)
-        for value, hop in zip(table_parts[early:], back[early:])
-    ]
+    home = []
+    for value, hop in zip(table_parts, back):
+        home.append(sent_across(value, hop, peers, groups, 1))
     source_lines, *halves = relation_grads(
         here, table, grad, heads, rels, edge_relation.reshape(-1, 1), groups, width
     )

time: 240 us -> 240 us (level)
  no operation moved by 1% of the time
where the time goes in v6:
time: 240 us; the launch traced here: 239 us
  waiting for transfers between devices  86 us (36%)
  starting transfers between devices  76.6 us (32%)
  Pallas kernels  57.1 us (24%)
  local copies, waits for them, and re-layouts  17.4 us (7%)
    ppermute x28, starting transfers between devices, sent_on(): lax.ppermute(value, 'shard', [(i, partner(i, hop, peers, 1)) for i in ran...  40.2 us
    ppermute x16, waiting for transfers between devices, sent_across(): return lax.ppermute(value, ('group', 'shard'), pairs)  34.9 us
    ppermute x16, starting transfers between devices, sent_across(): return lax.ppermute(value, ('group', 'shard'), pairs)  29.3 us
    ppermute x6, waiting for transfers between devices, sent_group(): return lax.ppermute(value, 'group', [(g, g ^ bit) for g in range(groups)])  27.1 us
    ppermute x28, waiting for transfers between devices, sent_on(): lax.ppermute(value, 'shard', [(i, partner(i, hop, peers, 1)) for i in ran...  24 us
    unnamed x102, local copies, waits for them, and re-layouts  14.1 us
    pallas_call x1, Pallas kernels, relation_grads(): kernel_call(functools.partial(relation_grad_kernel, steps), [shape((2, fe...  9.16 us
    pallas_call x1, Pallas kernels, score_spans(): kernel_call(functools.partial(score_kernel, peers), [shape((1, edges)), s...  7.54 us
  transfers between devices with their start and end apart: 50, of which 17 were waited for; matrix products, arithmetic and copies ran while one was open for 1% of the time, Pallas kernels for 14%

profile of v6, /device:TPU:0, one launch (start us, length us, event | category | flops | bytes accessed | tf_op | source)
XLA Modules:
  0.0 239.5 jit_solution(610281069174172533)
XLA Ops:
  0.8 1.1 copy-done.5
  2.7 2.6 %shard_map.134 = (f32[400,128]{1,0:T(8,128)}, f32[400,128]{1,0:T(8,128)}, f32[400,128]{1,0:T(8,128)}, f32[400,128]{1,0:T(8,128)}, f32[400,128]{1,0:T(8,128)}, /*index=5*/f32[400,128]{1,0:T(8,128)S(1)}) custom-call(s32[6]{0:T(128)S(1)} %stack.53.order_ref, f32[400,512]{1,0:T(8,128)S(1)} %bitcast.29, s32[8,128]{1,0:T(8,128)S(1)} %bitcast.39), custom_call_target="tpu_custom_call" | custom-call | flops 943718400 | bytes 2457600 | tf_op jit(solution)/shard_map/pallas_call | solution.py:126
  5.9 4.1 %collective-permute-start.2 = (f32[400,128]{1,0:T(8,128)}, f32[400,128]{1,0:T(8,128)}, u32[]{:S(2)}, u32[]{:S(2)}) collective-permute-start(f32[400,128]{1,0:T(8,128)} %get-tuple-element.62), channel_id=1, source_target_pairs={{0,4},{1,5},{2,6},{3,7},{4,0},{5,1},{6,2},{7,3},{8,12},{9,13},{10,... | collective-permute-start | bytes 614408 | tf_op jit(solution)/shard_map/ppermute | solution.py:607
  10.0 3.1 %collective-permute-start.4 = (f32[400,128]{1,0:T(8,128)}, f32[400,128]{1,0:T(8,128)}, u32[]{:S(2)}, u32[]{:S(2)}) collective-permute-start(f32[400,128]{1,0:T(8,128)} %get-tuple-element.64), channel_id=1, source_target_pairs={{0,6},{1,7},{2,0},{3,1},{4,2},{5,3},{6,4},{7,5},{8,14},{9,15},{10,... | collective-permute-start | bytes 614408 | tf_op jit(solution)/shard_map/ppermute | solution.py:607
  14.0 1.0 shard_map.133
  19.9 5.3 %shard_map.132.refs_1_.rels_ref = f32[400,1024]{1,0:T(8,128)S(1)} custom-call(f32[400,1345]{1,0:T(8,128)S(1)} %bitcast.27, s32[1,1024]{1,0:T(1,128)S(1)} %bitcast.36), custom_call_target="tpu_custom_call" | custom-call | flops 3460300800 | bytes 3276800 | tf_op jit(solution)/shard_map/pallas_call | solution.py:153
  25.3 2.0 shard_map.137
  27.3 6.4 %collective-permute-start = (f32[400,128]{1,0:T(8,128)S(1)}, f32[400,128]{1,0:T(8,128)S(1)}, u32[]{:S(2)}, u32[]{:S(2)}) collective-permute-start(f32[400,128]{1,0:T(8,128)S(1)} %copy-done.44), channel_id=1, source_target_pairs={{0,2},{1,3},{2,4},{3,5},{4,6},{5,7},{6,0},{7,1},{8,10},{9,11},{10,... | collective-permute-start | bytes 614408 | tf_op jit(solution)/shard_map/ppermute | solution.py:607
  33.8 3.9 %collective-permute-start.1 = (f32[400,128]{1,0:T(8,128)S(1)}, f32[400,128]{1,0:T(8,128)S(1)}, u32[]{:S(2)}, u32[]{:S(2)}) collective-permute-start(f32[400,128]{1,0:T(8,128)S(1)} %copy-done.42), channel_id=1, source_target_pairs={{0,3},{1,2},{2,5},{3,4},{4,7},{5,6},{6,1},{7,0},{8,11},{9,10},{10,... | collective-permute-start | bytes 614408 | tf_op jit(solution)/shard_map/ppermute | solution.py:607
  37.7 5.4 %collective-permute-start.10 = (f32[400,128]{1,0:T(8,128)S(1)}, f32[400,128]{1,0:T(8,128)S(1)}, u32[]{:S(2)}, u32[]{:S(2)}) collective-permute-start(f32[400,128]{1,0:T(8,128)S(1)} %get-tuple-element.72), channel_id=1, source_target_pairs={{0,29},{1,28},{2,31},{3,30},{4,25},{5,24},{6,27},{7,26},{8,5},{9,4... | collective-permute-start | bytes 614408 | tf_op jit(solution)/shard_map/ppermute | solution.py:616
  43.0 1.2 collective-permute-start.12
  44.3 1.4 collective-permute-start.13
  45.7 2.4 %collective-permute-start.14 = (f32[400,128]{1,0:T(8,128)S(1)}, f32[400,128]{1,0:T(8,128)S(1)}, u32[]{:S(2)}, u32[]{:S(2)}) collective-permute-start(f32[400,128]{1,0:T(8,128)S(1)} %get-tuple-element.76), channel_id=1, source_target_pairs={{0,24},{1,25},{2,26},{3,27},{4,28},{5,29},{6,30},{7,31},{8,0},{9,1... | collective-permute-start | bytes 614408 | tf_op jit(solution)/shard_map/ppermute | solution.py:616
  48.1 7.9 %collective-permute-done.10.refs_7_ = f32[400,128]{1,0:T(8,128)S(1)} collective-permute-done((f32[400,128]{1,0:T(8,128)S(1)}, f32[400,128]{1,0:T(8,128)S(1)}, u32[]{:S(2)}, u32[]{:S(2)}) %collective-permute-start.10) | collective-permute-done | bytes 204832 | tf_op jit(solution)/shard_map/ppermute | solution.py:616
  56.0 10.2 %collective-permute-start.7 = (f32[400,128]{1,0:T(8,128)S(1)}, f32[400,128]{1,0:T(8,128)S(1)}, u32[]{:S(2)}, u32[]{:S(2)}) collective-permute-start(f32[400,128]{1,0:T(8,128)S(1)} %get-tuple-element.69), channel_id=1, source_target_pairs={{0,26},{1,27},{2,28},{3,29},{4,30},{5,31},{6,24},{7,25},{8,2},{9,3... | collective-permute-start | bytes 614408 | tf_op jit(solution)/shard_map/ppermute | solution.py:616
  66.2 4.5 %collective-permute-start.9 = (f32[400,128]{1,0:T(8,128)S(1)}, f32[400,128]{1,0:T(8,128)S(1)}, u32[]{:S(2)}, u32[]{:S(2)}) collective-permute-start(f32[400,128]{1,0:T(8,128)S(1)} %get-tuple-element.71), channel_id=1, source_target_pairs={{0,28},{1,29},{2,30},{3,31},{4,24},{5,25},{6,26},{7,27},{8,4},{9,5... | collective-permute-start | bytes 614408 | tf_op jit(solution)/shard_map/ppermute | solution.py:616
  70.7 7.3 %shard_map.135 = (f32[400,1024]{1,0:T(8,128)S(1)}, bf16[2,400,1024]{2,1,0:T(8,128)(2,1)S(1)}, bf16[1024,1200]{1,0:T(8,128)(2,1)S(1)}) custom-call(s32[1,1024]{1,0:T(1,128)S(1)} %bitcast.33, f32[400,1024]{1,0:T(8,128)S(1)} %shard_map.132.refs_1_.rels_ref, f32[400,128]{1,0:T(8,128)S(1)} %collective-permute-done.refs_2_, ...), custom_call_target="tpu_custom_call" | custom-call | flops 2516582400 | bytes 8192000 | tf_op jit(solution)/shard_map/pallas_call | solution.py:221
  78.0 9.4 %collective-permute-done.9.refs_6_ = f32[400,128]{1,0:T(8,128)S(1)} collective-permute-done((f32[400,128]{1,0:T(8,128)S(1)}, f32[400,128]{1,0:T(8,128)S(1)}, u32[]{:S(2)}, u32[]{:S(2)}) %collective-permute-start.9) | collective-permute-done | bytes 204832 | tf_op jit(solution)/shard_map/ppermute | solution.py:616
  87.4 7.5 %shard_map.138 = (f32[1,1024]{1,0:T(1,128)}, bf16[2,1024,1024]{2,1,0:T(8,128)(2,1)S(1)}, bf16[1200,1024]{1,0:T(8,128)(2,1)S(1)}) custom-call(s32[1]{0:T(128)S(6)} %copy.21.refs_0_, bf16[1024,1200]{1,0:T(8,128)(2,1)S(1)} %get-tuple-element.68.refs_1_, f32[2,1,1024]{2,1,0:T(1,128)S(1)} %shard_map.136.refs_2_, s32[1024,1]{1,0:T(8,128)S(1)} %copy-done.9, ...), custom_call_target="tpu_custom_call" | custom-call | flops 2516582400 | bytes 12288000 | tf_op jit(solution)/shard_map/pallas_call | solution.py:312
  94.9 9.2 %shard_map.139 = (bf16[2,400,1024]{2,1,0:T(8,128)(2,1)S(1)}, f32[200,384]{1,0:T(8,128)S(1)}, f32[200,384]{1,0:T(8,128)S(1)}, f32[200,384]{1,0:T(8,128)S(1)}, f32...) custom-call(s32[2]{0:T(128)S(1)} %pad_add_fusion.me_ref, ...), custom_call_target="tpu_custom_call" | custom-call | flops 4194304000 | bytes 12288000 | tf_op jit(solution)/shard_map/pallas_call | solution.py:416
  107.2 1.5 collective-permute-start.34
  109.3 1.5 collective-permute-start.36
  110.8 2.7 %shard_map.142 = (f32[400,128]{1,0:T(8,128)S(1)}, f32[400,128]{1,0:T(8,128)S(1)}, f32[400,128]{1,0:T(8,128)}, f32[400,128]{1,0:T(8,128)}) custom-call(bf16[2,400,1024]{2,1,0:T(8,128)(2,1)S(1)} %get-tuple-element.82.columns_ref, bf16[2,1024,1024]{2,1,0:T(8,128)(2,1)S(1)} %get-tuple-element.78.grad_ref), custom_call_target="tpu_custom_call" | custom-call | flops 1258291200 | bytes 3735552 | tf_op jit(solution)/shard_map/pallas_call | solution.py:353
  113.5 3.9 %collective-permute-done.34.refs_1_ = f32[200,384]{1,0:T(8,128)S(1)} collective-permute-done((f32[200,384]{1,0:T(8,128)S(1)}, f32[200,384]{1,0:T(8,128)S(1)}, u32[]{:S(2)}, u32[]{:S(2)}) %collective-permute-start.34) | collective-permute-done | bytes 307232 | tf_op jit(solution)/shard_map/ppermute | solution.py:620
  117.4 20.1 %collective-permute-done.35.refs_2_ = f32[200,384]{1,0:T(8,128)S(1)} collective-permute-done((f32[200,384]{1,0:T(8,128)S(1)}, f32[200,384]{1,0:T(8,128)S(1)}, u32[]{:S(2)}, u32[]{:S(2)}) %collective-permute-start.35) | collective-permute-done | bytes 307232 | tf_op jit(solution)/shard_map/ppermute | solution.py:620
  138.7 3.3 %collective-permute-start.39 = (f32[56,384]{1,0:T(8,128)S(1)}, f32[56,384]{1,0:T(8,128)S(1)}, u32[]{:S(2)}, u32[]{:S(2)}) collective-permute-start(f32[56,384]{1,0:T(8,128)S(1)} %get-tuple-element.115), channel_id=1, source_target_pairs={{0,6},{1,7},{2,0},{3,1},{4,2},{5,3},{6,4},{7,5},{8,14},{9,15},{10,... | collective-permute-start | bytes 258056 | tf_op jit(solution)/shard_map/ppermute | solution.py:607
  142.1 2.8 %shard_map.141 = (f32[400,128]{1,0:T(8,128)}, f32[400,128]{1,0:T(8,128)}, f32[400,128]{1,0:T(8,128)}, f32[400,128]{1,0:T(8,128)S(1)}) custom-call(bf16[2,400,1024]{2,1,0:T(8,128)(2,1)S(1)} %get-tuple-element.82.columns_ref, bf16[2,1024,1024]{2,1,0:T(8,128)(2,1)S(1)} %get-tuple-element.78.grad_ref), custom_call_target="tpu_custom_call" | custom-call | flops 1258291200 | bytes 3735552 | tf_op jit(solution)/shard_map/pallas_call | solution.py:353
  146.2 2.0 collective-permute-start.15
  149.0 2.1 collective-permute-start.17
  153.9 1.4 copy-done.3
  155.4 2.1 shard_map.140
  157.5 5.2 %collective-permute-done.22.refs_7_ = f32[400,128]{1,0:T(8,128)} collective-permute-done((f32[400,128]{1,0:T(8,128)}, f32[400,128]{1,0:T(8,128)}, u32[]{:S(2)}, u32[]{:S(2)}) %collective-permute-start.22) | collective-permute-done | bytes 204832 | tf_op jit(solution)/shard_map/ppermute | solution.py:616
  162.7 5.2 %collective-permute-start.25 = (f32[400,128]{1,0:T(8,128)S(1)}, f32[400,128]{1,0:T(8,128)S(1)}, u32[]{:S(2)}, u32[]{:S(2)}) collective-permute-start(f32[400,128]{1,0:T(8,128)S(1)} %get-tuple-element.95), channel_id=1, source_target_pairs={{0,4},{1,5},{2,6},{3,7},{4,0},{5,1},{6,2},{7,3},{8,12},{9,13},{10,... | collective-permute-start | bytes 614408 | tf_op jit(solution)/shard_map/ppermute | solution.py:607
  168.8 12.4 %collective-permute-done.17.refs_2_ = f32[400,128]{1,0:T(8,128)} collective-permute-done((f32[400,128]{1,0:T(8,128)}, f32[400,128]{1,0:T(8,128)}, u32[]{:S(2)}, u32[]{:S(2)}) %collective-permute-start.17) | collective-permute-done | bytes 204832 | tf_op jit(solution)/shard_map/ppermute | solution.py:616
  181.2 3.3 %collective-permute-start.41 = (f32[56,384]{1,0:T(8,128)S(1)}, f32[56,384]{1,0:T(8,128)S(1)}, u32[]{:S(2)}, u32[]{:S(2)}) collective-permute-start(f32[56,384]{1,0:T(8,128)S(1)} %shard_map.148.refs_0_), channel_id=1, source_target_pairs={{0,4},{1,5},{2,6},{3,7},{4,0},{5,1},{6,2},{7,3},{8,12},{9,13},{10,... | collective-permute-start | bytes 258056 | tf_op jit(solution)/shard_map/ppermute | solution.py:607
  184.5 15.1 %collective-permute-done.41.refs_2_ = f32[56,384]{1,0:T(8,128)S(1)} collective-permute-done((f32[56,384]{1,0:T(8,128)S(1)}, f32[56,384]{1,0:T(8,128)S(1)}, u32[]{:S(2)}, u32[]{:S(2)}) %collective-permute-start.41) | collective-permute-done | bytes 86048 | tf_op jit(solution)/shard_map/ppermute | solution.py:607
  201.8 1.3 collective-permute-start.44
  203.2 1.6 collective-permute-start.45
  204.7 4.7 %collective-permute-done.27.refs_4_ = f32[400,128]{1,0:T(8,128)S(1)} collective-permute-done((f32[400,128]{1,0:T(8,128)S(1)}, f32[400,128]{1,0:T(8,128)S(1)}, u32[]{:S(2)}, u32[]{:S(2)}) %collective-permute-start.27) | collective-permute-done | bytes 204832 | tf_op jit(solution)/shard_map/ppermute | solution.py:607
  209.4 1.3 shard_map.144
  212.0 2.1 collective-permute-start.23
  215.6 1.4 collective-permute-done.44.refs_2_
  217.1 1.7 collective-permute-done.45.refs_3_
  218.8 1.1 collective-permute-done.23.refs_0_
  220.6 3.6 %collective-permute-start.24 = (f32[400,128]{1,0:T(8,128)}, f32[400,128]{1,0:T(8,128)}, u32[]{:S(2)}, u32[]{:S(2)}) collective-permute-start(f32[400,128]{1,0:T(8,128)} %get-tuple-element.94), channel_id=1, source_target_pairs={{0,7},{1,6},{2,1},{3,0},{4,3},{5,2},{6,5},{7,4},{8,15},{9,14},{10,... | collective-permute-start | bytes 614408 | tf_op jit(solution)/shard_map/ppermute | solution.py:607
  230.0 2.6 %shard_map.143 = (f32[400,512]{1,0:T(8,128)S(1)}, f32[400,512]{1,0:T(8,128)S(1)}) custom-call(bf16[1024,512]{1,0:T(8,128)(2,1)S(1)} %shard_map.130.hot_ref, bf16[1024,512]{1,0:T(8,128)(2,1)S(1)} %shard_map.131.source_hot_ref.hot_ref, f32[400,128]{1,0:T(8,128)S(1)} %copy-done.15, f32[400,512]{1,0:T(8,128)S(1)} %bitcast.32, ...), custom_call_target="tpu_custom_call" | custom-call | flops 838860800 | bytes 3276800 | tf_op jit(solution)/shard_map/pallas_call | solution.py:476
  232.7 3.0 %shard_map.145 = f32[400,512]{1,0:T(8,128)} custom-call(f32[400,512]{1,0:T(8,128)S(1)} %get-tuple-element.91.other_ref, f32[400,512]{1,0:T(8,128)S(1)} %get-tuple-element.92.entity_ref, f32[1,512]{1,0:T(1,128)S(1)} %bitcast.42, bf16[1024,512]{1,0:T(8,128)(2,1)S(1)} %shard_map.131.source_hot_ref.hot_ref, f32[400,128]{1,0:T(8,128)S(1)} %copy-done.29, ...), custom_call_target="tpu_custom_call" | custom-call | flops 838860800 | bytes 3276800 | tf_op jit(solution)/shard_map/pallas_call | solution.py:497
  235.8 3.7 %shard_map.150 = f32[400,1345]{1,0:T(8,128)} custom-call(s32[2]{0:T(128)S(1)} %pad_add_fusion.me_ref, f32[400,1345]{1,0:T(8,128)S(1)} %bitcast.28, f32[1,1345]{1,0:T(1,128)S(1)} %reshape.36.state_ref, f32[200,384]{1,0:T(8,128)S(1)} %shard_map.149.refs_0_, f32[200,384]{1,0:T(8,128)} %collective-permute-done.43.refs_1_, ...), custom_call_target="tpu_custom_call" | custom-call | flops 4304000 | bytes 6456000 | tf_op jit(solution)/shard_map/pallas_call | solution.py:598
  (191 shorter events, 28.6 us)
Async XLA Ops:
  5.9 21.4 %collective-permute-start.2 = (f32[400,128]{1,0:T(8,128)}, f32[400,128]{1,0:T(8,128)}, u32[]{:S(2)}, u32[]{:S(2)}) collective-permute-start(f32[400,128]{1,0:T(8,128)} %get-tuple-element.62), channel_id=1, source_target_pairs={{0,4},{1,5},{2,6},{3,7},{4,0},{5,1},{6,2},{7,3},{8,12},{9,13},{10,... | collective-permute-start | bytes 614408 | tf_op jit(solution)/shard_map/ppermute | solution.py:607
  10.0 23.8 %collective-permute-start.3 = (f32[400,128]{1,0:T(8,128)}, f32[400,128]{1,0:T(8,128)}, u32[]{:S(2)}, u32[]{:S(2)}) collective-permute-start(f32[400,128]{1,0:T(8,128)} %get-tuple-element.63), channel_id=1, source_target_pairs={{0,5},{1,4},{2,7},{3,6},{4,1},{5,0},{6,3},{7,2},{8,13},{9,12},{10,... | collective-permute-start | bytes 614408 | tf_op jit(solution)/shard_map/ppermute | solution.py:607
  10.0 27.7 %collective-permute-start.4 = (f32[400,128]{1,0:T(8,128)}, f32[400,128]{1,0:T(8,128)}, u32[]{:S(2)}, u32[]{:S(2)}) collective-permute-start(f32[400,128]{1,0:T(8,128)} %get-tuple-element.64), channel_id=1, source_target_pairs={{0,6},{1,7},{2,0},{3,1},{4,2},{5,3},{6,4},{7,5},{8,14},{9,15},{10,... | collective-permute-start | bytes 614408 | tf_op jit(solution)/shard_map/ppermute | solution.py:607
  13.1 30.0 %collective-permute-start.5 = (f32[400,128]{1,0:T(8,128)}, f32[400,128]{1,0:T(8,128)}, u32[]{:S(2)}, u32[]{:S(2)}) collective-permute-start(f32[400,128]{1,0:T(8,128)} %get-tuple-element.65), channel_id=1, source_target_pairs={{0,7},{1,6},{2,1},{3,0},{4,3},{5,2},{6,5},{7,4},{8,15},{9,14},{10,... | collective-permute-start | bytes 614408 | tf_op jit(solution)/shard_map/ppermute | solution.py:607
  13.8 29.2 %collective-permute-start.6 = (f32[400,128]{1,0:T(8,128)}, f32[400,128]{1,0:T(8,128)}, u32[]{:S(2)}, u32[]{:S(2)}) collective-permute-start(f32[400,128]{1,0:T(8,128)} %get-tuple-element.66), channel_id=1, source_target_pairs={{0,1},{1,0},{2,3},{3,2},{4,5},{5,4},{6,7},{7,6},{8,9},{9,8},{10,11... | collective-permute-start | bytes 614408 | tf_op jit(solution)/shard_map/ppermute | solution.py:607
  27.3 17.0 %collective-permute-start = (f32[400,128]{1,0:T(8,128)S(1)}, f32[400,128]{1,0:T(8,128)S(1)}, u32[]{:S(2)}, u32[]{:S(2)}) collective-permute-start(f32[400,128]{1,0:T(8,128)S(1)} %copy-done.44), channel_id=1, source_target_pairs={{0,2},{1,3},{2,4},{3,5},{4,6},{5,7},{6,0},{7,1},{8,10},{9,11},{10,... | collective-permute-start | bytes 614408 | tf_op jit(solution)/shard_map/ppermute | solution.py:607
  33.8 11.9 %collective-permute-start.1 = (f32[400,128]{1,0:T(8,128)S(1)}, f32[400,128]{1,0:T(8,128)S(1)}, u32[]{:S(2)}, u32[]{:S(2)}) collective-permute-start(f32[400,128]{1,0:T(8,128)S(1)} %copy-done.42), channel_id=1, source_target_pairs={{0,3},{1,2},{2,5},{3,4},{4,7},{5,6},{6,1},{7,0},{8,11},{9,10},{10,... | collective-permute-start | bytes 614408 | tf_op jit(solution)/shard_map/ppermute | solution.py:607
  37.7 18.3 %collective-permute-start.10 = (f32[400,128]{1,0:T(8,128)S(1)}, f32[400,128]{1,0:T(8,128)S(1)}, u32[]{:S(2)}, u32[]{:S(2)}) collective-permute-start(f32[400,128]{1,0:T(8,128)S(1)} %get-tuple-element.72), channel_id=1, source_target_pairs={{0,29},{1,28},{2,31},{3,30},{4,25},{5,24},{6,27},{7,26},{8,5},{9,4... | collective-permute-start | bytes 614408 | tf_op jit(solution)/shard_map/ppermute | solution.py:616
  43.0 23.1 %collective-permute-start.11 = (f32[400,128]{1,0:T(8,128)S(1)}, f32[400,128]{1,0:T(8,128)S(1)}, u32[]{:S(2)}, u32[]{:S(2)}) collective-permute-start(f32[400,128]{1,0:T(8,128)S(1)} %get-tuple-element.73), channel_id=1, source_target_pairs={{0,30},{1,31},{2,24},{3,25},{4,26},{5,27},{6,28},{7,29},{8,6},{9,7... | collective-permute-start | bytes 614408 | tf_op jit(solution)/shard_map/ppermute | solution.py:616
  43.0 23.1 %collective-permute-start.12 = (f32[400,128]{1,0:T(8,128)S(1)}, f32[400,128]{1,0:T(8,128)S(1)}, u32[]{:S(2)}, u32[]{:S(2)}) collective-permute-start(f32[400,128]{1,0:T(8,128)S(1)} %get-tuple-element.74), channel_id=1, source_target_pairs={{0,31},{1,30},{2,25},{3,24},{4,27},{5,26},{6,29},{7,28},{8,7},{9,6... | collective-permute-start | bytes 614408 | tf_op jit(solution)/shard_map/ppermute | solution.py:616
  44.3 33.7 %collective-permute-start.13 = (f32[400,128]{1,0:T(8,128)S(1)}, f32[400,128]{1,0:T(8,128)S(1)}, u32[]{:S(2)}, u32[]{:S(2)}) collective-permute-start(f32[400,128]{1,0:T(8,128)S(1)} %get-tuple-element.75), channel_id=1, source_target_pairs={{0,25},{1,24},{2,27},{3,26},{4,29},{5,28},{6,31},{7,30},{8,1},{9,0... | collective-permute-start | bytes 614408 | tf_op jit(solution)/shard_map/ppermute | solution.py:616
  45.7 32.3 %collective-permute-start.14 = (f32[400,128]{1,0:T(8,128)S(1)}, f32[400,128]{1,0:T(8,128)S(1)}, u32[]{:S(2)}, u32[]{:S(2)}) collective-permute-start(f32[400,128]{1,0:T(8,128)S(1)} %get-tuple-element.76), channel_id=1, source_target_pairs={{0,24},{1,25},{2,26},{3,27},{4,28},{5,29},{6,30},{7,31},{8,0},{9,1... | collective-permute-start | bytes 614408 | tf_op jit(solution)/shard_map/ppermute | solution.py:616
  56.0 22.0 %collective-permute-start.7 = (f32[400,128]{1,0:T(8,128)S(1)}, f32[400,128]{1,0:T(8,128)S(1)}, u32[]{:S(2)}, u32[]{:S(2)}) collective-permute-start(f32[400,128]{1,0:T(8,128)S(1)} %get-tuple-element.69), channel_id=1, source_target_pairs={{0,26},{1,27},{2,28},{3,29},{4,30},{5,31},{6,24},{7,25},{8,2},{9,3... | collective-permute-start | bytes 614408 | tf_op jit(solution)/shard_map/ppermute | solution.py:616
  66.2 11.9 %collective-permute-start.8 = (f32[400,128]{1,0:T(8,128)S(1)}, f32[400,128]{1,0:T(8,128)S(1)}, u32[]{:S(2)}, u32[]{:S(2)}) collective-permute-start(f32[400,128]{1,0:T(8,128)S(1)} %get-tuple-element.70), channel_id=1, source_target_pairs={{0,27},{1,26},{2,29},{3,28},{4,31},{5,30},{6,25},{7,24},{8,3},{9,2... | collective-permute-start | bytes 614408 | tf_op jit(solution)/shard_map/ppermute | solution.py:616
  66.2 21.2 %collective-permute-start.9 = (f32[400,128]{1,0:T(8,128)S(1)}, f32[400,128]{1,0:T(8,128)S(1)}, u32[]{:S(2)}, u32[]{:S(2)}) collective-permute-start(f32[400,128]{1,0:T(8,128)S(1)} %get-tuple-element.71), channel_id=1, source_target_pairs={{0,28},{1,29},{2,30},{3,31},{4,24},{5,25},{6,26},{7,27},{8,4},{9,5... | collective-permute-start | bytes 614408 | tf_op jit(solution)/shard_map/ppermute | solution.py:616
  104.2 2.0 collective-permute-start.31
  104.8 2.3 collective-permute-start.33
  107.2 10.2 %collective-permute-start.34 = (f32[200,384]{1,0:T(8,128)S(1)}, f32[200,384]{1,0:T(8,128)S(1)}, u32[]{:S(2)}, u32[]{:S(2)}) collective-permute-start(f32[200,384]{1,0:T(8,128)S(1)} %get-tuple-element.109), channel_id=1, source_target_pairs={{0,8},{8,0},{16,24},{24,16},{1,9},{9,1},{17,25},{25,17},{2,10},{10... | collective-permute-start | bytes 921608 | tf_op jit(solution)/shard_map/ppermute | solution.py:620
  108.8 28.8 %collective-permute-start.35 = (f32[200,384]{1,0:T(8,128)S(1)}, f32[200,384]{1,0:T(8,128)S(1)}, u32[]{:S(2)}, u32[]{:S(2)}) collective-permute-start(f32[200,384]{1,0:T(8,128)S(1)} %get-tuple-element.110), channel_id=1, source_target_pairs={{0,16},{8,24},{16,0},{24,8},{1,17},{9,25},{17,1},{25,9},{2,18},{10... | collective-permute-start | bytes 921608 | tf_op jit(solution)/shard_map/ppermute | solution.py:620
  109.3 28.3 %collective-permute-start.36 = (f32[200,384]{1,0:T(8,128)S(1)}, f32[200,384]{1,0:T(8,128)S(1)}, u32[]{:S(2)}, u32[]{:S(2)}) collective-permute-start(f32[200,384]{1,0:T(8,128)S(1)} %get-tuple-element.111), channel_id=1, source_target_pairs={{0,24},{8,16},{16,8},{24,0},{1,25},{9,17},{17,9},{25,1},{2,26},{10... | collective-permute-start | bytes 921608 | tf_op jit(solution)/shard_map/ppermute | solution.py:620
  113.5 25.2 %collective-permute-start.19 = (f32[400,128]{1,0:T(8,128)S(1)}, f32[400,128]{1,0:T(8,128)S(1)}, u32[]{:S(2)}, u32[]{:S(2)}) collective-permute-start(f32[400,128]{1,0:T(8,128)S(1)} %get-tuple-element.87), channel_id=1, source_target_pairs={{0,10},{1,11},{2,12},{3,13},{4,14},{5,15},{6,8},{7,9},{8,18},{9,19... | collective-permute-start | bytes 614408 | tf_op jit(solution)/shard_map/ppermute | solution.py:616
  113.5 32.0 %collective-permute-start.20 = (f32[400,128]{1,0:T(8,128)S(1)}, f32[400,128]{1,0:T(8,128)S(1)}, u32[]{:S(2)}, u32[]{:S(2)}) collective-permute-start(f32[400,128]{1,0:T(8,128)S(1)} %get-tuple-element.88), channel_id=1, source_target_pairs={{0,11},{1,10},{2,13},{3,12},{4,15},{5,14},{6,9},{7,8},{8,19},{9,18... | collective-permute-start | bytes 614408 | tf_op jit(solution)/shard_map/ppermute | solution.py:616
  117.4 35.7 %collective-permute-start.21 = (f32[400,128]{1,0:T(8,128)}, f32[400,128]{1,0:T(8,128)S(1)}, u32[]{:S(2)}, u32[]{:S(2)}) collective-permute-start(f32[400,128]{1,0:T(8,128)} %get-tuple-element.89), channel_id=1, source_target_pairs={{0,9},{1,8},{2,11},{3,10},{4,13},{5,12},{6,15},{7,14},{8,17},{9,16... | collective-permute-start | bytes 614408 | tf_op jit(solution)/shard_map/ppermute | solution.py:616
  138.2 8.1 %collective-permute-start.37 = (f32[56,384]{1,0:T(8,128)S(1)}, f32[56,384]{1,0:T(8,128)S(1)}, u32[]{:S(2)}, u32[]{:S(2)}) collective-permute-start(f32[56,384]{1,0:T(8,128)S(1)} %get-tuple-element.113), channel_id=1, source_target_pairs={{0,2},{1,3},{2,4},{3,5},{4,6},{5,7},{6,0},{7,1},{8,10},{9,11},{10,... | collective-permute-start | bytes 258056 | tf_op jit(solution)/shard_map/ppermute | solution.py:607
  138.3 10.0 %collective-permute-start.38 = (f32[56,384]{1,0:T(8,128)S(1)}, f32[56,384]{1,0:T(8,128)S(1)}, u32[]{:S(2)}, u32[]{:S(2)}) collective-permute-start(f32[56,384]{1,0:T(8,128)S(1)} %get-tuple-element.114), channel_id=1, source_target_pairs={{0,4},{1,5},{2,6},{3,7},{4,0},{5,1},{6,2},{7,3},{8,12},{9,13},{10,... | collective-permute-start | bytes 258056 | tf_op jit(solution)/shard_map/ppermute | solution.py:607
  138.7 9.6 %collective-permute-start.39 = (f32[56,384]{1,0:T(8,128)S(1)}, f32[56,384]{1,0:T(8,128)S(1)}, u32[]{:S(2)}, u32[]{:S(2)}) collective-permute-start(f32[56,384]{1,0:T(8,128)S(1)} %get-tuple-element.115), channel_id=1, source_target_pairs={{0,6},{1,7},{2,0},{3,1},{4,2},{5,3},{6,4},{7,5},{8,14},{9,15},{10,... | collective-permute-start | bytes 258056 | tf_op jit(solution)/shard_map/ppermute | solution.py:607
  146.2 16.4 %collective-permute-start.22 = (f32[400,128]{1,0:T(8,128)}, f32[400,128]{1,0:T(8,128)}, u32[]{:S(2)}, u32[]{:S(2)}) collective-permute-start(f32[400,128]{1,0:T(8,128)} %get-tuple-element.90), channel_id=1, source_target_pairs={{0,8},{1,9},{2,10},{3,11},{4,12},{5,13},{6,14},{7,15},{8,16},{9,17... | collective-permute-start | bytes 614408 | tf_op jit(solution)/shard_map/ppermute | solution.py:616
  146.2 16.4 %collective-permute-start.15 = (f32[400,128]{1,0:T(8,128)}, f32[400,128]{1,0:T(8,128)}, u32[]{:S(2)}, u32[]{:S(2)}) collective-permute-start(f32[400,128]{1,0:T(8,128)} %get-tuple-element.83), channel_id=1, source_target_pairs={{0,14},{1,15},{2,8},{3,9},{4,10},{5,11},{6,12},{7,13},{8,22},{9,23... | collective-permute-start | bytes 614408 | tf_op jit(solution)/shard_map/ppermute | solution.py:616
  148.3 19.6 %collective-permute-start.16 = (f32[400,128]{1,0:T(8,128)}, f32[400,128]{1,0:T(8,128)}, u32[]{:S(2)}, u32[]{:S(2)}) collective-permute-start(f32[400,128]{1,0:T(8,128)} %get-tuple-element.84), channel_id=1, source_target_pairs={{0,15},{1,14},{2,9},{3,8},{4,11},{5,10},{6,13},{7,12},{8,23},{9,22... | collective-permute-start | bytes 614408 | tf_op jit(solution)/shard_map/ppermute | solution.py:616
  149.0 32.2 %collective-permute-start.17 = (f32[400,128]{1,0:T(8,128)}, f32[400,128]{1,0:T(8,128)}, u32[]{:S(2)}, u32[]{:S(2)}) collective-permute-start(f32[400,128]{1,0:T(8,128)} %get-tuple-element.85), channel_id=1, source_target_pairs={{0,12},{1,13},{2,14},{3,15},{4,8},{5,9},{6,10},{7,11},{8,20},{9,21... | collective-permute-start | bytes 614408 | tf_op jit(solution)/shard_map/ppermute | solution.py:616
  153.2 31.3 %collective-permute-start.40 = (f32[56,384]{1,0:T(8,128)S(1)}, f32[56,384]{1,0:T(8,128)S(1)}, u32[]{:S(2)}, u32[]{:S(2)}) collective-permute-start(f32[56,384]{1,0:T(8,128)S(1)} %shard_map.148.refs_0_), channel_id=1, source_target_pairs={{0,2},{1,3},{2,4},{3,5},{4,6},{5,7},{6,0},{7,1},{8,10},{9,11},{10,... | collective-permute-start | bytes 258056 | tf_op jit(solution)/shard_map/ppermute | solution.py:607
  162.7 38.5 %collective-permute-start.18 = (f32[400,128]{1,0:T(8,128)S(1)}, f32[400,128]{1,0:T(8,128)S(1)}, u32[]{:S(2)}, u32[]{:S(2)}) collective-permute-start(f32[400,128]{1,0:T(8,128)S(1)} %copy-done.40), channel_id=1, source_target_pairs={{0,13},{1,12},{2,15},{3,14},{4,9},{5,8},{6,11},{7,10},{8,21},{9,20... | collective-permute-start | bytes 614408 | tf_op jit(solution)/shard_map/ppermute | solution.py:616
  162.7 39.2 %collective-permute-start.25 = (f32[400,128]{1,0:T(8,128)S(1)}, f32[400,128]{1,0:T(8,128)S(1)}, u32[]{:S(2)}, u32[]{:S(2)}) collective-permute-start(f32[400,128]{1,0:T(8,128)S(1)} %get-tuple-element.95), channel_id=1, source_target_pairs={{0,4},{1,5},{2,6},{3,7},{4,0},{5,1},{6,2},{7,3},{8,12},{9,13},{10,... | collective-permute-start | bytes 614408 | tf_op jit(solution)/shard_map/ppermute | solution.py:607
  167.9 35.3 %collective-permute-start.26 = (f32[400,128]{1,0:T(8,128)S(1)}, f32[400,128]{1,0:T(8,128)S(1)}, u32[]{:S(2)}, u32[]{:S(2)}) collective-permute-start(f32[400,128]{1,0:T(8,128)S(1)} %get-tuple-element.96), channel_id=1, source_target_pairs={{0,5},{1,4},{2,7},{3,6},{4,1},{5,0},{6,3},{7,2},{8,13},{9,12},{10,... | collective-permute-start | bytes 614408 | tf_op jit(solution)/shard_map/ppermute | solution.py:607
  181.2 18.5 %collective-permute-start.41 = (f32[56,384]{1,0:T(8,128)S(1)}, f32[56,384]{1,0:T(8,128)S(1)}, u32[]{:S(2)}, u32[]{:S(2)}) collective-permute-start(f32[56,384]{1,0:T(8,128)S(1)} %shard_map.148.refs_0_), channel_id=1, source_target_pairs={{0,4},{1,5},{2,6},{3,7},{4,0},{5,1},{6,2},{7,3},{8,12},{9,13},{10,... | collective-permute-start | bytes 258056 | tf_op jit(solution)/shard_map/ppermute | solution.py:607
  184.5 16.0 %collective-permute-start.42 = (f32[56,384]{1,0:T(8,128)S(1)}, f32[56,384]{1,0:T(8,128)S(1)}, u32[]{:S(2)}, u32[]{:S(2)}) collective-permute-start(f32[56,384]{1,0:T(8,128)S(1)} %shard_map.148.refs_0_), channel_id=1, source_target_pairs={{0,6},{1,7},{2,0},{3,1},{4,2},{5,3},{6,4},{7,5},{8,14},{9,15},{10,... | collective-permute-start | bytes 258056 | tf_op jit(solution)/shard_map/ppermute | solution.py:607
  199.7 9.7 %collective-permute-start.27 = (f32[400,128]{1,0:T(8,128)S(1)}, f32[400,128]{1,0:T(8,128)S(1)}, u32[]{:S(2)}, u32[]{:S(2)}) collective-permute-start(f32[400,128]{1,0:T(8,128)S(1)} %get-tuple-element.97), channel_id=1, source_target_pairs={{0,2},{1,3},{2,4},{3,5},{4,6},{5,7},{6,0},{7,1},{8,10},{9,11},{10,... | collective-permute-start | bytes 614408 | tf_op jit(solution)/shard_map/ppermute | solution.py:607
  200.5 10.8 %collective-permute-start.28 = (f32[400,128]{1,0:T(8,128)S(1)}, f32[400,128]{1,0:T(8,128)S(1)}, u32[]{:S(2)}, u32[]{:S(2)}) collective-permute-start(f32[400,128]{1,0:T(8,128)S(1)} %get-tuple-element.98), channel_id=1, source_target_pairs={{0,3},{1,2},{2,5},{3,4},{4,7},{5,6},{6,1},{7,0},{8,11},{9,10},{10,... | collective-permute-start | bytes 614408 | tf_op jit(solution)/shard_map/ppermute | solution.py:607
  201.2 14.5 %collective-permute-start.43 = (f32[200,384]{1,0:T(8,128)S(1)}, f32[200,384]{1,0:T(8,128)}, u32[]{:S(2)}, u32[]{:S(2)}) collective-permute-start(f32[200,384]{1,0:T(8,128)S(1)} %shard_map.149.refs_0_), channel_id=1, source_target_pairs={{0,8},{8,0},{16,24},{24,16},{1,9},{9,1},{17,25},{25,17},{2,10},{10... | collective-permute-start | bytes 921608 | tf_op jit(solution)/shard_map/ppermute | solution.py:620
  201.8 15.2 %collective-permute-start.44 = (f32[200,384]{1,0:T(8,128)S(1)}, f32[200,384]{1,0:T(8,128)}, u32[]{:S(2)}, u32[]{:S(2)}) collective-permute-start(f32[200,384]{1,0:T(8,128)S(1)} %shard_map.149.refs_0_), channel_id=1, source_target_pairs={{0,16},{8,24},{16,0},{24,8},{1,17},{9,25},{17,1},{25,9},{2,18},{10... | collective-permute-start | bytes 921608 | tf_op jit(solution)/shard_map/ppermute | solution.py:620
  203.2 15.6 %collective-permute-start.45 = (f32[200,384]{1,0:T(8,128)S(1)}, f32[200,384]{1,0:T(8,128)}, u32[]{:S(2)}, u32[]{:S(2)}) collective-permute-start(f32[200,384]{1,0:T(8,128)S(1)} %shard_map.149.refs_0_), channel_id=1, source_target_pairs={{0,24},{8,16},{16,8},{24,0},{1,25},{9,17},{17,9},{25,1},{2,26},{10... | collective-permute-start | bytes 921608 | tf_op jit(solution)/shard_map/ppermute | solution.py:620
  209.4 4.7 %collective-permute-start.29 = (f32[400,128]{1,0:T(8,128)S(1)}, f32[400,128]{1,0:T(8,128)S(1)}, u32[]{:S(2)}, u32[]{:S(2)}) collective-permute-start(f32[400,128]{1,0:T(8,128)S(1)} %get-tuple-element.99), channel_id=1, source_target_pairs={{0,1},{1,0},{2,3},{3,2},{4,5},{5,4},{6,7},{7,6},{8,9},{9,8},{10,11... | collective-permute-start | bytes 614408 | tf_op jit(solution)/shard_map/ppermute | solution.py:607
  212.0 7.9 %collective-permute-start.23 = (f32[400,128]{1,0:T(8,128)S(1)}, f32[400,128]{1,0:T(8,128)S(1)}, u32[]{:S(2)}, u32[]{:S(2)}) collective-permute-start(f32[400,128]{1,0:T(8,128)S(1)} %get-tuple-element.93), channel_id=1, source_target_pairs={{0,6},{1,7},{2,0},{3,1},{4,2},{5,3},{6,4},{7,5},{8,14},{9,15},{10,... | collective-permute-start | bytes 614408 | tf_op jit(solution)/shard_map/ppermute | solution.py:607
  214.8 20.9 %collective-permute-start.46 = (f32[200,384]{1,0:T(8,128)S(1)}, f32[200,384]{1,0:T(8,128)}, u32[]{:S(2)}, u32[]{:S(2)}) collective-permute-start(f32[200,384]{1,0:T(8,128)S(1)} %shard_map.149.refs_0_), channel_id=1, source_target_pairs={{0,1},{1,0},{2,3},{3,2},{4,5},{5,4},{6,7},{7,6},{8,9},{9,8},{10,11... | collective-permute-start | bytes 921608 | tf_op jit(solution)/shard_map/ppermute | solution.py:607
  215.6 20.1 %collective-permute-start.47 = (f32[200,384]{1,0:T(8,128)}, f32[200,384]{1,0:T(8,128)}, u32[]{:S(2)}, u32[]{:S(2)}) collective-permute-start(f32[200,384]{1,0:T(8,128)} %collective-permute-done.43.refs_1_), channel_id=1, source_target_pairs={{0,1},{1,0},{2,3},{3,2},{4,5},{5,4},{6,7},{7,6},{8,9},{9,8},{10,11... | collective-permute-start | bytes 921608 | tf_op jit(solution)/shard_map/ppermute | solution.py:607
  217.1 18.7 %collective-permute-start.48 = (f32[200,384]{1,0:T(8,128)}, f32[200,384]{1,0:T(8,128)}, u32[]{:S(2)}, u32[]{:S(2)}) collective-permute-start(f32[200,384]{1,0:T(8,128)} %collective-permute-done.44.refs_2_), channel_id=1, source_target_pairs={{0,1},{1,0},{2,3},{3,2},{4,5},{5,4},{6,7},{7,6},{8,9},{9,8},{10,11... | collective-permute-start | bytes 921608 | tf_op jit(solution)/shard_map/ppermute | solution.py:607
  218.8 17.0 %collective-permute-start.49 = (f32[200,384]{1,0:T(8,128)}, f32[200,384]{1,0:T(8,128)}, u32[]{:S(2)}, u32[]{:S(2)}) collective-permute-start(f32[200,384]{1,0:T(8,128)} %collective-permute-done.45.refs_3_), channel_id=1, source_target_pairs={{0,1},{1,0},{2,3},{3,2},{4,5},{5,4},{6,7},{7,6},{8,9},{9,8},{10,11... | collective-permute-start | bytes 921608 | tf_op jit(solution)/shard_map/ppermute | solution.py:607
  220.6 12.1 %collective-permute-start.24 = (f32[400,128]{1,0:T(8,128)}, f32[400,128]{1,0:T(8,128)}, u32[]{:S(2)}, u32[]{:S(2)}) collective-permute-start(f32[400,128]{1,0:T(8,128)} %get-tuple-element.94), channel_id=1, source_target_pairs={{0,7},{1,6},{2,1},{3,0},{4,3},{5,2},{6,5},{7,4},{8,15},{9,14},{10,... | collective-permute-start | bytes 614408 | tf_op jit(solution)/shard_map/ppermute | solution.py:607
  (53 other events, 495.9 us)

commit v7 on v6

--- a/solution.py
+++ b/solution.py
@@ -246,8 +246,7 @@
     sum_all = pos_weight + jnp.sum(weight, axis=1, keepdims=True)
     edge = step * score.shape[0] + lax.broadcasted_iota(I32, pos.shape, 0)
     is_live = jnp.where(edge < live, 1.0, 0.0)
-    loss = (peak - pos + jnp.log(sum_all)) * is_live
-    loss_ref[...] = jnp.broadcast_to(loss, (loss.shape[0], LANES)).T[:1]
+    loss_ref[...] = (peak - pos + jnp.log(sum_all)) * is_live
     scale = is_live / sum_all
     pos_grad = pos_weight * scale - is_live
     grad = weight * scale + jnp.where(own, pos_grad, 0.0)
@@ -312,7 +311,7 @@
     return kernel_call(
         functools.partial(score_kernel, peers),
         [
-            shape((1, edges)),
+            shape((edges, 1)),
             shape((2, edges, table_rows), BF16),
             shape((3 * features, table_rows), BF16),
         ],
@@ -325,12 +324,25 @@
             pl.BlockSpec((chunk, 1), lambda i: (before(i), 0)),
         ] + [held((features, block))] * peers,
         out_specs=[
-            pl.BlockSpec((1, chunk), lambda i: (0, before(i))),
+            pl.BlockSpec((chunk, 1), lambda i: (before(i), 0)),
             pl.BlockSpec((2, chunk, table_rows), lambda i: (0, before(i), 0)),
             held((3 * features, table_rows)),
         ],
         scratch_shapes=[pltpu.VMEM((2, chunk, table_rows), F32)],
     )(live, rows, counts, edge_target, *blocks)
+
+
+def loss_row_kernel(loss_ref, out_ref):
+    edges = loss_ref.shape[0]
+    out_ref[...] = jnp.broadcast_to(loss_ref[...], (edges, LANES)).T[:1]
+
+
+def loss_row(loss):
+    edges = loss.shape[0]
+    return kernel_call(
+        loss_row_kernel, shape((1, edges)), edges * LANES, 4 * edges * LANES,
+        in_specs=[VMEM], out_specs=VMEM,
+    )(loss)
 
 
 def table_grad_kernel(columns_ref, grad_ref, *outs):
@@ -675,7 +687,10 @@
     loss, grad, table = score_spans(
         edge_count, targets, query_lines, counts, edge_target.reshape(-1, 1)
     )
-    table_parts = table_grads(query_columns, grad, block, 0, early)
+    far = early - 2
+    far_parts = table_grads(query_columns, grad, block, far, 2)
+    table_parts = table_grads(query_columns, grad, block, 0, far)
+    table_parts += far_parts
     table_parts += table_grads(query_columns, grad, block, early, peers - early)
     back = [(-hop[0], hop[1]) for hop in ways]
     home = []
@@ -696,7 +711,7 @@
     entity_new = entity_update(
         source_hots, returned[:-1], target_part, entity_t, entity_state.reshape(1, -1)
     )
-    return entity_new.T, relation_new.T, loss.reshape(-1)
+    return entity_new.T, relation_new.T, loss_row(loss).reshape(-1)
 
 
 def solution(mesh):

time: 240 us -> 237 us (0.988)
  waiting for transfers between devices: 86 us -> 64.9 us
  starting transfers between devices: 76.6 us -> 91.8 us
    ppermute x28, starting transfers between devices: 40.2 us -> 52.2 us  [sent_on(): lax.ppermute(value, 'shard', [(i, partner(i, hop, peers, 1)) for i in ran...]
    ppermute x16, waiting for transfers between devices: 34.9 us -> 24.3 us  [sent_across(): return lax.ppermute(value, ('group', 'shard'), pairs)]
    ppermute x28, waiting for transfers between devices: 24 us -> 15.9 us  [sent_on(): lax.ppermute(value, 'shard', [(i, partner(i, hop, peers, 1)) for i in ran...]
    ppermute x16, starting transfers between devices: 29.3 us -> 32.4 us  [sent_across(): return lax.ppermute(value, ('group', 'shard'), pairs)]
    unnamed x102 -> x106, local copies, waits for them, and re-layouts: 14.1 us -> 16.1 us
    pallas_call x1 -> x2, Pallas kernels: 7.54 us -> 7.94 us  [the longest x1 7.02 us: score_spans(): kernel_call(functools.partial(score_kernel, peers), [shape((edges, 1)), s...]
    pallas_call x2 -> x3, Pallas kernels: 5.53 us -> 5.81 us  [table_grads(): kernel_call(table_grad_kernel, [shape((features, block))] * count, 6 * fe...]
  transfers between devices with their start and end apart: 50 -> 50, of which waited for: 17 -> 16; matrix products, arithmetic and copies ran while one was open for 1% -> 1% of each run, Pallas kernels for 14% -> 15%
where the time goes in v7:
time: 237 us; the launch traced here: 236 us
  starting transfers between devices  91.8 us (39%)
  waiting for transfers between devices  64.9 us (27%)
  Pallas kernels  57.8 us (24%)
  local copies, waits for them, and re-layouts  19.4 us (8%)
    ppermute x28, starting transfers between devices, sent_on(): lax.ppermute(value, 'shard', [(i, partner(i, hop, peers, 1)) for i in ran...  52.2 us
    ppermute x16, starting transfers between devices, sent_across(): return lax.ppermute(value, ('group', 'shard'), pairs)  32.4 us
    ppermute x6, waiting for transfers between devices, sent_group(): return lax.ppermute(value, 'group', [(g, g ^ bit) for g in range(groups)])  24.8 us
    ppermute x16, waiting for transfers between devices, sent_across(): return lax.ppermute(value, ('group', 'shard'), pairs)  24.3 us
    unnamed x106, local copies, waits for them, and re-layouts  16.1 us
    ppermute x28, waiting for transfers between devices, sent_on(): lax.ppermute(value, 'shard', [(i, partner(i, hop, peers, 1)) for i in ran...  15.9 us
    pallas_call x1, Pallas kernels, relation_grads(): kernel_call(functools.partial(relation_grad_kernel, steps), [shape((2, fe...  9.17 us
    pallas_call x1, Pallas kernels, query_rows(): kernel_call(query_kernel, [shape((features, edges)), shape((2, features,...  7.25 us
  transfers between devices with their start and end apart: 50, of which 16 were waited for; matrix products, arithmetic and copies ran while one was open for 1% of the time, Pallas kernels for 15%

profile of v7, /device:TPU:0, one launch (start us, length us, event | category | flops | bytes accessed | tf_op | source)
XLA Modules:
  0.0 236.2 jit_solution(14122094231395013596)
XLA Ops:
  2.7 2.6 %shard_map.134 = (f32[400,128]{1,0:T(8,128)}, f32[400,128]{1,0:T(8,128)}, f32[400,128]{1,0:T(8,128)}, f32[400,128]{1,0:T(8,128)}, f32[400,128]{1,0:T(8,128)}, /*index=5*/f32[400,128]{1,0:T(8,128)S(1)}) custom-call(s32[6]{0:T(128)S(1)} %stack.53.order_ref, f32[400,512]{1,0:T(8,128)S(1)} %bitcast.29, s32[8,128]{1,0:T(8,128)S(1)} %bitcast.39), custom_call_target="tpu_custom_call" | custom-call | flops 943718400 | bytes 2457600 | tf_op jit(solution)/shard_map/pallas_call | solution.py:126
  5.9 4.1 %collective-permute-start.2 = (f32[400,128]{1,0:T(8,128)}, f32[400,128]{1,0:T(8,128)}, u32[]{:S(2)}, u32[]{:S(2)}) collective-permute-start(f32[400,128]{1,0:T(8,128)} %get-tuple-element.62), channel_id=1, source_target_pairs={{0,4},{1,5},{2,6},{3,7},{4,0},{5,1},{6,2},{7,3},{8,12},{9,13},{10,... | collective-permute-start | bytes 614408 | tf_op jit(solution)/shard_map/ppermute | solution.py:619
  10.0 3.1 %collective-permute-start.4 = (f32[400,128]{1,0:T(8,128)}, f32[400,128]{1,0:T(8,128)}, u32[]{:S(2)}, u32[]{:S(2)}) collective-permute-start(f32[400,128]{1,0:T(8,128)} %get-tuple-element.64), channel_id=1, source_target_pairs={{0,6},{1,7},{2,0},{3,1},{4,2},{5,3},{6,4},{7,5},{8,14},{9,15},{10,... | collective-permute-start | bytes 614408 | tf_op jit(solution)/shard_map/ppermute | solution.py:619
  19.9 5.3 %shard_map.132.refs_1_.rels_ref = f32[400,1024]{1,0:T(8,128)S(1)} custom-call(f32[400,1345]{1,0:T(8,128)S(1)} %bitcast.27, s32[1,1024]{1,0:T(1,128)S(1)} %bitcast.36), custom_call_target="tpu_custom_call" | custom-call | flops 3460300800 | bytes 3276800 | tf_op jit(solution)/shard_map/pallas_call | solution.py:153
  25.2 2.0 shard_map.137
  27.3 6.4 %collective-permute-start = (f32[400,128]{1,0:T(8,128)S(1)}, f32[400,128]{1,0:T(8,128)S(1)}, u32[]{:S(2)}, u32[]{:S(2)}) collective-permute-start(f32[400,128]{1,0:T(8,128)S(1)} %copy-done.46), channel_id=1, source_target_pairs={{0,2},{1,3},{2,4},{3,5},{4,6},{5,7},{6,0},{7,1},{8,10},{9,11},{10,... | collective-permute-start | bytes 614408 | tf_op jit(solution)/shard_map/ppermute | solution.py:619
  33.7 3.9 %collective-permute-start.1 = (f32[400,128]{1,0:T(8,128)S(1)}, f32[400,128]{1,0:T(8,128)S(1)}, u32[]{:S(2)}, u32[]{:S(2)}) collective-permute-start(f32[400,128]{1,0:T(8,128)S(1)} %copy-done.44), channel_id=1, source_target_pairs={{0,3},{1,2},{2,5},{3,4},{4,7},{5,6},{6,1},{7,0},{8,11},{9,10},{10,... | collective-permute-start | bytes 614408 | tf_op jit(solution)/shard_map/ppermute | solution.py:619
  37.6 5.4 %collective-permute-start.10 = (f32[400,128]{1,0:T(8,128)S(1)}, f32[400,128]{1,0:T(8,128)S(1)}, u32[]{:S(2)}, u32[]{:S(2)}) collective-permute-start(f32[400,128]{1,0:T(8,128)S(1)} %get-tuple-element.72), channel_id=1, source_target_pairs={{0,29},{1,28},{2,31},{3,30},{4,25},{5,24},{6,27},{7,26},{8,5},{9,4... | collective-permute-start | bytes 614408 | tf_op jit(solution)/shard_map/ppermute | solution.py:628
  44.3 1.4 collective-permute-start.13
  45.7 2.4 %collective-permute-start.14 = (f32[400,128]{1,0:T(8,128)S(1)}, f32[400,128]{1,0:T(8,128)S(1)}, u32[]{:S(2)}, u32[]{:S(2)}) collective-permute-start(f32[400,128]{1,0:T(8,128)S(1)} %get-tuple-element.76), channel_id=1, source_target_pairs={{0,24},{1,25},{2,26},{3,27},{4,28},{5,29},{6,30},{7,31},{8,0},{9,1... | collective-permute-start | bytes 614408 | tf_op jit(solution)/shard_map/ppermute | solution.py:628
  48.1 7.9 %collective-permute-done.10.refs_7_ = f32[400,128]{1,0:T(8,128)S(1)} collective-permute-done((f32[400,128]{1,0:T(8,128)S(1)}, f32[400,128]{1,0:T(8,128)S(1)}, u32[]{:S(2)}, u32[]{:S(2)}) %collective-permute-start.10) | collective-permute-done | bytes 204832 | tf_op jit(solution)/shard_map/ppermute | solution.py:628
  55.9 10.2 %collective-permute-start.7 = (f32[400,128]{1,0:T(8,128)S(1)}, f32[400,128]{1,0:T(8,128)S(1)}, u32[]{:S(2)}, u32[]{:S(2)}) collective-permute-start(f32[400,128]{1,0:T(8,128)S(1)} %get-tuple-element.69), channel_id=1, source_target_pairs={{0,26},{1,27},{2,28},{3,29},{4,30},{5,31},{6,24},{7,25},{8,2},{9,3... | collective-permute-start | bytes 614408 | tf_op jit(solution)/shard_map/ppermute | solution.py:628
  66.1 4.5 %collective-permute-start.9 = (f32[400,128]{1,0:T(8,128)S(1)}, f32[400,128]{1,0:T(8,128)S(1)}, u32[]{:S(2)}, u32[]{:S(2)}) collective-permute-start(f32[400,128]{1,0:T(8,128)S(1)} %get-tuple-element.71), channel_id=1, source_target_pairs={{0,28},{1,29},{2,30},{3,31},{4,24},{5,25},{6,26},{7,27},{8,4},{9,5... | collective-permute-start | bytes 614408 | tf_op jit(solution)/shard_map/ppermute | solution.py:628
  70.7 7.3 %shard_map.135 = (f32[400,1024]{1,0:T(8,128)S(1)}, bf16[2,400,1024]{2,1,0:T(8,128)(2,1)S(1)}, bf16[1024,1200]{1,0:T(8,128)(2,1)S(1)}) custom-call(s32[1,1024]{1,0:T(1,128)S(1)} %bitcast.33, f32[400,1024]{1,0:T(8,128)S(1)} %shard_map.132.refs_1_.rels_ref, f32[400,128]{1,0:T(8,128)S(1)} %collective-permute-done.refs_2_, ...), custom_call_target="tpu_custom_call" | custom-call | flops 2516582400 | bytes 8192000 | tf_op jit(solution)/shard_map/pallas_call | solution.py:221
  78.0 9.4 %collective-permute-done.9.refs_6_ = f32[400,128]{1,0:T(8,128)S(1)} collective-permute-done((f32[400,128]{1,0:T(8,128)S(1)}, f32[400,128]{1,0:T(8,128)S(1)}, u32[]{:S(2)}, u32[]{:S(2)}) %collective-permute-start.9) | collective-permute-done | bytes 204832 | tf_op jit(solution)/shard_map/ppermute | solution.py:628
  87.3 7.0 %shard_map.138 = (f32[1024,1]{1,0:T(8,128)S(1)}, bf16[2,1024,1024]{2,1,0:T(8,128)(2,1)S(1)}, bf16[1200,1024]{1,0:T(8,128)(2,1)S(1)}) custom-call(s32[1]{0:T(128)S(6)} %copy.21.refs_0_, bf16[1024,1200]{1,0:T(8,128)(2,1)S(1)} %get-tuple-element.68.refs_1_, f32[2,1,1024]{2,1,0:T(1,128)S(1)} %shard_map.136.refs_2_, s32[1024,1]{1,0:T(8,128)S(1)} %copy-done.11, ...), custom_call_target="tpu_custom_call" | custom-call | flops 2516582400 | bytes 12288000 | tf_op jit(solution)/shard_map/pallas_call | solution.py:311
  95.2 9.2 %shard_map.139 = (bf16[2,400,1024]{2,1,0:T(8,128)(2,1)S(1)}, f32[200,384]{1,0:T(8,128)S(1)}, f32[200,384]{1,0:T(8,128)S(1)}, f32[200,384]{1,0:T(8,128)S(1)}, f32...) custom-call(s32[2]{0:T(128)S(1)} %pad_add_fusion.me_ref, ...), custom_call_target="tpu_custom_call" | custom-call | flops 4194304000 | bytes 12288000 | tf_op jit(solution)/shard_map/pallas_call | solution.py:428
  107.5 1.6 collective-permute-start.34
  109.6 1.5 collective-permute-start.36
  111.0 2.7 %shard_map.143 = (f32[400,128]{1,0:T(8,128)S(1)}, f32[400,128]{1,0:T(8,128)S(1)}, f32[400,128]{1,0:T(8,128)}, f32[400,128]{1,0:T(8,128)}) custom-call(bf16[2,400,1024]{2,1,0:T(8,128)(2,1)S(1)} %get-tuple-element.82.columns_ref, bf16[2,1024,1024]{2,1,0:T(8,128)(2,1)S(1)} %get-tuple-element.78.grad_ref), custom_call_target="tpu_custom_call" | custom-call | flops 1258291200 | bytes 3735552 | tf_op jit(solution)/shard_map/pallas_call | solution.py:365
  113.8 3.9 %collective-permute-done.34.refs_1_ = f32[200,384]{1,0:T(8,128)S(1)} collective-permute-done((f32[200,384]{1,0:T(8,128)S(1)}, f32[200,384]{1,0:T(8,128)S(1)}, u32[]{:S(2)}, u32[]{:S(2)}) %collective-permute-start.34) | collective-permute-done | bytes 307232 | tf_op jit(solution)/shard_map/ppermute | solution.py:632
  117.7 15.7 %collective-permute-done.35.refs_2_ = f32[200,384]{1,0:T(8,128)S(1)} collective-permute-done((f32[200,384]{1,0:T(8,128)S(1)}, f32[200,384]{1,0:T(8,128)S(1)}, u32[]{:S(2)}, u32[]{:S(2)}) %collective-permute-start.35) | collective-permute-done | bytes 307232 | tf_op jit(solution)/shard_map/ppermute | solution.py:632
  134.6 3.4 %collective-permute-start.39 = (f32[56,384]{1,0:T(8,128)S(1)}, f32[56,384]{1,0:T(8,128)S(1)}, u32[]{:S(2)}, u32[]{:S(2)}) collective-permute-start(f32[56,384]{1,0:T(8,128)S(1)} %get-tuple-element.115), channel_id=1, source_target_pairs={{0,6},{1,7},{2,0},{3,1},{4,2},{5,3},{6,4},{7,5},{8,14},{9,15},{10,... | collective-permute-start | bytes 258056 | tf_op jit(solution)/shard_map/ppermute | solution.py:619
  138.0 1.6 shard_map.142
  139.9 1.4 collective-permute-done.37.refs_1_
  141.3 1.7 collective-permute-start.17
  143.0 2.2 collective-permute-start.18
  145.2 1.5 shard_map.141
  151.9 1.4 copy-done.3
  153.4 2.1 shard_map.140
  155.5 2.5 %collective-permute-start.16 = (f32[400,128]{1,0:T(8,128)S(1)}, f32[400,128]{1,0:T(8,128)S(1)}, u32[]{:S(2)}, u32[]{:S(2)}) collective-permute-start(f32[400,128]{1,0:T(8,128)S(1)} %copy-done.42), channel_id=1, source_target_pairs={{0,15},{1,14},{2,9},{3,8},{4,11},{5,10},{6,13},{7,12},{8,23},{9,22... | collective-permute-start | bytes 614408 | tf_op jit(solution)/shard_map/ppermute | solution.py:628
  158.1 1.7 collective-permute-done.17.refs_2_
  159.7 3.4 %collective-permute-start.25 = (f32[400,128]{1,0:T(8,128)S(1)}, f32[400,128]{1,0:T(8,128)S(1)}, u32[]{:S(2)}, u32[]{:S(2)}) collective-permute-start(f32[400,128]{1,0:T(8,128)S(1)} %get-tuple-element.95), channel_id=1, source_target_pairs={{0,4},{1,5},{2,6},{3,7},{4,0},{5,1},{6,2},{7,3},{8,12},{9,13},{10,... | collective-permute-start | bytes 614408 | tf_op jit(solution)/shard_map/ppermute | solution.py:619
  163.1 2.6 %collective-permute-done.18.refs_3_ = f32[400,128]{1,0:T(8,128)} collective-permute-done((f32[400,128]{1,0:T(8,128)}, f32[400,128]{1,0:T(8,128)}, u32[]{:S(2)}, u32[]{:S(2)}) %collective-permute-start.18) | collective-permute-done | bytes 204832 | tf_op jit(solution)/shard_map/ppermute | solution.py:628
  165.8 2.7 %collective-permute-done.15.refs_0_ = f32[400,128]{1,0:T(8,128)} collective-permute-done((f32[400,128]{1,0:T(8,128)}, f32[400,128]{1,0:T(8,128)}, u32[]{:S(2)}, u32[]{:S(2)}) %collective-permute-start.15) | collective-permute-done | bytes 204832 | tf_op jit(solution)/shard_map/ppermute | solution.py:628
  168.5 2.7 %collective-permute-start.41 = (f32[56,384]{1,0:T(8,128)S(1)}, f32[56,384]{1,0:T(8,128)S(1)}, u32[]{:S(2)}, u32[]{:S(2)}) collective-permute-start(f32[56,384]{1,0:T(8,128)S(1)} %shard_map.149.refs_0_), channel_id=1, source_target_pairs={{0,4},{1,5},{2,6},{3,7},{4,0},{5,1},{6,2},{7,3},{8,12},{9,13},{10,... | collective-permute-start | bytes 258056 | tf_op jit(solution)/shard_map/ppermute | solution.py:619
  171.2 15.7 %collective-permute-start.42 = (f32[56,384]{1,0:T(8,128)S(1)}, f32[56,384]{1,0:T(8,128)S(1)}, u32[]{:S(2)}, u32[]{:S(2)}) collective-permute-start(f32[56,384]{1,0:T(8,128)S(1)} %shard_map.149.refs_0_), channel_id=1, source_target_pairs={{0,6},{1,7},{2,0},{3,1},{4,2},{5,3},{6,4},{7,5},{8,14},{9,15},{10,... | collective-permute-start | bytes 258056 | tf_op jit(solution)/shard_map/ppermute | solution.py:619
  186.9 8.3 %collective-permute-done.41.refs_2_ = f32[56,384]{1,0:T(8,128)S(1)} collective-permute-done((f32[56,384]{1,0:T(8,128)S(1)}, f32[56,384]{1,0:T(8,128)S(1)}, u32[]{:S(2)}, u32[]{:S(2)}) %collective-permute-start.41) | collective-permute-done | bytes 86048 | tf_op jit(solution)/shard_map/ppermute | solution.py:619
  195.2 1.6 collective-permute-start.28
  197.4 1.7 collective-permute-start.43
  199.6 1.4 collective-permute-start.45
  201.0 3.9 %collective-permute-done.27.refs_4_ = f32[400,128]{1,0:T(8,128)S(1)} collective-permute-done((f32[400,128]{1,0:T(8,128)S(1)}, f32[400,128]{1,0:T(8,128)S(1)}, u32[]{:S(2)}, u32[]{:S(2)}) %collective-permute-start.27) | collective-permute-done | bytes 204832 | tf_op jit(solution)/shard_map/ppermute | solution.py:619
  204.9 1.3 shard_map.145
  210.0 5.1 %collective-permute-done.44.refs_2_ = f32[200,384]{1,0:T(8,128)} collective-permute-done((f32[200,384]{1,0:T(8,128)S(1)}, f32[200,384]{1,0:T(8,128)}, u32[]{:S(2)}, u32[]{:S(2)}) %collective-permute-start.44) | collective-permute-done | bytes 307232 | tf_op jit(solution)/shard_map/ppermute | solution.py:632
  216.4 1.8 collective-permute-start.24
  226.8 2.6 %shard_map.144 = (f32[400,512]{1,0:T(8,128)S(1)}, f32[400,512]{1,0:T(8,128)S(1)}) custom-call(bf16[1024,512]{1,0:T(8,128)(2,1)S(1)} %shard_map.130.hot_ref, bf16[1024,512]{1,0:T(8,128)(2,1)S(1)} %shard_map.131.source_hot_ref.hot_ref, f32[400,128]{1,0:T(8,128)S(1)} %copy-done.17, f32[400,512]{1,0:T(8,128)S(1)} %bitcast.32, ...), custom_call_target="tpu_custom_call" | custom-call | flops 838860800 | bytes 3276800 | tf_op jit(solution)/shard_map/pallas_call | solution.py:488
  229.5 3.0 %shard_map.146 = f32[400,512]{1,0:T(8,128)} custom-call(f32[400,512]{1,0:T(8,128)S(1)} %get-tuple-element.91.other_ref, f32[400,512]{1,0:T(8,128)S(1)} %get-tuple-element.92.entity_ref, f32[1,512]{1,0:T(1,128)S(1)} %bitcast.42, bf16[1024,512]{1,0:T(8,128)(2,1)S(1)} %shard_map.131.source_hot_ref.hot_ref, f32[400,128]{1,0:T(8,128)S(1)} %copy-done.31, ...), custom_call_target="tpu_custom_call" | custom-call | flops 838860800 | bytes 3276800 | tf_op jit(solution)/shard_map/pallas_call | solution.py:509
  232.5 3.7 %shard_map.151 = f32[400,1345]{1,0:T(8,128)} custom-call(s32[2]{0:T(128)S(1)} %pad_add_fusion.me_ref, f32[400,1345]{1,0:T(8,128)S(1)} %bitcast.28, f32[1,1345]{1,0:T(1,128)S(1)} %reshape.36.state_ref, f32[200,384]{1,0:T(8,128)S(1)} %shard_map.150.refs_0_, f32[200,384]{1,0:T(8,128)} %collective-permute-done.43.refs_1_, ...), custom_call_target="tpu_custom_call" | custom-call | flops 4304000 | bytes 6456000 | tf_op jit(solution)/shard_map/pallas_call | solution.py:610
  (197 shorter events, 35.8 us)
Async XLA Ops:
  5.9 21.4 %collective-permute-start.2 = (f32[400,128]{1,0:T(8,128)}, f32[400,128]{1,0:T(8,128)}, u32[]{:S(2)}, u32[]{:S(2)}) collective-permute-start(f32[400,128]{1,0:T(8,128)} %get-tuple-element.62), channel_id=1, source_target_pairs={{0,4},{1,5},{2,6},{3,7},{4,0},{5,1},{6,2},{7,3},{8,12},{9,13},{10,... | collective-permute-start | bytes 614408 | tf_op jit(solution)/shard_map/ppermute | solution.py:619
  10.0 23.8 %collective-permute-start.3 = (f32[400,128]{1,0:T(8,128)}, f32[400,128]{1,0:T(8,128)}, u32[]{:S(2)}, u32[]{:S(2)}) collective-permute-start(f32[400,128]{1,0:T(8,128)} %get-tuple-element.63), channel_id=1, source_target_pairs={{0,5},{1,4},{2,7},{3,6},{4,1},{5,0},{6,3},{7,2},{8,13},{9,12},{10,... | collective-permute-start | bytes 614408 | tf_op jit(solution)/shard_map/ppermute | solution.py:619
  10.0 27.7 %collective-permute-start.4 = (f32[400,128]{1,0:T(8,128)}, f32[400,128]{1,0:T(8,128)}, u32[]{:S(2)}, u32[]{:S(2)}) collective-permute-start(f32[400,128]{1,0:T(8,128)} %get-tuple-element.64), channel_id=1, source_target_pairs={{0,6},{1,7},{2,0},{3,1},{4,2},{5,3},{6,4},{7,5},{8,14},{9,15},{10,... | collective-permute-start | bytes 614408 | tf_op jit(solution)/shard_map/ppermute | solution.py:619
  13.0 30.0 %collective-permute-start.5 = (f32[400,128]{1,0:T(8,128)}, f32[400,128]{1,0:T(8,128)}, u32[]{:S(2)}, u32[]{:S(2)}) collective-permute-start(f32[400,128]{1,0:T(8,128)} %get-tuple-element.65), channel_id=1, source_target_pairs={{0,7},{1,6},{2,1},{3,0},{4,3},{5,2},{6,5},{7,4},{8,15},{9,14},{10,... | collective-permute-start | bytes 614408 | tf_op jit(solution)/shard_map/ppermute | solution.py:619
  13.8 29.2 %collective-permute-start.6 = (f32[400,128]{1,0:T(8,128)}, f32[400,128]{1,0:T(8,128)}, u32[]{:S(2)}, u32[]{:S(2)}) collective-permute-start(f32[400,128]{1,0:T(8,128)} %get-tuple-element.66), channel_id=1, source_target_pairs={{0,1},{1,0},{2,3},{3,2},{4,5},{5,4},{6,7},{7,6},{8,9},{9,8},{10,11... | collective-permute-start | bytes 614408 | tf_op jit(solution)/shard_map/ppermute | solution.py:619
  27.3 16.9 %collective-permute-start = (f32[400,128]{1,0:T(8,128)S(1)}, f32[400,128]{1,0:T(8,128)S(1)}, u32[]{:S(2)}, u32[]{:S(2)}) collective-permute-start(f32[400,128]{1,0:T(8,128)S(1)} %copy-done.46), channel_id=1, source_target_pairs={{0,2},{1,3},{2,4},{3,5},{4,6},{5,7},{6,0},{7,1},{8,10},{9,11},{10,... | collective-permute-start | bytes 614408 | tf_op jit(solution)/shard_map/ppermute | solution.py:619
  33.7 12.0 %collective-permute-start.1 = (f32[400,128]{1,0:T(8,128)S(1)}, f32[400,128]{1,0:T(8,128)S(1)}, u32[]{:S(2)}, u32[]{:S(2)}) collective-permute-start(f32[400,128]{1,0:T(8,128)S(1)} %copy-done.44), channel_id=1, source_target_pairs={{0,3},{1,2},{2,5},{3,4},{4,7},{5,6},{6,1},{7,0},{8,11},{9,10},{10,... | collective-permute-start | bytes 614408 | tf_op jit(solution)/shard_map/ppermute | solution.py:619
  37.6 18.3 %collective-permute-start.10 = (f32[400,128]{1,0:T(8,128)S(1)}, f32[400,128]{1,0:T(8,128)S(1)}, u32[]{:S(2)}, u32[]{:S(2)}) collective-permute-start(f32[400,128]{1,0:T(8,128)S(1)} %get-tuple-element.72), channel_id=1, source_target_pairs={{0,29},{1,28},{2,31},{3,30},{4,25},{5,24},{6,27},{7,26},{8,5},{9,4... | collective-permute-start | bytes 614408 | tf_op jit(solution)/shard_map/ppermute | solution.py:628
  43.0 23.1 %collective-permute-start.11 = (f32[400,128]{1,0:T(8,128)S(1)}, f32[400,128]{1,0:T(8,128)S(1)}, u32[]{:S(2)}, u32[]{:S(2)}) collective-permute-start(f32[400,128]{1,0:T(8,128)S(1)} %get-tuple-element.73), channel_id=1, source_target_pairs={{0,30},{1,31},{2,24},{3,25},{4,26},{5,27},{6,28},{7,29},{8,6},{9,7... | collective-permute-start | bytes 614408 | tf_op jit(solution)/shard_map/ppermute | solution.py:628
  43.0 23.1 %collective-permute-start.12 = (f32[400,128]{1,0:T(8,128)S(1)}, f32[400,128]{1,0:T(8,128)S(1)}, u32[]{:S(2)}, u32[]{:S(2)}) collective-permute-start(f32[400,128]{1,0:T(8,128)S(1)} %get-tuple-element.74), channel_id=1, source_target_pairs={{0,31},{1,30},{2,25},{3,24},{4,27},{5,26},{6,29},{7,28},{8,7},{9,6... | collective-permute-start | bytes 614408 | tf_op jit(solution)/shard_map/ppermute | solution.py:628
  44.3 33.7 %collective-permute-start.13 = (f32[400,128]{1,0:T(8,128)S(1)}, f32[400,128]{1,0:T(8,128)S(1)}, u32[]{:S(2)}, u32[]{:S(2)}) collective-permute-start(f32[400,128]{1,0:T(8,128)S(1)} %get-tuple-element.75), channel_id=1, source_target_pairs={{0,25},{1,24},{2,27},{3,26},{4,29},{5,28},{6,31},{7,30},{8,1},{9,0... | collective-permute-start | bytes 614408 | tf_op jit(solution)/shard_map/ppermute | solution.py:628
  45.7 32.3 %collective-permute-start.14 = (f32[400,128]{1,0:T(8,128)S(1)}, f32[400,128]{1,0:T(8,128)S(1)}, u32[]{:S(2)}, u32[]{:S(2)}) collective-permute-start(f32[400,128]{1,0:T(8,128)S(1)} %get-tuple-element.76), channel_id=1, source_target_pairs={{0,24},{1,25},{2,26},{3,27},{4,28},{5,29},{6,30},{7,31},{8,0},{9,1... | collective-permute-start | bytes 614408 | tf_op jit(solution)/shard_map/ppermute | solution.py:628
  55.9 22.0 %collective-permute-start.7 = (f32[400,128]{1,0:T(8,128)S(1)}, f32[400,128]{1,0:T(8,128)S(1)}, u32[]{:S(2)}, u32[]{:S(2)}) collective-permute-start(f32[400,128]{1,0:T(8,128)S(1)} %get-tuple-element.69), channel_id=1, source_target_pairs={{0,26},{1,27},{2,28},{3,29},{4,30},{5,31},{6,24},{7,25},{8,2},{9,3... | collective-permute-start | bytes 614408 | tf_op jit(solution)/shard_map/ppermute | solution.py:628
  66.1 11.8 %collective-permute-start.8 = (f32[400,128]{1,0:T(8,128)S(1)}, f32[400,128]{1,0:T(8,128)S(1)}, u32[]{:S(2)}, u32[]{:S(2)}) collective-permute-start(f32[400,128]{1,0:T(8,128)S(1)} %get-tuple-element.70), channel_id=1, source_target_pairs={{0,27},{1,26},{2,29},{3,28},{4,31},{5,30},{6,25},{7,24},{8,3},{9,2... | collective-permute-start | bytes 614408 | tf_op jit(solution)/shard_map/ppermute | solution.py:628
  66.1 21.2 %collective-permute-start.9 = (f32[400,128]{1,0:T(8,128)S(1)}, f32[400,128]{1,0:T(8,128)S(1)}, u32[]{:S(2)}, u32[]{:S(2)}) collective-permute-start(f32[400,128]{1,0:T(8,128)S(1)} %get-tuple-element.71), channel_id=1, source_target_pairs={{0,28},{1,29},{2,30},{3,31},{4,24},{5,25},{6,26},{7,27},{8,4},{9,5... | collective-permute-start | bytes 614408 | tf_op jit(solution)/shard_map/ppermute | solution.py:628
  104.5 2.0 collective-permute-start.31
  105.0 2.3 collective-permute-start.33
  107.5 10.2 %collective-permute-start.34 = (f32[200,384]{1,0:T(8,128)S(1)}, f32[200,384]{1,0:T(8,128)S(1)}, u32[]{:S(2)}, u32[]{:S(2)}) collective-permute-start(f32[200,384]{1,0:T(8,128)S(1)} %get-tuple-element.109), channel_id=1, source_target_pairs={{0,8},{8,0},{16,24},{24,16},{1,9},{9,1},{17,25},{25,17},{2,10},{10... | collective-permute-start | bytes 921608 | tf_op jit(solution)/shard_map/ppermute | solution.py:632
  109.1 24.4 %collective-permute-start.35 = (f32[200,384]{1,0:T(8,128)S(1)}, f32[200,384]{1,0:T(8,128)S(1)}, u32[]{:S(2)}, u32[]{:S(2)}) collective-permute-start(f32[200,384]{1,0:T(8,128)S(1)} %get-tuple-element.110), channel_id=1, source_target_pairs={{0,16},{8,24},{16,0},{24,8},{1,17},{9,25},{17,1},{25,9},{2,18},{10... | collective-permute-start | bytes 921608 | tf_op jit(solution)/shard_map/ppermute | solution.py:632
  109.6 23.9 %collective-permute-start.36 = (f32[200,384]{1,0:T(8,128)S(1)}, f32[200,384]{1,0:T(8,128)S(1)}, u32[]{:S(2)}, u32[]{:S(2)}) collective-permute-start(f32[200,384]{1,0:T(8,128)S(1)} %get-tuple-element.111), channel_id=1, source_target_pairs={{0,24},{8,16},{16,8},{24,0},{1,25},{9,17},{17,9},{25,1},{2,26},{10... | collective-permute-start | bytes 921608 | tf_op jit(solution)/shard_map/ppermute | solution.py:632
  113.8 20.9 %collective-permute-start.19 = (f32[400,128]{1,0:T(8,128)S(1)}, f32[400,128]{1,0:T(8,128)S(1)}, u32[]{:S(2)}, u32[]{:S(2)}) collective-permute-start(f32[400,128]{1,0:T(8,128)S(1)} %get-tuple-element.87), channel_id=1, source_target_pairs={{0,10},{1,11},{2,12},{3,13},{4,14},{5,15},{6,8},{7,9},{8,18},{9,19... | collective-permute-start | bytes 614408 | tf_op jit(solution)/shard_map/ppermute | solution.py:628
  113.8 25.8 %collective-permute-start.20 = (f32[400,128]{1,0:T(8,128)S(1)}, f32[400,128]{1,0:T(8,128)S(1)}, u32[]{:S(2)}, u32[]{:S(2)}) collective-permute-start(f32[400,128]{1,0:T(8,128)S(1)} %get-tuple-element.88), channel_id=1, source_target_pairs={{0,11},{1,10},{2,13},{3,12},{4,15},{5,14},{6,9},{7,8},{8,19},{9,18... | collective-permute-start | bytes 614408 | tf_op jit(solution)/shard_map/ppermute | solution.py:628
  134.1 7.2 %collective-permute-start.37 = (f32[56,384]{1,0:T(8,128)S(1)}, f32[56,384]{1,0:T(8,128)S(1)}, u32[]{:S(2)}, u32[]{:S(2)}) collective-permute-start(f32[56,384]{1,0:T(8,128)S(1)} %get-tuple-element.113), channel_id=1, source_target_pairs={{0,2},{1,3},{2,4},{3,5},{4,6},{5,7},{6,0},{7,1},{8,10},{9,11},{10,... | collective-permute-start | bytes 258056 | tf_op jit(solution)/shard_map/ppermute | solution.py:619
  134.2 8.8 %collective-permute-start.38 = (f32[56,384]{1,0:T(8,128)S(1)}, f32[56,384]{1,0:T(8,128)S(1)}, u32[]{:S(2)}, u32[]{:S(2)}) collective-permute-start(f32[56,384]{1,0:T(8,128)S(1)} %get-tuple-element.114), channel_id=1, source_target_pairs={{0,4},{1,5},{2,6},{3,7},{4,0},{5,1},{6,2},{7,3},{8,12},{9,13},{10,... | collective-permute-start | bytes 258056 | tf_op jit(solution)/shard_map/ppermute | solution.py:619
  134.6 16.0 %collective-permute-start.21 = (f32[400,128]{1,0:T(8,128)}, f32[400,128]{1,0:T(8,128)S(1)}, u32[]{:S(2)}, u32[]{:S(2)}) collective-permute-start(f32[400,128]{1,0:T(8,128)} %get-tuple-element.89), channel_id=1, source_target_pairs={{0,9},{1,8},{2,11},{3,10},{4,13},{5,12},{6,15},{7,14},{8,17},{9,16... | collective-permute-start | bytes 614408 | tf_op jit(solution)/shard_map/ppermute | solution.py:628
  134.6 12.7 %collective-permute-start.39 = (f32[56,384]{1,0:T(8,128)S(1)}, f32[56,384]{1,0:T(8,128)S(1)}, u32[]{:S(2)}, u32[]{:S(2)}) collective-permute-start(f32[56,384]{1,0:T(8,128)S(1)} %get-tuple-element.115), channel_id=1, source_target_pairs={{0,6},{1,7},{2,0},{3,1},{4,2},{5,3},{6,4},{7,5},{8,14},{9,15},{10,... | collective-permute-start | bytes 258056 | tf_op jit(solution)/shard_map/ppermute | solution.py:619
  139.6 15.9 %collective-permute-start.22 = (f32[400,128]{1,0:T(8,128)}, f32[400,128]{1,0:T(8,128)}, u32[]{:S(2)}, u32[]{:S(2)}) collective-permute-start(f32[400,128]{1,0:T(8,128)} %get-tuple-element.90), channel_id=1, source_target_pairs={{0,8},{1,9},{2,10},{3,11},{4,12},{5,13},{6,14},{7,15},{8,16},{9,17... | collective-permute-start | bytes 614408 | tf_op jit(solution)/shard_map/ppermute | solution.py:628
  141.3 18.4 %collective-permute-start.17 = (f32[400,128]{1,0:T(8,128)}, f32[400,128]{1,0:T(8,128)}, u32[]{:S(2)}, u32[]{:S(2)}) collective-permute-start(f32[400,128]{1,0:T(8,128)} %get-tuple-element.85), channel_id=1, source_target_pairs={{0,12},{1,13},{2,14},{3,15},{4,8},{5,9},{6,10},{7,11},{8,20},{9,21... | collective-permute-start | bytes 614408 | tf_op jit(solution)/shard_map/ppermute | solution.py:628
  143.0 22.8 %collective-permute-start.18 = (f32[400,128]{1,0:T(8,128)}, f32[400,128]{1,0:T(8,128)}, u32[]{:S(2)}, u32[]{:S(2)}) collective-permute-start(f32[400,128]{1,0:T(8,128)} %get-tuple-element.86), channel_id=1, source_target_pairs={{0,13},{1,12},{2,15},{3,14},{4,9},{5,8},{6,11},{7,10},{8,21},{9,20... | collective-permute-start | bytes 614408 | tf_op jit(solution)/shard_map/ppermute | solution.py:628
  148.0 20.5 %collective-permute-start.15 = (f32[400,128]{1,0:T(8,128)}, f32[400,128]{1,0:T(8,128)}, u32[]{:S(2)}, u32[]{:S(2)}) collective-permute-start(f32[400,128]{1,0:T(8,128)} %get-tuple-element.83), channel_id=1, source_target_pairs={{0,14},{1,15},{2,8},{3,9},{4,10},{5,11},{6,12},{7,13},{8,22},{9,23... | collective-permute-start | bytes 614408 | tf_op jit(solution)/shard_map/ppermute | solution.py:628
  150.7 20.5 %collective-permute-start.40 = (f32[56,384]{1,0:T(8,128)S(1)}, f32[56,384]{1,0:T(8,128)S(1)}, u32[]{:S(2)}, u32[]{:S(2)}) collective-permute-start(f32[56,384]{1,0:T(8,128)S(1)} %shard_map.149.refs_0_), channel_id=1, source_target_pairs={{0,2},{1,3},{2,4},{3,5},{4,6},{5,7},{6,0},{7,1},{8,10},{9,11},{10,... | collective-permute-start | bytes 258056 | tf_op jit(solution)/shard_map/ppermute | solution.py:619
  155.5 41.9 %collective-permute-start.16 = (f32[400,128]{1,0:T(8,128)S(1)}, f32[400,128]{1,0:T(8,128)S(1)}, u32[]{:S(2)}, u32[]{:S(2)}) collective-permute-start(f32[400,128]{1,0:T(8,128)S(1)} %copy-done.42), channel_id=1, source_target_pairs={{0,15},{1,14},{2,9},{3,8},{4,11},{5,10},{6,13},{7,12},{8,23},{9,22... | collective-permute-start | bytes 614408 | tf_op jit(solution)/shard_map/ppermute | solution.py:628
  159.7 39.4 %collective-permute-start.25 = (f32[400,128]{1,0:T(8,128)S(1)}, f32[400,128]{1,0:T(8,128)S(1)}, u32[]{:S(2)}, u32[]{:S(2)}) collective-permute-start(f32[400,128]{1,0:T(8,128)S(1)} %get-tuple-element.95), channel_id=1, source_target_pairs={{0,4},{1,5},{2,6},{3,7},{4,0},{5,1},{6,2},{7,3},{8,12},{9,13},{10,... | collective-permute-start | bytes 614408 | tf_op jit(solution)/shard_map/ppermute | solution.py:619
  165.8 33.8 %collective-permute-start.26 = (f32[400,128]{1,0:T(8,128)S(1)}, f32[400,128]{1,0:T(8,128)S(1)}, u32[]{:S(2)}, u32[]{:S(2)}) collective-permute-start(f32[400,128]{1,0:T(8,128)S(1)} %get-tuple-element.96), channel_id=1, source_target_pairs={{0,5},{1,4},{2,7},{3,6},{4,1},{5,0},{6,3},{7,2},{8,13},{9,12},{10,... | collective-permute-start | bytes 614408 | tf_op jit(solution)/shard_map/ppermute | solution.py:619
  168.5 26.7 %collective-permute-start.41 = (f32[56,384]{1,0:T(8,128)S(1)}, f32[56,384]{1,0:T(8,128)S(1)}, u32[]{:S(2)}, u32[]{:S(2)}) collective-permute-start(f32[56,384]{1,0:T(8,128)S(1)} %shard_map.149.refs_0_), channel_id=1, source_target_pairs={{0,4},{1,5},{2,6},{3,7},{4,0},{5,1},{6,2},{7,3},{8,12},{9,13},{10,... | collective-permute-start | bytes 258056 | tf_op jit(solution)/shard_map/ppermute | solution.py:619
  171.2 23.9 %collective-permute-start.42 = (f32[56,384]{1,0:T(8,128)S(1)}, f32[56,384]{1,0:T(8,128)S(1)}, u32[]{:S(2)}, u32[]{:S(2)}) collective-permute-start(f32[56,384]{1,0:T(8,128)S(1)} %shard_map.149.refs_0_), channel_id=1, source_target_pairs={{0,6},{1,7},{2,0},{3,1},{4,2},{5,3},{6,4},{7,5},{8,14},{9,15},{10,... | collective-permute-start | bytes 258056 | tf_op jit(solution)/shard_map/ppermute | solution.py:619
  195.2 9.7 %collective-permute-start.27 = (f32[400,128]{1,0:T(8,128)S(1)}, f32[400,128]{1,0:T(8,128)S(1)}, u32[]{:S(2)}, u32[]{:S(2)}) collective-permute-start(f32[400,128]{1,0:T(8,128)S(1)} %get-tuple-element.97), channel_id=1, source_target_pairs={{0,2},{1,3},{2,4},{3,5},{4,6},{5,7},{6,0},{7,1},{8,10},{9,11},{10,... | collective-permute-start | bytes 614408 | tf_op jit(solution)/shard_map/ppermute | solution.py:619
  195.2 11.4 %collective-permute-start.28 = (f32[400,128]{1,0:T(8,128)S(1)}, f32[400,128]{1,0:T(8,128)S(1)}, u32[]{:S(2)}, u32[]{:S(2)}) collective-permute-start(f32[400,128]{1,0:T(8,128)S(1)} %get-tuple-element.98), channel_id=1, source_target_pairs={{0,3},{1,2},{2,5},{3,4},{4,7},{5,6},{6,1},{7,0},{8,11},{9,10},{10,... | collective-permute-start | bytes 614408 | tf_op jit(solution)/shard_map/ppermute | solution.py:619
  197.4 12.6 %collective-permute-start.43 = (f32[200,384]{1,0:T(8,128)S(1)}, f32[200,384]{1,0:T(8,128)}, u32[]{:S(2)}, u32[]{:S(2)}) collective-permute-start(f32[200,384]{1,0:T(8,128)S(1)} %shard_map.150.refs_0_), channel_id=1, source_target_pairs={{0,8},{8,0},{16,24},{24,16},{1,9},{9,1},{17,25},{25,17},{2,10},{10... | collective-permute-start | bytes 921608 | tf_op jit(solution)/shard_map/ppermute | solution.py:632
  199.1 16.0 %collective-permute-start.44 = (f32[200,384]{1,0:T(8,128)S(1)}, f32[200,384]{1,0:T(8,128)}, u32[]{:S(2)}, u32[]{:S(2)}) collective-permute-start(f32[200,384]{1,0:T(8,128)S(1)} %shard_map.150.refs_0_), channel_id=1, source_target_pairs={{0,16},{8,24},{16,0},{24,8},{1,17},{9,25},{17,1},{25,9},{2,18},{10... | collective-permute-start | bytes 921608 | tf_op jit(solution)/shard_map/ppermute | solution.py:632
  199.6 15.5 %collective-permute-start.45 = (f32[200,384]{1,0:T(8,128)S(1)}, f32[200,384]{1,0:T(8,128)}, u32[]{:S(2)}, u32[]{:S(2)}) collective-permute-start(f32[200,384]{1,0:T(8,128)S(1)} %shard_map.150.refs_0_), channel_id=1, source_target_pairs={{0,24},{8,16},{16,8},{24,0},{1,25},{9,17},{17,9},{25,1},{2,26},{10... | collective-permute-start | bytes 921608 | tf_op jit(solution)/shard_map/ppermute | solution.py:632
  204.9 3.4 %collective-permute-start.29 = (f32[400,128]{1,0:T(8,128)S(1)}, f32[400,128]{1,0:T(8,128)S(1)}, u32[]{:S(2)}, u32[]{:S(2)}) collective-permute-start(f32[400,128]{1,0:T(8,128)S(1)} %get-tuple-element.99), channel_id=1, source_target_pairs={{0,1},{1,0},{2,3},{3,2},{4,5},{5,4},{6,7},{7,6},{8,9},{9,8},{10,11... | collective-permute-start | bytes 614408 | tf_op jit(solution)/shard_map/ppermute | solution.py:619
  207.3 8.4 %collective-permute-start.23 = (f32[400,128]{1,0:T(8,128)S(1)}, f32[400,128]{1,0:T(8,128)S(1)}, u32[]{:S(2)}, u32[]{:S(2)}) collective-permute-start(f32[400,128]{1,0:T(8,128)S(1)} %get-tuple-element.93), channel_id=1, source_target_pairs={{0,6},{1,7},{2,0},{3,1},{4,2},{5,3},{6,4},{7,5},{8,14},{9,15},{10,... | collective-permute-start | bytes 614408 | tf_op jit(solution)/shard_map/ppermute | solution.py:619
  209.0 23.5 %collective-permute-start.46 = (f32[200,384]{1,0:T(8,128)S(1)}, f32[200,384]{1,0:T(8,128)}, u32[]{:S(2)}, u32[]{:S(2)}) collective-permute-start(f32[200,384]{1,0:T(8,128)S(1)} %shard_map.150.refs_0_), channel_id=1, source_target_pairs={{0,1},{1,0},{2,3},{3,2},{4,5},{5,4},{6,7},{7,6},{8,9},{9,8},{10,11... | collective-permute-start | bytes 921608 | tf_op jit(solution)/shard_map/ppermute | solution.py:619
  210.0 22.5 %collective-permute-start.47 = (f32[200,384]{1,0:T(8,128)}, f32[200,384]{1,0:T(8,128)}, u32[]{:S(2)}, u32[]{:S(2)}) collective-permute-start(f32[200,384]{1,0:T(8,128)} %collective-permute-done.43.refs_1_), channel_id=1, source_target_pairs={{0,1},{1,0},{2,3},{3,2},{4,5},{5,4},{6,7},{7,6},{8,9},{9,8},{10,11... | collective-permute-start | bytes 921608 | tf_op jit(solution)/shard_map/ppermute | solution.py:619
  215.1 17.4 %collective-permute-start.48 = (f32[200,384]{1,0:T(8,128)}, f32[200,384]{1,0:T(8,128)}, u32[]{:S(2)}, u32[]{:S(2)}) collective-permute-start(f32[200,384]{1,0:T(8,128)} %collective-permute-done.44.refs_2_), channel_id=1, source_target_pairs={{0,1},{1,0},{2,3},{3,2},{4,5},{5,4},{6,7},{7,6},{8,9},{9,8},{10,11... | collective-permute-start | bytes 921608 | tf_op jit(solution)/shard_map/ppermute | solution.py:619
  215.1 17.4 %collective-permute-start.49 = (f32[200,384]{1,0:T(8,128)}, f32[200,384]{1,0:T(8,128)}, u32[]{:S(2)}, u32[]{:S(2)}) collective-permute-start(f32[200,384]{1,0:T(8,128)} %collective-permute-done.45.refs_3_), channel_id=1, source_target_pairs={{0,1},{1,0},{2,3},{3,2},{4,5},{5,4},{6,7},{7,6},{8,9},{9,8},{10,11... | collective-permute-start | bytes 921608 | tf_op jit(solution)/shard_map/ppermute | solution.py:619
  216.4 13.0 %collective-permute-start.24 = (f32[400,128]{1,0:T(8,128)}, f32[400,128]{1,0:T(8,128)}, u32[]{:S(2)}, u32[]{:S(2)}) collective-permute-start(f32[400,128]{1,0:T(8,128)} %get-tuple-element.94), channel_id=1, source_target_pairs={{0,7},{1,6},{2,1},{3,0},{4,3},{5,2},{6,5},{7,4},{8,15},{9,14},{10,... | collective-permute-start | bytes 614408 | tf_op jit(solution)/shard_map/ppermute | solution.py:619
  (55 other events, 488.8 us)

commit v8 on v7

--- a/solution.py
+++ b/solution.py
@@ -687,10 +687,7 @@
     loss, grad, table = score_spans(
         edge_count, targets, query_lines, counts, edge_target.reshape(-1, 1)
     )
-    far = early - 2
-    far_parts = table_grads(query_columns, grad, block, far, 2)
-    table_parts = table_grads(query_columns, grad, block, 0, far)
-    table_parts += far_parts
+    table_parts = table_grads(query_columns, grad, block, 0, early)
     table_parts += table_grads(query_columns, grad, block, early, peers - early)
     back = [(-hop[0], hop[1]) for hop in ways]
     home = []

time: 237 us -> 243 us (1.025)
  waiting for transfers between devices: 64.9 us -> 86 us
  starting transfers between devices: 91.8 us -> 76.6 us
    ppermute x28, starting transfers between devices: 52.2 us -> 40.2 us  [sent_on(): lax.ppermute(value, 'shard', [(i, partner(i, hop, peers, 1)) for i in ran...]
    ppermute x16, waiting for transfers between devices: 24.3 us -> 34.9 us  [sent_across(): return lax.ppermute(value, ('group', 'shard'), pairs)]
    ppermute x28, waiting for transfers between devices: 15.9 us -> 24 us  [sent_on(): lax.ppermute(value, 'shard', [(i, partner(i, hop, peers, 1)) for i in ran...]
    ppermute x16, starting transfers between devices: 32.4 us -> 29.3 us  [sent_across(): return lax.ppermute(value, ('group', 'shard'), pairs)]
    pallas_call x3 -> x2, Pallas kernels: 5.81 us -> 5.51 us  [table_grads(): kernel_call(table_grad_kernel, [shape((features, block))] * count, 6 * fe...]
  transfers between devices with their start and end apart: 50 -> 50, of which waited for: 16 -> 17; matrix products, arithmetic and copies ran while one was open for 1% -> 1% of each run, Pallas kernels for 15% -> 14%
where the time goes in v8:
time: 243 us
  waiting for transfers between devices  86 us (35%)
  starting transfers between devices  76.6 us (32%)
  Pallas kernels  57.5 us (24%)
  local copies, waits for them, and re-layouts  20.1 us (8%)
    ppermute x28, starting transfers between devices, sent_on(): lax.ppermute(value, 'shard', [(i, partner(i, hop, peers, 1)) for i in ran...  40.2 us
    ppermute x16, waiting for transfers between devices, sent_across(): return lax.ppermute(value, ('group', 'shard'), pairs)  34.9 us
    ppermute x16, starting transfers between devices, sent_across(): return lax.ppermute(value, ('group', 'shard'), pairs)  29.3 us
    ppermute x6, waiting for transfers between devices, sent_group(): return lax.ppermute(value, 'group', [(g, g ^ bit) for g in range(groups)])  27.2 us
    ppermute x28, waiting for transfers between devices, sent_on(): lax.ppermute(value, 'shard', [(i, partner(i, hop, peers, 1)) for i in ran...  24 us
    unnamed x106, local copies, waits for them, and re-layouts  16.8 us
    pallas_call x1, Pallas kernels, relation_grads(): kernel_call(functools.partial(relation_grad_kernel, steps), [shape((2, fe...  9.17 us
    pallas_call x1, Pallas kernels, query_rows(): kernel_call(query_kernel, [shape((features, edges)), shape((2, features,...  7.26 us
  transfers between devices with their start and end apart: 50, of which 17 were waited for; matrix products, arithmetic and copies ran while one was open for 1% of the time, Pallas kernels for 14%

profile of v8, /device:TPU:0, one launch (start us, length us, event | category | flops | bytes accessed | tf_op | source)
XLA Modules:
  0.0 242.6 jit_solution(13589474366047846867)
XLA Ops:
  0.8 1.1 copy-done.5
  2.7 2.6 %shard_map.134 = (f32[400,128]{1,0:T(8,128)}, f32[400,128]{1,0:T(8,128)}, f32[400,128]{1,0:T(8,128)}, f32[400,128]{1,0:T(8,128)}, f32[400,128]{1,0:T(8,128)}, /*index=5*/f32[400,128]{1,0:T(8,128)S(1)}) custom-call(s32[6]{0:T(128)S(1)} %stack.53.order_ref, f32[400,512]{1,0:T(8,128)S(1)} %bitcast.29, s32[8,128]{1,0:T(8,128)S(1)} %bitcast.39), custom_call_target="tpu_custom_call" | custom-call | flops 943718400 | bytes 2457600 | tf_op jit(solution)/shard_map/pallas_call | solution.py:126
  5.9 4.1 %collective-permute-start.2 = (f32[400,128]{1,0:T(8,128)}, f32[400,128]{1,0:T(8,128)}, u32[]{:S(2)}, u32[]{:S(2)}) collective-permute-start(f32[400,128]{1,0:T(8,128)} %get-tuple-element.62), channel_id=1, source_target_pairs={{0,4},{1,5},{2,6},{3,7},{4,0},{5,1},{6,2},{7,3},{8,12},{9,13},{10,... | collective-permute-start | bytes 614408 | tf_op jit(solution)/shard_map/ppermute | solution.py:619
  10.0 3.1 %collective-permute-start.4 = (f32[400,128]{1,0:T(8,128)}, f32[400,128]{1,0:T(8,128)}, u32[]{:S(2)}, u32[]{:S(2)}) collective-permute-start(f32[400,128]{1,0:T(8,128)} %get-tuple-element.64), channel_id=1, source_target_pairs={{0,6},{1,7},{2,0},{3,1},{4,2},{5,3},{6,4},{7,5},{8,14},{9,15},{10,... | collective-permute-start | bytes 614408 | tf_op jit(solution)/shard_map/ppermute | solution.py:619
  14.0 1.0 shard_map.133
  19.9 5.3 %shard_map.132.refs_1_.rels_ref = f32[400,1024]{1,0:T(8,128)S(1)} custom-call(f32[400,1345]{1,0:T(8,128)S(1)} %bitcast.27, s32[1,1024]{1,0:T(1,128)S(1)} %bitcast.36), custom_call_target="tpu_custom_call" | custom-call | flops 3460300800 | bytes 3276800 | tf_op jit(solution)/shard_map/pallas_call | solution.py:153
  25.3 2.0 shard_map.137
  27.3 6.4 %collective-permute-start = (f32[400,128]{1,0:T(8,128)S(1)}, f32[400,128]{1,0:T(8,128)S(1)}, u32[]{:S(2)}, u32[]{:S(2)}) collective-permute-start(f32[400,128]{1,0:T(8,128)S(1)} %copy-done.46), channel_id=1, source_target_pairs={{0,2},{1,3},{2,4},{3,5},{4,6},{5,7},{6,0},{7,1},{8,10},{9,11},{10,... | collective-permute-start | bytes 614408 | tf_op jit(solution)/shard_map/ppermute | solution.py:619
  33.7 3.9 %collective-permute-start.1 = (f32[400,128]{1,0:T(8,128)S(1)}, f32[400,128]{1,0:T(8,128)S(1)}, u32[]{:S(2)}, u32[]{:S(2)}) collective-permute-start(f32[400,128]{1,0:T(8,128)S(1)} %copy-done.44), channel_id=1, source_target_pairs={{0,3},{1,2},{2,5},{3,4},{4,7},{5,6},{6,1},{7,0},{8,11},{9,10},{10,... | collective-permute-start | bytes 614408 | tf_op jit(solution)/shard_map/ppermute | solution.py:619
  37.6 5.4 %collective-permute-start.10 = (f32[400,128]{1,0:T(8,128)S(1)}, f32[400,128]{1,0:T(8,128)S(1)}, u32[]{:S(2)}, u32[]{:S(2)}) collective-permute-start(f32[400,128]{1,0:T(8,128)S(1)} %get-tuple-element.72), channel_id=1, source_target_pairs={{0,29},{1,28},{2,31},{3,30},{4,25},{5,24},{6,27},{7,26},{8,5},{9,4... | collective-permute-start | bytes 614408 | tf_op jit(solution)/shard_map/ppermute | solution.py:628
  43.0 1.2 collective-permute-start.12
  44.3 1.4 collective-permute-start.13
  45.7 2.4 collective-permute-start.14
  48.1 7.9 %collective-permute-done.10.refs_7_ = f32[400,128]{1,0:T(8,128)S(1)} collective-permute-done((f32[400,128]{1,0:T(8,128)S(1)}, f32[400,128]{1,0:T(8,128)S(1)}, u32[]{:S(2)}, u32[]{:S(2)}) %collective-permute-start.10) | collective-permute-done | bytes 204832 | tf_op jit(solution)/shard_map/ppermute | solution.py:628
  56.0 10.2 %collective-permute-start.7 = (f32[400,128]{1,0:T(8,128)S(1)}, f32[400,128]{1,0:T(8,128)S(1)}, u32[]{:S(2)}, u32[]{:S(2)}) collective-permute-start(f32[400,128]{1,0:T(8,128)S(1)} %get-tuple-element.69), channel_id=1, source_target_pairs={{0,26},{1,27},{2,28},{3,29},{4,30},{5,31},{6,24},{7,25},{8,2},{9,3... | collective-permute-start | bytes 614408 | tf_op jit(solution)/shard_map/ppermute | solution.py:628
  66.2 4.5 %collective-permute-start.9 = (f32[400,128]{1,0:T(8,128)S(1)}, f32[400,128]{1,0:T(8,128)S(1)}, u32[]{:S(2)}, u32[]{:S(2)}) collective-permute-start(f32[400,128]{1,0:T(8,128)S(1)} %get-tuple-element.71), channel_id=1, source_target_pairs={{0,28},{1,29},{2,30},{3,31},{4,24},{5,25},{6,26},{7,27},{8,4},{9,5... | collective-permute-start | bytes 614408 | tf_op jit(solution)/shard_map/ppermute | solution.py:628
  70.7 7.3 %shard_map.135 = (f32[400,1024]{1,0:T(8,128)S(1)}, bf16[2,400,1024]{2,1,0:T(8,128)(2,1)S(1)}, bf16[1024,1200]{1,0:T(8,128)(2,1)S(1)}) custom-call(s32[1,1024]{1,0:T(1,128)S(1)} %bitcast.33, f32[400,1024]{1,0:T(8,128)S(1)} %shard_map.132.refs_1_.rels_ref, f32[400,128]{1,0:T(8,128)S(1)} %collective-permute-done.refs_2_, ...), custom_call_target="tpu_custom_call" | custom-call | flops 2516582400 | bytes 8192000 | tf_op jit(solution)/shard_map/pallas_call | solution.py:221
  78.0 9.4 %collective-permute-done.9.refs_6_ = f32[400,128]{1,0:T(8,128)S(1)} collective-permute-done((f32[400,128]{1,0:T(8,128)S(1)}, f32[400,128]{1,0:T(8,128)S(1)}, u32[]{:S(2)}, u32[]{:S(2)}) %collective-permute-start.9) | collective-permute-done | bytes 204832 | tf_op jit(solution)/shard_map/ppermute | solution.py:628
  87.4 7.0 %shard_map.138 = (f32[1024,1]{1,0:T(8,128)S(1)}, bf16[2,1024,1024]{2,1,0:T(8,128)(2,1)S(1)}, bf16[1200,1024]{1,0:T(8,128)(2,1)S(1)}) custom-call(s32[1]{0:T(128)S(6)} %copy.21.refs_0_, bf16[1024,1200]{1,0:T(8,128)(2,1)S(1)} %get-tuple-element.68.refs_1_, f32[2,1,1024]{2,1,0:T(1,128)S(1)} %shard_map.136.refs_2_, s32[1024,1]{1,0:T(8,128)S(1)} %copy-done.11, ...), custom_call_target="tpu_custom_call" | custom-call | flops 2516582400 | bytes 12288000 | tf_op jit(solution)/shard_map/pallas_call | solution.py:311
  95.2 9.2 %shard_map.139 = (bf16[2,400,1024]{2,1,0:T(8,128)(2,1)S(1)}, f32[200,384]{1,0:T(8,128)S(1)}, f32[200,384]{1,0:T(8,128)S(1)}, f32[200,384]{1,0:T(8,128)S(1)}, f32...) custom-call(s32[2]{0:T(128)S(1)} %pad_add_fusion.me_ref, ...), custom_call_target="tpu_custom_call" | custom-call | flops 4194304000 | bytes 12288000 | tf_op jit(solution)/shard_map/pallas_call | solution.py:428
  107.5 1.6 collective-permute-start.34
  109.6 1.5 collective-permute-start.36
  111.1 2.7 %shard_map.142 = (f32[400,128]{1,0:T(8,128)S(1)}, f32[400,128]{1,0:T(8,128)S(1)}, f32[400,128]{1,0:T(8,128)}, f32[400,128]{1,0:T(8,128)}) custom-call(bf16[2,400,1024]{2,1,0:T(8,128)(2,1)S(1)} %get-tuple-element.82.columns_ref, bf16[2,1024,1024]{2,1,0:T(8,128)(2,1)S(1)} %get-tuple-element.78.grad_ref), custom_call_target="tpu_custom_call" | custom-call | flops 1258291200 | bytes 3735552 | tf_op jit(solution)/shard_map/pallas_call | solution.py:365
  113.8 3.9 %collective-permute-done.34.refs_1_ = f32[200,384]{1,0:T(8,128)S(1)} collective-permute-done((f32[200,384]{1,0:T(8,128)S(1)}, f32[200,384]{1,0:T(8,128)S(1)}, u32[]{:S(2)}, u32[]{:S(2)}) %collective-permute-start.34) | collective-permute-done | bytes 307232 | tf_op jit(solution)/shard_map/ppermute | solution.py:632
  117.7 20.1 %collective-permute-done.35.refs_2_ = f32[200,384]{1,0:T(8,128)S(1)} collective-permute-done((f32[200,384]{1,0:T(8,128)S(1)}, f32[200,384]{1,0:T(8,128)S(1)}, u32[]{:S(2)}, u32[]{:S(2)}) %collective-permute-start.35) | collective-permute-done | bytes 307232 | tf_op jit(solution)/shard_map/ppermute | solution.py:632
  139.0 3.3 %collective-permute-start.39 = (f32[56,384]{1,0:T(8,128)S(1)}, f32[56,384]{1,0:T(8,128)S(1)}, u32[]{:S(2)}, u32[]{:S(2)}) collective-permute-start(f32[56,384]{1,0:T(8,128)S(1)} %get-tuple-element.115), channel_id=1, source_target_pairs={{0,6},{1,7},{2,0},{3,1},{4,2},{5,3},{6,4},{7,5},{8,14},{9,15},{10,... | collective-permute-start | bytes 258056 | tf_op jit(solution)/shard_map/ppermute | solution.py:619
  142.4 2.8 %shard_map.141 = (f32[400,128]{1,0:T(8,128)}, f32[400,128]{1,0:T(8,128)}, f32[400,128]{1,0:T(8,128)}, f32[400,128]{1,0:T(8,128)S(1)}) custom-call(bf16[2,400,1024]{2,1,0:T(8,128)(2,1)S(1)} %get-tuple-element.82.columns_ref, bf16[2,1024,1024]{2,1,0:T(8,128)(2,1)S(1)} %get-tuple-element.78.grad_ref), custom_call_target="tpu_custom_call" | custom-call | flops 1258291200 | bytes 3735552 | tf_op jit(solution)/shard_map/pallas_call | solution.py:365
  146.6 2.0 collective-permute-start.15
  149.3 2.1 collective-permute-start.17
  154.3 1.4 copy-done.3
  155.7 2.1 shard_map.140
  157.8 5.1 %collective-permute-done.22.refs_7_ = f32[400,128]{1,0:T(8,128)} collective-permute-done((f32[400,128]{1,0:T(8,128)}, f32[400,128]{1,0:T(8,128)}, u32[]{:S(2)}, u32[]{:S(2)}) %collective-permute-start.22) | collective-permute-done | bytes 204832 | tf_op jit(solution)/shard_map/ppermute | solution.py:628
  163.0 5.2 %collective-permute-start.25 = (f32[400,128]{1,0:T(8,128)S(1)}, f32[400,128]{1,0:T(8,128)S(1)}, u32[]{:S(2)}, u32[]{:S(2)}) collective-permute-start(f32[400,128]{1,0:T(8,128)S(1)} %get-tuple-element.95), channel_id=1, source_target_pairs={{0,4},{1,5},{2,6},{3,7},{4,0},{5,1},{6,2},{7,3},{8,12},{9,13},{10,... | collective-permute-start | bytes 614408 | tf_op jit(solution)/shard_map/ppermute | solution.py:619
  169.1 12.5 %collective-permute-done.17.refs_2_ = f32[400,128]{1,0:T(8,128)} collective-permute-done((f32[400,128]{1,0:T(8,128)}, f32[400,128]{1,0:T(8,128)}, u32[]{:S(2)}, u32[]{:S(2)}) %collective-permute-start.17) | collective-permute-done | bytes 204832 | tf_op jit(solution)/shard_map/ppermute | solution.py:628
  181.5 3.3 %collective-permute-start.41 = (f32[56,384]{1,0:T(8,128)S(1)}, f32[56,384]{1,0:T(8,128)S(1)}, u32[]{:S(2)}, u32[]{:S(2)}) collective-permute-start(f32[56,384]{1,0:T(8,128)S(1)} %shard_map.148.refs_0_), channel_id=1, source_target_pairs={{0,4},{1,5},{2,6},{3,7},{4,0},{5,1},{6,2},{7,3},{8,12},{9,13},{10,... | collective-permute-start | bytes 258056 | tf_op jit(solution)/shard_map/ppermute | solution.py:619
  184.8 15.1 %collective-permute-done.41.refs_2_ = f32[56,384]{1,0:T(8,128)S(1)} collective-permute-done((f32[56,384]{1,0:T(8,128)S(1)}, f32[56,384]{1,0:T(8,128)S(1)}, u32[]{:S(2)}, u32[]{:S(2)}) %collective-permute-start.41) | collective-permute-done | bytes 86048 | tf_op jit(solution)/shard_map/ppermute | solution.py:619
  202.2 1.3 collective-permute-start.44
  203.5 1.6 collective-permute-start.45
  205.1 4.7 %collective-permute-done.27.refs_4_ = f32[400,128]{1,0:T(8,128)S(1)} collective-permute-done((f32[400,128]{1,0:T(8,128)S(1)}, f32[400,128]{1,0:T(8,128)S(1)}, u32[]{:S(2)}, u32[]{:S(2)}) %collective-permute-start.27) | collective-permute-done | bytes 204832 | tf_op jit(solution)/shard_map/ppermute | solution.py:619
  209.7 1.3 shard_map.144
  212.4 2.1 collective-permute-start.23
  216.0 1.4 collective-permute-done.44.refs_2_
  217.4 1.7 collective-permute-done.45.refs_3_
  219.1 1.1 collective-permute-done.23.refs_0_
  220.9 3.6 %collective-permute-start.24 = (f32[400,128]{1,0:T(8,128)}, f32[400,128]{1,0:T(8,128)}, u32[]{:S(2)}, u32[]{:S(2)}) collective-permute-start(f32[400,128]{1,0:T(8,128)} %get-tuple-element.94), channel_id=1, source_target_pairs={{0,7},{1,6},{2,1},{3,0},{4,3},{5,2},{6,5},{7,4},{8,15},{9,14},{10,... | collective-permute-start | bytes 614408 | tf_op jit(solution)/shard_map/ppermute | solution.py:619
  233.1 2.6 %shard_map.143 = (f32[400,512]{1,0:T(8,128)S(1)}, f32[400,512]{1,0:T(8,128)S(1)}) custom-call(bf16[1024,512]{1,0:T(8,128)(2,1)S(1)} %shard_map.130.hot_ref, bf16[1024,512]{1,0:T(8,128)(2,1)S(1)} %shard_map.131.source_hot_ref.hot_ref, f32[400,128]{1,0:T(8,128)S(1)} %copy-done.17, f32[400,512]{1,0:T(8,128)S(1)} %bitcast.32, ...), custom_call_target="tpu_custom_call" | custom-call | flops 838860800 | bytes 3276800 | tf_op jit(solution)/shard_map/pallas_call | solution.py:488
  235.8 3.0 %shard_map.145 = f32[400,512]{1,0:T(8,128)} custom-call(f32[400,512]{1,0:T(8,128)S(1)} %get-tuple-element.91.other_ref, f32[400,512]{1,0:T(8,128)S(1)} %get-tuple-element.92.entity_ref, f32[1,512]{1,0:T(1,128)S(1)} %bitcast.42, bf16[1024,512]{1,0:T(8,128)(2,1)S(1)} %shard_map.131.source_hot_ref.hot_ref, f32[400,128]{1,0:T(8,128)S(1)} %copy-done.31, ...), custom_call_target="tpu_custom_call" | custom-call | flops 838860800 | bytes 3276800 | tf_op jit(solution)/shard_map/pallas_call | solution.py:509
  238.9 3.7 %shard_map.150 = f32[400,1345]{1,0:T(8,128)} custom-call(s32[2]{0:T(128)S(1)} %pad_add_fusion.me_ref, f32[400,1345]{1,0:T(8,128)S(1)} %bitcast.28, f32[1,1345]{1,0:T(1,128)S(1)} %reshape.36.state_ref, f32[200,384]{1,0:T(8,128)S(1)} %shard_map.149.refs_0_, f32[200,384]{1,0:T(8,128)} %collective-permute-done.43.refs_1_, ...), custom_call_target="tpu_custom_call" | custom-call | flops 4304000 | bytes 6456000 | tf_op jit(solution)/shard_map/pallas_call | solution.py:610
  (196 shorter events, 32.2 us)
Async XLA Ops:
  5.9 21.4 %collective-permute-start.2 = (f32[400,128]{1,0:T(8,128)}, f32[400,128]{1,0:T(8,128)}, u32[]{:S(2)}, u32[]{:S(2)}) collective-permute-start(f32[400,128]{1,0:T(8,128)} %get-tuple-element.62), channel_id=1, source_target_pairs={{0,4},{1,5},{2,6},{3,7},{4,0},{5,1},{6,2},{7,3},{8,12},{9,13},{10,... | collective-permute-start | bytes 614408 | tf_op jit(solution)/shard_map/ppermute | solution.py:619
  10.0 23.8 %collective-permute-start.3 = (f32[400,128]{1,0:T(8,128)}, f32[400,128]{1,0:T(8,128)}, u32[]{:S(2)}, u32[]{:S(2)}) collective-permute-start(f32[400,128]{1,0:T(8,128)} %get-tuple-element.63), channel_id=1, source_target_pairs={{0,5},{1,4},{2,7},{3,6},{4,1},{5,0},{6,3},{7,2},{8,13},{9,12},{10,... | collective-permute-start | bytes 614408 | tf_op jit(solution)/shard_map/ppermute | solution.py:619
  10.0 27.7 %collective-permute-start.4 = (f32[400,128]{1,0:T(8,128)}, f32[400,128]{1,0:T(8,128)}, u32[]{:S(2)}, u32[]{:S(2)}) collective-permute-start(f32[400,128]{1,0:T(8,128)} %get-tuple-element.64), channel_id=1, source_target_pairs={{0,6},{1,7},{2,0},{3,1},{4,2},{5,3},{6,4},{7,5},{8,14},{9,15},{10,... | collective-permute-start | bytes 614408 | tf_op jit(solution)/shard_map/ppermute | solution.py:619
  13.1 30.0 %collective-permute-start.5 = (f32[400,128]{1,0:T(8,128)}, f32[400,128]{1,0:T(8,128)}, u32[]{:S(2)}, u32[]{:S(2)}) collective-permute-start(f32[400,128]{1,0:T(8,128)} %get-tuple-element.65), channel_id=1, source_target_pairs={{0,7},{1,6},{2,1},{3,0},{4,3},{5,2},{6,5},{7,4},{8,15},{9,14},{10,... | collective-permute-start | bytes 614408 | tf_op jit(solution)/shard_map/ppermute | solution.py:619
  13.8 29.2 %collective-permute-start.6 = (f32[400,128]{1,0:T(8,128)}, f32[400,128]{1,0:T(8,128)}, u32[]{:S(2)}, u32[]{:S(2)}) collective-permute-start(f32[400,128]{1,0:T(8,128)} %get-tuple-element.66), channel_id=1, source_target_pairs={{0,1},{1,0},{2,3},{3,2},{4,5},{5,4},{6,7},{7,6},{8,9},{9,8},{10,11... | collective-permute-start | bytes 614408 | tf_op jit(solution)/shard_map/ppermute | solution.py:619
  27.3 17.0 %collective-permute-start = (f32[400,128]{1,0:T(8,128)S(1)}, f32[400,128]{1,0:T(8,128)S(1)}, u32[]{:S(2)}, u32[]{:S(2)}) collective-permute-start(f32[400,128]{1,0:T(8,128)S(1)} %copy-done.46), channel_id=1, source_target_pairs={{0,2},{1,3},{2,4},{3,5},{4,6},{5,7},{6,0},{7,1},{8,10},{9,11},{10,... | collective-permute-start | bytes 614408 | tf_op jit(solution)/shard_map/ppermute | solution.py:619
  33.7 12.0 %collective-permute-start.1 = (f32[400,128]{1,0:T(8,128)S(1)}, f32[400,128]{1,0:T(8,128)S(1)}, u32[]{:S(2)}, u32[]{:S(2)}) collective-permute-start(f32[400,128]{1,0:T(8,128)S(1)} %copy-done.44), channel_id=1, source_target_pairs={{0,3},{1,2},{2,5},{3,4},{4,7},{5,6},{6,1},{7,0},{8,11},{9,10},{10,... | collective-permute-start | bytes 614408 | tf_op jit(solution)/shard_map/ppermute | solution.py:619
  37.6 18.3 %collective-permute-start.10 = (f32[400,128]{1,0:T(8,128)S(1)}, f32[400,128]{1,0:T(8,128)S(1)}, u32[]{:S(2)}, u32[]{:S(2)}) collective-permute-start(f32[400,128]{1,0:T(8,128)S(1)} %get-tuple-element.72), channel_id=1, source_target_pairs={{0,29},{1,28},{2,31},{3,30},{4,25},{5,24},{6,27},{7,26},{8,5},{9,4... | collective-permute-start | bytes 614408 | tf_op jit(solution)/shard_map/ppermute | solution.py:628
  43.0 23.1 %collective-permute-start.11 = (f32[400,128]{1,0:T(8,128)S(1)}, f32[400,128]{1,0:T(8,128)S(1)}, u32[]{:S(2)}, u32[]{:S(2)}) collective-permute-start(f32[400,128]{1,0:T(8,128)S(1)} %get-tuple-element.73), channel_id=1, source_target_pairs={{0,30},{1,31},{2,24},{3,25},{4,26},{5,27},{6,28},{7,29},{8,6},{9,7... | collective-permute-start | bytes 614408 | tf_op jit(solution)/shard_map/ppermute | solution.py:628
  43.0 23.1 %collective-permute-start.12 = (f32[400,128]{1,0:T(8,128)S(1)}, f32[400,128]{1,0:T(8,128)S(1)}, u32[]{:S(2)}, u32[]{:S(2)}) collective-permute-start(f32[400,128]{1,0:T(8,128)S(1)} %get-tuple-element.74), channel_id=1, source_target_pairs={{0,31},{1,30},{2,25},{3,24},{4,27},{5,26},{6,29},{7,28},{8,7},{9,6... | collective-permute-start | bytes 614408 | tf_op jit(solution)/shard_map/ppermute | solution.py:628
  44.3 33.7 %collective-permute-start.13 = (f32[400,128]{1,0:T(8,128)S(1)}, f32[400,128]{1,0:T(8,128)S(1)}, u32[]{:S(2)}, u32[]{:S(2)}) collective-permute-start(f32[400,128]{1,0:T(8,128)S(1)} %get-tuple-element.75), channel_id=1, source_target_pairs={{0,25},{1,24},{2,27},{3,26},{4,29},{5,28},{6,31},{7,30},{8,1},{9,0... | collective-permute-start | bytes 614408 | tf_op jit(solution)/shard_map/ppermute | solution.py:628
  45.7 32.3 %collective-permute-start.14 = (f32[400,128]{1,0:T(8,128)S(1)}, f32[400,128]{1,0:T(8,128)S(1)}, u32[]{:S(2)}, u32[]{:S(2)}) collective-permute-start(f32[400,128]{1,0:T(8,128)S(1)} %get-tuple-element.76), channel_id=1, source_target_pairs={{0,24},{1,25},{2,26},{3,27},{4,28},{5,29},{6,30},{7,31},{8,0},{9,1... | collective-permute-start | bytes 614408 | tf_op jit(solution)/shard_map/ppermute | solution.py:628
  56.0 22.0 %collective-permute-start.7 = (f32[400,128]{1,0:T(8,128)S(1)}, f32[400,128]{1,0:T(8,128)S(1)}, u32[]{:S(2)}, u32[]{:S(2)}) collective-permute-start(f32[400,128]{1,0:T(8,128)S(1)} %get-tuple-element.69), channel_id=1, source_target_pairs={{0,26},{1,27},{2,28},{3,29},{4,30},{5,31},{6,24},{7,25},{8,2},{9,3... | collective-permute-start | bytes 614408 | tf_op jit(solution)/shard_map/ppermute | solution.py:628
  66.2 11.8 %collective-permute-start.8 = (f32[400,128]{1,0:T(8,128)S(1)}, f32[400,128]{1,0:T(8,128)S(1)}, u32[]{:S(2)}, u32[]{:S(2)}) collective-permute-start(f32[400,128]{1,0:T(8,128)S(1)} %get-tuple-element.70), channel_id=1, source_target_pairs={{0,27},{1,26},{2,29},{3,28},{4,31},{5,30},{6,25},{7,24},{8,3},{9,2... | collective-permute-start | bytes 614408 | tf_op jit(solution)/shard_map/ppermute | solution.py:628
  66.2 21.2 %collective-permute-start.9 = (f32[400,128]{1,0:T(8,128)S(1)}, f32[400,128]{1,0:T(8,128)S(1)}, u32[]{:S(2)}, u32[]{:S(2)}) collective-permute-start(f32[400,128]{1,0:T(8,128)S(1)} %get-tuple-element.71), channel_id=1, source_target_pairs={{0,28},{1,29},{2,30},{3,31},{4,24},{5,25},{6,26},{7,27},{8,4},{9,5... | collective-permute-start | bytes 614408 | tf_op jit(solution)/shard_map/ppermute | solution.py:628
  104.5 2.0 collective-permute-start.31
  105.0 2.3 collective-permute-start.33
  107.5 10.2 %collective-permute-start.34 = (f32[200,384]{1,0:T(8,128)S(1)}, f32[200,384]{1,0:T(8,128)S(1)}, u32[]{:S(2)}, u32[]{:S(2)}) collective-permute-start(f32[200,384]{1,0:T(8,128)S(1)} %get-tuple-element.109), channel_id=1, source_target_pairs={{0,8},{8,0},{16,24},{24,16},{1,9},{9,1},{17,25},{25,17},{2,10},{10... | collective-permute-start | bytes 921608 | tf_op jit(solution)/shard_map/ppermute | solution.py:632
  109.1 28.8 %collective-permute-start.35 = (f32[200,384]{1,0:T(8,128)S(1)}, f32[200,384]{1,0:T(8,128)S(1)}, u32[]{:S(2)}, u32[]{:S(2)}) collective-permute-start(f32[200,384]{1,0:T(8,128)S(1)} %get-tuple-element.110), channel_id=1, source_target_pairs={{0,16},{8,24},{16,0},{24,8},{1,17},{9,25},{17,1},{25,9},{2,18},{10... | collective-permute-start | bytes 921608 | tf_op jit(solution)/shard_map/ppermute | solution.py:632
  109.6 28.3 %collective-permute-start.36 = (f32[200,384]{1,0:T(8,128)S(1)}, f32[200,384]{1,0:T(8,128)S(1)}, u32[]{:S(2)}, u32[]{:S(2)}) collective-permute-start(f32[200,384]{1,0:T(8,128)S(1)} %get-tuple-element.111), channel_id=1, source_target_pairs={{0,24},{8,16},{16,8},{24,0},{1,25},{9,17},{17,9},{25,1},{2,26},{10... | collective-permute-start | bytes 921608 | tf_op jit(solution)/shard_map/ppermute | solution.py:632
  113.8 25.2 %collective-permute-start.19 = (f32[400,128]{1,0:T(8,128)S(1)}, f32[400,128]{1,0:T(8,128)S(1)}, u32[]{:S(2)}, u32[]{:S(2)}) collective-permute-start(f32[400,128]{1,0:T(8,128)S(1)} %get-tuple-element.87), channel_id=1, source_target_pairs={{0,10},{1,11},{2,12},{3,13},{4,14},{5,15},{6,8},{7,9},{8,18},{9,19... | collective-permute-start | bytes 614408 | tf_op jit(solution)/shard_map/ppermute | solution.py:628
  113.8 32.1 %collective-permute-start.20 = (f32[400,128]{1,0:T(8,128)S(1)}, f32[400,128]{1,0:T(8,128)S(1)}, u32[]{:S(2)}, u32[]{:S(2)}) collective-permute-start(f32[400,128]{1,0:T(8,128)S(1)} %get-tuple-element.88), channel_id=1, source_target_pairs={{0,11},{1,10},{2,13},{3,12},{4,15},{5,14},{6,9},{7,8},{8,19},{9,18... | collective-permute-start | bytes 614408 | tf_op jit(solution)/shard_map/ppermute | solution.py:628
  117.7 35.8 %collective-permute-start.21 = (f32[400,128]{1,0:T(8,128)}, f32[400,128]{1,0:T(8,128)S(1)}, u32[]{:S(2)}, u32[]{:S(2)}) collective-permute-start(f32[400,128]{1,0:T(8,128)} %get-tuple-element.89), channel_id=1, source_target_pairs={{0,9},{1,8},{2,11},{3,10},{4,13},{5,12},{6,15},{7,14},{8,17},{9,16... | collective-permute-start | bytes 614408 | tf_op jit(solution)/shard_map/ppermute | solution.py:628
  138.5 8.1 %collective-permute-start.37 = (f32[56,384]{1,0:T(8,128)S(1)}, f32[56,384]{1,0:T(8,128)S(1)}, u32[]{:S(2)}, u32[]{:S(2)}) collective-permute-start(f32[56,384]{1,0:T(8,128)S(1)} %get-tuple-element.113), channel_id=1, source_target_pairs={{0,2},{1,3},{2,4},{3,5},{4,6},{5,7},{6,0},{7,1},{8,10},{9,11},{10,... | collective-permute-start | bytes 258056 | tf_op jit(solution)/shard_map/ppermute | solution.py:619
  138.6 10.1 %collective-permute-start.38 = (f32[56,384]{1,0:T(8,128)S(1)}, f32[56,384]{1,0:T(8,128)S(1)}, u32[]{:S(2)}, u32[]{:S(2)}) collective-permute-start(f32[56,384]{1,0:T(8,128)S(1)} %get-tuple-element.114), channel_id=1, source_target_pairs={{0,4},{1,5},{2,6},{3,7},{4,0},{5,1},{6,2},{7,3},{8,12},{9,13},{10,... | collective-permute-start | bytes 258056 | tf_op jit(solution)/shard_map/ppermute | solution.py:619
  139.0 9.6 %collective-permute-start.39 = (f32[56,384]{1,0:T(8,128)S(1)}, f32[56,384]{1,0:T(8,128)S(1)}, u32[]{:S(2)}, u32[]{:S(2)}) collective-permute-start(f32[56,384]{1,0:T(8,128)S(1)} %get-tuple-element.115), channel_id=1, source_target_pairs={{0,6},{1,7},{2,0},{3,1},{4,2},{5,3},{6,4},{7,5},{8,14},{9,15},{10,... | collective-permute-start | bytes 258056 | tf_op jit(solution)/shard_map/ppermute | solution.py:619
  146.6 16.4 %collective-permute-start.22 = (f32[400,128]{1,0:T(8,128)}, f32[400,128]{1,0:T(8,128)}, u32[]{:S(2)}, u32[]{:S(2)}) collective-permute-start(f32[400,128]{1,0:T(8,128)} %get-tuple-element.90), channel_id=1, source_target_pairs={{0,8},{1,9},{2,10},{3,11},{4,12},{5,13},{6,14},{7,15},{8,16},{9,17... | collective-permute-start | bytes 614408 | tf_op jit(solution)/shard_map/ppermute | solution.py:628
  146.6 16.4 %collective-permute-start.15 = (f32[400,128]{1,0:T(8,128)}, f32[400,128]{1,0:T(8,128)}, u32[]{:S(2)}, u32[]{:S(2)}) collective-permute-start(f32[400,128]{1,0:T(8,128)} %get-tuple-element.83), channel_id=1, source_target_pairs={{0,14},{1,15},{2,8},{3,9},{4,10},{5,11},{6,12},{7,13},{8,22},{9,23... | collective-permute-start | bytes 614408 | tf_op jit(solution)/shard_map/ppermute | solution.py:628
  148.6 19.6 %collective-permute-start.16 = (f32[400,128]{1,0:T(8,128)}, f32[400,128]{1,0:T(8,128)}, u32[]{:S(2)}, u32[]{:S(2)}) collective-permute-start(f32[400,128]{1,0:T(8,128)} %get-tuple-element.84), channel_id=1, source_target_pairs={{0,15},{1,14},{2,9},{3,8},{4,11},{5,10},{6,13},{7,12},{8,23},{9,22... | collective-permute-start | bytes 614408 | tf_op jit(solution)/shard_map/ppermute | solution.py:628
  149.3 32.2 %collective-permute-start.17 = (f32[400,128]{1,0:T(8,128)}, f32[400,128]{1,0:T(8,128)}, u32[]{:S(2)}, u32[]{:S(2)}) collective-permute-start(f32[400,128]{1,0:T(8,128)} %get-tuple-element.85), channel_id=1, source_target_pairs={{0,12},{1,13},{2,14},{3,15},{4,8},{5,9},{6,10},{7,11},{8,20},{9,21... | collective-permute-start | bytes 614408 | tf_op jit(solution)/shard_map/ppermute | solution.py:628
  153.5 31.3 %collective-permute-start.40 = (f32[56,384]{1,0:T(8,128)S(1)}, f32[56,384]{1,0:T(8,128)S(1)}, u32[]{:S(2)}, u32[]{:S(2)}) collective-permute-start(f32[56,384]{1,0:T(8,128)S(1)} %shard_map.148.refs_0_), channel_id=1, source_target_pairs={{0,2},{1,3},{2,4},{3,5},{4,6},{5,7},{6,0},{7,1},{8,10},{9,11},{10,... | collective-permute-start | bytes 258056 | tf_op jit(solution)/shard_map/ppermute | solution.py:619
  163.0 38.5 %collective-permute-start.18 = (f32[400,128]{1,0:T(8,128)S(1)}, f32[400,128]{1,0:T(8,128)S(1)}, u32[]{:S(2)}, u32[]{:S(2)}) collective-permute-start(f32[400,128]{1,0:T(8,128)S(1)} %copy-done.42), channel_id=1, source_target_pairs={{0,13},{1,12},{2,15},{3,14},{4,9},{5,8},{6,11},{7,10},{8,21},{9,20... | collective-permute-start | bytes 614408 | tf_op jit(solution)/shard_map/ppermute | solution.py:628
  163.0 39.2 %collective-permute-start.25 = (f32[400,128]{1,0:T(8,128)S(1)}, f32[400,128]{1,0:T(8,128)S(1)}, u32[]{:S(2)}, u32[]{:S(2)}) collective-permute-start(f32[400,128]{1,0:T(8,128)S(1)} %get-tuple-element.95), channel_id=1, source_target_pairs={{0,4},{1,5},{2,6},{3,7},{4,0},{5,1},{6,2},{7,3},{8,12},{9,13},{10,... | collective-permute-start | bytes 614408 | tf_op jit(solution)/shard_map/ppermute | solution.py:619
  168.2 35.3 %collective-permute-start.26 = (f32[400,128]{1,0:T(8,128)S(1)}, f32[400,128]{1,0:T(8,128)S(1)}, u32[]{:S(2)}, u32[]{:S(2)}) collective-permute-start(f32[400,128]{1,0:T(8,128)S(1)} %get-tuple-element.96), channel_id=1, source_target_pairs={{0,5},{1,4},{2,7},{3,6},{4,1},{5,0},{6,3},{7,2},{8,13},{9,12},{10,... | collective-permute-start | bytes 614408 | tf_op jit(solution)/shard_map/ppermute | solution.py:619
  181.5 18.4 %collective-permute-start.41 = (f32[56,384]{1,0:T(8,128)S(1)}, f32[56,384]{1,0:T(8,128)S(1)}, u32[]{:S(2)}, u32[]{:S(2)}) collective-permute-start(f32[56,384]{1,0:T(8,128)S(1)} %shard_map.148.refs_0_), channel_id=1, source_target_pairs={{0,4},{1,5},{2,6},{3,7},{4,0},{5,1},{6,2},{7,3},{8,12},{9,13},{10,... | collective-permute-start | bytes 258056 | tf_op jit(solution)/shard_map/ppermute | solution.py:619
  184.8 16.0 %collective-permute-start.42 = (f32[56,384]{1,0:T(8,128)S(1)}, f32[56,384]{1,0:T(8,128)S(1)}, u32[]{:S(2)}, u32[]{:S(2)}) collective-permute-start(f32[56,384]{1,0:T(8,128)S(1)} %shard_map.148.refs_0_), channel_id=1, source_target_pairs={{0,6},{1,7},{2,0},{3,1},{4,2},{5,3},{6,4},{7,5},{8,14},{9,15},{10,... | collective-permute-start | bytes 258056 | tf_op jit(solution)/shard_map/ppermute | solution.py:619
  200.0 9.7 %collective-permute-start.27 = (f32[400,128]{1,0:T(8,128)S(1)}, f32[400,128]{1,0:T(8,128)S(1)}, u32[]{:S(2)}, u32[]{:S(2)}) collective-permute-start(f32[400,128]{1,0:T(8,128)S(1)} %get-tuple-element.97), channel_id=1, source_target_pairs={{0,2},{1,3},{2,4},{3,5},{4,6},{5,7},{6,0},{7,1},{8,10},{9,11},{10,... | collective-permute-start | bytes 614408 | tf_op jit(solution)/shard_map/ppermute | solution.py:619
  200.9 10.8 %collective-permute-start.28 = (f32[400,128]{1,0:T(8,128)S(1)}, f32[400,128]{1,0:T(8,128)S(1)}, u32[]{:S(2)}, u32[]{:S(2)}) collective-permute-start(f32[400,128]{1,0:T(8,128)S(1)} %get-tuple-element.98), channel_id=1, source_target_pairs={{0,3},{1,2},{2,5},{3,4},{4,7},{5,6},{6,1},{7,0},{8,11},{9,10},{10,... | collective-permute-start | bytes 614408 | tf_op jit(solution)/shard_map/ppermute | solution.py:619
  201.5 14.5 %collective-permute-start.43 = (f32[200,384]{1,0:T(8,128)S(1)}, f32[200,384]{1,0:T(8,128)}, u32[]{:S(2)}, u32[]{:S(2)}) collective-permute-start(f32[200,384]{1,0:T(8,128)S(1)} %shard_map.149.refs_0_), channel_id=1, source_target_pairs={{0,8},{8,0},{16,24},{24,16},{1,9},{9,1},{17,25},{25,17},{2,10},{10... | collective-permute-start | bytes 921608 | tf_op jit(solution)/shard_map/ppermute | solution.py:632
  202.2 15.2 %collective-permute-start.44 = (f32[200,384]{1,0:T(8,128)S(1)}, f32[200,384]{1,0:T(8,128)}, u32[]{:S(2)}, u32[]{:S(2)}) collective-permute-start(f32[200,384]{1,0:T(8,128)S(1)} %shard_map.149.refs_0_), channel_id=1, source_target_pairs={{0,16},{8,24},{16,0},{24,8},{1,17},{9,25},{17,1},{25,9},{2,18},{10... | collective-permute-start | bytes 921608 | tf_op jit(solution)/shard_map/ppermute | solution.py:632
  203.5 15.6 %collective-permute-start.45 = (f32[200,384]{1,0:T(8,128)S(1)}, f32[200,384]{1,0:T(8,128)}, u32[]{:S(2)}, u32[]{:S(2)}) collective-permute-start(f32[200,384]{1,0:T(8,128)S(1)} %shard_map.149.refs_0_), channel_id=1, source_target_pairs={{0,24},{8,16},{16,8},{24,0},{1,25},{9,17},{17,9},{25,1},{2,26},{10... | collective-permute-start | bytes 921608 | tf_op jit(solution)/shard_map/ppermute | solution.py:632
  209.7 4.8 %collective-permute-start.29 = (f32[400,128]{1,0:T(8,128)S(1)}, f32[400,128]{1,0:T(8,128)S(1)}, u32[]{:S(2)}, u32[]{:S(2)}) collective-permute-start(f32[400,128]{1,0:T(8,128)S(1)} %get-tuple-element.99), channel_id=1, source_target_pairs={{0,1},{1,0},{2,3},{3,2},{4,5},{5,4},{6,7},{7,6},{8,9},{9,8},{10,11... | collective-permute-start | bytes 614408 | tf_op jit(solution)/shard_map/ppermute | solution.py:619
  212.4 7.9 %collective-permute-start.23 = (f32[400,128]{1,0:T(8,128)S(1)}, f32[400,128]{1,0:T(8,128)S(1)}, u32[]{:S(2)}, u32[]{:S(2)}) collective-permute-start(f32[400,128]{1,0:T(8,128)S(1)} %get-tuple-element.93), channel_id=1, source_target_pairs={{0,6},{1,7},{2,0},{3,1},{4,2},{5,3},{6,4},{7,5},{8,14},{9,15},{10,... | collective-permute-start | bytes 614408 | tf_op jit(solution)/shard_map/ppermute | solution.py:619
  215.2 23.7 %collective-permute-start.46 = (f32[200,384]{1,0:T(8,128)S(1)}, f32[200,384]{1,0:T(8,128)}, u32[]{:S(2)}, u32[]{:S(2)}) collective-permute-start(f32[200,384]{1,0:T(8,128)S(1)} %shard_map.149.refs_0_), channel_id=1, source_target_pairs={{0,1},{1,0},{2,3},{3,2},{4,5},{5,4},{6,7},{7,6},{8,9},{9,8},{10,11... | collective-permute-start | bytes 921608 | tf_op jit(solution)/shard_map/ppermute | solution.py:619
  216.0 22.9 %collective-permute-start.47 = (f32[200,384]{1,0:T(8,128)}, f32[200,384]{1,0:T(8,128)}, u32[]{:S(2)}, u32[]{:S(2)}) collective-permute-start(f32[200,384]{1,0:T(8,128)} %collective-permute-done.43.refs_1_), channel_id=1, source_target_pairs={{0,1},{1,0},{2,3},{3,2},{4,5},{5,4},{6,7},{7,6},{8,9},{9,8},{10,11... | collective-permute-start | bytes 921608 | tf_op jit(solution)/shard_map/ppermute | solution.py:619
  217.4 21.4 %collective-permute-start.48 = (f32[200,384]{1,0:T(8,128)}, f32[200,384]{1,0:T(8,128)}, u32[]{:S(2)}, u32[]{:S(2)}) collective-permute-start(f32[200,384]{1,0:T(8,128)} %collective-permute-done.44.refs_2_), channel_id=1, source_target_pairs={{0,1},{1,0},{2,3},{3,2},{4,5},{5,4},{6,7},{7,6},{8,9},{9,8},{10,11... | collective-permute-start | bytes 921608 | tf_op jit(solution)/shard_map/ppermute | solution.py:619
  219.1 19.8 %collective-permute-start.49 = (f32[200,384]{1,0:T(8,128)}, f32[200,384]{1,0:T(8,128)}, u32[]{:S(2)}, u32[]{:S(2)}) collective-permute-start(f32[200,384]{1,0:T(8,128)} %collective-permute-done.45.refs_3_), channel_id=1, source_target_pairs={{0,1},{1,0},{2,3},{3,2},{4,5},{5,4},{6,7},{7,6},{8,9},{9,8},{10,11... | collective-permute-start | bytes 921608 | tf_op jit(solution)/shard_map/ppermute | solution.py:619
  220.9 14.8 %collective-permute-start.24 = (f32[400,128]{1,0:T(8,128)}, f32[400,128]{1,0:T(8,128)}, u32[]{:S(2)}, u32[]{:S(2)}) collective-permute-start(f32[400,128]{1,0:T(8,128)} %get-tuple-element.94), channel_id=1, source_target_pairs={{0,7},{1,6},{2,1},{3,0},{4,3},{5,2},{6,5},{7,4},{8,15},{9,14},{10,... | collective-permute-start | bytes 614408 | tf_op jit(solution)/shard_map/ppermute | solution.py:619
  (55 other events, 497.9 us)
